TPU v7x, 32 devices: a whole 2x2x4 slice. The times are simulated.
32 devices in a mesh: batch: 8 (over z, y), head: 4 (over x, core).
Axes of the slice: x: 2, y: 2, z: 4, core: 2. Of those that a mesh axis runs over, the one named last changes fastest.
Arguments:
- inputs: bfloat16 [16384, 768], P(('batch', 'head')), may hold values from -6 to 6
- lengths: int32 [8, 8], P('batch'), may hold values from 1 to 1024, 2048 in all within a row
- cotangent: bfloat16 [16384, 768], P(('batch', 'head')), may hold values from -6 to 6
- gain_attn: float32 [768], replicated, may hold values from 0.1 to 1.9
- shift_attn: float32 [768], replicated, may hold values from -2 to 2
- weight_qkv: bfloat16 [768, 12, 192], P(None, 'head'), may hold values from -0.21875 to 0.21875
- bias_qkv: float32 [12, 192], P('head'), may hold values from -3 to 3
- weight_proj: bfloat16 [12, 64, 768], P('head'), may hold values from -1.75 to 1.75
- bias_proj: float32 [768], replicated, may hold values from -2 to 2
- gain_mlp: float32 [768], replicated, may hold values from 0.1 to 1.9
- shift_mlp: float32 [768], replicated, may hold values from -2 to 2
- weight_up: bfloat16 [768, 3072], P(None, 'head'), may hold values from -0.21875 to 0.21875
- bias_up: float32 [3072], P('head'), may hold values from -2 to 2
- weight_down: bfloat16 [3072, 768], P('head'), may hold values from -0.109375 to 0.109375
- bias_down: float32 [768], replicated, may hold values from -2 to 2
Outputs:
- output: bfloat16 [16384, 768], P(('batch', 'head'))
- grad_inputs: bfloat16 [16384, 768], P(('batch', 'head'))
- grad_gain_attn: float32 [768], replicated
- grad_shift_attn: float32 [768], replicated
- grad_weight_qkv: float32 [768, 12, 192], P(None, 'head')
- grad_bias_qkv: float32 [12, 192], P('head')
- grad_weight_proj: float32 [12, 64, 768], P('head')
- grad_bias_proj: float32 [768], replicated
- grad_gain_mlp: float32 [768], replicated
- grad_shift_mlp: float32 [768], replicated
- grad_weight_up: float32 [768, 3072], P(None, 'head')
- grad_bias_up: float32 [3072], P('head')
- grad_weight_down: float32 [3072, 768], P('head')
- grad_bias_down: float32 [768], replicated
Inputs may be any that keep to these rules, and one draw needn't show every extreme that they name: `lengths`: in each row the 8 entries sum to 2048; the last one counts the pad rows at the group's end; the largest entry of every row is exactly 1024.
All inputs are finite; a program needn't handle non-finite values.
Results may differ from a plain program's by a relative error of at most 0.013.
The roundings to bfloat16 on the way count: a program that leaves them out, or rounds other values in their place, can miss the bound.
Values may be sent and summed in bfloat16 or wider, within the bound.
No kernel may reach another device: no remote copies, remote signals or barrier semaphores. Data moves between devices by JAX's collectives and lax.ppermute only.
A program may use at most 192 MiB of HBM per device.

v0:
```python
import math

import jax
import jax.numpy as jnp
from jax import lax
from jax.sharding import PartitionSpec as P

QBLK = 512


epsilon = 1e-05
floor_value = -1e30


def layer_norm(value, gain, shift):
    center = value - jnp.mean(value, axis=-1, keepdims=True)
    spread = jnp.mean(center * center, axis=-1, keepdims=True)
    return center * lax.rsqrt(spread + epsilon) * gain + shift


def gelu_tanh(value):
    return jax.nn.gelu(value, approximate=True)


def segment_ids(row, count):
    ends = jnp.cumsum(row)
    places = jnp.arange(count, dtype=jnp.int32)
    return jnp.sum((places[:, None] >= ends[None, :]).astype(jnp.int32), axis=1)


def block_mask(segment, row_start, query_count, key_count, pad_segment):
    query_place = row_start + jnp.arange(query_count, dtype=jnp.int32)
    key_place = jnp.arange(key_count, dtype=jnp.int32)
    query_seg = segment[row_start : row_start + query_count]
    key_seg = segment[:key_count]
    return (
        (query_seg[:, None] == key_seg[None, :])
        & (key_place[None, :] <= query_place[:, None])
        & ((query_seg[:, None] < pad_segment) | (key_place[None, :] == query_place[:, None]))
    )


def block_scores(queries, key_rows, allowed, score_scale):
    scores_raw = (
        jnp.einsum("qhd,khd->hqk", queries, key_rows, preferred_element_type=jnp.float32)
        * score_scale
    )
    magnitude = jnp.where(allowed[None], jnp.abs(scores_raw), floor_value)
    return (scores_raw, magnitude)


def signed_weights(scores_raw, allowed, exponent, row_top, row_total):
    offset = jnp.where(allowed[None], jnp.exp(-row_top), 0.0)
    return jnp.sign(scores_raw) * ((exponent - offset) / row_total)


def contract_rows(left, right):
    return lax.dot_general(
        left, right, (((0,), (0,)), ((), ())), preferred_element_type=jnp.float32
    )


def contract_cols(left, right):
    return lax.dot_general(
        left, right, (((1,), (1,)), ((), ())), preferred_element_type=jnp.float32
    )


def per_device(
    inputs,
    lengths,
    cotangent,
    gain_attn,
    shift_attn,
    weight_qkv,
    bias_qkv,
    weight_proj,
    bias_proj,
    gain_mlp,
    shift_mlp,
    weight_up,
    bias_up,
    weight_down,
    bias_down,
):
    row_count = inputs.shape[0]
    head_count = lax.axis_size("head")
    group_rows = row_count * head_count
    own_start = lax.axis_index("head") * row_count
    model_width = inputs.shape[1]
    local_heads = weight_qkv.shape[1]
    triple_width = weight_qkv.shape[2]
    head_width = triple_width // 3
    score_scale = 1.0 / math.sqrt(head_width)
    pad_segment = lengths.shape[1] - 1
    segment = segment_ids(lengths[0], group_rows)
    own_segment = lax.dynamic_slice_in_dim(segment, own_start, row_count)
    live = (own_segment < pad_segment).astype(jnp.float32)[:, None]
    qkv_matrix = weight_qkv.reshape(model_width, local_heads * triple_width)
    proj_matrix = weight_proj.reshape(local_heads * head_width, model_width)
    tokens_own = inputs.astype(jnp.float32)
    norm_one = layer_norm(tokens_own, gain_attn, shift_attn)
    h_one = lax.all_gather(norm_one.astype(jnp.bfloat16), "head", axis=0, tiled=True)
    packed = (
        jnp.dot(h_one, qkv_matrix, preferred_element_type=jnp.float32)
        + bias_qkv.reshape(local_heads * triple_width)
    ).astype(jnp.bfloat16)
    split = packed.reshape(group_rows, local_heads, 3, head_width)
    queries = split[:, :, 0]
    key_rows = split[:, :, 1]
    values = split[:, :, 2]
    block_rows = QBLK
    block_count = group_rows // block_rows
    row_tops = []
    row_totals = []
    outputs = []
    for block_index in range(block_count):
        row_start = block_index * block_rows
        row_stop = row_start + block_rows
        allowed = block_mask(segment, row_start, block_rows, row_stop, pad_segment)
        scores_raw, magnitude = block_scores(
            queries[row_start:row_stop], key_rows[:row_stop], allowed, score_scale
        )
        row_top = jnp.max(magnitude, axis=2, keepdims=True)
        exponent = jnp.where(allowed[None], jnp.exp(magnitude - row_top), 0.0)
        row_total = jnp.sum(exponent, axis=2, keepdims=True)
        weights = signed_weights(scores_raw, allowed, exponent, row_top, row_total).astype(
            jnp.bfloat16
        )
        outputs.append(
            jnp.einsum(
                "hqk,khd->qhd", weights, values[:row_stop], preferred_element_type=jnp.float32
            )
        )
        row_tops.append(row_top)
        row_totals.append(row_total)
    merged = (
        jnp.concatenate(outputs, axis=0)
        .reshape(group_rows, local_heads * head_width)
        .astype(jnp.bfloat16)
    )
    attended = lax.psum_scatter(
        jnp.dot(merged, proj_matrix, preferred_element_type=jnp.float32),
        "head",
        scatter_dimension=0,
        tiled=True,
    )
    resid = tokens_own + attended + bias_proj
    norm_two = layer_norm(resid, gain_mlp, shift_mlp)
    h_two = lax.all_gather(norm_two.astype(jnp.bfloat16), "head", axis=0, tiled=True)
    hidden_pre = jnp.dot(h_two, weight_up, preferred_element_type=jnp.float32) + bias_up
    hidden_act = gelu_tanh(hidden_pre).astype(jnp.bfloat16)
    down_own = lax.psum_scatter(
        jnp.dot(hidden_act, weight_down, preferred_element_type=jnp.float32).astype(jnp.bfloat16),
        "head",
        scatter_dimension=0,
        tiled=True,
    ).astype(jnp.float32)
    output = (resid + down_own + bias_down).astype(jnp.bfloat16)
    grad_own = cotangent.astype(jnp.float32) * live
    grad_full = lax.all_gather(grad_own.astype(jnp.bfloat16), "head", axis=0, tiled=True)
    grad_act = contract_cols(grad_full, weight_down)
    grad_wdown = contract_rows(hidden_act, grad_full)
    gelu_value, gelu_pull = jax.vjp(gelu_tanh, hidden_pre)
    grad_up = gelu_pull(grad_act)[0].astype(jnp.bfloat16)
    grad_bup = jnp.sum(grad_up.astype(jnp.float32), axis=0)
    grad_wup = contract_rows(h_two, grad_up)
    grad_norm_two = lax.psum_scatter(
        contract_cols(grad_up, weight_up), "head", scatter_dimension=0, tiled=True
    )
    norm_value, norm_pull = jax.vjp(layer_norm, resid, gain_mlp, shift_mlp)
    grad_resid_norm, grad_gmlp, grad_smlp = norm_pull(grad_norm_two)
    grad_resid = grad_own + grad_resid_norm
    grad_bdown = jnp.sum(grad_own, axis=0)
    grad_bproj = jnp.sum(grad_resid, axis=0)
    grad_att = lax.all_gather(grad_resid.astype(jnp.bfloat16), "head", axis=0, tiled=True)
    grad_wproj = contract_rows(merged, grad_att).reshape(local_heads, head_width, model_width)
    grad_merged = (
        contract_cols(grad_att, proj_matrix)
        .astype(jnp.bfloat16)
        .reshape(group_rows, local_heads, head_width)
    )
    grad_query = []
    grad_key = jnp.zeros((group_rows, local_heads, head_width), jnp.float32)
    grad_value = jnp.zeros((group_rows, local_heads, head_width), jnp.float32)
    for block_index in range(block_count):
        row_start = block_index * block_rows
        row_stop = row_start + block_rows
        allowed = block_mask(segment, row_start, block_rows, row_stop, pad_segment)
        query_block = queries[row_start:row_stop]
        scores_raw, magnitude = block_scores(query_block, key_rows[:row_stop], allowed, score_scale)
        exponent = jnp.where(allowed[None], jnp.exp(magnitude - row_tops[block_index]), 0.0)
        probability = exponent / row_totals[block_index]
        signs = jnp.sign(scores_raw)
        weights_exact = signed_weights(
            scores_raw, allowed, exponent, row_tops[block_index], row_totals[block_index]
        )
        weights = weights_exact.astype(jnp.bfloat16)
        grad_block = grad_merged[row_start:row_stop]
        grad_weights = jnp.einsum(
            "qhd,khd->hqk", grad_block, values[:row_stop], preferred_element_type=jnp.float32
        )
        inner = jnp.sum(grad_weights * weights_exact, axis=2, keepdims=True)
        grad_scores = (probability * (grad_weights - signs * inner)).astype(jnp.bfloat16)
        grad_query.append(
            jnp.einsum(
                "hqk,khd->qhd", grad_scores, key_rows[:row_stop], preferred_element_type=jnp.float32
            )
            * score_scale
        )
        grad_key = grad_key.at[:row_stop].add(
            jnp.einsum("hqk,qhd->khd", grad_scores, query_block, preferred_element_type=jnp.float32)
            * score_scale
        )
        grad_value = grad_value.at[:row_stop].add(
            jnp.einsum("hqk,qhd->khd", weights, grad_block, preferred_element_type=jnp.float32)
        )
    grad_packed = jnp.stack((jnp.concatenate(grad_query, axis=0), grad_key, grad_value), axis=2)
    grad_packed = grad_packed.reshape(group_rows, local_heads * triple_width).astype(jnp.bfloat16)
    grad_bqkv = jnp.sum(grad_packed.astype(jnp.float32), axis=0).reshape(local_heads, triple_width)
    grad_wqkv = contract_rows(h_one, grad_packed).reshape(model_width, local_heads, triple_width)
    grad_norm_one = lax.psum_scatter(
        contract_cols(grad_packed, qkv_matrix), "head", scatter_dimension=0, tiled=True
    )
    first_value, first_pull = jax.vjp(layer_norm, tokens_own, gain_attn, shift_attn)
    grad_tokens_norm, grad_gattn, grad_sattn = first_pull(grad_norm_one)
    grad_inputs = (grad_resid + grad_tokens_norm).astype(jnp.bfloat16)
    small_sums = lax.psum(
        (grad_gattn, grad_sattn, grad_bproj, grad_gmlp, grad_smlp, grad_bdown), ("batch", "head")
    )
    sum_wqkv, sum_bqkv, sum_wproj, sum_wup, sum_bup, sum_wdown = lax.psum(
        (grad_wqkv, grad_bqkv, grad_wproj, grad_wup, grad_bup, grad_wdown), "batch"
    )
    return (
        output,
        grad_inputs,
        small_sums[0],
        small_sums[1],
        sum_wqkv,
        sum_bqkv,
        sum_wproj,
        small_sums[2],
        small_sums[3],
        small_sums[4],
        sum_wup,
        sum_bup,
        sum_wdown,
        small_sums[5],
    )


def solution(mesh):
    in_specs = (
        P(("batch", "head"), None),
        P("batch", None),
        P(("batch", "head"), None),
        P(),
        P(),
        P(None, "head", None),
        P("head", None),
        P("head", None, None),
        P(),
        P(),
        P(),
        P(None, "head"),
        P("head"),
        P("head", None),
        P(),
    )
    out_specs = (
        P(("batch", "head"), None),
        P(("batch", "head"), None),
        P(),
        P(),
        P(None, "head", None),
        P("head", None),
        P("head", None, None),
        P(),
        P(),
        P(),
        P(None, "head"),
        P("head"),
        P("head", None),
        P(),
    )
    return jax.shard_map(
        per_device, mesh=mesh, in_specs=in_specs, out_specs=out_specs, check_vma=False
    )
```

profile of v0, /device:TPU:0, one launch (start us, length us, event | category | flops | bytes accessed | tf_op | source)
XLA Modules:
  0.0 835.7 jit_solution(4386529339230821315)
XLA Ops:
  20.5 24.7 %all-gather.5.cloned.1.call-done = bf16[2048,768]{1,0:T(8,128)(2,1)} async-done(((bf16[512,768]{1,0:T(8,128)(2,1)}), bf16[2048,768]{1,0:T(8,128)(2,1)}) %all-gather.5.cloned.1.call-update) | async-done | bytes 3145744 | tf_op jit(solution)/shard_map/all_gather | solution.py:103
  45.1 4.2 add_convert_fusion
  58.0 4.6 divide_multiply_fusion.2
  73.2 7.0 divide_multiply_fusion.1
  87.0 4.6 fusion.6
  91.7 9.6 %fusion.98 = bf16[512,3,64]{0,2,1:T(8,128)(2,1)S(1)} fusion(bf16[2048,3,3,64]{0,3,2,1:T(8,128)(2,1)S(1)} %bitcast.247, f32[3,512,2048]{2,1,0:T(8,128)S(1)} %get-tuple-element.172, f32[3,512]{1,0:T(4,128)S(1)} %fusion.6, f32[3,512]{1,0:T(4,128)S(1)} %negate_exponential_fusion, f32[3,512]{1,0:T(4,128)S(1)} %get-tuple-element.171, ...), kind=kOutput, calls=%fused_computation.133 | convolution fusion | flops 437256192 | bytes 14639104 | tf_op jit(solution)/shard_map/hqk,khd->qhd/dot_general | solution.py:131
  106.3 58.5 %reduce-scatter.5.cloned.1.call-done = f32[512,768]{1,0:T(8,128)} async-done(((f32[2048,768]{1,0:T(8,128)}), f32[512,768]{1,0:T(8,128)}) %reduce-scatter.5.cloned.1.call-update) | async-done | bytes 1572880 | tf_op jit(solution)/shard_map/reduce_scatter | solution.py:142
  171.8 26.8 %all-gather.7.cloned.1.call-done = bf16[2048,768]{1,0:T(8,128)(2,1)} async-done(((bf16[512,768]{1,0:T(8,128)(2,1)}), bf16[2048,768]{1,0:T(8,128)(2,1)}) %all-gather.7.cloned.1.call-update) | async-done | bytes 3145744 | tf_op jit(solution)/shard_map/all_gather | solution.py:150
  198.6 7.5 fusion.149
  206.0 23.1 %all-gather.9.cloned.1.call-done = bf16[2048,768]{1,0:T(8,128)(2,1)} async-done(((bf16[512,768]{1,0:T(8,128)(2,1)}), bf16[2048,768]{1,0:T(8,128)(2,1)}) %all-gather.9.cloned.1.call-update) | async-done | bytes 3145744 | tf_op jit(solution)/shard_map/all_gather | solution.py:161
  229.1 12.4 %convert_reduce_fusion = (f32[768]{0:T(1024)}, bf16[2048,768]{1,0:T(8,128)(2,1)S(1)}, bf16[2048,768]{1,0:T(8,128)(2,1)}) fusion(f32[2048,768]{1,0:T(8,128)} %fusion.149, f32[768]{0:T(1024)} %param.47, bf16[2048,768]{1,0:T(8,128)(2,1)} %all-gather.9.cloned.1.call-done, bf16[768,768]{1,0:T(8,128)(2,1)S(1)} %copy-done), kind=kOutput, calls=%fused_computation.29 | convolution fusion | flops 2455239936 | bytes 16914432 | tf_op jit(solution)/shard_map/dot_general | solution.py:64
  243.1 4.5 fusion.150
  247.8 6.5 convolution_convert_fusion
  254.6 52.1 %reduce-scatter.9.cloned.1.call-done = f32[512,768]{1,0:T(8,128)} async-done(((f32[2048,768]{1,0:T(8,128)}), f32[512,768]{1,0:T(8,128)}) %reduce-scatter.9.cloned.1.call-update) | async-done | bytes 1572880 | tf_op jit(solution)/shard_map/reduce_scatter | solution.py:168
  309.4 37.7 %reduce-scatter.7.cloned.1.call-done = bf16[512,768]{1,0:T(8,128)(2,1)} async-done(((bf16[2048,768]{1,0:T(8,128)(2,1)}), bf16[512,768]{1,0:T(8,128)(2,1)}) %reduce-scatter.7.cloned.1.call-update) | async-done | bytes 786448 | tf_op jit(solution)/shard_map/reduce_scatter | solution.py:153
  352.6 28.6 %all-gather.11.cloned.1.call-done = bf16[2048,768]{1,0:T(8,128)(2,1)} async-done(((bf16[512,768]{1,0:T(8,128)(2,1)}), bf16[2048,768]{1,0:T(8,128)(2,1)}) %all-gather.11.cloned.1.call-update) | async-done | bytes 3145744 | tf_op jit(solution)/shard_map/all_gather | solution.py:176
  385.3 6.7 multiply_convert_fusion.4
  397.0 11.9 %multiply_convert_fusion.2 = bf16[3,512,1024]{2,1,0:T(8,128)(2,1)} fusion(f32[3,512,1024]{2,1,0:T(8,128)} %copy-done.8, f32[3,512]{1,0:T(4,128)} %copy-done.59, f32[3,512]{1,0:T(4,128)S(1)} %copy-done.45, pred[512,1024]{1,0:T(8,128)(4,1)} %copy-done.22, f32[3,512,1024]{2,1,0:T(8,128)} %copy-done.3, bf16[512,3,64]{0,2,1:T(8,128)(2,1)} %bitcast.268, ...), kind=kOutput, calls=%fused_computation.30 | convolution fusion | flops 421530112 | bytes 17448960 | tf_op jit(solution)/shard_map/mul | solution.py:204
  408.9 15.1 %multiply_convert_fusion.1 = bf16[3,512,1536]{2,1,0:T(8,128)(2,1)} fusion(f32[3,512,1536]{2,1,0:T(8,128)} %copy-done.6, f32[3,512,1536]{2,1,0:T(8,128)} %copy-done.2, f32[3,512]{1,0:T(4,128)} %copy-done.52, f32[3,512]{1,0:T(4,128)S(1)} %get-tuple-element.173, pred[512,1536]{1,0:T(8,128)(4,1)S(1)} %copy-done.17, bf16[512,3,64]{0,2,1:T(8,128)(2,1)} %bitcast.266, ...), kind=kOutput, calls=%fused_computation.12 | convolution fusion | flops 632294400 | bytes 25968640 | tf_op jit(solution)/shard_map/mul | solution.py:204
  424.0 4.7 fusion.111
  428.7 3.7 fusion.109
  441.6 7.3 fusion.122
  449.0 10.8 %fusion.57 = bf16[2048,3,1,64]{0,3,1,2:T(8,128)(2,1)} fusion(f32[2048,3,64]{0,2,1:T(8,128)S(1)} %fusion.50, bf16[512,3,64]{0,2,1:T(8,128)(2,1)S(1)} %bitcast.263, f32[3,512,2048]{2,1,0:T(8,128)S(1)} %bitcast.239, f32[3,512]{1,0:T(4,128)S(1)} %copy-done.73, f32[3,512]{1,0:T(4,128)S(1)} %copy-done.71, f32[3,512]{1,0:T(4,128)S(1)} %copy-done.61, ...), kind=kOutput, calls=%fused_computation.83 | convolution fusion | flops 438042624 | bytes 16205824 | tf_op jit(solution)/shard_map/hqk,qhd->khd/dot_general | solution.py:216
  459.8 27.9 %fusion.107 = bf16[512,3,64]{0,2,1:T(8,128)(2,1)S(1)} fusion(bf16[2048,3,3,64]{0,3,2,1:T(8,128)(2,1)} %bitcast.248, f32[3,512,2048]{2,1,0:T(8,128)} %fusion.122, f32[3,512,2048]{2,1,0:T(8,128)} %copy-done.13, f32[3,512]{1,0:T(4,128)S(1)} %copy-done.73, f32[3,512]{1,0:T(4,128)S(1)} %copy-done.61, pred[512,2048]{1,0:T(8,128)(4,1)S(1)} %copy-done.24, ...), kind=kOutput, calls=%fused_computation.138 | convolution fusion | flops 472059392 | bytes 53452800 | tf_op jit(solution)/shard_map/hqk,khd->qhd/dot_general | solution.py:206
  487.7 29.5 %fusion.53 = bf16[2048,3,1,64]{0,3,1,2:T(8,128)(2,1)} fusion(f32[2048,3,64]{0,2,1:T(8,128)S(1)} %fusion.45, bf16[2048,3,3,64]{0,3,2,1:T(8,128)(2,1)} %bitcast.249, f32[3,512,2048]{2,1,0:T(8,128)} %fusion.122, f32[3,512,2048]{2,1,0:T(8,128)} %copy-done.13, f32[3,512]{1,0:T(4,128)S(1)} %copy-done.73, f32[3,512]{1,0:T(4,128)S(1)} %copy-done.61, ...), kind=kOutput, calls=%fused_computation.81 | convolution fusion | flops 473042432 | bytes 55025664 | tf_op jit(solution)/shard_map/hqk,qhd->khd/dot_general | solution.py:212
  520.3 4.8 fusion.151
  525.1 7.1 fusion.153
  532.2 4.2 fusion.152
  542.7 22.2 %all-reduce.3 = (f32[3,192]{1,0:T(4,128)}, f32[768]{0:T(1024)}) all-reduce(f32[3,192]{1,0:T(4,128)S(1)} %reshape.761, f32[768]{0:T(1024)S(1)} %copy-done.76), channel_id=1, replica_groups=mesh['batch'=8,'head'=4] {'batch'}, use_global_device_ids=true, to_apply=%region_32.33 | all-reduce | flops 1344 | bytes 10752 | tf_op jit(solution)/shard_map/psum | solution.py:231
  564.9 19.1 %reduce-scatter.11.cloned.1.call-done = f32[512,768]{1,0:T(8,128)} async-done(((f32[2048,768]{1,0:T(8,128)}), f32[512,768]{1,0:T(8,128)}) %reduce-scatter.11.cloned.1.call-update) | async-done | bytes 1572880 | tf_op jit(solution)/shard_map/reduce_scatter | solution.py:222
  588.8 44.1 %all-reduce.2 = (f32[768]{0:T(1024)}, f32[768]{0:T(1024)}, f32[768]{0:T(1024)}, f32[768]{0:T(1024)}, f32[768]{0:T(1024)}, /*index=5*/f32[768]{0:T(1024)}) all-reduce(f32[768]{0:T(1024)S(1)} %get-tuple-element.128, f32[768]{0:T(1024)S(1)} %get-tuple-element.131, ...), channel_id=1, replica_groups=mesh['batch'=8,'head'=4] {'batch','head'}, use_global_device_ids=true, to_apply=%region_27.28 | all-reduce | flops 4608 | bytes 36864 | tf_op jit(solution)/shard_map/psum | solution.py:228
  632.9 189.5 %all-reduce.7.cloned.1.call-done = (f32[768,3,192]{0,2,1:T(8,128)}, f32[3,64,768]{2,1,0:T(8,128)}, f32[768,768]{1,0:T(8,128)}, f32[768,768]{1,0:T(8,128)}) async-done(((f32[768,3,192]{0,2,1:T(8,128)}, f32[3,64,768]{2,1,0:T(8,128)}, f32[768,768]{1,0:T(8,128)}, f32[768,768]{1,0:T(8,128)}), (f32[768,3,192]{0,2,1:T(8,128)}, f32[3,64,768]{2,1,0:T(8,128)}, f32[768,768]{1,0:T(8,128)}, ...) | async-done | bytes 7077904 | tf_op jit(solution)/shard_map/psum | solution.py:231
  (292 shorter events, 99.7 us)
Async XLA Ops:
  7.2 221.9 %copy-start = (bf16[768,768]{1,0:T(8,128)(2,1)S(1)}, bf16[768,768]{1,0:T(8,128)(2,1)}, u32[]{:S(2)}) copy-start(bf16[768,768]{1,0:T(8,128)(2,1)} %param.48) | copy-start | bytes 3538948
  7.2 37.9 %all-gather.5.cloned.1.call-start = ((), (), s32[]{:S(2)}) async-start(), calls=%async_computation.4 | async-start | bytes 3932160 | tf_op jit(solution)/shard_map/all_gather | solution.py:103
  13.8 151.0 %reduce-scatter.5.cloned.1.call-start = ((), (), s32[]{:S(2)}) async-start(), calls=%async_computation.5 | async-start | bytes 7864320 | tf_op jit(solution)/shard_map/reduce_scatter | solution.py:142
  16.7 41.2 %copy-start.22 = (pred[512,1024]{1,0:T(8,128)(4,1)}, pred[512,1024]{1,0:T(8,128)(4,1)S(1)}, u32[]{:S(2)}) copy-start(pred[512,1024]{1,0:T(8,128)(4,1)S(1)} %fusion.68) | copy-start | bytes 1572868
  19.0 72.6 %copy-start.23 = (pred[512,2048]{1,0:T(8,128)(4,1)}, pred[512,2048]{1,0:T(8,128)(4,1)S(1)}, u32[]{:S(2)}) copy-start(pred[512,2048]{1,0:T(8,128)(4,1)S(1)} %fusion.25) | copy-start | bytes 3145732
  20.5 51.9 %copy-start.16 = (pred[512,1536]{1,0:T(8,128)(4,1)}, pred[512,1536]{1,0:T(8,128)(4,1)S(1)}, u32[]{:S(2)}) copy-start(pred[512,1536]{1,0:T(8,128)(4,1)S(1)} %fusion.37) | copy-start | bytes 2359300
  49.3 42.3 %copy-start.18 = (bf16[2048,576]{0,1:T(8,128)(2,1)}, bf16[2048,576]{0,1:T(8,128)(2,1)S(1)}, u32[]{:S(2)}) copy-start(bf16[2048,576]{0,1:T(8,128)(2,1)S(1)} %add_convert_fusion) | copy-start | bytes 7077892
  53.6 47.8 %copy-start.36 = (bf16[512,3,64]{0,2,1:T(8,128)(2,1)}, bf16[512,3,64]{0,2,1:T(8,128)(2,1)S(1)}, u32[]{:S(2)}) copy-start(bf16[512,3,64]{0,2,1:T(8,128)(2,1)S(1)} %convolution_bitcast_fusion.3) | copy-start | bytes 589828
  66.4 34.9 %copy-start.38 = (bf16[512,3,64]{0,2,1:T(8,128)(2,1)}, bf16[512,3,64]{0,2,1:T(8,128)(2,1)S(1)}, u32[]{:S(2)}) copy-start(bf16[512,3,64]{0,2,1:T(8,128)(2,1)S(1)} %fusion.101) | copy-start | bytes 589828
  105.7 59.0 %copy-start.4 = (bf16[512,768]{1,0:T(8,128)(2,1)S(1)}, bf16[512,768]{1,0:T(8,128)(2,1)}, u32[]{:S(2)}) copy-start(bf16[512,768]{1,0:T(8,128)(2,1)} %param.35) | copy-start | bytes 2359300
  105.8 92.8 %all-gather.7.cloned.1.call-start = ((), (), s32[]{:S(2)}) async-start(), calls=%async_computation.6 | async-start | bytes 3932160 | tf_op jit(solution)/shard_map/all_gather | solution.py:150
  169.9 59.2 %all-gather.9.cloned.1.call-start = ((), (), s32[]{:S(2)}) async-start(), calls=%async_computation.8 | async-start | bytes 3932160 | tf_op jit(solution)/shard_map/all_gather | solution.py:161
  171.7 135.0 %reduce-scatter.9.cloned.1.call-start = ((), (), s32[]{:S(2)}) async-start(), calls=%async_computation.9 | async-start | bytes 7864320 | tf_op jit(solution)/shard_map/reduce_scatter | solution.py:168
  247.7 99.3 %reduce-scatter.7.cloned.1.call-start = ((), (), s32[]{:S(2)}) async-start(), calls=%async_computation.7 | async-start | bytes 3932160 | tf_op jit(solution)/shard_map/reduce_scatter | solution.py:153
  254.3 52.4 %copy-start.48 = (f32[512]{0:T(512)S(1)}, f32[512]{0:T(512)}, u32[]{:S(2)}) copy-start(f32[512]{0:T(512)} %copy-done.47) | copy-start | bytes 6148
  254.3 52.4 %copy-start.49 = (f32[768]{0:T(1024)S(1)}, f32[768]{0:T(1024)}, u32[]{:S(2)}) copy-start(f32[768]{0:T(1024)} %param.44) | copy-start | bytes 9220
  254.3 52.4 %copy-start.58 = (f32[512]{0:T(512)S(1)}, f32[512]{0:T(512)}, u32[]{:S(2)}) copy-start(f32[512]{0:T(512)} %copy-done.57) | copy-start | bytes 6148
  254.3 55.0 %copy-start.67 = (f32[512]{0:T(512)S(1)}, f32[512]{0:T(512)}, u32[]{:S(2)}) copy-start(f32[512]{0:T(512)} %copy-done.66) | copy-start | bytes 6148
  254.3 92.7 %copy-start.74 = (f32[768]{0:T(1024)S(1)}, f32[768]{0:T(1024)}, u32[]{:S(2)}) copy-start(f32[768]{0:T(1024)} %param.49) | copy-start | bytes 9220
  254.4 126.9 %all-gather.11.cloned.1.call-start = ((), (), s32[]{:S(2)}) async-start(), calls=%async_computation.10 | async-start | bytes 3932160 | tf_op jit(solution)/shard_map/all_gather | solution.py:176
  309.4 42.0 %copy-start.55 = (f32[512]{0:T(512)S(1)}, f32[512]{0:T(512)}, u32[]{:S(2)}) copy-start(f32[512]{0:T(512)} %get-tuple-element.162) | copy-start | bytes 6148
  352.6 231.5 %reduce-scatter.11.cloned.1.call-start = ((), (), s32[]{:S(2)}) async-start(), calls=%async_computation.11 | async-start | bytes 7864320 | tf_op jit(solution)/shard_map/reduce_scatter | solution.py:222
  525.1 297.3 %all-reduce.7.cloned.1.call-start = ((), (), s32[]{:S(2)}) async-start(), calls=%async_computation.12 | async-start | bytes 14155776 | tf_op jit(solution)/shard_map/psum | solution.py:231
  542.0 42.0 %copy-start.5 = (bf16[512,768]{1,0:T(8,128)(2,1)S(1)}, bf16[512,768]{1,0:T(8,128)(2,1)}, u32[]{:S(2)}) copy-start(bf16[512,768]{1,0:T(8,128)(2,1)} %param.35) | copy-start | bytes 2359300
  542.0 42.0 %copy-start.43 = (f32[512]{0:T(512)S(1)}, f32[512]{0:T(512)}, u32[]{:S(2)}) copy-start(f32[512]{0:T(512)} %copy-done.42) | copy-start | bytes 6148
  542.0 42.0 %copy-start.46 = (f32[768]{0:T(1024)S(1)}, f32[768]{0:T(1024)}, u32[]{:S(2)}) copy-start(f32[768]{0:T(1024)} %param.38) | copy-start | bytes 9220
  542.0 44.0 %copy-start.65 = (f32[512]{0:T(512)S(1)}, f32[512]{0:T(512)}, u32[]{:S(2)}) copy-start(f32[512]{0:T(512)} %copy-done.64) | copy-start | bytes 6148
  542.1 44.0 %copy-start.54 = (f32[512]{0:T(512)S(1)}, f32[512]{0:T(512)}, u32[]{:S(2)}) copy-start(f32[512]{0:T(512)} %copy-done.53) | copy-start | bytes 6148
  542.1 44.9 %copy-start.11 = (f32[512,768]{1,0:T(8,128)S(1)}, f32[512,768]{1,0:T(8,128)}, u32[]{:S(2)}) copy-start(f32[512,768]{1,0:T(8,128)} %copy-done.10) | copy-start | bytes 4718596
  542.1 44.9 %copy-start.15 = (bf16[512,768]{1,0:T(8,128)(2,1)S(1)}, bf16[512,768]{1,0:T(8,128)(2,1)}, u32[]{:S(2)}) copy-start(bf16[512,768]{1,0:T(8,128)(2,1)} %param.37) | copy-start | bytes 2359300
  542.1 44.9 %copy-start.56 = (f32[512]{0:T(512)S(1)}, f32[512]{0:T(512)}, u32[]{:S(2)}) copy-start(f32[512]{0:T(512)} %get-tuple-element.162) | copy-start | bytes 6148
  542.1 44.9 %copy-start.63 = (f32[512]{0:T(512)S(1)}, f32[512]{0:T(512)}, u32[]{:S(2)}) copy-start(f32[512]{0:T(512)} %copy-done.62) | copy-start | bytes 6148
  (76 other events, 477.5 us)
Sparse Core Ops, SparseCore 0:
  13.9 31.2 all-gather.4
  105.9 58.8 reduce-scatter.4
  170.0 28.4 all-gather.6
  200.5 28.4 all-gather.8
  247.8 58.8 reduce-scatter.8
  309.1 37.8 reduce-scatter.6
  352.7 28.4 all-gather.10
  525.2 58.8 reduce-scatter.10
  589.6 232.6 all-reduce.6
where the time goes:
time: 839 us; the launch traced here: 836 us
  waiting for transfers between devices  460 us (55%)
  matrix products  212 us (25%)
  blocking collectives  66.3 us (8%)
  other arithmetic  56 us (7%)
  local copies, waits for them, and re-layouts  25 us (3%)
  between operations  15.2 us (2%)
    psum x1, waiting for transfers between devices, per_device(): lax.psum((grad_wqkv, grad_bqkv, grad_wproj, grad_wup, grad_bup, grad_wdow...  189 us
    reduce_scatter x1, waiting for transfers between devices, per_device(): lax.psum_scatter(jnp.dot(merged, proj_matrix, preferred_element_type=jnp....  58.5 us
    reduce_scatter x1, waiting for transfers between devices, per_device(): lax.psum_scatter(contract_cols(grad_up, weight_up), 'head', scatter_dimen...  52.1 us
    psum x1, blocking collectives, per_device(): lax.psum((grad_gattn, grad_sattn, grad_bproj, grad_gmlp, grad_smlp, grad_...  44.1 us
    reduce_scatter x1, waiting for transfers between devices, per_device(): lax.psum_scatter(jnp.dot(hidden_act, weight_down, preferred_element_type=...  37.7 us
    dot_general x4, matrix products, per_device(): jnp.einsum('hqk,khd->qhd', grad_scores, key_rows[:row_stop], preferred_el...  37.3 us
    dot_general x4, matrix products, per_device(): jnp.einsum('hqk,qhd->khd', grad_scores, query_block, preferred_element_ty...  34.6 us
    mul x3, matrix products, per_device(): signs * inner  33.6 us
  transfers between devices with their start and end apart: 9, of which 9 were waited for; matrix products, arithmetic and copies ran while one was open for 5% of the time, Pallas kernels for 0%

commit v1 on v0

v1 whole, which is shorter than its diff:
```python
import functools
import math

import jax
import jax.numpy as jnp
from jax import lax
from jax.experimental import pallas as pl
from jax.experimental.pallas import tpu as pltpu
from jax.sharding import PartitionSpec as P

F32 = jnp.float32
BF = jnp.bfloat16
BLK = 256
NEG = -1e30
EPS = 1e-05
GELU_C = math.sqrt(2.0 / math.pi)
GELU_A = 0.044715


def dot_nn(a, b):
    return lax.dot_general(a, b, (((1,), (0,)), ((), ())), preferred_element_type=F32)


def dot_nt(a, b):
    return lax.dot_general(a, b, (((1,), (1,)), ((), ())), preferred_element_type=F32)


def dot_tn(a, b):
    return lax.dot_general(a, b, (((0,), (0,)), ((), ())), preferred_element_type=F32)


def cost(flops, nbytes, trans=0):
    return pl.CostEstimate(flops=int(flops), bytes_accessed=int(nbytes), transcendentals=int(trans))


def swap(x, axis, bits):
    size = lax.axis_size(axis)
    return lax.ppermute(x, axis, [(i, i ^ bits) for i in range(size)])


def normalize(v):
    center = v - jnp.mean(v, axis=-1, keepdims=True)
    rstd = lax.rsqrt(jnp.mean(center * center, axis=-1, keepdims=True) + EPS)
    return center * rstd, rstd


def qkv_kernel(heads, hd, steps, h_ref, a_ref, b_ref, v_ref, w_ref, bias_ref, *rest):
    q_out, k_out, v_out, vt_out = rest[-4:]
    t = pl.program_id(0)
    x = jnp.where(t < steps // 2, a_ref[...], b_ref[...]).astype(F32)
    xhat, _ = normalize(x)
    h1 = (xhat * v_ref[0:1, :] + v_ref[1:2, :]).astype(BF)
    bias = jnp.concatenate([bias_ref[h : h + 1, :] for h in range(heads)], axis=1)
    packed = (dot_nt(h1, w_ref[...]) + bias).astype(BF)
    for h in range(heads):
        o = 3 * hd * h
        q_out[h] = packed[:, o : o + hd]
        k_out[h] = packed[:, o + hd : o + 2 * hd]
        v = packed[:, o + 2 * hd : o + 3 * hd]
        v_out[h] = v
        vt_out[h] = v.T


def qkv_call(hid, a, b, vectors, w, bias, first, group_rows, before):
    rows, width = a.shape
    heads, triple = bias.shape
    hd = triple // 3
    per = rows // BLK
    steps = 2 * per
    place = lambda t, h: (h[0] ^ (first + t // per)) * per + t % per
    whole = lambda t, h: (0, 0)
    out_shape = tuple(
        jax.ShapeDtypeStruct(s, BF)
        for s in ((heads, group_rows, hd),) * 3 + ((heads, hd, group_rows),)
    )
    in_specs = [
        pl.BlockSpec((BLK, width), lambda t, h: (jnp.minimum(t, per - 1), 0)),
        pl.BlockSpec((BLK, width), lambda t, h: (jnp.maximum(t - per, 0), 0)),
        pl.BlockSpec(vectors.shape, whole),
        pl.BlockSpec(w.shape, whole),
        pl.BlockSpec(bias.shape, whole),
    ] + [pl.BlockSpec(memory_space=pl.ANY)] * len(before)
    return pl.pallas_call(
        functools.partial(qkv_kernel, heads, hd, steps),
        out_shape=out_shape,
        grid_spec=pltpu.PrefetchScalarGridSpec(
            num_scalar_prefetch=1,
            grid=(steps,),
            in_specs=in_specs,
            out_specs=[pl.BlockSpec((heads, BLK, hd), lambda t, h: (0, place(t, h), 0))] * 3
            + [pl.BlockSpec((heads, hd, BLK), lambda t, h: (0, 0, place(t, h)))],
        ),
        input_output_aliases={6 + i: i for i in range(len(before))},
        cost_estimate=cost(4 * rows * width * w.shape[0], 12 * rows * width),
        name="qkv",
    )(hid, a, b, vectors, w, bias, *before)


def row_segment(len_ref, row):
    low = row
    high = row + 1
    start = jnp.int32(0)
    for k in range(len_ref.shape[0] - 1):
        stop = start + len_ref[k]
        inside = (row >= start) & (row < stop)
        low = jnp.where(inside, start, low)
        high = jnp.where(inside, stop, high)
        start = stop
    return low, high


def lane_starts(len_ref, row, width):
    i = row + lax.broadcasted_iota(jnp.int32, (1, width), 1)
    start = jnp.zeros((1, width), jnp.int32)
    stop = jnp.int32(0)
    for k in range(len_ref.shape[0] - 1):
        stop = stop + len_ref[k]
        start = jnp.where(i >= stop, stop, start)
    return jnp.where(i >= stop, i, start), i


def attend_kernel(heads, first, per, scale, len_ref, h_ref, q_ref, k_ref, vt_ref, o_ref, l_ref, m_s, z_s, acc_s):
    t = pl.program_id(0)
    row = ((h_ref[0] ^ (first + t // per)) * per + t % per) * BLK
    start, i = lane_starts(len_ref, row, BLK)
    low, _ = row_segment(len_ref, row)
    m_s[...] = jnp.full_like(m_s, NEG)
    z_s[...] = jnp.zeros_like(z_s)
    acc_s[...] = jnp.zeros_like(acc_s)
    qs = [q_ref[h] * jnp.asarray(scale, BF) for h in range(heads)]

    def body(jb, carry):
        j0 = pl.multiple_of(jb * BLK, BLK)
        j = j0 + lax.broadcasted_iota(jnp.int32, (BLK, BLK), 0)
        mask = (j >= start) & (j <= i)
        for h in range(heads):
            s = dot_nt(k_ref[h, pl.ds(j0, BLK), :], qs[h])
            magnitude = jnp.where(mask, jnp.abs(s), NEG)
            old = m_s[h : h + 1, :]
            top = jnp.maximum(old, jnp.max(magnitude, axis=0, keepdims=True))
            decay = jnp.exp(old - top)
            e = jnp.exp(magnitude - top)
            z_s[h : h + 1, :] = z_s[h : h + 1, :] * decay + jnp.sum(e, axis=0, keepdims=True)
            m_s[h : h + 1, :] = top
            u = e - jnp.where(mask, jnp.exp(-top), 0.0)
            w = jnp.where(s < 0, -u, u).astype(BF)
            acc_s[h] = acc_s[h] * decay + dot_nn(vt_ref[h, :, pl.ds(j0, BLK)], w)
        return carry

    lax.fori_loop(low // BLK, row // BLK + 1, body, 0)
    outs = []
    for h in range(heads):
        z = z_s[h : h + 1, :]
        outs.append((acc_s[h] / z).T)
        l_ref[h : h + 1, :] = m_s[h : h + 1, :] + jnp.log(z)
    o_ref[...] = jnp.concatenate(outs, axis=1).astype(BF)


def attend_call(lengths, hid, q, k, vt, first, chunk):
    heads, rows, hd = q.shape
    per = chunk // BLK
    steps = 2 * per
    place = lambda t, n, h: (0, (h[0] ^ (first + t // per)) * per + t % per, 0)
    whole = lambda t, n, h: (0, 0, 0)
    return pl.pallas_call(
        functools.partial(attend_kernel, heads, first, per, 1.0 / math.sqrt(hd)),
        out_shape=(
            jax.ShapeDtypeStruct((steps * BLK, heads * hd), BF),
            jax.ShapeDtypeStruct((8, steps * BLK), F32),
        ),
        grid_spec=pltpu.PrefetchScalarGridSpec(
            num_scalar_prefetch=2,
            grid=(steps,),
            in_specs=[
                pl.BlockSpec((heads, BLK, hd), place),
                pl.BlockSpec((heads, rows, hd), whole),
                pl.BlockSpec((heads, hd, rows), whole),
            ],
            out_specs=[
                pl.BlockSpec((BLK, heads * hd), lambda t, n, h: (t, 0)),
                pl.BlockSpec((8, BLK), lambda t, n, h: (0, t)),
            ],
            scratch_shapes=[
                pltpu.VMEM((8, BLK), F32),
                pltpu.VMEM((8, BLK), F32),
                pltpu.VMEM((heads, hd, BLK), F32),
            ],
        ),
        cost_estimate=cost(heads * rows * rows * hd * 4, 12 * rows * heads * hd, heads * rows * rows // 4),
        name="attend",
    )(lengths, hid, q, k, vt)


def attend_back_kernel(chunk, scale, len_ref, h_ref, q_ref, k_ref, v_ref, *rest):
    g_refs, o_refs, l_refs = rest[0:4], rest[4:6], rest[6:8]
    gp_ref, q_s, g_s, kt_s, l_s, c_s, d_s, dq_s, dk_s, dv_s = rest[8:]
    heads, rows, hd = q_ref.shape
    blocks = rows // BLK
    per = chunk // BLK
    own = h_ref[0]
    for c in range(4):
        r0 = pl.multiple_of((own ^ c) * chunk, chunk)
        part = slice((c % 2) * chunk, (c % 2 + 1) * chunk)
        g = g_refs[c][part, :]
        o = o_refs[c // 2][part, :]
        for h in range(heads):
            gh = g[:, h * hd : (h + 1) * hd]
            g_s[h, pl.ds(r0, chunk), :] = gh
            both = gh.astype(F32) * o[:, h * hd : (h + 1) * hd].astype(F32)
            d_s[h : h + 1, pl.ds(r0, chunk)] = jnp.sum(both.T, axis=0, keepdims=True)
        level = l_refs[c // 2][:, part]
        l_s[:, pl.ds(r0, chunk)] = level
        c_s[:, pl.ds(r0, chunk)] = jnp.exp(-level)
    for h in range(heads):
        q_s[h] = q_ref[h] * jnp.asarray(scale, BF)
    dq_s[...] = jnp.zeros_like(dq_s)

    def out_row(block):
        return pl.multiple_of(((own ^ (block // per)) * per + block % per) * BLK, BLK)

    def outer(jb, carry):
        j0 = pl.multiple_of(jb * BLK, BLK)
        dk_s[...] = jnp.zeros_like(dk_s)
        dv_s[...] = jnp.zeros_like(dv_s)
        for h in range(heads):
            kt_s[h] = k_ref[h, pl.ds(j0, BLK), :].T
        _, stop = row_segment(len_ref, j0 + BLK - 1)
        j = j0 + lax.broadcasted_iota(jnp.int32, (BLK, BLK), 0)

        def inner(ib, carry):
            i0 = pl.multiple_of(ib * BLK, BLK)
            start, i = lane_starts(len_ref, i0, BLK)
            mask = (j >= start) & (j <= i)
            for h in range(heads):
                qh = q_s[h, pl.ds(i0, BLK), :]
                gh = g_s[h, pl.ds(i0, BLK), :]
                s = dot_nt(k_ref[h, pl.ds(j0, BLK), :], qh)
                gw = dot_nt(v_ref[h, pl.ds(j0, BLK), :], gh)
                level = l_s[h : h + 1, pl.ds(i0, BLK)]
                offset = c_s[h : h + 1, pl.ds(i0, BLK)]
                d = d_s[h : h + 1, pl.ds(i0, BLK)]
                p = jnp.exp(jnp.where(mask, jnp.abs(s), NEG) - level)
                u = p - jnp.where(mask, offset, 0.0)
                minus = s < 0
                w = jnp.where(minus, -u, u).astype(BF)
                signed = jnp.where(minus, -d, jnp.where(s == 0, 0.0, d))
                gs = (p * (gw - signed)).astype(BF)
                dv_s[h] += dot_nn(w, gh)
                dk_s[h] += dot_nn(gs, qh)
                dq_s[h, :, pl.ds(i0, BLK)] += dot_nn(kt_s[h], gs)
            return carry

        lax.fori_loop(jb, (stop - 1) // BLK + 1, inner, 0)
        for h in range(heads):
            at = pl.ds(out_row(jb), BLK)
            gp_ref[at, (3 * h + 1) * hd : (3 * h + 2) * hd] = dk_s[h].astype(BF)
            gp_ref[at, (3 * h + 2) * hd : (3 * h + 3) * hd] = dv_s[h].astype(BF)
        return carry

    lax.fori_loop(0, blocks, outer, 0)

    def finish(ib, carry):
        i0 = pl.multiple_of(ib * BLK, BLK)
        for h in range(heads):
            dq = (dq_s[h, :, pl.ds(i0, BLK)] * scale).T.astype(BF)
            gp_ref[pl.ds(out_row(ib), BLK), 3 * h * hd : (3 * h + 1) * hd] = dq
        return carry

    lax.fori_loop(0, blocks, finish, 0)


def attend_back_call(lengths, hid, q, k, v, grads, outs, levels, chunk):
    heads, rows, hd = q.shape
    vm = pl.BlockSpec(memory_space=pltpu.VMEM)
    sm = pl.BlockSpec(memory_space=pltpu.SMEM)
    return pl.pallas_call(
        functools.partial(attend_back_kernel, chunk, 1.0 / math.sqrt(hd)),
        out_shape=jax.ShapeDtypeStruct((rows, heads * 3 * hd), BF),
        in_specs=[sm, sm] + [vm] * 11,
        out_specs=vm,
        scratch_shapes=[
            pltpu.VMEM((heads, rows, hd), BF),
            pltpu.VMEM((heads, rows, hd), BF),
            pltpu.VMEM((heads, hd, BLK), BF),
            pltpu.VMEM((8, rows), F32),
            pltpu.VMEM((8, rows), F32),
            pltpu.VMEM((8, rows), F32),
            pltpu.VMEM((heads, hd, rows), F32),
            pltpu.VMEM((heads, BLK, hd), F32),
            pltpu.VMEM((heads, BLK, hd), F32),
        ],
        cost_estimate=cost(heads * rows * rows * hd * 20, 30 * rows * heads * hd, heads * rows * rows // 2),
        name="attend_back",
    )(lengths, hid, q, k, v, *grads, *outs, *levels)


def feed_kernel(steps, ha_ref, hb_ref, ga_ref, gb_ref, up_ref, v_ref, down_ref, *rest):
    act_ref, gup_ref, gn_ref, out_ref = rest[-4:]
    early = pl.program_id(0) < steps // 2
    h2 = jnp.where(early, ha_ref[...], hb_ref[...])
    grad = jnp.where(early, ga_ref[...], gb_ref[...])
    u = dot_nn(h2, up_ref[...]) + v_ref[5:6, :]
    square = u * u
    tanh = jnp.tanh(u * (GELU_C + (GELU_C * GELU_A) * square))
    half = 0.5 * (1.0 + tanh)
    act = (u * half).astype(BF)
    slope = half + (0.5 * u) * (1.0 - tanh * tanh) * (GELU_C + (3.0 * GELU_C * GELU_A) * square)
    gup = (dot_nt(grad, down_ref[...]) * slope).astype(BF)
    act_ref[...] = act
    gup_ref[...] = gup
    gn_ref[...] = dot_nt(gup, up_ref[...]).astype(BF)
    out_ref[...] = dot_nn(act, down_ref[...]).astype(BF)


def feed_call(ha, hb, ga, gb, up, vectors, down, first, group_rows, before):
    rows, width = ha.shape
    hidden = up.shape[1]
    per = rows // BLK
    steps = 2 * per
    whole = lambda t: (0, 0)
    early = pl.BlockSpec((BLK, width), lambda t: (jnp.minimum(t, per - 1), 0))
    late = pl.BlockSpec((BLK, width), lambda t: (jnp.maximum(t - per, 0), 0))
    return pl.pallas_call(
        functools.partial(feed_kernel, steps),
        out_shape=(
            jax.ShapeDtypeStruct((group_rows, hidden), BF),
            jax.ShapeDtypeStruct((group_rows, hidden), BF),
            jax.ShapeDtypeStruct((2 * rows, width), BF),
            jax.ShapeDtypeStruct((2 * rows, width), BF),
        ),
        grid=(steps,),
        in_specs=[
            early,
            late,
            early,
            late,
            pl.BlockSpec(up.shape, whole),
            pl.BlockSpec(vectors.shape, whole),
            pl.BlockSpec(down.shape, whole),
        ]
        + [pl.BlockSpec(memory_space=pl.ANY)] * len(before),
        out_specs=[
            pl.BlockSpec((BLK, hidden), lambda t: (first * per + t, 0)),
            pl.BlockSpec((BLK, hidden), lambda t: (first * per + t, 0)),
            pl.BlockSpec((BLK, width), lambda t: (t, 0)),
            pl.BlockSpec((BLK, width), lambda t: (t, 0)),
        ],
        input_output_aliases={7 + i: i for i in range(len(before))},
        cost_estimate=cost(16 * rows * width * hidden, 16 * rows * width, 2 * rows * hidden),
        name="feed",
    )(ha, hb, ga, gb, up, vectors, down, *before)


def spots(b_ref, pieces):
    return [b_ref[0] ^ (2 * (spot % 4) + spot // 4) for spot in range(pieces)]


def split_out(b_ref, acc, keep_ref, send_ref):
    piece = acc.shape[0] // 8
    for spot, block in enumerate(spots(b_ref, 8)):
        out = keep_ref if spot < 4 else send_ref
        value = acc[pl.ds(pl.multiple_of(block * piece, 8), piece), :]
        out[(spot % 4) * piece : (spot % 4 + 1) * piece, :] = value.astype(BF)


def weigh_kernel(tiles, b_ref, h0, h1, h2, h3, act_ref, up_ref, g0, g1, g2, g3, keep_ref, send_ref, bias_ref, acc):
    t = pl.program_id(0)
    tile = acc.shape[0] // (2 * tiles)
    chunk = h0.shape[0]
    at = pl.ds(pl.multiple_of(t * tile, tile), tile)

    @pl.when(t == 0)
    def _():
        bias_ref[...] = jnp.sum(up_ref[...].astype(F32), axis=0, keepdims=True)

    @pl.when(t < tiles)
    def _():
        total = dot_tn(h0[...], up_ref[:chunk, :])
        for k, h in enumerate((h1, h2, h3)):
            total = total + dot_tn(h[...], up_ref[(k + 1) * chunk : (k + 2) * chunk, :])
        acc[at, :] = total

    @pl.when(t >= tiles)
    def _():
        total = dot_tn(act_ref[:chunk, :], g0[...])
        for k, g in enumerate((g1, g2, g3)):
            total = total + dot_tn(act_ref[(k + 1) * chunk : (k + 2) * chunk, :], g[...])
        acc[at, :] = total

    @pl.when(t == 2 * tiles - 1)
    def _():
        split_out(b_ref, acc, keep_ref, send_ref)


def weigh_call(bid, hs, act, up, grads):
    chunk, width = hs[0].shape
    rows, hidden = act.shape
    tile = 256
    tiles = width // tile
    whole = lambda t, b: (0, 0)
    total = width + hidden
    half = jax.ShapeDtypeStruct((total // 2, width), BF)
    return pl.pallas_call(
        functools.partial(weigh_kernel, tiles),
        out_shape=(half, half, jax.ShapeDtypeStruct((1, hidden), F32)),
        grid_spec=pltpu.PrefetchScalarGridSpec(
            num_scalar_prefetch=1,
            grid=(2 * tiles,),
            in_specs=[pl.BlockSpec((chunk, tile), lambda t, b: (0, jnp.minimum(t, tiles - 1)))] * 4
            + [
                pl.BlockSpec((rows, tile), lambda t, b: (0, jnp.maximum(t - tiles, 0))),
                pl.BlockSpec((rows, hidden), whole),
            ]
            + [pl.BlockSpec((chunk, width), whole)] * 4,
            out_specs=[
                pl.BlockSpec(half.shape, whole),
                pl.BlockSpec(half.shape, whole),
                pl.BlockSpec((1, hidden), whole),
            ],
            scratch_shapes=[pltpu.VMEM((total, width), F32)],
        ),
        cost_estimate=cost(4 * rows * width * hidden, 12 * rows * width),
        name="weigh",
    )(bid, *hs, act, up, *grads)


def mix_kernel(m0, m1, m2, m3, p0, p1, p2, p3, x_ref, v_ref, resid_ref, h_ref):
    total = x_ref[...].astype(F32) + v_ref[2:3, :]
    for m, p in ((m0, p0), (m1, p1), (m2, p2), (m3, p3)):
        total = total + dot_nn(m[...], p[...])
    resid_ref[...] = total
    hat, _ = normalize(total)
    h_ref[...] = (hat * v_ref[3:4, :] + v_ref[4:5, :]).astype(BF)


def mix_call(parts, projs, x, vectors):
    rows, width = x.shape
    per = rows // BLK
    inner = parts[0].shape[1]
    low = pl.BlockSpec((BLK, inner), lambda t: (t, 0))
    high = pl.BlockSpec((BLK, inner), lambda t: (t + per, 0))
    whole = lambda t: (0, 0)
    return pl.pallas_call(
        mix_kernel,
        out_shape=(jax.ShapeDtypeStruct((rows, width), F32), jax.ShapeDtypeStruct((rows, width), BF)),
        grid=(per,),
        in_specs=[low, high, low, high]
        + [pl.BlockSpec(projs[0].shape, whole)] * 4
        + [pl.BlockSpec((BLK, width), lambda t: (t, 0)), pl.BlockSpec(vectors.shape, whole)],
        out_specs=[pl.BlockSpec((BLK, width), lambda t: (t, 0))] * 2,
        cost_estimate=cost(8 * rows * width * inner, 12 * rows * width),
        name="mix",
    )(*parts, *projs, x, vectors)


def turn_kernel(n_ref, s_ref, f_ref, resid_ref, cot_ref, v_ref, p0, p1, p2, p3, gr_ref, ga_ref, gn_ref, gf_ref, sum_ref):
    grad = n_ref[...].astype(F32) + s_ref[...].astype(F32) + f_ref[...].astype(F32)
    hat, rstd = normalize(resid_ref[...])
    cot = cot_ref[...].astype(F32)
    e = grad * v_ref[3:4, :]
    back = e - jnp.mean(e, axis=-1, keepdims=True) - hat * jnp.mean(e * hat, axis=-1, keepdims=True)
    grad_resid = cot + rstd * back
    gr_ref[...] = grad_resid
    att = grad_resid.astype(BF)
    ga_ref[...] = att
    gn_ref[0] = dot_nt(att, p0[...]).astype(BF)
    gn_ref[1] = dot_nt(att, p1[...]).astype(BF)
    gf_ref[0] = dot_nt(att, p2[...]).astype(BF)
    gf_ref[1] = dot_nt(att, p3[...]).astype(BF)

    @pl.when(pl.program_id(0) == 0)
    def _():
        sum_ref[...] = jnp.zeros_like(sum_ref)

    for k, v in enumerate((grad_resid, grad * hat, grad, cot)):
        sum_ref[k + 4 : k + 5, :] += jnp.sum(v, axis=0, keepdims=True)


def turn_call(near, swapped, far, resid, cot, vectors, projs):
    rows, width = resid.shape
    per = rows // BLK
    inner = projs[0].shape[0]
    low = pl.BlockSpec((BLK, width), lambda t: (t, 0))
    high = pl.BlockSpec((BLK, width), lambda t: (t + per, 0))
    whole = lambda t: (0, 0)
    pair = jax.ShapeDtypeStruct((2, rows, inner), BF)
    pair_spec = pl.BlockSpec((2, BLK, inner), lambda t: (0, t, 0))
    return pl.pallas_call(
        turn_kernel,
        out_shape=(
            jax.ShapeDtypeStruct((rows, width), F32),
            jax.ShapeDtypeStruct((rows, width), BF),
            pair,
            pair,
            jax.ShapeDtypeStruct((8, width), F32),
        ),
        grid=(per,),
        in_specs=[low, high, low, low, low, pl.BlockSpec(vectors.shape, whole)]
        + [pl.BlockSpec(projs[0].shape, whole)] * 4,
        out_specs=[low, low, pair_spec, pair_spec, pl.BlockSpec((8, width), whole)],
        cost_estimate=cost(8 * rows * width * inner, 20 * rows * width),
        name="turn",
    )(near, swapped, far, resid, cot, vectors, *projs)


def close_kernel(per, b_ref, x0, x1, x2, x3, gp_ref, w_ref, v_ref, pw_ref, up_ref, s_ref, near_ref, far_ref, keep_ref, send_ref, sum_ref, acc):
    t = pl.program_id(0)
    steps = 4 * per
    x = jnp.where(t < 2 * per, jnp.where(t < per, x0[...], x1[...]), jnp.where(t < 3 * per, x2[...], x3[...]))
    hat, _ = normalize(x.astype(F32))
    h1 = (hat * v_ref[0:1, :] + v_ref[1:2, :]).astype(BF)
    gp = gp_ref[...]
    cols = gp.shape[1]
    e = dot_nn(gp, w_ref[...])

    @pl.when(t < 2 * per)
    def _():
        near_ref[...] = e.astype(BF)

    @pl.when(t >= 2 * per)
    def _():
        far_ref[...] = e.astype(BF)

    @pl.when(t == 0)
    def _():
        sum_ref[...] = s_ref[...]
        acc[...] = jnp.zeros_like(acc)
        acc[cols : cols + pw_ref.shape[0], :] = pw_ref[...]
        acc[cols + pw_ref.shape[0] + 1 : cols + pw_ref.shape[0] + 2, :] = up_ref[...]

    sum_ref[0:1, :] += jnp.sum(e * hat, axis=0, keepdims=True)
    sum_ref[1:2, :] += jnp.sum(e, axis=0, keepdims=True)
    acc[:cols, :] += dot_tn(gp, h1)
    base = cols + pw_ref.shape[0]
    acc[base : base + 1, :cols] += jnp.sum(gp.astype(F32), axis=0, keepdims=True)

    @pl.when(t == steps - 1)
    def _():
        split_out(b_ref, acc, keep_ref, send_ref)
        half = acc.shape[0] // 2
        keep_ref[half:, :] = sum_ref[...].astype(BF)
        send_ref[half:, :] = sum_ref[...].astype(BF)


def close_call(bid, rows, gp, w, vectors, proj_grad, up_grad, sums, total):
    chunk, width = rows[0].shape
    cols = gp.shape[1]
    per = chunk // BLK
    steps = 4 * per
    whole = lambda t, b: (0, 0)
    part = lambda k: pl.BlockSpec((BLK, width), lambda t, b: (jnp.clip(t - k * per, 0, per - 1), 0))
    half = jax.ShapeDtypeStruct((total // 2 + sums.shape[0], width), BF)
    return pl.pallas_call(
        functools.partial(close_kernel, per),
        out_shape=(
            jax.ShapeDtypeStruct((2 * chunk, width), BF),
            jax.ShapeDtypeStruct((2 * chunk, width), BF),
            half,
            half,
        ),
        grid_spec=pltpu.PrefetchScalarGridSpec(
            num_scalar_prefetch=1,
            grid=(steps,),
            in_specs=[part(0), part(1), part(2), part(3)]
            + [pl.BlockSpec((BLK, cols), lambda t, b: (t, 0))]
            + [pl.BlockSpec(v.shape, whole) for v in (w, vectors, proj_grad, up_grad, sums)],
            out_specs=[
                pl.BlockSpec((BLK, width), lambda t, b: (jnp.minimum(t, 2 * per - 1), 0)),
                pl.BlockSpec((BLK, width), lambda t, b: (jnp.maximum(t - 2 * per, 0), 0)),
                pl.BlockSpec(half.shape, whole),
                pl.BlockSpec(half.shape, whole),
            ],
            scratch_shapes=[pltpu.VMEM((8, width), F32), pltpu.VMEM((total, width), F32)],
        ),
        cost_estimate=cost(16 * chunk * width * cols, 20 * chunk * width),
        name="close",
    )(bid, *rows, gp, w, vectors, proj_grad, up_grad, sums)


def unpack_kernel(counts, b_ref, keep_ref, other_ref, *rest):
    acc = rest[-1]
    piece = acc.shape[0] // 8
    for spot, block in enumerate(spots(b_ref, 8)):
        src = keep_ref if spot < 4 else other_ref
        value = src[(spot % 4) * piece : (spot % 4 + 1) * piece, :].astype(F32)
        acc[pl.ds(pl.multiple_of(block * piece, 8), piece), :] = value
    start = 0
    for out, count in zip(rest[:-1], counts, strict=True):
        out[...] = acc[start : start + count, :]
        start += count


def unpack_call(bid, keep, other, counts):
    half, width = keep.shape
    vm = pl.BlockSpec(memory_space=pltpu.VMEM)
    return pl.pallas_call(
        functools.partial(unpack_kernel, counts),
        out_shape=tuple(jax.ShapeDtypeStruct((n, width), F32) for n in counts),
        in_specs=[pl.BlockSpec(memory_space=pltpu.SMEM), vm, vm],
        out_specs=[vm] * len(counts),
        scratch_shapes=[pltpu.VMEM((2 * half, width), F32)],
        cost_estimate=cost(half * width, 12 * half * width),
        name="unpack",
    )(bid, keep, other)


def tie(x, *needed):
    return lax.optimization_barrier((x,) + needed)[0]


def across(pieces):
    return [swap(piece, "batch", 2 * d) for d, piece in enumerate(pieces, 1)]


def sum_rest(x):
    for level in range(3, lax.axis_size("batch").bit_length() - 1):
        x = (x.astype(F32) + swap(x, "batch", 1 << level).astype(F32)).astype(x.dtype)
    return x


def fold(kept, got):
    piece = kept.shape[0] // 4
    total = kept[:piece].astype(F32)
    for g in got:
        total = total + g[:piece].astype(F32)
    return sum_rest(total.astype(BF))


def quarters(x):
    piece = x.shape[0] // 4
    return [x[d * piece : (d + 1) * piece] for d in range(1, 4)]


def sum_group(x):
    x = x + swap(x, "head", 1)
    return x + swap(x, "head", 2)


def per_device(
    inputs,
    lengths,
    cotangent,
    gain_attn,
    shift_attn,
    weight_qkv,
    bias_qkv,
    weight_proj,
    bias_proj,
    gain_mlp,
    shift_mlp,
    weight_up,
    bias_up,
    weight_down,
    bias_down,
):
    chunk, width = inputs.shape
    group_rows = chunk * lax.axis_size("head")
    heads, triple = weight_qkv.shape[1:]
    cols = heads * triple
    inner = cols // 3
    own = lax.axis_index("head")
    hid = own.astype(jnp.int32).reshape(1)
    bid = (lax.axis_index("batch") % 8).astype(jnp.int32).reshape(1)
    lens = lengths[0]
    live_rows = jnp.sum(lens[:-1])
    places = own * chunk + jnp.arange(chunk, dtype=jnp.int32)
    live = (places < live_rows)[:, None]
    qkv_t = weight_qkv.transpose(1, 2, 0).reshape(cols, width)
    proj = weight_proj.reshape(inner, width)
    zero = jnp.zeros((width,), F32)
    vectors = jnp.stack(
        (gain_attn, shift_attn, bias_proj, gain_mlp, shift_mlp, bias_up, bias_down, zero)
    )

    x_far = swap(inputs, "head", 2)
    x_near = swap(inputs, "head", 1)
    begun = qkv_call(hid, inputs, x_near, vectors, qkv_t, bias_qkv, 0, group_rows, ())
    x_far = tie(x_far, begun[0])
    x_last = swap(x_far, "head", 1)
    queries, keys, values, values_t = qkv_call(
        hid, x_far, x_last, vectors, qkv_t, bias_qkv, 2, group_rows, begun
    )
    rows = (inputs, x_near, x_far, x_last)
    grad_own = jnp.where(live, cotangent, jnp.zeros_like(cotangent))
    grad_far = swap(tie(grad_own, x_far), "head", 2)
    proj_far = swap(tie(proj, x_far), "head", 2)
    projs = (proj, swap(proj, "head", 1), proj_far, swap(proj_far, "head", 1))

    merged_far, level_far = attend_call(lens, hid, queries, keys, values_t, 2, chunk)
    from_far = swap(merged_far, "head", 2)
    merged_near, level_near = attend_call(
        lens, hid, tie(queries, merged_far, grad_far), keys, values_t, 0, chunk
    )
    grads = (grad_own, swap(grad_own, "head", 1), grad_far, swap(grad_far, "head", 1))
    parts = (merged_near, swap(merged_near, "head", 1), from_far, swap(from_far, "head", 1))
    resid, h_own = mix_call(parts, projs, inputs, vectors)
    h_far = swap(h_own, "head", 2)
    h_near = swap(h_own, "head", 1)

    near = feed_call(h_own, h_near, grads[0], grads[1], weight_up, vectors, weight_down, 0, group_rows, ())
    h_far = tie(h_far, near[0])
    h_last = swap(h_far, "head", 1)
    act, grad_up, grad_norm_far, down_far = feed_call(
        h_far, h_last, grads[2], grads[3], weight_up, vectors, weight_down, 2, group_rows, near[:2]
    )
    swapped = swap(grad_norm_far, "head", 1)
    far_sum = (grad_norm_far[:chunk].astype(F32) + swapped[chunk:].astype(F32)).astype(BF)
    grad_far_sum = swap(far_sum, "head", 2)
    near_swapped = swap(near[2], "head", 1)

    keep_feed, send_feed, grad_bup = weigh_call(
        bid, (h_own, h_near, h_far, h_last), tie(act, far_sum), grad_up, grads
    )
    other_feed = swap(send_feed, "batch", 1)

    grad_resid, grad_att, grad_near, grad_cross, sums = turn_call(
        near[2], near_swapped, tie(grad_far_sum, grad_bup), resid, grad_own, vectors, projs
    )
    grad_near = grad_near.reshape(2 * chunk, inner)
    got = swap(grad_cross.reshape(2 * chunk, inner), "head", 2)
    grad_mate = swap(grad_near, "head", 1)
    grad_att = tie(grad_att, grad_mate)
    low = slice(0, chunk)
    high = slice(chunk, 2 * chunk)
    grad_proj = [
        dot_tn(p[at], grad_att) for p, at in zip(parts, (low, high, low, high), strict=True)
    ]
    near_sent, far_sent = grad_proj[1].astype(BF), grad_proj[3].astype(BF)
    got = tie(got, near_sent, far_sent)
    merged_grads = (grad_near, grad_mate, got, swap(got, "head", 1))
    grad_near_proj = grad_proj[0] + swap(near_sent, "head", 1).astype(F32)
    far_proj = (grad_proj[2] + swap(far_sent, "head", 1).astype(F32)).astype(BF)
    far_proj = swap(far_proj, "head", 2)

    kept_feed = (keep_feed.astype(F32) + tie(other_feed, got).astype(F32)).astype(BF)
    got_feed = across(quarters(kept_feed))

    grad_packed = attend_back_call(
        lens,
        hid,
        tie(queries, kept_feed, grad_near_proj),
        keys,
        values,
        merged_grads,
        (merged_near, merged_far),
        (level_near, level_far),
        chunk,
    )
    got_feed = [tie(g, grad_packed) for g in got_feed]
    grad_wproj = grad_near_proj + tie(far_proj, grad_packed).astype(F32)
    total_feed = fold(kept_feed, got_feed)
    gathered_feed = across([total_feed] * 3)
    total = -(-(cols + inner + 8) // 64) * 64
    e_near, e_far, keep, send = close_call(
        bid, rows, tie(grad_packed, total_feed), qkv_t, vectors, grad_wproj, grad_bup, sums, total
    )
    e_swapped = swap(e_far, "head", 1)
    e_sum = (e_far[:chunk].astype(F32) + e_swapped[chunk:].astype(F32)).astype(BF)
    e_other = swap(e_sum, "head", 2)
    e_mate = swap(e_near, "head", 1)
    e_own = e_near[:chunk].astype(F32) + e_mate[chunk:].astype(F32) + e_other.astype(F32)
    half_feed = jnp.concatenate([total_feed] + [tie(g, e_far) for g in gathered_feed], axis=0)
    last_feed = swap(tie(half_feed, e_sum), "batch", 1)
    other = tie(swap(send, "batch", 1), half_feed)
    kept = (keep.astype(F32) + other.astype(F32)).astype(BF)
    kept, small = kept[:-8], kept[-8:]
    got_attn = across([jnp.concatenate((q, small), axis=0) for q in quarters(kept)])
    tiny = [small.astype(F32)] + [g[-8:].astype(F32) for g in got_attn]
    small = sum_group(sum_rest((tiny[0] + tiny[1]) + (tiny[2] + tiny[3])))
    total_attn = fold(kept, got_attn)

    down_swapped = swap(tie(down_far, kept), "head", 1)
    down_sum = (down_far[:chunk].astype(F32) + down_swapped[chunk:].astype(F32)).astype(BF)
    down_other = swap(tie(down_sum, e_other), "head", 2)
    near_down = near[3][:chunk].astype(F32) + swap(tie(near[3], kept), "head", 1)[chunk:].astype(F32)
    output = (resid + near_down + down_other.astype(F32) + bias_down).astype(BF)

    half = jnp.concatenate([total_attn] + across([total_attn] * 3), axis=0)
    last = swap(tie(half, last_feed), "batch", 1)
    sum_wup, sum_wdown = unpack_call(bid, half_feed, tie(last_feed, half), (width, width))
    sum_wqkv, sum_wproj, sum_bias = unpack_call(bid, half, tie(last, sum_wup), (cols, inner, 8))

    x_hat, x_rstd = normalize(inputs.astype(F32))
    e_own = e_own * gain_attn
    grad_inputs = (
        grad_resid
        + x_rstd
        * (
            e_own
            - jnp.mean(e_own, axis=-1, keepdims=True)
            - x_hat * jnp.mean(e_own * x_hat, axis=-1, keepdims=True)
        )
    ).astype(BF)
    return (
        output,
        grad_inputs,
        small[0],
        small[1],
        sum_wqkv.reshape(heads, triple, width).transpose(2, 0, 1),
        sum_bias[0, :cols].reshape(heads, triple),
        sum_wproj.reshape(heads, inner // heads, width),
        small[4],
        small[5],
        small[6],
        sum_wup,
        sum_bias[1],
        sum_wdown,
        small[7],
    )


def solution(mesh):
    rows = P(("batch", "head"), None)
    in_specs = (
        rows,
        P("batch", None),
        rows,
        P(),
        P(),
        P(None, "head", None),
        P("head", None),
        P("head", None, None),
        P(),
        P(),
        P(),
        P(None, "head"),
        P("head"),
        P("head", None),
        P(),
    )
    out_specs = (
        rows,
        rows,
        P(),
        P(),
        P(None, "head", None),
        P("head", None),
        P("head", None, None),
        P(),
        P(),
        P(),
        P(None, "head"),
        P("head"),
        P("head", None),
        P(),
    )
    return jax.shard_map(
        per_device, mesh=mesh, in_specs=in_specs, out_specs=out_specs, check_vma=False
    )
```

time: 839 us -> 338 us (0.40)
  waiting for transfers between devices: 460 us -> 110 us
  matrix products: 212 us -> 3.74 us
  Pallas kernels: 0 us -> 143 us
  blocking collectives: 66.3 us -> 0 us
  starting transfers between devices: 1.02 us -> 46.3 us
  other arithmetic: 56 us -> 16 us
  between operations: 15.2 us -> 1.13 us
    psum x1 -> x0, waiting for transfers between devices: 189 us -> none  [per_device(): lax.psum((grad_wqkv, grad_bqkv, grad_wproj, grad_wup, grad_bup, grad_wdow...]
    dot_general x33 -> x4, matrix products: 178 us -> 3.74 us  [dot_tn(): lax.dot_general(a, b, (((0,), (0,)), ((), ())), preferred_element_type=F32)]
    reduce_scatter x4 -> x0, waiting for transfers between devices: 167 us -> none  [the longest x1 58.5 us: per_device(): lax.psum_scatter(jnp.dot(merged, proj_matrix, preferred_element_type=jnp....]
    pallas_call x0 -> x13, Pallas kernels: none -> 143 us  [the longest x2 35.5 us: attend_call(): pl.pallas_call(functools.partial(attend_kernel, heads, first, per, 1.0 /...]
    ppermute x0 -> x48, waiting for transfers between devices: none -> 110 us  [swap(): return lax.ppermute(x, axis, [(i, i ^ bits) for i in range(size)])]
    all_gather x4 -> x0, waiting for transfers between devices: 103 us -> none  [the longest x1 28.6 us: per_device(): lax.all_gather(grad_resid.astype(jnp.bfloat16), 'head', axis=0, tiled=True)]
    psum x2 -> x0, blocking collectives: 66.3 us -> none  [the longest x1 44.1 us: per_device(): lax.psum((grad_gattn, grad_sattn, grad_bproj, grad_gmlp, grad_smlp, grad_...]
    ppermute x0 -> x48, starting transfers between devices: none -> 46.3 us  [swap(): return lax.ppermute(x, axis, [(i, i ^ bits) for i in range(size)])]
  transfers between devices with their start and end apart: 9 -> 48, of which waited for: 9 -> 20; matrix products, arithmetic and copies ran while one was open for 5% -> 7% of each run, Pallas kernels for 0% -> 35%
where the time goes in v1:
time: 338 us
  Pallas kernels  143 us (42%)
  waiting for transfers between devices  110 us (33%)
  starting transfers between devices  46.3 us (14%)
  local copies, waits for them, and re-layouts  17.2 us (5%)
  other arithmetic  16 us (5%)
  matrix products  3.74 us (1%)
    ppermute x48, waiting for transfers between devices, swap(): return lax.ppermute(x, axis, [(i, i ^ bits) for i in range(size)])  110 us
    ppermute x48, starting transfers between devices, swap(): return lax.ppermute(x, axis, [(i, i ^ bits) for i in range(size)])  46.3 us
    pallas_call x2, Pallas kernels, attend_call(): pl.pallas_call(functools.partial(attend_kernel, heads, first, per, 1.0 /...  35.5 us
    pallas_call x1, Pallas kernels, attend_back_call(): pl.pallas_call(functools.partial(attend_back_kernel, chunk, 1.0 / math.sq...  33.6 us
    pallas_call x2, Pallas kernels, feed_call(): pl.pallas_call(functools.partial(feed_kernel, steps), out_shape=(jax.Shap...  17.9 us
    pallas_call x1, Pallas kernels, close_call(): pl.pallas_call(functools.partial(close_kernel, per), out_shape=(jax.Shape...  14 us
    pallas_call x1, Pallas kernels, weigh_call(): pl.pallas_call(functools.partial(weigh_kernel, tiles), out_shape=(half, h...  12.4 us
    pallas_call x2, Pallas kernels, qkv_call(): pl.pallas_call(functools.partial(qkv_kernel, heads, hd, steps), out_shape...  12.2 us
  transfers between devices with their start and end apart: 48, of which 20 were waited for; matrix products, arithmetic and copies ran while one was open for 7% of the time, Pallas kernels for 35%

profile of v1, /device:TPU:0, one launch (start us, length us, event | category | flops | bytes accessed | tf_op | source)
XLA Modules:
  0.0 337.9 jit_solution(12880971500650179917)
XLA Ops:
  10.1 6.2 %qkv.2 = (bf16[3,2048,64]{2,1,0:T(8,128)(2,1)}, bf16[3,2048,64]{2,1,0:T(8,128)(2,1)}, bf16[3,2048,64]{2,1,0:T(8,128)(2,1)}, bf16[3,64,2048]{2,1,0:T(8,128)(2,1)}) custom-call(s32[1]{0:T(128)} %bitcast.1.h_ref, bf16[512,768]{1,0:T(8,128)(2,1)} %x0.1, bf16[512,768]{1,0:T(8,128)(2,1)} %copy-done.30, f32[8,768]{1,0:T(8,128)} %stack.31.v_ref, ...), custom_call_target="tpu_custom_call" | custom-call | flops 905969664 | bytes 4718592 | tf_op jit(solution)/shard_map/qkv/pallas_call | solution.py:83
  16.3 5.8 %collective-permute-done.a_ref.x2 = bf16[512,768]{1,0:T(8,128)(2,1)S(1)} collective-permute-done((bf16[512,768]{1,0:T(8,128)(2,1)}, bf16[512,768]{1,0:T(8,128)(2,1)S(1)}, u32[]{:S(2)}, u32[]{:S(2)}) %collective-permute-start) | collective-permute-done | bytes 786464 | tf_op jit(solution)/shard_map/ppermute | solution.py:38
  26.4 6.0 %qkv.3 = (bf16[3,2048,64]{2,1,0:T(8,128)(2,1)}, bf16[3,2048,64]{2,1,0:T(8,128)(2,1)}, bf16[3,2048,64]{2,1,0:T(8,128)(2,1)}, bf16[3,64,2048]{2,1,0:T(8,128)(2,1)}) custom-call(s32[1]{0:T(128)} %bitcast.1.h_ref, bf16[512,768]{1,0:T(8,128)(2,1)} %copy-done.21, ...), custom_call_target="tpu_custom_call", output_to_operand_aliasing={{0}: (6, {}), {1}: (7, {}), {2}: (8, {}), {3}: (9, {})} | custom-call | flops 905969664 | bytes 4718592 | tf_op jit(solution)/shard_map/qkv/pallas_call | solution.py:83
  32.4 21.6 %attend.2 = (bf16[1024,192]{1,0:T(8,128)(2,1)}, f32[8,1024]{1,0:T(8,128)}) custom-call(s32[8]{0:T(128)} %bitcast.29, s32[1]{0:T(128)} %bitcast.1.h_ref, bf16[3,2048,64]{2,1,0:T(8,128)(2,1)} %get-tuple-element.114.q_ref, bf16[3,2048,64]{2,1,0:T(8,128)(2,1)} %get-tuple-element.86.k_ref, bf16[3,64,2048]{2,1,0:T(8,128)(2,1)} %get-tuple-element.87.vt_ref), custom_call_target="tpu_custom_call" | custom-call | flops 3221225472 | bytes 4718592 | tf_op jit(solution)/shard_map/attend/pallas_call | solution.py:165
  56.0 14.0 %attend.3 = (bf16[1024,192]{1,0:T(8,128)(2,1)}, f32[8,1024]{1,0:T(8,128)}) custom-call(s32[8]{0:T(128)} %bitcast.30, s32[1]{0:T(128)} %bitcast.1.h_ref, bf16[3,2048,64]{2,1,0:T(8,128)(2,1)} %get-tuple-element.114.q_ref, bf16[3,2048,64]{2,1,0:T(8,128)(2,1)} %get-tuple-element.86.k_ref, bf16[3,64,2048]{2,1,0:T(8,128)(2,1)} %get-tuple-element.87.vt_ref), custom_call_target="tpu_custom_call" | custom-call | flops 3221225472 | bytes 4718592 | tf_op jit(solution)/shard_map/attend/pallas_call | solution.py:165
  70.6 3.8 %collective-permute-done.8.p2 = bf16[192,768]{1,0:T(8,128)(2,1)S(1)} collective-permute-done((bf16[192,768]{1,0:T(8,128)(2,1)S(1)}, bf16[192,768]{1,0:T(8,128)(2,1)S(1)}, u32[]{:S(2)}, u32[]{:S(2)}) %collective-permute-start.8) | collective-permute-done | bytes 294944 | tf_op jit(solution)/shard_map/ppermute | solution.py:38
  76.9 4.1 %mix.1 = (f32[512,768]{1,0:T(8,128)}, bf16[512,768]{1,0:T(8,128)(2,1)}) custom-call(bf16[1024,192]{1,0:T(8,128)(2,1)} %get-tuple-element.91.m0.rest_4_, bf16[1024,192]{1,0:T(8,128)(2,1)} %copy-done.18, bf16[1024,192]{1,0:T(8,128)(2,1)} %copy-done.16, bf16[1024,192]{1,0:T(8,128)(2,1)} %collective-permute-done.6.m3, bf16[192,768]{1,0:T(8,128)(2,1)} %bitcast.17, ...), custom_call_target="tpu_custom_call" | custom-call | flops 603979776 | bytes 4718592 | tf_op jit(solution)/shard_map/mix/pallas_call | solution.py:443
  81.2 5.2 %collective-permute-start.12 = (bf16[512,768]{1,0:T(8,128)(2,1)}, bf16[512,768]{1,0:T(8,128)(2,1)S(1)}, u32[]{:S(2)}, u32[]{:S(2)}) collective-permute-start(bf16[512,768]{1,0:T(8,128)(2,1)} %get-tuple-element.94.ha_ref.h0), channel_id=1, source_target_pairs={{0,2},{1,3},{2,0},{3,1},{4,6},{5,7},{6,4},{7,5},{8,10},{9,11},{10,... | collective-permute-start | bytes 2359304 | tf_op jit(solution)/shard_map/ppermute | solution.py:38
  87.4 8.9 %feed.2 = (bf16[2048,768]{1,0:T(8,128)(2,1)}, bf16[2048,768]{1,0:T(8,128)(2,1)}, bf16[1024,768]{1,0:T(8,128)(2,1)}, bf16[1024,768]{1,0:T(8,128)(2,1)}) custom-call(bf16[512,768]{1,0:T(8,128)(2,1)} %get-tuple-element.94.ha_ref.h0, bf16[512,768]{1,0:T(8,128)(2,1)} %copy-done.33, bf16[512,768]{1,0:T(8,128)(2,1)} %copy-done.4, ...), custom_call_target="tpu_custom_call" | custom-call | flops 4831838208 | bytes 6291456 | tf_op jit(solution)/shard_map/feed/pallas_call | solution.py:323
  96.2 8.4 %collective-permute-done.12.ha_ref.h2 = bf16[512,768]{1,0:T(8,128)(2,1)S(1)} collective-permute-done((bf16[512,768]{1,0:T(8,128)(2,1)}, bf16[512,768]{1,0:T(8,128)(2,1)S(1)}, u32[]{:S(2)}, u32[]{:S(2)}) %collective-permute-start.12) | collective-permute-done | bytes 786464 | tf_op jit(solution)/shard_map/ppermute | solution.py:38
  107.8 9.0 %feed.3 = (bf16[2048,768]{1,0:T(8,128)(2,1)}, bf16[2048,768]{1,0:T(8,128)(2,1)}, bf16[1024,768]{1,0:T(8,128)(2,1)}, bf16[1024,768]{1,0:T(8,128)(2,1)}) custom-call(bf16[512,768]{1,0:T(8,128)(2,1)} %copy-done.34, bf16[512,768]{1,0:T(8,128)(2,1)} %copy-done.35, bf16[512,768]{1,0:T(8,128)(2,1)} %copy-done.31, ...), custom_call_target="tpu_custom_call", output_to_operand_aliasing={{0}: (7, {}), {1}: (8, {})} | custom-call | flops 4831838208 | bytes 6291456 | tf_op jit(solution)/shard_map/feed/pallas_call | solution.py:323
  117.4 3.1 collective-permute-done.15
  124.4 12.4 %weigh.1 = (bf16[768,768]{1,0:T(8,128)(2,1)}, bf16[768,768]{1,0:T(8,128)(2,1)}, f32[1,768]{1,0:T(1,128)}) custom-call(s32[1]{0:T(128)} %bitcast.5.b_ref, bf16[512,768]{1,0:T(8,128)(2,1)} %get-tuple-element.94.ha_ref.h0, bf16[512,768]{1,0:T(8,128)(2,1)} %copy-done.33, bf16[512,768]{1,0:T(8,128)(2,1)} %copy-done.34, bf16[512,768]{1,0:T(8,128)(2,1)} %copy-done.35, ...), custom_call_target="tpu_custom_call" | custom-call | flops 4831838208 | bytes 18874368 | tf_op jit(solution)/shard_map/weigh/pallas_call | solution.py:403
  136.9 5.7 %collective-permute-done.18.f_ref = bf16[512,768]{1,0:T(8,128)(2,1)} collective-permute-done((bf16[512,768]{1,0:T(8,128)(2,1)}, bf16[512,768]{1,0:T(8,128)(2,1)}, u32[]{:S(2)}, u32[]{:S(2)}) %collective-permute-start.18) | collective-permute-done | bytes 786464 | tf_op jit(solution)/shard_map/ppermute | solution.py:38
  143.8 6.2 %turn.1 = (f32[512,768]{1,0:T(8,128)}, bf16[512,768]{1,0:T(8,128)(2,1)}, bf16[2,512,192]{2,1,0:T(8,128)(2,1)}, bf16[2,512,192]{2,1,0:T(8,128)(2,1)}, f32[8,768]{1,0:T(8,128)}) custom-call(bf16[1024,768]{1,0:T(8,128)(2,1)} %get-tuple-element.105.n_ref, bf16[1024,768]{1,0:T(8,128)(2,1)} %copy-done.9, bf16[512,768]{1,0:T(8,128)(2,1)} %collective-permute-done.18.f_ref, ...), custom_call_target="tpu_custom_call" | custom-call | flops 603979776 | bytes 7864320 | tf_op jit(solution)/shard_map/turn/pallas_call | solution.py:488
  156.7 7.9 %collective-permute-done.19.rest_2_ = bf16[1024,192]{1,0:T(8,128)(2,1)S(1)} collective-permute-done((bf16[1024,192]{1,0:T(8,128)(2,1)}, bf16[1024,192]{1,0:T(8,128)(2,1)S(1)}, u32[]{:S(2)}, u32[]{:S(2)}) %collective-permute-start.19) | collective-permute-done | bytes 393248 | tf_op jit(solution)/shard_map/ppermute | solution.py:38
  166.7 4.1 %collective-permute-start.24 = (bf16[192,768]{1,0:T(8,128)(2,1)S(1)}, bf16[192,768]{1,0:T(8,128)(2,1)}, u32[]{:S(2)}, u32[]{:S(2)}) collective-permute-start(bf16[192,768]{1,0:T(8,128)(2,1)S(1)} %get-tuple-element.156), channel_id=1, source_target_pairs={{0,16},{4,20},{8,24},{12,28},{16,0},{20,4},{24,8},{28,12},{1,17},{... | collective-permute-start | bytes 884744 | tf_op jit(solution)/shard_map/ppermute | solution.py:38
  174.4 33.6 %attend_back.1.gp_ref = bf16[2048,576]{1,0:T(8,128)(2,1)} custom-call(s32[8]{0:T(128)} %bitcast.31, s32[1]{0:T(128)} %bitcast.1.h_ref, bf16[3,2048,64]{2,1,0:T(8,128)(2,1)} %get-tuple-element.114.q_ref, bf16[3,2048,64]{2,1,0:T(8,128)(2,1)} %get-tuple-element.86.k_ref, bf16[3,2048,64]{2,1,0:T(8,128)(2,1)} %get-tuple-element.115.v_ref, ...), custom_call_target="tpu_custom_call" | custom-call | flops 16106127360 | bytes 11796480 | tf_op jit(solution)/shard_map/attend_back/pallas_call | solution.py:276
  211.2 14.0 %close.1 = (bf16[1024,768]{1,0:T(8,128)(2,1)}, bf16[1024,768]{1,0:T(8,128)(2,1)}, bf16[424,768]{1,0:T(8,128)(2,1)}, bf16[424,768]{1,0:T(8,128)(2,1)}) custom-call(s32[1]{0:T(128)} %bitcast.5.b_ref, bf16[512,768]{1,0:T(8,128)(2,1)} %x0.1, bf16[512,768]{1,0:T(8,128)(2,1)} %copy-done.30, bf16[512,768]{1,0:T(8,128)(2,1)} %copy-done.21, ...), custom_call_target="tpu_custom_call" | custom-call | flops 3623878656 | bytes 7864320 | tf_op jit(solution)/shard_map/close/pallas_call | solution.py:553
  225.6 3.8 %collective-permute-start.30 = (bf16[192,768]{1,0:T(8,128)(2,1)S(1)}, bf16[192,768]{1,0:T(8,128)(2,1)S(1)}, u32[]{:S(2)}, u32[]{:S(2)}) collective-permute-start(bf16[192,768]{1,0:T(8,128)(2,1)S(1)} %add_convert_fusion.6), channel_id=1, source_target_pairs={{0,16},{4,20},{8,24},{12,28},{16,0},{20,4},{24,8},{28,12},{1,17},{... | collective-permute-start | bytes 884744 | tf_op jit(solution)/shard_map/ppermute | solution.py:38
  229.9 8.9 %collective-permute-done.29 = bf16[192,768]{1,0:T(8,128)(2,1)S(1)} collective-permute-done((bf16[192,768]{1,0:T(8,128)(2,1)S(1)}, bf16[192,768]{1,0:T(8,128)(2,1)S(1)}, u32[]{:S(2)}, u32[]{:S(2)}) %collective-permute-start.29) | collective-permute-done | bytes 294944 | tf_op jit(solution)/shard_map/ppermute | solution.py:38
  238.8 11.1 %collective-permute-done.30 = bf16[192,768]{1,0:T(8,128)(2,1)S(1)} collective-permute-done((bf16[192,768]{1,0:T(8,128)(2,1)S(1)}, bf16[192,768]{1,0:T(8,128)(2,1)S(1)}, u32[]{:S(2)}, u32[]{:S(2)}) %collective-permute-start.30) | collective-permute-done | bytes 294944 | tf_op jit(solution)/shard_map/ppermute | solution.py:38
  250.4 5.2 %collective-permute-start.38 = (bf16[112,768]{1,0:T(8,128)(2,1)S(1)}, bf16[112,768]{1,0:T(8,128)(2,1)S(1)}, u32[]{:S(2)}, u32[]{:S(2)}) collective-permute-start(bf16[112,768]{1,0:T(8,128)(2,1)S(1)} %get-tuple-element.159), channel_id=1, source_target_pairs={{0,8},{4,12},{8,0},{12,4},{16,24},{20,28},{24,16},{28,20},{1,9},{5... | collective-permute-start | bytes 516104 | tf_op jit(solution)/shard_map/ppermute | solution.py:38
  258.1 3.0 collective-permute-done.38
  261.1 9.1 %collective-permute-done.39 = bf16[112,768]{1,0:T(8,128)(2,1)S(1)} collective-permute-done((bf16[112,768]{1,0:T(8,128)(2,1)S(1)}, bf16[112,768]{1,0:T(8,128)(2,1)S(1)}, u32[]{:S(2)}, u32[]{:S(2)}) %collective-permute-start.39) | collective-permute-done | bytes 172064 | tf_op jit(solution)/shard_map/ppermute | solution.py:38
  275.3 3.4 collective-permute-done.42
  281.4 5.6 %collective-permute-done.44 = bf16[104,768]{1,0:T(8,128)(2,1)S(1)} collective-permute-done((bf16[104,768]{1,0:T(8,128)(2,1)S(1)}, bf16[104,768]{1,0:T(8,128)(2,1)S(1)}, u32[]{:S(2)}, u32[]{:S(2)}) %collective-permute-start.44) | collective-permute-done | bytes 159776 | tf_op jit(solution)/shard_map/ppermute | solution.py:38
  290.3 9.8 %collective-permute-done.35 = bf16[512,768]{1,0:T(8,128)(2,1)S(1)} collective-permute-done((bf16[512,768]{1,0:T(8,128)(2,1)S(1)}, bf16[512,768]{1,0:T(8,128)(2,1)S(1)}, u32[]{:S(2)}, u32[]{:S(2)}) %collective-permute-start.35) | collective-permute-done | bytes 786464 | tf_op jit(solution)/shard_map/ppermute | solution.py:38
  301.2 14.2 %collective-permute-done.46.other_ref = bf16[768,768]{1,0:T(8,128)(2,1)S(1)} collective-permute-done((bf16[768,768]{1,0:T(8,128)(2,1)S(1)}, bf16[768,768]{1,0:T(8,128)(2,1)S(1)}, u32[]{:S(2)}, u32[]{:S(2)}) %collective-permute-start.46) | collective-permute-done | bytes 1179680 | tf_op jit(solution)/shard_map/ppermute | solution.py:38
  318.5 4.4 %unpack.2 = (f32[768,768]{1,0:T(8,128)}, f32[768,768]{1,0:T(8,128)}) custom-call(s32[1]{0:T(128)} %bitcast.5.b_ref, bf16[768,768]{1,0:T(8,128)(2,1)} %copy-done.3, bf16[768,768]{1,0:T(8,128)(2,1)} %copy-done.15), custom_call_target="tpu_custom_call" | custom-call | flops 589824 | bytes 7077888 | tf_op jit(solution)/shard_map/unpack/pallas_call | solution.py:596
  325.8 5.6 %collective-permute-done.47.other_ref = bf16[416,768]{1,0:T(8,128)(2,1)S(1)} collective-permute-done((bf16[416,768]{1,0:T(8,128)(2,1)S(1)}, bf16[416,768]{1,0:T(8,128)(2,1)S(1)}, u32[]{:S(2)}, u32[]{:S(2)}) %collective-permute-start.47) | collective-permute-done | bytes 639008 | tf_op jit(solution)/shard_map/ppermute | solution.py:38
  332.3 2.9 unpack.3
  (203 shorter events, 69.5 us)
Async XLA Ops:
  1.2 20.9 %collective-permute-start = (bf16[512,768]{1,0:T(8,128)(2,1)}, bf16[512,768]{1,0:T(8,128)(2,1)S(1)}, u32[]{:S(2)}, u32[]{:S(2)}) collective-permute-start(bf16[512,768]{1,0:T(8,128)(2,1)} %x0.1), channel_id=1, source_target_pairs={{0,2},{1,3},{2,0},{3,1},{4,6},{5,7},{6,4},{7,5},{8,10},{9,11},{10,... | collective-permute-start | bytes 2359304 | tf_op jit(solution)/shard_map/ppermute | solution.py:38
  23.7 32.3 %collective-permute-start.3 = (bf16[512,768]{1,0:T(8,128)(2,1)S(1)}, bf16[512,768]{1,0:T(8,128)(2,1)S(1)}, u32[]{:S(2)}, u32[]{:S(2)}) collective-permute-start(bf16[512,768]{1,0:T(8,128)(2,1)S(1)} %broadcast_select_fusion.ga_ref.g0.cot_ref), channel_id=1, source_target_pairs={{0,2},{1,3},{2,0},{3,1},{4,6},{5,7},{6,4},{7,5},{8,10},{9,11},{10,... | collective-permute-start | bytes 2359304 | tf_op jit(solution)/shard_map/ppermute | solution.py:38
  54.0 16.0 %collective-permute-start.5 = (bf16[1024,192]{1,0:T(8,128)(2,1)}, bf16[1024,192]{1,0:T(8,128)(2,1)S(1)}, u32[]{:S(2)}, u32[]{:S(2)}) collective-permute-start(bf16[1024,192]{1,0:T(8,128)(2,1)} %get-tuple-element.88.rest_5_), channel_id=1, source_target_pairs={{0,2},{1,3},{2,0},{3,1},{4,6},{5,7},{6,4},{7,5},{8,10},{9,11},{10,... | collective-permute-start | bytes 1179656 | tf_op jit(solution)/shard_map/ppermute | solution.py:38
  54.0 20.5 %collective-permute-start.8 = (bf16[192,768]{1,0:T(8,128)(2,1)S(1)}, bf16[192,768]{1,0:T(8,128)(2,1)S(1)}, u32[]{:S(2)}, u32[]{:S(2)}) collective-permute-start(bf16[192,768]{1,0:T(8,128)(2,1)S(1)} %bitcast.19), channel_id=1, source_target_pairs={{0,2},{1,3},{2,0},{3,1},{4,6},{5,7},{6,4},{7,5},{8,10},{9,11},{10,... | collective-permute-start | bytes 884744 | tf_op jit(solution)/shard_map/ppermute | solution.py:38
  74.5 12.0 %collective-permute-start.11 = (bf16[512,768]{1,0:T(8,128)(2,1)S(1)}, bf16[512,768]{1,0:T(8,128)(2,1)}, u32[]{:S(2)}, u32[]{:S(2)}) collective-permute-start(bf16[512,768]{1,0:T(8,128)(2,1)S(1)} %broadcast_select_fusion.ga_ref.g0.cot_ref), channel_id=1, source_target_pairs={{0,1},{1,0},{2,3},{3,2},{4,5},{5,4},{6,7},{7,6},{8,9},{9,8},{10,11... | collective-permute-start | bytes 2359304 | tf_op jit(solution)/shard_map/ppermute | solution.py:38
  81.2 23.5 %collective-permute-start.12 = (bf16[512,768]{1,0:T(8,128)(2,1)}, bf16[512,768]{1,0:T(8,128)(2,1)S(1)}, u32[]{:S(2)}, u32[]{:S(2)}) collective-permute-start(bf16[512,768]{1,0:T(8,128)(2,1)} %get-tuple-element.94.ha_ref.h0), channel_id=1, source_target_pairs={{0,2},{1,3},{2,0},{3,1},{4,6},{5,7},{6,4},{7,5},{8,10},{9,11},{10,... | collective-permute-start | bytes 2359304 | tf_op jit(solution)/shard_map/ppermute | solution.py:38
  86.4 18.3 %collective-permute-start.14 = (bf16[512,768]{1,0:T(8,128)(2,1)S(1)}, bf16[512,768]{1,0:T(8,128)(2,1)}, u32[]{:S(2)}, u32[]{:S(2)}) collective-permute-start(bf16[512,768]{1,0:T(8,128)(2,1)S(1)} %copy-done.32), channel_id=1, source_target_pairs={{0,1},{1,0},{2,3},{3,2},{4,5},{5,4},{6,7},{7,6},{8,9},{9,8},{10,11... | collective-permute-start | bytes 2359304 | tf_op jit(solution)/shard_map/ppermute | solution.py:38
  117.0 25.6 %collective-permute-start.17 = (bf16[1024,768]{1,0:T(8,128)(2,1)S(1)}, bf16[1024,768]{1,0:T(8,128)(2,1)S(1)}, u32[]{:S(2)}, u32[]{:S(2)}) collective-permute-start(bf16[1024,768]{1,0:T(8,128)(2,1)S(1)} %copy-done.8), channel_id=1, source_target_pairs={{0,1},{1,0},{2,3},{3,2},{4,5},{5,4},{6,7},{7,6},{8,9},{9,8},{10,11... | collective-permute-start | bytes 4718600 | tf_op jit(solution)/shard_map/ppermute | solution.py:38
  122.7 19.9 %collective-permute-start.18 = (bf16[512,768]{1,0:T(8,128)(2,1)}, bf16[512,768]{1,0:T(8,128)(2,1)}, u32[]{:S(2)}, u32[]{:S(2)}) collective-permute-start(bf16[512,768]{1,0:T(8,128)(2,1)} %add_convert_fusion.4), channel_id=1, source_target_pairs={{0,2},{1,3},{2,0},{3,1},{4,6},{5,7},{6,4},{7,5},{8,10},{9,11},{10,... | collective-permute-start | bytes 2359304 | tf_op jit(solution)/shard_map/ppermute | solution.py:38
  136.9 28.0 %collective-permute-start.16 = (bf16[768,768]{1,0:T(8,128)(2,1)}, bf16[768,768]{1,0:T(8,128)(2,1)}, u32[]{:S(2)}, u32[]{:S(2)}) collective-permute-start(bf16[768,768]{1,0:T(8,128)(2,1)} %get-tuple-element.104), channel_id=1, source_target_pairs={{0,4},{4,0},{8,12},{12,8},{16,20},{20,16},{24,28},{28,24},{1,5},{5... | collective-permute-start | bytes 3538952 | tf_op jit(solution)/shard_map/ppermute | solution.py:38
  150.1 14.5 %collective-permute-start.19 = (bf16[1024,192]{1,0:T(8,128)(2,1)}, bf16[1024,192]{1,0:T(8,128)(2,1)S(1)}, u32[]{:S(2)}, u32[]{:S(2)}) collective-permute-start(bf16[1024,192]{1,0:T(8,128)(2,1)} %bitcast.28), channel_id=1, source_target_pairs={{0,2},{1,3},{2,0},{3,1},{4,6},{5,7},{6,4},{7,5},{8,10},{9,11},{10,... | collective-permute-start | bytes 1179656 | tf_op jit(solution)/shard_map/ppermute | solution.py:38
  154.6 16.2 %collective-permute-start.26 = (bf16[192,768]{1,0:T(8,128)(2,1)S(1)}, bf16[192,768]{1,0:T(8,128)(2,1)S(1)}, u32[]{:S(2)}, u32[]{:S(2)}) collective-permute-start(bf16[192,768]{1,0:T(8,128)(2,1)S(1)} %convolution_convert_fusion), channel_id=1, source_target_pairs={{0,1},{1,0},{2,3},{3,2},{4,5},{5,4},{6,7},{7,6},{8,9},{9,8},{10,11... | collective-permute-start | bytes 884744 | tf_op jit(solution)/shard_map/ppermute | solution.py:38
  156.3 15.1 %collective-permute-start.21 = (bf16[192,768]{1,0:T(8,128)(2,1)S(1)}, bf16[192,768]{1,0:T(8,128)(2,1)S(1)}, u32[]{:S(2)}, u32[]{:S(2)}) collective-permute-start(bf16[192,768]{1,0:T(8,128)(2,1)S(1)} %convolution_convert_fusion.1), channel_id=1, source_target_pairs={{0,1},{1,0},{2,3},{3,2},{4,5},{5,4},{6,7},{7,6},{8,9},{9,8},{10,11... | collective-permute-start | bytes 884744 | tf_op jit(solution)/shard_map/ppermute | solution.py:38
  166.6 41.4 %collective-permute-start.23 = (bf16[192,768]{1,0:T(8,128)(2,1)S(1)}, bf16[192,768]{1,0:T(8,128)(2,1)}, u32[]{:S(2)}, u32[]{:S(2)}) collective-permute-start(bf16[192,768]{1,0:T(8,128)(2,1)S(1)} %get-tuple-element.154), channel_id=1, source_target_pairs={{0,8},{4,12},{8,0},{12,4},{16,24},{20,28},{24,16},{28,20},{1,9},{5... | collective-permute-start | bytes 884744 | tf_op jit(solution)/shard_map/ppermute | solution.py:38
  166.7 41.3 %collective-permute-start.24 = (bf16[192,768]{1,0:T(8,128)(2,1)S(1)}, bf16[192,768]{1,0:T(8,128)(2,1)}, u32[]{:S(2)}, u32[]{:S(2)}) collective-permute-start(bf16[192,768]{1,0:T(8,128)(2,1)S(1)} %get-tuple-element.156), channel_id=1, source_target_pairs={{0,16},{4,20},{8,24},{12,28},{16,0},{20,4},{24,8},{28,12},{1,17},{... | collective-permute-start | bytes 884744 | tf_op jit(solution)/shard_map/ppermute | solution.py:38
  170.9 37.2 %collective-permute-start.25 = (bf16[192,768]{1,0:T(8,128)(2,1)S(1)}, bf16[192,768]{1,0:T(8,128)(2,1)}, u32[]{:S(2)}, u32[]{:S(2)}) collective-permute-start(bf16[192,768]{1,0:T(8,128)(2,1)S(1)} %get-tuple-element.155), channel_id=1, source_target_pairs={{0,24},{4,28},{8,16},{12,20},{16,8},{20,12},{24,0},{28,4},{1,25},{... | collective-permute-start | bytes 884744 | tf_op jit(solution)/shard_map/ppermute | solution.py:38
  171.5 37.9 %collective-permute-start.27 = (bf16[192,768]{1,0:T(8,128)(2,1)S(1)}, bf16[192,768]{1,0:T(8,128)(2,1)}, u32[]{:S(2)}, u32[]{:S(2)}) collective-permute-start(bf16[192,768]{1,0:T(8,128)(2,1)S(1)} %fusion.10), channel_id=1, source_target_pairs={{0,2},{1,3},{2,0},{3,1},{4,6},{5,7},{6,4},{7,5},{8,10},{9,11},{10,... | collective-permute-start | bytes 884744 | tf_op jit(solution)/shard_map/ppermute | solution.py:38
  225.2 24.9 %collective-permute-start.28 = (bf16[424,768]{1,0:T(8,128)(2,1)}, bf16[424,768]{1,0:T(8,128)(2,1)S(1)}, u32[]{:S(2)}, u32[]{:S(2)}) collective-permute-start(bf16[424,768]{1,0:T(8,128)(2,1)} %get-tuple-element.125), channel_id=1, source_target_pairs={{0,4},{4,0},{8,12},{12,8},{16,20},{20,16},{24,28},{28,24},{1,5},{5... | collective-permute-start | bytes 1953800 | tf_op jit(solution)/shard_map/ppermute | solution.py:38
  225.2 13.6 %collective-permute-start.29 = (bf16[192,768]{1,0:T(8,128)(2,1)S(1)}, bf16[192,768]{1,0:T(8,128)(2,1)S(1)}, u32[]{:S(2)}, u32[]{:S(2)}) collective-permute-start(bf16[192,768]{1,0:T(8,128)(2,1)S(1)} %add_convert_fusion.6), channel_id=1, source_target_pairs={{0,8},{4,12},{8,0},{12,4},{16,24},{20,28},{24,16},{28,20},{1,9},{5... | collective-permute-start | bytes 884744 | tf_op jit(solution)/shard_map/ppermute | solution.py:38
  225.6 24.3 %collective-permute-start.30 = (bf16[192,768]{1,0:T(8,128)(2,1)S(1)}, bf16[192,768]{1,0:T(8,128)(2,1)S(1)}, u32[]{:S(2)}, u32[]{:S(2)}) collective-permute-start(bf16[192,768]{1,0:T(8,128)(2,1)S(1)} %add_convert_fusion.6), channel_id=1, source_target_pairs={{0,16},{4,20},{8,24},{12,28},{16,0},{20,4},{24,8},{28,12},{1,17},{... | collective-permute-start | bytes 884744 | tf_op jit(solution)/shard_map/ppermute | solution.py:38
  229.5 20.5 %collective-permute-start.31 = (bf16[192,768]{1,0:T(8,128)(2,1)S(1)}, bf16[192,768]{1,0:T(8,128)(2,1)S(1)}, u32[]{:S(2)}, u32[]{:S(2)}) collective-permute-start(bf16[192,768]{1,0:T(8,128)(2,1)S(1)} %add_convert_fusion.6), channel_id=1, source_target_pairs={{0,24},{4,28},{8,16},{12,20},{16,8},{20,12},{24,0},{28,4},{1,25},{... | collective-permute-start | bytes 884744 | tf_op jit(solution)/shard_map/ppermute | solution.py:38
  229.7 45.1 %collective-permute-start.34 = (bf16[1024,768]{1,0:T(8,128)(2,1)}, bf16[1024,768]{1,0:T(8,128)(2,1)S(1)}, u32[]{:S(2)}, u32[]{:S(2)}) collective-permute-start(bf16[1024,768]{1,0:T(8,128)(2,1)} %get-tuple-element.126), channel_id=1, source_target_pairs={{0,1},{1,0},{2,3},{3,2},{4,5},{5,4},{6,7},{7,6},{8,9},{9,8},{10,11... | collective-permute-start | bytes 4718600 | tf_op jit(solution)/shard_map/ppermute | solution.py:38
  255.6 14.5 %collective-permute-start.39 = (bf16[112,768]{1,0:T(8,128)(2,1)S(1)}, bf16[112,768]{1,0:T(8,128)(2,1)S(1)}, u32[]{:S(2)}, u32[]{:S(2)}) collective-permute-start(bf16[112,768]{1,0:T(8,128)(2,1)S(1)} %get-tuple-element.160), channel_id=1, source_target_pairs={{0,16},{4,20},{8,24},{12,28},{16,0},{20,4},{24,8},{28,12},{1,17},{... | collective-permute-start | bytes 516104 | tf_op jit(solution)/shard_map/ppermute | solution.py:38
  256.7 13.5 %collective-permute-start.40 = (bf16[112,768]{1,0:T(8,128)(2,1)S(1)}, bf16[112,768]{1,0:T(8,128)(2,1)S(1)}, u32[]{:S(2)}, u32[]{:S(2)}) collective-permute-start(bf16[112,768]{1,0:T(8,128)(2,1)S(1)} %concatenate.20), channel_id=1, source_target_pairs={{0,24},{4,28},{8,16},{12,20},{16,8},{20,12},{24,0},{28,4},{1,25},{... | collective-permute-start | bytes 516104 | tf_op jit(solution)/shard_map/ppermute | solution.py:38
  258.0 31.2 %collective-permute-start.33 = (bf16[1024,768]{1,0:T(8,128)(2,1)S(1)}, bf16[1024,768]{1,0:T(8,128)(2,1)S(1)}, u32[]{:S(2)}, u32[]{:S(2)}) collective-permute-start(bf16[1024,768]{1,0:T(8,128)(2,1)S(1)} %copy-done.26), channel_id=1, source_target_pairs={{0,1},{1,0},{2,3},{3,2},{4,5},{5,4},{6,7},{7,6},{8,9},{9,8},{10,11... | collective-permute-start | bytes 4718600 | tf_op jit(solution)/shard_map/ppermute | solution.py:38
  261.1 39.4 %collective-permute-start.37 = (bf16[1024,768]{1,0:T(8,128)(2,1)S(1)}, bf16[1024,768]{1,0:T(8,128)(2,1)S(1)}, u32[]{:S(2)}, u32[]{:S(2)}) collective-permute-start(bf16[1024,768]{1,0:T(8,128)(2,1)S(1)} %copy-done.6), channel_id=1, source_target_pairs={{0,1},{1,0},{2,3},{3,2},{4,5},{5,4},{6,7},{7,6},{8,9},{9,8},{10,11... | collective-permute-start | bytes 4718600 | tf_op jit(solution)/shard_map/ppermute | solution.py:38
  272.8 14.2 %collective-permute-start.44 = (bf16[104,768]{1,0:T(8,128)(2,1)S(1)}, bf16[104,768]{1,0:T(8,128)(2,1)S(1)}, u32[]{:S(2)}, u32[]{:S(2)}) collective-permute-start(bf16[104,768]{1,0:T(8,128)(2,1)S(1)} %add_convert_fusion.7), channel_id=1, source_target_pairs={{0,16},{4,20},{8,24},{12,28},{16,0},{20,4},{24,8},{28,12},{1,17},{... | collective-permute-start | bytes 479240 | tf_op jit(solution)/shard_map/ppermute | solution.py:38
  280.8 19.4 %collective-permute-start.35 = (bf16[512,768]{1,0:T(8,128)(2,1)S(1)}, bf16[512,768]{1,0:T(8,128)(2,1)S(1)}, u32[]{:S(2)}, u32[]{:S(2)}) collective-permute-start(bf16[512,768]{1,0:T(8,128)(2,1)S(1)} %add_convert_fusion.2), channel_id=1, source_target_pairs={{0,2},{1,3},{2,0},{3,1},{4,6},{5,7},{6,4},{7,5},{8,10},{9,11},{10,... | collective-permute-start | bytes 2359304 | tf_op jit(solution)/shard_map/ppermute | solution.py:38
  287.0 35.8 %collective-permute-start.32 = (bf16[1024,768]{1,0:T(8,128)(2,1)}, bf16[1024,768]{1,0:T(8,128)(2,1)}, u32[]{:S(2)}, u32[]{:S(2)}) collective-permute-start(bf16[1024,768]{1,0:T(8,128)(2,1)} %get-tuple-element.131), channel_id=1, source_target_pairs={{0,1},{1,0},{2,3},{3,2},{4,5},{5,4},{6,7},{7,6},{8,9},{9,8},{10,11... | collective-permute-start | bytes 4718600 | tf_op jit(solution)/shard_map/ppermute | solution.py:38
  287.1 28.4 %collective-permute-start.46 = (bf16[768,768]{1,0:T(8,128)(2,1)S(1)}, bf16[768,768]{1,0:T(8,128)(2,1)S(1)}, u32[]{:S(2)}, u32[]{:S(2)}) collective-permute-start(bf16[768,768]{1,0:T(8,128)(2,1)S(1)} %pad_maximum_fusion.keep_ref), channel_id=1, source_target_pairs={{0,4},{4,0},{8,12},{12,8},{16,20},{20,16},{24,28},{28,24},{1,5},{5... | collective-permute-start | bytes 3538952 | tf_op jit(solution)/shard_map/ppermute | solution.py:38
  300.2 22.7 %collective-permute-start.36 = (bf16[512,768]{1,0:T(8,128)(2,1)}, bf16[512,768]{1,0:T(8,128)(2,1)}, u32[]{:S(2)}, u32[]{:S(2)}) collective-permute-start(bf16[512,768]{1,0:T(8,128)(2,1)} %add_convert_fusion.3), channel_id=1, source_target_pairs={{0,2},{1,3},{2,0},{3,1},{4,6},{5,7},{6,4},{7,5},{8,10},{9,11},{10,... | collective-permute-start | bytes 2359304 | tf_op jit(solution)/shard_map/ppermute | solution.py:38
  315.4 16.0 %collective-permute-start.47 = (bf16[416,768]{1,0:T(8,128)(2,1)S(1)}, bf16[416,768]{1,0:T(8,128)(2,1)S(1)}, u32[]{:S(2)}, u32[]{:S(2)}) collective-permute-start(bf16[416,768]{1,0:T(8,128)(2,1)S(1)} %pad_maximum_fusion.1.keep_ref), channel_id=1, source_target_pairs={{0,4},{4,0},{8,12},{12,8},{16,20},{20,16},{24,28},{28,24},{1,5},{5... | collective-permute-start | bytes 1916936 | tf_op jit(solution)/shard_map/ppermute | solution.py:38
  (56 other events, 482.8 us)

commit v2 on v1

--- a/solution.py
+++ b/solution.py
@@ -45,10 +45,11 @@
 
 
 def qkv_kernel(heads, hd, steps, h_ref, a_ref, b_ref, v_ref, w_ref, bias_ref, *rest):
-    q_out, k_out, v_out, vt_out = rest[-4:]
+    q_out, k_out, v_out, vt_out, hat_out = rest[-5:]
     t = pl.program_id(0)
     x = jnp.where(t < steps // 2, a_ref[...], b_ref[...]).astype(F32)
     xhat, _ = normalize(x)
+    hat_out[...] = xhat.astype(BF)
     h1 = (xhat * v_ref[0:1, :] + v_ref[1:2, :]).astype(BF)
     bias = jnp.concatenate([bias_ref[h : h + 1, :] for h in range(heads)], axis=1)
     packed = (dot_nt(h1, w_ref[...]) + bias).astype(BF)
@@ -71,7 +72,7 @@
     whole = lambda t, h: (0, 0)
     out_shape = tuple(
         jax.ShapeDtypeStruct(s, BF)
-        for s in ((heads, group_rows, hd),) * 3 + ((heads, hd, group_rows),)
+        for s in ((heads, group_rows, hd),) * 3 + ((heads, hd, group_rows), (group_rows, width))
     )
     in_specs = [
         pl.BlockSpec((BLK, width), lambda t, h: (jnp.minimum(t, per - 1), 0)),
@@ -88,7 +89,10 @@
             grid=(steps,),
             in_specs=in_specs,
             out_specs=[pl.BlockSpec((heads, BLK, hd), lambda t, h: (0, place(t, h), 0))] * 3
-            + [pl.BlockSpec((heads, hd, BLK), lambda t, h: (0, 0, place(t, h)))],
+            + [
+                pl.BlockSpec((heads, hd, BLK), lambda t, h: (0, 0, place(t, h))),
+                pl.BlockSpec((BLK, width), lambda t, h: (first * per + t, 0)),
+            ],
         ),
         input_output_aliases={6 + i: i for i in range(len(before))},
         cost_estimate=cost(4 * rows * width * w.shape[0], 12 * rows * width),
@@ -503,105 +507,125 @@
     )(near, swapped, far, resid, cot, vectors, *projs)
 
 
-def close_kernel(per, b_ref, x0, x1, x2, x3, gp_ref, w_ref, v_ref, pw_ref, up_ref, s_ref, near_ref, far_ref, keep_ref, send_ref, sum_ref, acc):
+def tally_kernel(steps, b_ref, gp_ref, hat_ref, w_ref, v_ref, pw_ref, up_ref, s_ref, keep_ref, send_ref, acc, col):
     t = pl.program_id(0)
-    steps = 4 * per
-    x = jnp.where(t < 2 * per, jnp.where(t < per, x0[...], x1[...]), jnp.where(t < 3 * per, x2[...], x3[...]))
-    hat, _ = normalize(x.astype(F32))
-    h1 = (hat * v_ref[0:1, :] + v_ref[1:2, :]).astype(BF)
     gp = gp_ref[...]
     cols = gp.shape[1]
-    e = dot_nn(gp, w_ref[...])
-
-    @pl.when(t < 2 * per)
-    def _():
-        near_ref[...] = e.astype(BF)
-
-    @pl.when(t >= 2 * per)
-    def _():
-        far_ref[...] = e.astype(BF)
+    half = acc.shape[0] // 2
 
     @pl.when(t == 0)
     def _():
-        sum_ref[...] = s_ref[...]
-        acc[...] = jnp.zeros_like(acc)
-        acc[cols : cols + pw_ref.shape[0], :] = pw_ref[...]
-        acc[cols + pw_ref.shape[0] + 1 : cols + pw_ref.shape[0] + 2, :] = up_ref[...]
-
-    sum_ref[0:1, :] += jnp.sum(e * hat, axis=0, keepdims=True)
-    sum_ref[1:2, :] += jnp.sum(e, axis=0, keepdims=True)
-    acc[:cols, :] += dot_tn(gp, h1)
-    base = cols + pw_ref.shape[0]
-    acc[base : base + 1, :cols] += jnp.sum(gp.astype(F32), axis=0, keepdims=True)
+        acc[:cols, :] = jnp.zeros((cols, acc.shape[1]), F32)
+        acc[cols:, :] = pw_ref[...]
+        col[...] = jnp.zeros_like(col)
+
+    acc[:cols, :] += dot_tn(gp, hat_ref[...])
+    col[...] += dot_tn(gp, jnp.ones((gp.shape[0], 128), BF))
 
     @pl.when(t == steps - 1)
     def _():
+        total = col[:, 0:1]
+        moment = acc[:cols, :]
+        w = w_ref[...].astype(F32)
+        small = s_ref[...]
+        row = lax.broadcasted_iota(jnp.int32, small.shape, 0)
+        small = jnp.where(row == 0, jnp.sum(w * moment, axis=0, keepdims=True), small)
+        small = jnp.where(row == 1, jnp.sum(w * total, axis=0, keepdims=True), small)
+        bias = jnp.concatenate((col[...].T[0:1, :], jnp.zeros((1, small.shape[1] - cols), F32)), axis=1)
+        small = jnp.where(row == 2, bias, small)
+        small = jnp.where(row == 3, up_ref[...], small).astype(BF)
+        acc[:cols, :] = moment * v_ref[0:1, :] + total * v_ref[1:2, :]
         split_out(b_ref, acc, keep_ref, send_ref)
-        half = acc.shape[0] // 2
-        keep_ref[half:, :] = sum_ref[...].astype(BF)
-        send_ref[half:, :] = sum_ref[...].astype(BF)
-
-
-def close_call(bid, rows, gp, w, vectors, proj_grad, up_grad, sums, total):
-    chunk, width = rows[0].shape
+        keep_ref[half:, :] = small
+        send_ref[half:, :] = small
+
+
+def tally_call(bid, gp, hat, w, vectors, proj_grad, up_grad, sums):
+    rows, width = hat.shape
     cols = gp.shape[1]
-    per = chunk // BLK
-    steps = 4 * per
+    total = cols + proj_grad.shape[0]
+    block = 2 * BLK
+    steps = rows // block
     whole = lambda t, b: (0, 0)
-    part = lambda k: pl.BlockSpec((BLK, width), lambda t, b: (jnp.clip(t - k * per, 0, per - 1), 0))
     half = jax.ShapeDtypeStruct((total // 2 + sums.shape[0], width), BF)
     return pl.pallas_call(
-        functools.partial(close_kernel, per),
-        out_shape=(
-            jax.ShapeDtypeStruct((2 * chunk, width), BF),
-            jax.ShapeDtypeStruct((2 * chunk, width), BF),
-            half,
-            half,
-        ),
+        functools.partial(tally_kernel, steps),
+        out_shape=(half, half),
         grid_spec=pltpu.PrefetchScalarGridSpec(
             num_scalar_prefetch=1,
             grid=(steps,),
-            in_specs=[part(0), part(1), part(2), part(3)]
-            + [pl.BlockSpec((BLK, cols), lambda t, b: (t, 0))]
+            in_specs=[
+                pl.BlockSpec((block, cols), lambda t, b: (t, 0)),
+                pl.BlockSpec((block, width), lambda t, b: (t, 0)),
+            ]
             + [pl.BlockSpec(v.shape, whole) for v in (w, vectors, proj_grad, up_grad, sums)],
-            out_specs=[
-                pl.BlockSpec((BLK, width), lambda t, b: (jnp.minimum(t, 2 * per - 1), 0)),
-                pl.BlockSpec((BLK, width), lambda t, b: (jnp.maximum(t - 2 * per, 0), 0)),
-                pl.BlockSpec(half.shape, whole),
-                pl.BlockSpec(half.shape, whole),
-            ],
-            scratch_shapes=[pltpu.VMEM((8, width), F32), pltpu.VMEM((total, width), F32)],
+            out_specs=[pl.BlockSpec(half.shape, whole)] * 2,
+            scratch_shapes=[pltpu.VMEM((total, width), F32), pltpu.VMEM((cols, 128), F32)],
         ),
-        cost_estimate=cost(16 * chunk * width * cols, 20 * chunk * width),
-        name="close",
-    )(bid, *rows, gp, w, vectors, proj_grad, up_grad, sums)
-
-
-def unpack_kernel(counts, b_ref, keep_ref, other_ref, *rest):
+        cost_estimate=cost(cols, width),
+        name="tally",
+    )(bid, gp, hat, w, vectors, proj_grad, up_grad, sums)
+
+
+def spread_kernel(steps, gp_ref, w_ref, near_ref, far_ref):
+    t = pl.program_id(0)
+    e = dot_nn(gp_ref[...], w_ref[...]).astype(BF)
+
+    @pl.when(t < steps // 2)
+    def _():
+        near_ref[...] = e
+
+    @pl.when(t >= steps // 2)
+    def _():
+        far_ref[...] = e
+
+
+def spread_call(gp, w):
+    rows, cols = gp.shape
+    width = w.shape[1]
+    block = 2 * BLK
+    steps = rows // block
+    return pl.pallas_call(
+        functools.partial(spread_kernel, steps),
+        out_shape=(jax.ShapeDtypeStruct((rows // 2, width), BF),) * 2,
+        grid=(steps,),
+        in_specs=[pl.BlockSpec((block, cols), lambda t: (t, 0)), pl.BlockSpec(w.shape, lambda t: (0, 0))],
+        out_specs=[
+            pl.BlockSpec((block, width), lambda t: (jnp.minimum(t, steps // 2 - 1), 0)),
+            pl.BlockSpec((block, width), lambda t: (jnp.maximum(t - steps // 2, 0), 0)),
+        ],
+        cost_estimate=cost(cols, width),
+        name="spread",
+    )(gp, w)
+
+
+def unpack_kernel(counts, parts, b_ref, *rest):
     acc = rest[-1]
     piece = acc.shape[0] // 8
+    per = 8 // parts
     for spot, block in enumerate(spots(b_ref, 8)):
-        src = keep_ref if spot < 4 else other_ref
-        value = src[(spot % 4) * piece : (spot % 4 + 1) * piece, :].astype(F32)
+        at = spot % per * piece
+        value = rest[spot // per][at : at + piece, :].astype(F32)
         acc[pl.ds(pl.multiple_of(block * piece, 8), piece), :] = value
     start = 0
-    for out, count in zip(rest[:-1], counts, strict=True):
+    for out, count in zip(rest[parts:-1], counts, strict=True):
         out[...] = acc[start : start + count, :]
         start += count
 
 
-def unpack_call(bid, keep, other, counts):
-    half, width = keep.shape
+def unpack_call(bid, parts, counts):
+    total = sum(part.shape[0] for part in parts)
+    width = parts[0].shape[1]
     vm = pl.BlockSpec(memory_space=pltpu.VMEM)
     return pl.pallas_call(
-        functools.partial(unpack_kernel, counts),
+        functools.partial(unpack_kernel, counts, len(parts)),
         out_shape=tuple(jax.ShapeDtypeStruct((n, width), F32) for n in counts),
-        in_specs=[pl.BlockSpec(memory_space=pltpu.SMEM), vm, vm],
+        in_specs=[pl.BlockSpec(memory_space=pltpu.SMEM)] + [vm] * len(parts),
         out_specs=[vm] * len(counts),
-        scratch_shapes=[pltpu.VMEM((2 * half, width), F32)],
-        cost_estimate=cost(half * width, 12 * half * width),
+        scratch_shapes=[pltpu.VMEM((total, width), F32)],
+        cost_estimate=cost(total, width),
         name="unpack",
-    )(bid, keep, other)
+    )(bid, *parts)
 
 
 def tie(x, *needed):
@@ -677,10 +701,9 @@
     begun = qkv_call(hid, inputs, x_near, vectors, qkv_t, bias_qkv, 0, group_rows, ())
     x_far = tie(x_far, begun[0])
     x_last = swap(x_far, "head", 1)
-    queries, keys, values, values_t = qkv_call(
+    queries, keys, values, values_t, hats = qkv_call(
         hid, x_far, x_last, vectors, qkv_t, bias_qkv, 2, group_rows, begun
     )
-    rows = (inputs, x_near, x_far, x_last)
     grad_own = jnp.where(live, cotangent, jnp.zeros_like(cotangent))
     grad_far = swap(tie(grad_own, x_far), "head", 2)
     proj_far = swap(tie(proj, x_far), "head", 2)
@@ -707,14 +730,15 @@
     far_sum = (grad_norm_far[:chunk].astype(F32) + swapped[chunk:].astype(F32)).astype(BF)
     grad_far_sum = swap(far_sum, "head", 2)
     near_swapped = swap(near[2], "head", 1)
+    down_swapped = swap(tie(down_far, far_sum), "head", 1)
+    near_down = swap(tie(near[3], far_sum), "head", 1)
 
     keep_feed, send_feed, grad_bup = weigh_call(
         bid, (h_own, h_near, h_far, h_last), tie(act, far_sum), grad_up, grads
     )
     other_feed = swap(send_feed, "batch", 1)
-
     grad_resid, grad_att, grad_near, grad_cross, sums = turn_call(
-        near[2], near_swapped, tie(grad_far_sum, grad_bup), resid, grad_own, vectors, projs
+        near[2], near_swapped, tie(grad_far_sum, grad_bup, down_swapped, near_down), resid, grad_own, vectors, projs
     )
     grad_near = grad_near.reshape(2 * chunk, inner)
     got = swap(grad_cross.reshape(2 * chunk, inner), "head", 2)
@@ -726,7 +750,9 @@
         dot_tn(p[at], grad_att) for p, at in zip(parts, (low, high, low, high), strict=True)
     ]
     near_sent, far_sent = grad_proj[1].astype(BF), grad_proj[3].astype(BF)
-    got = tie(got, near_sent, far_sent)
+    down_far = tie(down_far, grad_att)
+    down_sum = (down_far[:chunk].astype(F32) + down_swapped[chunk:].astype(F32)).astype(BF)
+    got = tie(got, near_sent, far_sent, down_sum)
     merged_grads = (grad_near, grad_mate, got, swap(got, "head", 1))
     grad_near_proj = grad_proj[0] + swap(near_sent, "head", 1).astype(F32)
     far_proj = (grad_proj[2] + swap(far_sent, "head", 1).astype(F32)).astype(BF)
@@ -734,6 +760,7 @@
 
     kept_feed = (keep_feed.astype(F32) + tie(other_feed, got).astype(F32)).astype(BF)
     got_feed = across(quarters(kept_feed))
+    down_other = swap(tie(down_sum, kept_feed), "head", 2)
 
     grad_packed = attend_back_call(
         lens,
@@ -750,37 +777,39 @@
     grad_wproj = grad_near_proj + tie(far_proj, grad_packed).astype(F32)
     total_feed = fold(kept_feed, got_feed)
     gathered_feed = across([total_feed] * 3)
-    total = -(-(cols + inner + 8) // 64) * 64
-    e_near, e_far, keep, send = close_call(
-        bid, rows, tie(grad_packed, total_feed), qkv_t, vectors, grad_wproj, grad_bup, sums, total
-    )
-    e_swapped = swap(e_far, "head", 1)
+    keep, send = tally_call(
+        bid, tie(grad_packed, total_feed, down_other), hats, qkv_t, vectors, grad_wproj, grad_bup, sums
+    )
+    other = swap(send, "batch", 1)
+    e_near, e_far = spread_call(tie(grad_packed, keep), qkv_t)
+    gathered_feed, e_near, e_far = lax.optimization_barrier((gathered_feed, e_near, e_far))
+
+    feed_a = jnp.concatenate((total_feed, gathered_feed[0]), axis=0)
+    feed_b = jnp.concatenate(gathered_feed[1:], axis=0)
+    last_a = swap(feed_a, "batch", 1)
+    summed = (keep.astype(F32) + tie(other, feed_a, feed_b).astype(F32)).astype(BF)
+    kept, small = summed[:-8], summed[-8:]
+    pieces = [jnp.concatenate((q, small), axis=0) for q in quarters(kept)]
+    e_swapped = swap(tie(e_far, *pieces), "head", 1)
     e_sum = (e_far[:chunk].astype(F32) + e_swapped[chunk:].astype(F32)).astype(BF)
-    e_other = swap(e_sum, "head", 2)
-    e_mate = swap(e_near, "head", 1)
-    e_own = e_near[:chunk].astype(F32) + e_mate[chunk:].astype(F32) + e_other.astype(F32)
-    half_feed = jnp.concatenate([total_feed] + [tie(g, e_far) for g in gathered_feed], axis=0)
-    last_feed = swap(tie(half_feed, e_sum), "batch", 1)
-    other = tie(swap(send, "batch", 1), half_feed)
-    kept = (keep.astype(F32) + other.astype(F32)).astype(BF)
-    kept, small = kept[:-8], kept[-8:]
-    got_attn = across([jnp.concatenate((q, small), axis=0) for q in quarters(kept)])
+    got_attn = [tie(g, last_a, e_sum) for g in across(pieces)]
+
     tiny = [small.astype(F32)] + [g[-8:].astype(F32) for g in got_attn]
-    small = sum_group(sum_rest((tiny[0] + tiny[1]) + (tiny[2] + tiny[3])))
+    small = sum_rest((tiny[0] + tiny[1]) + (tiny[2] + tiny[3]))
     total_attn = fold(kept, got_attn)
-
-    down_swapped = swap(tie(down_far, kept), "head", 1)
-    down_sum = (down_far[:chunk].astype(F32) + down_swapped[chunk:].astype(F32)).astype(BF)
-    down_other = swap(tie(down_sum, e_other), "head", 2)
-    near_down = near[3][:chunk].astype(F32) + swap(tie(near[3], kept), "head", 1)[chunk:].astype(F32)
-    output = (resid + near_down + down_other.astype(F32) + bias_down).astype(BF)
-
-    half = jnp.concatenate([total_attn] + across([total_attn] * 3), axis=0)
-    last = swap(tie(half, last_feed), "batch", 1)
-    sum_wup, sum_wdown = unpack_call(bid, half_feed, tie(last_feed, half), (width, width))
-    sum_wqkv, sum_wproj, sum_bias = unpack_call(bid, half, tie(last, sum_wup), (cols, inner, 8))
-
-    x_hat, x_rstd = normalize(inputs.astype(F32))
+    gathered_attn = across([total_attn] * 3)
+    last_b = swap(tie(feed_b, total_attn), "batch", 1)
+    e_other = swap(tie(e_sum, total_attn), "head", 2)
+    half = jnp.concatenate([total_attn] + [tie(g, last_b) for g in gathered_attn], axis=0)
+    e_mate = swap(tie(e_near, half), "head", 1)
+    last = swap(half, "batch", 1)
+    biases = small[2:4]
+    small = sum_group(tie(small, half))
+    e_own = e_near[:chunk].astype(F32) + e_mate[chunk:].astype(F32) + tie(e_other, half).astype(F32)
+
+    near_down = near[3][:chunk].astype(F32) + near_down[chunk:].astype(F32)
+    output = (resid + near_down + tie(down_other, half).astype(F32) + bias_down).astype(BF)
+    x_hat, x_rstd = normalize(tie(inputs, half).astype(F32))
     e_own = e_own * gain_attn
     grad_inputs = (
         grad_resid
@@ -791,19 +820,21 @@
             - x_hat * jnp.mean(e_own * x_hat, axis=-1, keepdims=True)
         )
     ).astype(BF)
+    sum_wup, sum_wdown = unpack_call(bid, (feed_a, feed_b, last_a, tie(last_b, half)), (width, width))
+    sum_wqkv, sum_wproj = unpack_call(bid, (half, tie(last, sum_wup, grad_inputs)), (cols, inner))
     return (
         output,
         grad_inputs,
         small[0],
         small[1],
         sum_wqkv.reshape(heads, triple, width).transpose(2, 0, 1),
-        sum_bias[0, :cols].reshape(heads, triple),
+        biases[0, :cols].reshape(heads, triple),
         sum_wproj.reshape(heads, inner // heads, width),
         small[4],
         small[5],
         small[6],
         sum_wup,
-        sum_bias[1],
+        biases[1],
         sum_wdown,
         small[7],
     )

time: 338 us -> 311 us (0.920)
  waiting for transfers between devices: 110 us -> 76.7 us
  starting transfers between devices: 46.3 us -> 51.1 us
    ppermute x48 -> x49, waiting for transfers between devices: 110 us -> 76.7 us  [swap(): return lax.ppermute(x, axis, [(i, i ^ bits) for i in range(size)])]
    ppermute x48 -> x49, starting transfers between devices: 46.3 us -> 51.1 us  [swap(): return lax.ppermute(x, axis, [(i, i ^ bits) for i in range(size)])]
    unnamed x80 -> x79, local copies, waits for them, and re-layouts: 8.19 us -> 6.64 us
    pallas_call x3 -> x4, Pallas kernels: 21.3 us -> 21.3 us  [the longest x1 7.69 us: tally_call(): pl.pallas_call(functools.partial(tally_kernel, steps), out_shape=(half, h...]
  transfers between devices with their start and end apart: 48 -> 49, of which waited for: 20 -> 17; matrix products, arithmetic and copies ran while one was open for 7% -> 10% of each run, Pallas kernels for 35% -> 40%
where the time goes in v2:
time: 311 us; the launch traced here: 310 us
  Pallas kernels  142 us (46%)
  waiting for transfers between devices  76.7 us (25%)
  starting transfers between devices  51.1 us (16%)
  other arithmetic  19.3 us (6%)
  local copies, waits for them, and re-layouts  15 us (5%)
  matrix products  4.78 us (2%)
    ppermute x49, waiting for transfers between devices, swap(): return lax.ppermute(x, axis, [(i, i ^ bits) for i in range(size)])  76.7 us
    ppermute x49, starting transfers between devices, swap(): return lax.ppermute(x, axis, [(i, i ^ bits) for i in range(size)])  51.1 us
    pallas_call x2, Pallas kernels, attend_call(): pl.pallas_call(functools.partial(attend_kernel, heads, first, per, 1.0 /...  34.3 us
    pallas_call x1, Pallas kernels, attend_back_call(): pl.pallas_call(functools.partial(attend_back_kernel, chunk, 1.0 / math.sq...  32.6 us
    pallas_call x2, Pallas kernels, feed_call(): pl.pallas_call(functools.partial(feed_kernel, steps), out_shape=(jax.Shap...  17.8 us
    pallas_call x2, Pallas kernels, qkv_call(): pl.pallas_call(functools.partial(qkv_kernel, heads, hd, steps), out_shape...  12.8 us
    pallas_call x1, Pallas kernels, weigh_call(): pl.pallas_call(functools.partial(weigh_kernel, tiles), out_shape=(half, h...  12.5 us
    pallas_call x1, Pallas kernels, tally_call(): pl.pallas_call(functools.partial(tally_kernel, steps), out_shape=(half, h...  7.69 us
  transfers between devices with their start and end apart: 49, of which 17 were waited for; matrix products, arithmetic and copies ran while one was open for 10% of the time, Pallas kernels for 40%

profile of v2, /device:TPU:0, one launch (start us, length us, event | category | flops | bytes accessed | tf_op | source)
XLA Modules:
  0.0 309.7 jit_solution(7121694271079278721)
XLA Ops:
  10.1 6.5 %qkv.2 = (bf16[3,2048,64]{2,1,0:T(8,128)(2,1)}, bf16[3,2048,64]{2,1,0:T(8,128)(2,1)}, bf16[3,2048,64]{2,1,0:T(8,128)(2,1)}, bf16[3,64,2048]{2,1,0:T(8,128)(2,1)}, bf16[2048,768]{1,0:T(8,128)(2,1)}) custom-call(s32[1]{0:T(128)} %bitcast.1.h_ref, bf16[512,768]{1,0:T(8,128)(2,1)} %x_ref.1, bf16[512,768]{1,0:T(8,128)(2,1)} %copy-done.34, f32[8,768]{1,0:T(8,128)} %stack.31.v_ref, ...), custom_call_target="tpu_custom_call" | custom-call | flops 905969664 | bytes 4718592 | tf_op jit(solution)/shard_map/qkv/pallas_call | solution.py:84
  16.6 5.5 %collective-permute-done.a_ref = bf16[512,768]{1,0:T(8,128)(2,1)S(1)} collective-permute-done((bf16[512,768]{1,0:T(8,128)(2,1)}, bf16[512,768]{1,0:T(8,128)(2,1)S(1)}, u32[]{:S(2)}, u32[]{:S(2)}) %collective-permute-start) | collective-permute-done | bytes 786464 | tf_op jit(solution)/shard_map/ppermute | solution.py:38
  26.4 6.3 %qkv.3 = (bf16[3,2048,64]{2,1,0:T(8,128)(2,1)}, bf16[3,2048,64]{2,1,0:T(8,128)(2,1)}, bf16[3,2048,64]{2,1,0:T(8,128)(2,1)}, bf16[3,64,2048]{2,1,0:T(8,128)(2,1)}, bf16[2048,768]{1,0:T(8,128)(2,1)}) custom-call(s32[1]{0:T(128)} %bitcast.1.h_ref, ...), custom_call_target="tpu_custom_call", output_to_operand_aliasing={{0}: (6, {}), {1}: (7, {}), {2}: (8, {}), {3}: (9, {}), {4}... | custom-call | flops 905969664 | bytes 4718592 | tf_op jit(solution)/shard_map/qkv/pallas_call | solution.py:84
  32.7 20.3 %attend.2 = (bf16[1024,192]{1,0:T(8,128)(2,1)}, f32[8,1024]{1,0:T(8,128)}) custom-call(s32[8]{0:T(128)} %bitcast.30, s32[1]{0:T(128)} %bitcast.1.h_ref, bf16[3,2048,64]{2,1,0:T(8,128)(2,1)} %get-tuple-element.137.q_ref, bf16[3,2048,64]{2,1,0:T(8,128)(2,1)} %get-tuple-element.104.k_ref, bf16[3,64,2048]{2,1,0:T(8,128)(2,1)} %get-tuple-element.105.vt_ref), custom_call_target="tpu_custom_call" | custom-call | flops 3221225472 | bytes 4718592 | tf_op jit(solution)/shard_map/attend/pallas_call | solution.py:169
  55.0 14.0 %attend.3 = (bf16[1024,192]{1,0:T(8,128)(2,1)}, f32[8,1024]{1,0:T(8,128)}) custom-call(s32[8]{0:T(128)} %bitcast.31, s32[1]{0:T(128)} %bitcast.1.h_ref, bf16[3,2048,64]{2,1,0:T(8,128)(2,1)} %get-tuple-element.137.q_ref, bf16[3,2048,64]{2,1,0:T(8,128)(2,1)} %get-tuple-element.104.k_ref, bf16[3,64,2048]{2,1,0:T(8,128)(2,1)} %get-tuple-element.105.vt_ref), custom_call_target="tpu_custom_call" | custom-call | flops 3221225472 | bytes 4718592 | tf_op jit(solution)/shard_map/attend/pallas_call | solution.py:169
  69.6 3.8 %collective-permute-done.8.p2 = bf16[192,768]{1,0:T(8,128)(2,1)S(1)} collective-permute-done((bf16[192,768]{1,0:T(8,128)(2,1)S(1)}, bf16[192,768]{1,0:T(8,128)(2,1)S(1)}, u32[]{:S(2)}, u32[]{:S(2)}) %collective-permute-start.8) | collective-permute-done | bytes 294944 | tf_op jit(solution)/shard_map/ppermute | solution.py:38
  76.0 4.1 %mix.1 = (f32[512,768]{1,0:T(8,128)}, bf16[512,768]{1,0:T(8,128)(2,1)}) custom-call(bf16[1024,192]{1,0:T(8,128)(2,1)} %get-tuple-element.109.m0.rest_4_, bf16[1024,192]{1,0:T(8,128)(2,1)} %copy-done.16, bf16[1024,192]{1,0:T(8,128)(2,1)} %copy-done.14, bf16[1024,192]{1,0:T(8,128)(2,1)} %collective-permute-done.6.m3, bf16[192,768]{1,0:T(8,128)(2,1)} %bitcast.21, ...), custom_call_target="tpu_custom_call" | custom-call | flops 603979776 | bytes 4718592 | tf_op jit(solution)/shard_map/mix/pallas_call | solution.py:447
  80.3 3.9 %collective-permute-start.12 = (bf16[512,768]{1,0:T(8,128)(2,1)}, bf16[512,768]{1,0:T(8,128)(2,1)S(1)}, u32[]{:S(2)}, u32[]{:S(2)}) collective-permute-start(bf16[512,768]{1,0:T(8,128)(2,1)} %get-tuple-element.112.ha_ref.h0), channel_id=1, source_target_pairs={{0,2},{1,3},{2,0},{3,1},{4,6},{5,7},{6,4},{7,5},{8,10},{9,11},{10,... | collective-permute-start | bytes 2359304 | tf_op jit(solution)/shard_map/ppermute | solution.py:38
  85.3 8.9 %feed.2 = (bf16[2048,768]{1,0:T(8,128)(2,1)}, bf16[2048,768]{1,0:T(8,128)(2,1)}, bf16[1024,768]{1,0:T(8,128)(2,1)}, bf16[1024,768]{1,0:T(8,128)(2,1)}) custom-call(bf16[512,768]{1,0:T(8,128)(2,1)} %get-tuple-element.112.ha_ref.h0, bf16[512,768]{1,0:T(8,128)(2,1)} %copy-done.30, bf16[512,768]{1,0:T(8,128)(2,1)} %copy-done.3, ...), custom_call_target="tpu_custom_call" | custom-call | flops 4831838208 | bytes 6291456 | tf_op jit(solution)/shard_map/feed/pallas_call | solution.py:327
  94.2 8.3 %collective-permute-done.12.ha_ref.h2 = bf16[512,768]{1,0:T(8,128)(2,1)S(1)} collective-permute-done((bf16[512,768]{1,0:T(8,128)(2,1)}, bf16[512,768]{1,0:T(8,128)(2,1)S(1)}, u32[]{:S(2)}, u32[]{:S(2)}) %collective-permute-start.12) | collective-permute-done | bytes 786464 | tf_op jit(solution)/shard_map/ppermute | solution.py:38
  105.6 8.9 %feed.3 = (bf16[2048,768]{1,0:T(8,128)(2,1)}, bf16[2048,768]{1,0:T(8,128)(2,1)}, bf16[1024,768]{1,0:T(8,128)(2,1)}, bf16[1024,768]{1,0:T(8,128)(2,1)}) custom-call(bf16[512,768]{1,0:T(8,128)(2,1)} %copy-done.31, bf16[512,768]{1,0:T(8,128)(2,1)} %copy-done.33, bf16[512,768]{1,0:T(8,128)(2,1)} %copy-done.29, ...), custom_call_target="tpu_custom_call", output_to_operand_aliasing={{0}: (7, {}), {1}: (8, {})} | custom-call | flops 4831838208 | bytes 6291456 | tf_op jit(solution)/shard_map/feed/pallas_call | solution.py:327
  114.8 3.5 %collective-permute-done.15 = bf16[1024,768]{1,0:T(8,128)(2,1)S(1)} collective-permute-done((bf16[1024,768]{1,0:T(8,128)(2,1)}, bf16[1024,768]{1,0:T(8,128)(2,1)S(1)}, u32[]{:S(2)}, u32[]{:S(2)}) %collective-permute-start.15) | collective-permute-done | bytes 1572896 | tf_op jit(solution)/shard_map/ppermute | solution.py:38
  122.9 12.5 %weigh.1 = (bf16[768,768]{1,0:T(8,128)(2,1)}, bf16[768,768]{1,0:T(8,128)(2,1)}, f32[1,768]{1,0:T(1,128)}) custom-call(s32[1]{0:T(128)} %bitcast.5.b_ref, bf16[512,768]{1,0:T(8,128)(2,1)} %get-tuple-element.112.ha_ref.h0, bf16[512,768]{1,0:T(8,128)(2,1)} %copy-done.30, bf16[512,768]{1,0:T(8,128)(2,1)} %copy-done.31, bf16[512,768]{1,0:T(8,128)(2,1)} %copy-done.33, ...), custom_call_target="tpu_custom_call" | custom-call | flops 4831838208 | bytes 18874368 | tf_op jit(solution)/shard_map/weigh/pallas_call | solution.py:407
  135.4 5.9 %collective-permute-done.18.f_ref = bf16[512,768]{1,0:T(8,128)(2,1)} collective-permute-done((bf16[512,768]{1,0:T(8,128)(2,1)}, bf16[512,768]{1,0:T(8,128)(2,1)}, u32[]{:S(2)}, u32[]{:S(2)}) %collective-permute-start.18) | collective-permute-done | bytes 786464 | tf_op jit(solution)/shard_map/ppermute | solution.py:38
  142.5 6.2 %turn.1 = (f32[512,768]{1,0:T(8,128)}, bf16[512,768]{1,0:T(8,128)(2,1)}, bf16[2,512,192]{2,1,0:T(8,128)(2,1)}, bf16[2,512,192]{2,1,0:T(8,128)(2,1)}, f32[8,768]{1,0:T(8,128)}) custom-call(bf16[1024,768]{1,0:T(8,128)(2,1)} %get-tuple-element.120.n_ref, bf16[1024,768]{1,0:T(8,128)(2,1)} %copy-done.7, bf16[512,768]{1,0:T(8,128)(2,1)} %collective-permute-done.18.f_ref, ...), custom_call_target="tpu_custom_call" | custom-call | flops 603979776 | bytes 7864320 | tf_op jit(solution)/shard_map/turn/pallas_call | solution.py:492
  156.2 7.2 %collective-permute-done.22.rest_2_ = bf16[1024,192]{1,0:T(8,128)(2,1)S(1)} collective-permute-done((bf16[1024,192]{1,0:T(8,128)(2,1)}, bf16[1024,192]{1,0:T(8,128)(2,1)S(1)}, u32[]{:S(2)}, u32[]{:S(2)}) %collective-permute-start.22) | collective-permute-done | bytes 393248 | tf_op jit(solution)/shard_map/ppermute | solution.py:38
  163.4 14.0 %collective-permute-done.21 = bf16[768,768]{1,0:T(8,128)(2,1)S(1)} collective-permute-done((bf16[768,768]{1,0:T(8,128)(2,1)}, bf16[768,768]{1,0:T(8,128)(2,1)S(1)}, u32[]{:S(2)}, u32[]{:S(2)}) %collective-permute-start.21) | collective-permute-done | bytes 1179680 | tf_op jit(solution)/shard_map/ppermute | solution.py:38
  180.2 5.1 %collective-permute-start.27 = (bf16[192,768]{1,0:T(8,128)(2,1)}, bf16[192,768]{1,0:T(8,128)(2,1)S(1)}, u32[]{:S(2)}, u32[]{:S(2)}) collective-permute-start(bf16[192,768]{1,0:T(8,128)(2,1)} %get-tuple-element.190), channel_id=1, source_target_pairs={{0,16},{4,20},{8,24},{12,28},{16,0},{20,4},{24,8},{28,12},{1,17},{... | collective-permute-start | bytes 884744 | tf_op jit(solution)/shard_map/ppermute | solution.py:38
  189.6 32.6 %attend_back.1.gp_ref = bf16[2048,576]{1,0:T(8,128)(2,1)} custom-call(s32[8]{0:T(128)} %bitcast.32, s32[1]{0:T(128)} %bitcast.1.h_ref, bf16[3,2048,64]{2,1,0:T(8,128)(2,1)} %get-tuple-element.137.q_ref, bf16[3,2048,64]{2,1,0:T(8,128)(2,1)} %get-tuple-element.104.k_ref, bf16[3,2048,64]{2,1,0:T(8,128)(2,1)} %get-tuple-element.138.v_ref, ...), custom_call_target="tpu_custom_call" | custom-call | flops 16106127360 | bytes 11796480 | tf_op jit(solution)/shard_map/attend_back/pallas_call | solution.py:280
  223.4 4.4 %collective-permute-start.33 = (bf16[192,768]{1,0:T(8,128)(2,1)S(1)}, bf16[192,768]{1,0:T(8,128)(2,1)S(1)}, u32[]{:S(2)}, u32[]{:S(2)}) collective-permute-start(bf16[192,768]{1,0:T(8,128)(2,1)S(1)} %add_convert_fusion.6), channel_id=1, source_target_pairs={{0,16},{4,20},{8,24},{12,28},{16,0},{20,4},{24,8},{28,12},{1,17},{... | collective-permute-start | bytes 884744 | tf_op jit(solution)/shard_map/ppermute | solution.py:38
  229.7 7.7 %tally.1 = (bf16[392,768]{1,0:T(8,128)(2,1)}, bf16[392,768]{1,0:T(8,128)(2,1)}) custom-call(s32[1]{0:T(128)} %bitcast.5.b_ref, bf16[2048,576]{1,0:T(8,128)(2,1)} %attend_back.1.gp_ref, bf16[2048,768]{1,0:T(8,128)(2,1)} %get-tuple-element.145.hat_ref, bf16[576,768]{1,0:T(8,128)(2,1)} %bitcast.19, f32[8,768]{1,0:T(8,128)} %stack.31.v_ref, ...), custom_call_target="tpu_custom_call" | custom-call | flops 576 | bytes 768 | tf_op jit(solution)/shard_map/tally/pallas_call | solution.py:551
  239.8 6.5 %spread.1 = (bf16[1024,768]{1,0:T(8,128)(2,1)}, bf16[1024,768]{1,0:T(8,128)(2,1)}) custom-call(bf16[2048,576]{1,0:T(8,128)(2,1)} %attend_back.1.gp_ref, bf16[576,768]{1,0:T(8,128)(2,1)} %bitcast.20), custom_call_target="tpu_custom_call" | custom-call | flops 576 | bytes 768 | tf_op jit(solution)/shard_map/spread/pallas_call | solution.py:588
  248.4 2.9 collective-permute-done.31
  259.6 7.8 %collective-permute-done.36.rest_2_ = bf16[384,768]{1,0:T(8,128)(2,1)S(1)} collective-permute-done((bf16[384,768]{1,0:T(8,128)(2,1)S(1)}, bf16[384,768]{1,0:T(8,128)(2,1)S(1)}, u32[]{:S(2)}, u32[]{:S(2)}) %collective-permute-start.36) | collective-permute-done | bytes 589856 | tf_op jit(solution)/shard_map/ppermute | solution.py:38
  267.4 3.0 collective-permute-done.38
  271.3 3.0 collective-permute-start.40
  279.1 5.3 %collective-permute-done.41.rest_3_ = bf16[384,768]{1,0:T(8,128)(2,1)S(1)} collective-permute-done((bf16[384,768]{1,0:T(8,128)(2,1)S(1)}, bf16[384,768]{1,0:T(8,128)(2,1)S(1)}, u32[]{:S(2)}, u32[]{:S(2)}) %collective-permute-start.41) | collective-permute-done | bytes 589856 | tf_op jit(solution)/shard_map/ppermute | solution.py:38
  284.4 3.0 collective-permute-done.42
  291.3 2.9 add_convert_fusion.1
  296.5 4.2 %unpack.2 = (f32[768,768]{1,0:T(8,128)}, f32[768,768]{1,0:T(8,128)}) custom-call(s32[1]{0:T(128)} %bitcast.5.b_ref, bf16[384,768]{1,0:T(8,128)(2,1)} %copy-done.4, bf16[384,768]{1,0:T(8,128)(2,1)} %copy-done.8, bf16[384,768]{1,0:T(8,128)(2,1)} %copy-done.23, bf16[384,768]{1,0:T(8,128)(2,1)} %copy-done.24), custom_call_target="tpu_custom_call" | custom-call | flops 1536 | bytes 768 | tf_op jit(solution)/shard_map/unpack/pallas_call | solution.py:620
  303.7 3.0 fusion.8
  306.8 2.9 unpack.3
  (206 shorter events, 74.2 us)
Async XLA Ops:
  1.2 20.9 %collective-permute-start = (bf16[512,768]{1,0:T(8,128)(2,1)}, bf16[512,768]{1,0:T(8,128)(2,1)S(1)}, u32[]{:S(2)}, u32[]{:S(2)}) collective-permute-start(bf16[512,768]{1,0:T(8,128)(2,1)} %x_ref.1), channel_id=1, source_target_pairs={{0,2},{1,3},{2,0},{3,1},{4,6},{5,7},{6,4},{7,5},{8,10},{9,11},{10,... | collective-permute-start | bytes 2359304 | tf_op jit(solution)/shard_map/ppermute | solution.py:38
  23.7 31.3 %collective-permute-start.3 = (bf16[512,768]{1,0:T(8,128)(2,1)S(1)}, bf16[512,768]{1,0:T(8,128)(2,1)S(1)}, u32[]{:S(2)}, u32[]{:S(2)}) collective-permute-start(bf16[512,768]{1,0:T(8,128)(2,1)S(1)} %broadcast_select_fusion.ga_ref.g0.cot_ref), channel_id=1, source_target_pairs={{0,2},{1,3},{2,0},{3,1},{4,6},{5,7},{6,4},{7,5},{8,10},{9,11},{10,... | collective-permute-start | bytes 2359304 | tf_op jit(solution)/shard_map/ppermute | solution.py:38
  53.0 16.0 %collective-permute-start.5 = (bf16[1024,192]{1,0:T(8,128)(2,1)}, bf16[1024,192]{1,0:T(8,128)(2,1)S(1)}, u32[]{:S(2)}, u32[]{:S(2)}) collective-permute-start(bf16[1024,192]{1,0:T(8,128)(2,1)} %get-tuple-element.106.rest_5_), channel_id=1, source_target_pairs={{0,2},{1,3},{2,0},{3,1},{4,6},{5,7},{6,4},{7,5},{8,10},{9,11},{10,... | collective-permute-start | bytes 1179656 | tf_op jit(solution)/shard_map/ppermute | solution.py:38
  53.0 20.5 %collective-permute-start.8 = (bf16[192,768]{1,0:T(8,128)(2,1)S(1)}, bf16[192,768]{1,0:T(8,128)(2,1)S(1)}, u32[]{:S(2)}, u32[]{:S(2)}) collective-permute-start(bf16[192,768]{1,0:T(8,128)(2,1)S(1)} %bitcast.23), channel_id=1, source_target_pairs={{0,2},{1,3},{2,0},{3,1},{4,6},{5,7},{6,4},{7,5},{8,10},{9,11},{10,... | collective-permute-start | bytes 884744 | tf_op jit(solution)/shard_map/ppermute | solution.py:38
  80.3 22.2 %collective-permute-start.12 = (bf16[512,768]{1,0:T(8,128)(2,1)}, bf16[512,768]{1,0:T(8,128)(2,1)S(1)}, u32[]{:S(2)}, u32[]{:S(2)}) collective-permute-start(bf16[512,768]{1,0:T(8,128)(2,1)} %get-tuple-element.112.ha_ref.h0), channel_id=1, source_target_pairs={{0,2},{1,3},{2,0},{3,1},{4,6},{5,7},{6,4},{7,5},{8,10},{9,11},{10,... | collective-permute-start | bytes 2359304 | tf_op jit(solution)/shard_map/ppermute | solution.py:38
  84.2 18.3 %collective-permute-start.14 = (bf16[512,768]{1,0:T(8,128)(2,1)}, bf16[512,768]{1,0:T(8,128)(2,1)S(1)}, u32[]{:S(2)}, u32[]{:S(2)}) collective-permute-start(bf16[512,768]{1,0:T(8,128)(2,1)} %copy-done.29), channel_id=1, source_target_pairs={{0,1},{1,0},{2,3},{3,2},{4,5},{5,4},{6,7},{7,6},{8,9},{9,8},{10,11... | collective-permute-start | bytes 2359304 | tf_op jit(solution)/shard_map/ppermute | solution.py:38
  120.5 20.8 %collective-permute-start.16 = (bf16[1024,768]{1,0:T(8,128)(2,1)}, bf16[1024,768]{1,0:T(8,128)(2,1)}, u32[]{:S(2)}, u32[]{:S(2)}) collective-permute-start(bf16[1024,768]{1,0:T(8,128)(2,1)} %get-tuple-element.118), channel_id=1, source_target_pairs={{0,1},{1,0},{2,3},{3,2},{4,5},{5,4},{6,7},{7,6},{8,9},{9,8},{10,11... | collective-permute-start | bytes 4718600 | tf_op jit(solution)/shard_map/ppermute | solution.py:38
  120.6 20.7 %collective-permute-start.19 = (bf16[1024,768]{1,0:T(8,128)(2,1)}, bf16[1024,768]{1,0:T(8,128)(2,1)}, u32[]{:S(2)}, u32[]{:S(2)}) collective-permute-start(bf16[1024,768]{1,0:T(8,128)(2,1)} %get-tuple-element.130), channel_id=1, source_target_pairs={{0,1},{1,0},{2,3},{3,2},{4,5},{5,4},{6,7},{7,6},{8,9},{9,8},{10,11... | collective-permute-start | bytes 4718600 | tf_op jit(solution)/shard_map/ppermute | solution.py:38
  121.0 20.3 %collective-permute-start.17 = (bf16[1024,768]{1,0:T(8,128)(2,1)S(1)}, bf16[1024,768]{1,0:T(8,128)(2,1)S(1)}, u32[]{:S(2)}, u32[]{:S(2)}) collective-permute-start(bf16[1024,768]{1,0:T(8,128)(2,1)S(1)} %copy-done.6), channel_id=1, source_target_pairs={{0,1},{1,0},{2,3},{3,2},{4,5},{5,4},{6,7},{7,6},{8,9},{9,8},{10,11... | collective-permute-start | bytes 4718600 | tf_op jit(solution)/shard_map/ppermute | solution.py:38
  121.1 20.1 %collective-permute-start.18 = (bf16[512,768]{1,0:T(8,128)(2,1)}, bf16[512,768]{1,0:T(8,128)(2,1)}, u32[]{:S(2)}, u32[]{:S(2)}) collective-permute-start(bf16[512,768]{1,0:T(8,128)(2,1)} %add_convert_fusion.4), channel_id=1, source_target_pairs={{0,2},{1,3},{2,0},{3,1},{4,6},{5,7},{6,4},{7,5},{8,10},{9,11},{10,... | collective-permute-start | bytes 2359304 | tf_op jit(solution)/shard_map/ppermute | solution.py:38
  148.8 28.6 %collective-permute-start.21 = (bf16[768,768]{1,0:T(8,128)(2,1)}, bf16[768,768]{1,0:T(8,128)(2,1)S(1)}, u32[]{:S(2)}, u32[]{:S(2)}) collective-permute-start(bf16[768,768]{1,0:T(8,128)(2,1)} %get-tuple-element.132), channel_id=1, source_target_pairs={{0,4},{4,0},{8,12},{12,8},{16,20},{20,16},{24,28},{28,24},{1,5},{5... | collective-permute-start | bytes 3538952 | tf_op jit(solution)/shard_map/ppermute | solution.py:38
  148.9 14.5 %collective-permute-start.22 = (bf16[1024,192]{1,0:T(8,128)(2,1)}, bf16[1024,192]{1,0:T(8,128)(2,1)S(1)}, u32[]{:S(2)}, u32[]{:S(2)}) collective-permute-start(bf16[1024,192]{1,0:T(8,128)(2,1)} %bitcast.29), channel_id=1, source_target_pairs={{0,2},{1,3},{2,0},{3,1},{4,6},{5,7},{6,4},{7,5},{8,10},{9,11},{10,... | collective-permute-start | bytes 1179656 | tf_op jit(solution)/shard_map/ppermute | solution.py:38
  152.7 32.9 %collective-permute-start.29 = (bf16[192,768]{1,0:T(8,128)(2,1)S(1)}, bf16[192,768]{1,0:T(8,128)(2,1)S(1)}, u32[]{:S(2)}, u32[]{:S(2)}) collective-permute-start(bf16[192,768]{1,0:T(8,128)(2,1)S(1)} %convolution_convert_fusion), channel_id=1, source_target_pairs={{0,1},{1,0},{2,3},{3,2},{4,5},{5,4},{6,7},{7,6},{8,9},{9,8},{10,11... | collective-permute-start | bytes 884744 | tf_op jit(solution)/shard_map/ppermute | solution.py:38
  154.5 30.8 %collective-permute-start.24 = (bf16[192,768]{1,0:T(8,128)(2,1)S(1)}, bf16[192,768]{1,0:T(8,128)(2,1)S(1)}, u32[]{:S(2)}, u32[]{:S(2)}) collective-permute-start(bf16[192,768]{1,0:T(8,128)(2,1)S(1)} %convolution_convert_fusion.1), channel_id=1, source_target_pairs={{0,1},{1,0},{2,3},{3,2},{4,5},{5,4},{6,7},{7,6},{8,9},{9,8},{10,11... | collective-permute-start | bytes 884744 | tf_op jit(solution)/shard_map/ppermute | solution.py:38
  163.4 25.2 %collective-permute-start.25 = (bf16[1024,192]{1,0:T(8,128)(2,1)S(1)}, bf16[1024,192]{1,0:T(8,128)(2,1)S(1)}, u32[]{:S(2)}, u32[]{:S(2)}) collective-permute-start(bf16[1024,192]{1,0:T(8,128)(2,1)S(1)} %collective-permute-done.22.rest_2_), channel_id=1, source_target_pairs={{0,1},{1,0},{2,3},{3,2},{4,5},{5,4},{6,7},{7,6},{8,9},{9,8},{10,11... | collective-permute-start | bytes 1179656 | tf_op jit(solution)/shard_map/ppermute | solution.py:38
  178.6 43.6 %collective-permute-start.26 = (bf16[192,768]{1,0:T(8,128)(2,1)}, bf16[192,768]{1,0:T(8,128)(2,1)S(1)}, u32[]{:S(2)}, u32[]{:S(2)}) collective-permute-start(bf16[192,768]{1,0:T(8,128)(2,1)} %get-tuple-element.188), channel_id=1, source_target_pairs={{0,8},{4,12},{8,0},{12,4},{16,24},{20,28},{24,16},{28,20},{1,9},{5... | collective-permute-start | bytes 884744 | tf_op jit(solution)/shard_map/ppermute | solution.py:38
  180.2 42.0 %collective-permute-start.27 = (bf16[192,768]{1,0:T(8,128)(2,1)}, bf16[192,768]{1,0:T(8,128)(2,1)S(1)}, u32[]{:S(2)}, u32[]{:S(2)}) collective-permute-start(bf16[192,768]{1,0:T(8,128)(2,1)} %get-tuple-element.190), channel_id=1, source_target_pairs={{0,16},{4,20},{8,24},{12,28},{16,0},{20,4},{24,8},{28,12},{1,17},{... | collective-permute-start | bytes 884744 | tf_op jit(solution)/shard_map/ppermute | solution.py:38
  185.3 37.0 %collective-permute-start.28 = (bf16[192,768]{1,0:T(8,128)(2,1)S(1)}, bf16[192,768]{1,0:T(8,128)(2,1)}, u32[]{:S(2)}, u32[]{:S(2)}) collective-permute-start(bf16[192,768]{1,0:T(8,128)(2,1)S(1)} %get-tuple-element.189), channel_id=1, source_target_pairs={{0,24},{4,28},{8,16},{12,20},{16,8},{20,12},{24,0},{28,4},{1,25},{... | collective-permute-start | bytes 884744 | tf_op jit(solution)/shard_map/ppermute | solution.py:38
  185.7 44.0 %collective-permute-start.23 = (bf16[512,768]{1,0:T(8,128)(2,1)S(1)}, bf16[512,768]{1,0:T(8,128)(2,1)}, u32[]{:S(2)}, u32[]{:S(2)}) collective-permute-start(bf16[512,768]{1,0:T(8,128)(2,1)S(1)} %add_convert_fusion.3), channel_id=1, source_target_pairs={{0,2},{1,3},{2,0},{3,1},{4,6},{5,7},{6,4},{7,5},{8,10},{9,11},{10,... | collective-permute-start | bytes 2359304 | tf_op jit(solution)/shard_map/ppermute | solution.py:38
  189.4 38.5 %collective-permute-start.30 = (bf16[192,768]{1,0:T(8,128)(2,1)}, bf16[192,768]{1,0:T(8,128)(2,1)}, u32[]{:S(2)}, u32[]{:S(2)}) collective-permute-start(bf16[192,768]{1,0:T(8,128)(2,1)} %fusion.10), channel_id=1, source_target_pairs={{0,2},{1,3},{2,0},{3,1},{4,6},{5,7},{6,4},{7,5},{8,10},{9,11},{10,... | collective-permute-start | bytes 884744 | tf_op jit(solution)/shard_map/ppermute | solution.py:38
  223.4 22.9 %collective-permute-start.32 = (bf16[192,768]{1,0:T(8,128)(2,1)S(1)}, bf16[192,768]{1,0:T(8,128)(2,1)S(1)}, u32[]{:S(2)}, u32[]{:S(2)}) collective-permute-start(bf16[192,768]{1,0:T(8,128)(2,1)S(1)} %add_convert_fusion.6), channel_id=1, source_target_pairs={{0,8},{4,12},{8,0},{12,4},{16,24},{20,28},{24,16},{28,20},{1,9},{5... | collective-permute-start | bytes 884744 | tf_op jit(solution)/shard_map/ppermute | solution.py:38
  223.4 24.9 %collective-permute-start.33 = (bf16[192,768]{1,0:T(8,128)(2,1)S(1)}, bf16[192,768]{1,0:T(8,128)(2,1)S(1)}, u32[]{:S(2)}, u32[]{:S(2)}) collective-permute-start(bf16[192,768]{1,0:T(8,128)(2,1)S(1)} %add_convert_fusion.6), channel_id=1, source_target_pairs={{0,16},{4,20},{8,24},{12,28},{16,0},{20,4},{24,8},{28,12},{1,17},{... | collective-permute-start | bytes 884744 | tf_op jit(solution)/shard_map/ppermute | solution.py:38
  227.8 20.5 %collective-permute-start.34 = (bf16[192,768]{1,0:T(8,128)(2,1)S(1)}, bf16[192,768]{1,0:T(8,128)(2,1)S(1)}, u32[]{:S(2)}, u32[]{:S(2)}) collective-permute-start(bf16[192,768]{1,0:T(8,128)(2,1)S(1)} %add_convert_fusion.6), channel_id=1, source_target_pairs={{0,24},{4,28},{8,16},{12,20},{16,8},{20,12},{24,0},{28,4},{1,25},{... | collective-permute-start | bytes 884744 | tf_op jit(solution)/shard_map/ppermute | solution.py:38
  237.3 14.0 %collective-permute-start.31 = (bf16[392,768]{1,0:T(8,128)(2,1)}, bf16[392,768]{1,0:T(8,128)(2,1)S(1)}, u32[]{:S(2)}, u32[]{:S(2)}) collective-permute-start(bf16[392,768]{1,0:T(8,128)(2,1)} %get-tuple-element.149), channel_id=1, source_target_pairs={{0,4},{4,0},{8,12},{12,8},{16,20},{20,16},{24,28},{28,24},{1,5},{5... | collective-permute-start | bytes 1806344 | tf_op jit(solution)/shard_map/ppermute | solution.py:38
  251.7 15.7 %collective-permute-start.36 = (bf16[384,768]{1,0:T(8,128)(2,1)S(1)}, bf16[384,768]{1,0:T(8,128)(2,1)S(1)}, u32[]{:S(2)}, u32[]{:S(2)}) collective-permute-start(bf16[384,768]{1,0:T(8,128)(2,1)S(1)} %pad_maximum_fusion.rest_0_), channel_id=1, source_target_pairs={{0,4},{4,0},{8,12},{12,8},{16,20},{20,16},{24,28},{28,24},{1,5},{5... | collective-permute-start | bytes 1769480 | tf_op jit(solution)/shard_map/ppermute | solution.py:38
  253.5 13.9 %collective-permute-start.35 = (bf16[104,768]{1,0:T(8,128)(2,1)S(1)}, bf16[104,768]{1,0:T(8,128)(2,1)S(1)}, u32[]{:S(2)}, u32[]{:S(2)}) collective-permute-start(bf16[104,768]{1,0:T(8,128)(2,1)S(1)} %get-tuple-element.194), channel_id=1, source_target_pairs={{0,8},{4,12},{8,0},{12,4},{16,24},{20,28},{24,16},{28,20},{1,9},{5... | collective-permute-start | bytes 479240 | tf_op jit(solution)/shard_map/ppermute | solution.py:38
  255.7 14.7 %collective-permute-start.38 = (bf16[104,768]{1,0:T(8,128)(2,1)S(1)}, bf16[104,768]{1,0:T(8,128)(2,1)S(1)}, u32[]{:S(2)}, u32[]{:S(2)}) collective-permute-start(bf16[104,768]{1,0:T(8,128)(2,1)S(1)} %get-tuple-element.193), channel_id=1, source_target_pairs={{0,16},{4,20},{8,24},{12,28},{16,0},{20,4},{24,8},{28,12},{1,17},{... | collective-permute-start | bytes 479240 | tf_op jit(solution)/shard_map/ppermute | solution.py:38
  257.1 13.4 %collective-permute-start.39 = (bf16[104,768]{1,0:T(8,128)(2,1)S(1)}, bf16[104,768]{1,0:T(8,128)(2,1)S(1)}, u32[]{:S(2)}, u32[]{:S(2)}) collective-permute-start(bf16[104,768]{1,0:T(8,128)(2,1)S(1)} %concatenate.24), channel_id=1, source_target_pairs={{0,24},{4,28},{8,16},{12,20},{16,8},{20,12},{24,0},{28,4},{1,25},{... | collective-permute-start | bytes 479240 | tf_op jit(solution)/shard_map/ppermute | solution.py:38
  270.5 13.9 %collective-permute-start.41 = (bf16[384,768]{1,0:T(8,128)(2,1)S(1)}, bf16[384,768]{1,0:T(8,128)(2,1)S(1)}, u32[]{:S(2)}, u32[]{:S(2)}) collective-permute-start(bf16[384,768]{1,0:T(8,128)(2,1)S(1)} %constant_dynamic-update-slice_fusion.rest_1_), channel_id=1, source_target_pairs={{0,4},{4,0},{8,12},{12,8},{16,20},{20,16},{24,28},{28,24},{1,5},{5... | collective-permute-start | bytes 1769480 | tf_op jit(solution)/shard_map/ppermute | solution.py:38
  274.3 13.2 %collective-permute-start.42 = (bf16[96,768]{1,0:T(8,128)(2,1)S(1)}, bf16[96,768]{1,0:T(8,128)(2,1)S(1)}, u32[]{:S(2)}, u32[]{:S(2)}) collective-permute-start(bf16[96,768]{1,0:T(8,128)(2,1)S(1)} %add_convert_fusion.7), channel_id=1, source_target_pairs={{0,16},{4,20},{8,24},{12,28},{16,0},{20,4},{24,8},{28,12},{1,17},{... | collective-permute-start | bytes 442376 | tf_op jit(solution)/shard_map/ppermute | solution.py:38
  276.7 24.7 %collective-permute-start.45 = (bf16[512,768]{1,0:T(8,128)(2,1)}, bf16[512,768]{1,0:T(8,128)(2,1)S(1)}, u32[]{:S(2)}, u32[]{:S(2)}) collective-permute-start(bf16[512,768]{1,0:T(8,128)(2,1)} %add_convert_fusion.2), channel_id=1, source_target_pairs={{0,2},{1,3},{2,0},{3,1},{4,6},{5,7},{6,4},{7,5},{8,10},{9,11},{10,... | collective-permute-start | bytes 2359304 | tf_op jit(solution)/shard_map/ppermute | solution.py:38
  289.7 17.1 %collective-permute-start.48 = (bf16[384,768]{1,0:T(8,128)(2,1)}, bf16[384,768]{1,0:T(8,128)(2,1)}, u32[]{:S(2)}, u32[]{:S(2)}) collective-permute-start(bf16[384,768]{1,0:T(8,128)(2,1)} %pad_maximum_fusion.1.rest_0_), channel_id=1, source_target_pairs={{0,4},{4,0},{8,12},{12,8},{16,20},{20,16},{24,28},{28,24},{1,5},{5... | collective-permute-start | bytes 1769480 | tf_op jit(solution)/shard_map/ppermute | solution.py:38
  (56 other events, 464.4 us)

commit v3 on v2

--- a/solution.py
+++ b/solution.py
@@ -205,7 +205,7 @@
     for c in range(4):
         r0 = pl.multiple_of((own ^ c) * chunk, chunk)
         part = slice((c % 2) * chunk, (c % 2 + 1) * chunk)
-        g = g_refs[c][part, :]
+        g = g_refs[c][...]
         o = o_refs[c // 2][part, :]
         for h in range(heads):
             gh = g[:, h * hd : (h + 1) * hd]
@@ -299,7 +299,7 @@
 
 
 def feed_kernel(steps, ha_ref, hb_ref, ga_ref, gb_ref, up_ref, v_ref, down_ref, *rest):
-    act_ref, gup_ref, gn_ref, out_ref = rest[-4:]
+    act_ref, gup_ref, gna_ref, gnb_ref, outa_ref, outb_ref = rest[-6:]
     early = pl.program_id(0) < steps // 2
     h2 = jnp.where(early, ha_ref[...], hb_ref[...])
     grad = jnp.where(early, ga_ref[...], gb_ref[...])
@@ -312,8 +312,18 @@
     gup = (dot_nt(grad, down_ref[...]) * slope).astype(BF)
     act_ref[...] = act
     gup_ref[...] = gup
-    gn_ref[...] = dot_nt(gup, up_ref[...]).astype(BF)
-    out_ref[...] = dot_nn(act, down_ref[...]).astype(BF)
+    gn = dot_nt(gup, up_ref[...]).astype(BF)
+    out = dot_nn(act, down_ref[...]).astype(BF)
+
+    @pl.when(early)
+    def _():
+        gna_ref[...] = gn
+        outa_ref[...] = out
+
+    @pl.when(jnp.logical_not(early))
+    def _():
+        gnb_ref[...] = gn
+        outb_ref[...] = out
 
 
 def feed_call(ha, hb, ga, gb, up, vectors, down, first, group_rows, before):
@@ -329,9 +339,8 @@
         out_shape=(
             jax.ShapeDtypeStruct((group_rows, hidden), BF),
             jax.ShapeDtypeStruct((group_rows, hidden), BF),
-            jax.ShapeDtypeStruct((2 * rows, width), BF),
-            jax.ShapeDtypeStruct((2 * rows, width), BF),
-        ),
+        )
+        + (jax.ShapeDtypeStruct((rows, width), BF),) * 4,
         grid=(steps,),
         in_specs=[
             early,
@@ -346,8 +355,10 @@
         out_specs=[
             pl.BlockSpec((BLK, hidden), lambda t: (first * per + t, 0)),
             pl.BlockSpec((BLK, hidden), lambda t: (first * per + t, 0)),
-            pl.BlockSpec((BLK, width), lambda t: (t, 0)),
-            pl.BlockSpec((BLK, width), lambda t: (t, 0)),
+            early,
+            late,
+            early,
+            late,
         ],
         input_output_aliases={7 + i: i for i in range(len(before))},
         cost_estimate=cost(16 * rows * width * hidden, 16 * rows * width, 2 * rows * hidden),
@@ -457,7 +468,7 @@
     )(*parts, *projs, x, vectors)
 
 
-def turn_kernel(n_ref, s_ref, f_ref, resid_ref, cot_ref, v_ref, p0, p1, p2, p3, gr_ref, ga_ref, gn_ref, gf_ref, sum_ref):
+def turn_kernel(n_ref, s_ref, f_ref, resid_ref, cot_ref, v_ref, p0, p1, p2, p3, gr_ref, ga_ref, g0, g1, g2, g3, sum_ref):
     grad = n_ref[...].astype(F32) + s_ref[...].astype(F32) + f_ref[...].astype(F32)
     hat, rstd = normalize(resid_ref[...])
     cot = cot_ref[...].astype(F32)
@@ -467,10 +478,8 @@
     gr_ref[...] = grad_resid
     att = grad_resid.astype(BF)
     ga_ref[...] = att
-    gn_ref[0] = dot_nt(att, p0[...]).astype(BF)
-    gn_ref[1] = dot_nt(att, p1[...]).astype(BF)
-    gf_ref[0] = dot_nt(att, p2[...]).astype(BF)
-    gf_ref[1] = dot_nt(att, p3[...]).astype(BF)
+    for g, p in ((g0, p0), (g1, p1), (g2, p2), (g3, p3)):
+        g[...] = dot_nt(att, p[...]).astype(BF)
 
     @pl.when(pl.program_id(0) == 0)
     def _():
@@ -485,24 +494,23 @@
     per = rows // BLK
     inner = projs[0].shape[0]
     low = pl.BlockSpec((BLK, width), lambda t: (t, 0))
-    high = pl.BlockSpec((BLK, width), lambda t: (t + per, 0))
     whole = lambda t: (0, 0)
-    pair = jax.ShapeDtypeStruct((2, rows, inner), BF)
-    pair_spec = pl.BlockSpec((2, BLK, inner), lambda t: (0, t, 0))
     return pl.pallas_call(
         turn_kernel,
         out_shape=(
             jax.ShapeDtypeStruct((rows, width), F32),
             jax.ShapeDtypeStruct((rows, width), BF),
-            pair,
-            pair,
-            jax.ShapeDtypeStruct((8, width), F32),
-        ),
+        )
+        + (jax.ShapeDtypeStruct((rows, inner), BF),) * 4
+        + (jax.ShapeDtypeStruct((8, width), F32),),
         grid=(per,),
-        in_specs=[low, high, low, low, low, pl.BlockSpec(vectors.shape, whole)]
+        in_specs=[low] * 5
+        + [pl.BlockSpec(vectors.shape, whole)]
         + [pl.BlockSpec(projs[0].shape, whole)] * 4,
-        out_specs=[low, low, pair_spec, pair_spec, pl.BlockSpec((8, width), whole)],
-        cost_estimate=cost(8 * rows * width * inner, 20 * rows * width),
+        out_specs=[low, low]
+        + [pl.BlockSpec((BLK, inner), lambda t: (t, 0))] * 4
+        + [pl.BlockSpec((8, width), whole)],
+        cost_estimate=cost(rows, width),
         name="turn",
     )(near, swapped, far, resid, cot, vectors, *projs)
 
@@ -567,33 +575,24 @@
     )(bid, gp, hat, w, vectors, proj_grad, up_grad, sums)
 
 
-def spread_kernel(steps, gp_ref, w_ref, near_ref, far_ref):
-    t = pl.program_id(0)
+def spread_kernel(gp_ref, w_ref, *outs):
     e = dot_nn(gp_ref[...], w_ref[...]).astype(BF)
-
-    @pl.when(t < steps // 2)
-    def _():
-        near_ref[...] = e
-
-    @pl.when(t >= steps // 2)
-    def _():
-        far_ref[...] = e
-
-
-def spread_call(gp, w):
-    rows, cols = gp.shape
-    width = w.shape[1]
-    block = 2 * BLK
-    steps = rows // block
-    return pl.pallas_call(
-        functools.partial(spread_kernel, steps),
-        out_shape=(jax.ShapeDtypeStruct((rows // 2, width), BF),) * 2,
-        grid=(steps,),
-        in_specs=[pl.BlockSpec((block, cols), lambda t: (t, 0)), pl.BlockSpec(w.shape, lambda t: (0, 0))],
-        out_specs=[
-            pl.BlockSpec((block, width), lambda t: (jnp.minimum(t, steps // 2 - 1), 0)),
-            pl.BlockSpec((block, width), lambda t: (jnp.maximum(t - steps // 2, 0), 0)),
-        ],
+    for k, out in enumerate(outs):
+
+        @pl.when(pl.program_id(0) == k)
+        def _(out=out):
+            out[...] = e
+
+
+def spread_call(gp, w, chunk):
+    cols, width = w.shape
+    whole = lambda t: (0, 0)
+    return pl.pallas_call(
+        spread_kernel,
+        out_shape=(jax.ShapeDtypeStruct((chunk, width), BF),) * 4,
+        grid=(4,),
+        in_specs=[pl.BlockSpec((chunk, cols), lambda t: (t, 0)), pl.BlockSpec(w.shape, whole)],
+        out_specs=[pl.BlockSpec((chunk, width), whole)] * 4,
         cost_estimate=cost(cols, width),
         name="spread",
     )(gp, w)
@@ -723,26 +722,31 @@
     near = feed_call(h_own, h_near, grads[0], grads[1], weight_up, vectors, weight_down, 0, group_rows, ())
     h_far = tie(h_far, near[0])
     h_last = swap(h_far, "head", 1)
-    act, grad_up, grad_norm_far, down_far = feed_call(
+    act, grad_up, norm_far, norm_last, down_far, down_last = feed_call(
         h_far, h_last, grads[2], grads[3], weight_up, vectors, weight_down, 2, group_rows, near[:2]
     )
-    swapped = swap(grad_norm_far, "head", 1)
-    far_sum = (grad_norm_far[:chunk].astype(F32) + swapped[chunk:].astype(F32)).astype(BF)
+    far_sum = (norm_far.astype(F32) + swap(norm_last, "head", 1).astype(F32)).astype(BF)
     grad_far_sum = swap(far_sum, "head", 2)
-    near_swapped = swap(near[2], "head", 1)
-    down_swapped = swap(tie(down_far, far_sum), "head", 1)
-    near_down = swap(tie(near[3], far_sum), "head", 1)
+    near_swapped = swap(near[3], "head", 1)
+    down_swapped = swap(tie(down_last, far_sum), "head", 1)
+    near_down = swap(tie(near[5], far_sum), "head", 1)
 
     keep_feed, send_feed, grad_bup = weigh_call(
         bid, (h_own, h_near, h_far, h_last), tie(act, far_sum), grad_up, grads
     )
     other_feed = swap(send_feed, "batch", 1)
-    grad_resid, grad_att, grad_near, grad_cross, sums = turn_call(
-        near[2], near_swapped, tie(grad_far_sum, grad_bup, down_swapped, near_down), resid, grad_own, vectors, projs
-    )
-    grad_near = grad_near.reshape(2 * chunk, inner)
-    got = swap(grad_cross.reshape(2 * chunk, inner), "head", 2)
-    grad_mate = swap(grad_near, "head", 1)
+    grad_resid, grad_att, grad_near, grad_mate, grad_cross, grad_last, sums = turn_call(
+        near[2],
+        near_swapped,
+        tie(grad_far_sum, grad_bup, down_swapped, near_down),
+        resid,
+        grad_own,
+        vectors,
+        projs,
+    )
+    got_last = swap(grad_last, "head", 2)
+    got = swap(grad_cross, "head", 2)
+    grad_mate = swap(grad_mate, "head", 1)
     grad_att = tie(grad_att, grad_mate)
     low = slice(0, chunk)
     high = slice(chunk, 2 * chunk)
@@ -751,9 +755,9 @@
     ]
     near_sent, far_sent = grad_proj[1].astype(BF), grad_proj[3].astype(BF)
     down_far = tie(down_far, grad_att)
-    down_sum = (down_far[:chunk].astype(F32) + down_swapped[chunk:].astype(F32)).astype(BF)
-    got = tie(got, near_sent, far_sent, down_sum)
-    merged_grads = (grad_near, grad_mate, got, swap(got, "head", 1))
+    down_sum = (down_far.astype(F32) + down_swapped.astype(F32)).astype(BF)
+    got_last = tie(got_last, near_sent, far_sent, down_sum)
+    merged_grads = (grad_near, grad_mate, got, swap(got_last, "head", 1))
     grad_near_proj = grad_proj[0] + swap(near_sent, "head", 1).astype(F32)
     far_proj = (grad_proj[2] + swap(far_sent, "head", 1).astype(F32)).astype(BF)
     far_proj = swap(far_proj, "head", 2)
@@ -781,8 +785,9 @@
         bid, tie(grad_packed, total_feed, down_other), hats, qkv_t, vectors, grad_wproj, grad_bup, sums
     )
     other = swap(send, "batch", 1)
-    e_near, e_far = spread_call(tie(grad_packed, keep), qkv_t)
-    gathered_feed, e_near, e_far = lax.optimization_barrier((gathered_feed, e_near, e_far))
+    spread = spread_call(tie(grad_packed, keep), qkv_t, chunk)
+    gathered_feed, spread = lax.optimization_barrier((gathered_feed, spread))
+    e_own, e_near, e_far, e_last = spread
 
     feed_a = jnp.concatenate((total_feed, gathered_feed[0]), axis=0)
     feed_b = jnp.concatenate(gathered_feed[1:], axis=0)
@@ -790,8 +795,8 @@
     summed = (keep.astype(F32) + tie(other, feed_a, feed_b).astype(F32)).astype(BF)
     kept, small = summed[:-8], summed[-8:]
     pieces = [jnp.concatenate((q, small), axis=0) for q in quarters(kept)]
-    e_swapped = swap(tie(e_far, *pieces), "head", 1)
-    e_sum = (e_far[:chunk].astype(F32) + e_swapped[chunk:].astype(F32)).astype(BF)
+    e_swapped = swap(tie(e_last, *pieces), "head", 1)
+    e_sum = (e_far.astype(F32) + e_swapped.astype(F32)).astype(BF)
     got_attn = [tie(g, last_a, e_sum) for g in across(pieces)]
 
     tiny = [small.astype(F32)] + [g[-8:].astype(F32) for g in got_attn]
@@ -805,9 +810,9 @@
     last = swap(half, "batch", 1)
     biases = small[2:4]
     small = sum_group(tie(small, half))
-    e_own = e_near[:chunk].astype(F32) + e_mate[chunk:].astype(F32) + tie(e_other, half).astype(F32)
-
-    near_down = near[3][:chunk].astype(F32) + near_down[chunk:].astype(F32)
+    e_own = e_own.astype(F32) + e_mate.astype(F32) + tie(e_other, half).astype(F32)
+
+    near_down = near[4].astype(F32) + near_down.astype(F32)
     output = (resid + near_down + tie(down_other, half).astype(F32) + bias_down).astype(BF)
     x_hat, x_rstd = normalize(tie(inputs, half).astype(F32))
     e_own = e_own * gain_attn

time: 311 us -> 289 us (0.929)
  waiting for transfers between devices: 76.7 us -> 63.8 us
  starting transfers between devices: 51.1 us -> 41.9 us
  Pallas kernels: 142 us -> 146 us
    ppermute x49 -> x50, waiting for transfers between devices: 76.7 us -> 63.8 us  [swap(): return lax.ppermute(x, axis, [(i, i ^ bits) for i in range(size)])]
    ppermute x49 -> x50, starting transfers between devices: 51.1 us -> 41.9 us  [swap(): return lax.ppermute(x, axis, [(i, i ^ bits) for i in range(size)])]
    unnamed x79 -> x75, local copies, waits for them, and re-layouts: 6.64 us -> 4.87 us
  transfers between devices with their start and end apart: 49 -> 50, of which waited for: 17 -> 15; matrix products, arithmetic and copies ran while one was open for 10% -> 10% of each run, Pallas kernels for 40% -> 46%
where the time goes in v3:
time: 289 us; the launch traced here: 288 us
  Pallas kernels  146 us (51%)
  waiting for transfers between devices  63.8 us (22%)
  starting transfers between devices  41.9 us (14%)
  other arithmetic  18.7 us (6%)
  local copies, waits for them, and re-layouts  12.4 us (4%)
  matrix products  3.91 us (1%)
    ppermute x50, waiting for transfers between devices, swap(): return lax.ppermute(x, axis, [(i, i ^ bits) for i in range(size)])  63.8 us
    ppermute x50, starting transfers between devices, swap(): return lax.ppermute(x, axis, [(i, i ^ bits) for i in range(size)])  41.9 us
    pallas_call x2, Pallas kernels, attend_call(): pl.pallas_call(functools.partial(attend_kernel, heads, first, per, 1.0 /...  35.5 us
    pallas_call x1, Pallas kernels, attend_back_call(): pl.pallas_call(functools.partial(attend_back_kernel, chunk, 1.0 / math.sq...  33.4 us
    pallas_call x2, Pallas kernels, feed_call(): pl.pallas_call(functools.partial(feed_kernel, steps), out_shape=(jax.Shap...  20 us
    pallas_call x2, Pallas kernels, qkv_call(): pl.pallas_call(functools.partial(qkv_kernel, heads, hd, steps), out_shape...  12.8 us
    pallas_call x1, Pallas kernels, weigh_call(): pl.pallas_call(functools.partial(weigh_kernel, tiles), out_shape=(half, h...  12.5 us
    pallas_call x1, Pallas kernels, tally_call(): pl.pallas_call(functools.partial(tally_kernel, steps), out_shape=(half, h...  7.71 us
  transfers between devices with their start and end apart: 50, of which 15 were waited for; matrix products, arithmetic and copies ran while one was open for 10% of the time, Pallas kernels for 46%

profile of v3, /device:TPU:0, one launch (start us, length us, event | category | flops | bytes accessed | tf_op | source)
XLA Modules:
  0.0 287.8 jit_solution(2224925255288948165)
XLA Ops:
  1.2 2.6 collective-permute-start
  10.1 6.5 %qkv.2 = (bf16[3,2048,64]{2,1,0:T(8,128)(2,1)}, bf16[3,2048,64]{2,1,0:T(8,128)(2,1)}, bf16[3,2048,64]{2,1,0:T(8,128)(2,1)}, bf16[3,64,2048]{2,1,0:T(8,128)(2,1)}, bf16[2048,768]{1,0:T(8,128)(2,1)}) custom-call(s32[1]{0:T(128)} %bitcast.1.h_ref, bf16[512,768]{1,0:T(8,128)(2,1)} %x_ref.1, bf16[512,768]{1,0:T(8,128)(2,1)} %copy-done.32, f32[8,768]{1,0:T(8,128)} %stack.31.v_ref, ...), custom_call_target="tpu_custom_call" | custom-call | flops 905969664 | bytes 4718592 | tf_op jit(solution)/shard_map/qkv/pallas_call | solution.py:84
  16.6 5.5 %collective-permute-done.a_ref = bf16[512,768]{1,0:T(8,128)(2,1)S(1)} collective-permute-done((bf16[512,768]{1,0:T(8,128)(2,1)}, bf16[512,768]{1,0:T(8,128)(2,1)S(1)}, u32[]{:S(2)}, u32[]{:S(2)}) %collective-permute-start) | collective-permute-done | bytes 786464 | tf_op jit(solution)/shard_map/ppermute | solution.py:38
  26.4 6.3 %qkv.3 = (bf16[3,2048,64]{2,1,0:T(8,128)(2,1)}, bf16[3,2048,64]{2,1,0:T(8,128)(2,1)}, bf16[3,2048,64]{2,1,0:T(8,128)(2,1)}, bf16[3,64,2048]{2,1,0:T(8,128)(2,1)}, bf16[2048,768]{1,0:T(8,128)(2,1)}) custom-call(s32[1]{0:T(128)} %bitcast.1.h_ref, ...), custom_call_target="tpu_custom_call", output_to_operand_aliasing={{0}: (6, {}), {1}: (7, {}), {2}: (8, {}), {3}: (9, {}), {4}... | custom-call | flops 905969664 | bytes 4718592 | tf_op jit(solution)/shard_map/qkv/pallas_call | solution.py:84
  32.7 21.5 %attend.2 = (bf16[1024,192]{1,0:T(8,128)(2,1)}, f32[8,1024]{1,0:T(8,128)}) custom-call(s32[8]{0:T(128)} %bitcast.25, s32[1]{0:T(128)} %bitcast.1.h_ref, bf16[3,2048,64]{2,1,0:T(8,128)(2,1)} %get-tuple-element.150.q_ref, bf16[3,2048,64]{2,1,0:T(8,128)(2,1)} %get-tuple-element.114.k_ref, bf16[3,64,2048]{2,1,0:T(8,128)(2,1)} %get-tuple-element.115.vt_ref), custom_call_target="tpu_custom_call" | custom-call | flops 3221225472 | bytes 4718592 | tf_op jit(solution)/shard_map/attend/pallas_call | solution.py:169
  56.3 14.0 %attend.3 = (bf16[1024,192]{1,0:T(8,128)(2,1)}, f32[8,1024]{1,0:T(8,128)}) custom-call(s32[8]{0:T(128)} %bitcast.26, s32[1]{0:T(128)} %bitcast.1.h_ref, bf16[3,2048,64]{2,1,0:T(8,128)(2,1)} %get-tuple-element.150.q_ref, bf16[3,2048,64]{2,1,0:T(8,128)(2,1)} %get-tuple-element.114.k_ref, bf16[3,64,2048]{2,1,0:T(8,128)(2,1)} %get-tuple-element.115.vt_ref), custom_call_target="tpu_custom_call" | custom-call | flops 3221225472 | bytes 4718592 | tf_op jit(solution)/shard_map/attend/pallas_call | solution.py:169
  70.9 3.9 %collective-permute-done.8.p2 = bf16[192,768]{1,0:T(8,128)(2,1)S(1)} collective-permute-done((bf16[192,768]{1,0:T(8,128)(2,1)S(1)}, bf16[192,768]{1,0:T(8,128)(2,1)S(1)}, u32[]{:S(2)}, u32[]{:S(2)}) %collective-permute-start.8) | collective-permute-done | bytes 294944 | tf_op jit(solution)/shard_map/ppermute | solution.py:38
  77.2 4.1 %mix.1 = (f32[512,768]{1,0:T(8,128)}, bf16[512,768]{1,0:T(8,128)(2,1)}) custom-call(bf16[1024,192]{1,0:T(8,128)(2,1)} %get-tuple-element.119.m0.rest_4_, bf16[1024,192]{1,0:T(8,128)(2,1)} %copy-done.15, bf16[1024,192]{1,0:T(8,128)(2,1)} %copy-done.13, bf16[1024,192]{1,0:T(8,128)(2,1)} %collective-permute-done.6.m3, bf16[192,768]{1,0:T(8,128)(2,1)} %bitcast.19, ...), custom_call_target="tpu_custom_call" | custom-call | flops 603979776 | bytes 4718592 | tf_op jit(solution)/shard_map/mix/pallas_call | solution.py:458
  81.4 5.2 %collective-permute-start.12 = (bf16[512,768]{1,0:T(8,128)(2,1)}, bf16[512,768]{1,0:T(8,128)(2,1)S(1)}, u32[]{:S(2)}, u32[]{:S(2)}) collective-permute-start(bf16[512,768]{1,0:T(8,128)(2,1)} %get-tuple-element.122.ha_ref.h0), channel_id=1, source_target_pairs={{0,2},{1,3},{2,0},{3,1},{4,6},{5,7},{6,4},{7,5},{8,10},{9,11},{10,... | collective-permute-start | bytes 2359304 | tf_op jit(solution)/shard_map/ppermute | solution.py:38
  87.6 10.0 %feed.2 = (bf16[2048,768]{1,0:T(8,128)(2,1)}, bf16[2048,768]{1,0:T(8,128)(2,1)}, bf16[512,768]{1,0:T(8,128)(2,1)}, bf16[512,768]{1,0:T(8,128)(2,1)}, bf16[512,768]{1,0:T(8,128)(2,1)}, /*index=5*/bf16[512,768]{1,0:T(8,128)(2,1)}) custom-call(bf16[512,768]{1,0:T(8,128)(2,1)} %get-tuple-element.122.ha_ref.h0, bf16[512,768]{1,0:T(8,128)(2,1)} %copy-done.27, ...), custom_call_target="tpu_custom_call" | custom-call | flops 4831838208 | bytes 6291456 | tf_op jit(solution)/shard_map/feed/pallas_call | solution.py:337
  97.6 7.3 %collective-permute-done.12.ha_ref.h2 = bf16[512,768]{1,0:T(8,128)(2,1)S(1)} collective-permute-done((bf16[512,768]{1,0:T(8,128)(2,1)}, bf16[512,768]{1,0:T(8,128)(2,1)S(1)}, u32[]{:S(2)}, u32[]{:S(2)}) %collective-permute-start.12) | collective-permute-done | bytes 786464 | tf_op jit(solution)/shard_map/ppermute | solution.py:38
  104.9 2.3 collective-permute-done.13.hb_ref.h3
  108.1 10.0 %feed.3 = (bf16[2048,768]{1,0:T(8,128)(2,1)}, bf16[2048,768]{1,0:T(8,128)(2,1)}, bf16[512,768]{1,0:T(8,128)(2,1)}, bf16[512,768]{1,0:T(8,128)(2,1)}, bf16[512,768]{1,0:T(8,128)(2,1)}, /*index=5*/bf16[512,768]{1,0:T(8,128)(2,1)}) custom-call(bf16[512,768]{1,0:T(8,128)(2,1)} %copy-done.28, ...), custom_call_target="tpu_custom_call", output_to_operand_aliasing={{0}: (7, {}), {1}: (8, {})} | custom-call | flops 4831838208 | bytes 6291456 | tf_op jit(solution)/shard_map/feed/pallas_call | solution.py:337
  118.2 2.3 collective-permute-done.15
  124.2 12.5 %weigh.1 = (bf16[768,768]{1,0:T(8,128)(2,1)}, bf16[768,768]{1,0:T(8,128)(2,1)}, f32[1,768]{1,0:T(1,128)}) custom-call(s32[1]{0:T(128)} %bitcast.5.b_ref, bf16[512,768]{1,0:T(8,128)(2,1)} %get-tuple-element.122.ha_ref.h0, bf16[512,768]{1,0:T(8,128)(2,1)} %copy-done.27, bf16[512,768]{1,0:T(8,128)(2,1)} %copy-done.28, bf16[512,768]{1,0:T(8,128)(2,1)} %copy-done.30, ...), custom_call_target="tpu_custom_call" | custom-call | flops 4831838208 | bytes 18874368 | tf_op jit(solution)/shard_map/weigh/pallas_call | solution.py:418
  136.8 5.3 %collective-permute-done.18.f_ref = bf16[512,768]{1,0:T(8,128)(2,1)} collective-permute-done((bf16[512,768]{1,0:T(8,128)(2,1)S(1)}, bf16[512,768]{1,0:T(8,128)(2,1)}, u32[]{:S(2)}, u32[]{:S(2)}) %collective-permute-start.18) | collective-permute-done | bytes 786464 | tf_op jit(solution)/shard_map/ppermute | solution.py:38
  142.2 6.1 %turn.1 = (f32[512,768]{1,0:T(8,128)}, bf16[512,768]{1,0:T(8,128)(2,1)}, bf16[512,192]{1,0:T(8,128)(2,1)}, bf16[512,192]{1,0:T(8,128)(2,1)}, bf16[512,192]{1,0:T...) custom-call(bf16[512,768]{1,0:T(8,128)(2,1)} %get-tuple-element.132.n_ref, ...), custom_call_target="tpu_custom_call" | custom-call | flops 512 | bytes 768 | tf_op jit(solution)/shard_map/turn/pallas_call | solution.py:498
  155.3 7.6 %collective-permute-done.25 = bf16[512,192]{1,0:T(8,128)(2,1)S(1)} collective-permute-done((bf16[512,192]{1,0:T(8,128)(2,1)}, bf16[512,192]{1,0:T(8,128)(2,1)S(1)}, u32[]{:S(2)}, u32[]{:S(2)}) %collective-permute-start.25) | collective-permute-done | bytes 196640 | tf_op jit(solution)/shard_map/ppermute | solution.py:38
  162.9 2.5 collective-permute-done.21
  167.7 2.5 collective-permute-start.29
  173.0 33.4 %attend_back.1.gp_ref = bf16[2048,576]{1,0:T(8,128)(2,1)} custom-call(s32[8]{0:T(128)} %bitcast.27, s32[1]{0:T(128)} %bitcast.1.h_ref, bf16[3,2048,64]{2,1,0:T(8,128)(2,1)} %get-tuple-element.150.q_ref, bf16[3,2048,64]{2,1,0:T(8,128)(2,1)} %get-tuple-element.114.k_ref, bf16[3,2048,64]{2,1,0:T(8,128)(2,1)} %get-tuple-element.151.v_ref, ...), custom_call_target="tpu_custom_call" | custom-call | flops 16106127360 | bytes 11796480 | tf_op jit(solution)/shard_map/attend_back/pallas_call | solution.py:280
  213.8 7.7 %tally.1 = (bf16[392,768]{1,0:T(8,128)(2,1)}, bf16[392,768]{1,0:T(8,128)(2,1)}) custom-call(s32[1]{0:T(128)} %bitcast.5.b_ref, bf16[2048,576]{1,0:T(8,128)(2,1)} %attend_back.1.gp_ref, bf16[2048,768]{1,0:T(8,128)(2,1)} %get-tuple-element.161.hat_ref, bf16[576,768]{1,0:T(8,128)(2,1)} %bitcast.17, f32[8,768]{1,0:T(8,128)} %stack.31.v_ref, ...), custom_call_target="tpu_custom_call" | custom-call | flops 576 | bytes 768 | tf_op jit(solution)/shard_map/tally/pallas_call | solution.py:559
  221.9 6.8 %spread.1 = (bf16[512,768]{1,0:T(8,128)(2,1)}, bf16[512,768]{1,0:T(8,128)(2,1)}, bf16[512,768]{1,0:T(8,128)(2,1)}, bf16[512,768]{1,0:T(8,128)(2,1)}) custom-call(bf16[2048,576]{1,0:T(8,128)(2,1)} %attend_back.1.gp_ref, bf16[576,768]{1,0:T(8,128)(2,1)} %bitcast.18), custom_call_target="tpu_custom_call" | custom-call | flops 576 | bytes 768 | tf_op jit(solution)/shard_map/spread/pallas_call | solution.py:590
  228.7 5.2 %collective-permute-done.34 = bf16[192,768]{1,0:T(8,128)(2,1)S(1)} collective-permute-done((bf16[192,768]{1,0:T(8,128)(2,1)S(1)}, bf16[192,768]{1,0:T(8,128)(2,1)S(1)}, u32[]{:S(2)}, u32[]{:S(2)}) %collective-permute-start.34) | collective-permute-done | bytes 294944 | tf_op jit(solution)/shard_map/ppermute | solution.py:38
  235.7 2.9 collective-permute-start.40
  241.2 10.1 %collective-permute-done.37.rest_2_ = bf16[384,768]{1,0:T(8,128)(2,1)S(1)} collective-permute-done((bf16[384,768]{1,0:T(8,128)(2,1)S(1)}, bf16[384,768]{1,0:T(8,128)(2,1)S(1)}, u32[]{:S(2)}, u32[]{:S(2)}) %collective-permute-start.37) | collective-permute-done | bytes 589856 | tf_op jit(solution)/shard_map/ppermute | solution.py:38
  255.4 2.7 collective-permute-start.41
  262.3 5.8 %collective-permute-done.42.rest_3_ = bf16[384,768]{1,0:T(8,128)(2,1)} collective-permute-done((bf16[384,768]{1,0:T(8,128)(2,1)S(1)}, bf16[384,768]{1,0:T(8,128)(2,1)}, u32[]{:S(2)}, u32[]{:S(2)}) %collective-permute-start.42) | collective-permute-done | bytes 589856 | tf_op jit(solution)/shard_map/ppermute | solution.py:38
  270.7 3.0 %add_convert_fusion.1 = bf16[512,768]{1,0:T(8,128)(2,1)} fusion(bf16[512,768]{1,0:T(8,128)(2,1)} %collective-permute-done.23, f32[512,768]{1,0:T(8,128)S(1)} %copy-done.2, bf16[512,768]{1,0:T(8,128)(2,1)} %collective-permute-done.16, bf16[512,768]{1,0:T(8,128)(2,1)} %get-tuple-element.123, f32[768]{0:T(1024)S(1)} %copy-done.26), kind=kLoop, calls=%fused_computation.14 | loop fusion | flops 3145728 | bytes 4721664 | tf_op jit(solution)/shard_map/convert_element_type | solution.py:816
  275.2 4.2 %unpack.2 = (f32[768,768]{1,0:T(8,128)}, f32[768,768]{1,0:T(8,128)}) custom-call(s32[1]{0:T(128)} %bitcast.5.b_ref, bf16[384,768]{1,0:T(8,128)(2,1)} %copy-done.5, bf16[384,768]{1,0:T(8,128)(2,1)} %copy-done.7, bf16[384,768]{1,0:T(8,128)(2,1)} %copy-done.24, bf16[384,768]{1,0:T(8,128)(2,1)} %collective-permute-done.42.rest_3_), custom_call_target="tpu_custom_call" | custom-call | flops 1536 | bytes 768 | tf_op jit(solution)/shard_map/unpack/pallas_call | solution.py:619
  282.1 2.8 fusion.8
  284.9 2.9 %unpack.3 = (f32[576,768]{1,0:T(8,128)}, f32[192,768]{1,0:T(8,128)}) custom-call(s32[1]{0:T(128)} %bitcast.5.b_ref, bf16[384,768]{1,0:T(8,128)(2,1)} %pad_maximum_fusion.1.rest_0_, bf16[384,768]{1,0:T(8,128)(2,1)} %collective-permute-done.49.rest_1_), custom_call_target="tpu_custom_call" | custom-call | flops 768 | bytes 768 | tf_op jit(solution)/shard_map/unpack/pallas_call | solution.py:619
  (204 shorter events, 61.5 us)
Async XLA Ops:
  1.2 20.9 %collective-permute-start = (bf16[512,768]{1,0:T(8,128)(2,1)}, bf16[512,768]{1,0:T(8,128)(2,1)S(1)}, u32[]{:S(2)}, u32[]{:S(2)}) collective-permute-start(bf16[512,768]{1,0:T(8,128)(2,1)} %x_ref.1), channel_id=1, source_target_pairs={{0,2},{1,3},{2,0},{3,1},{4,6},{5,7},{6,4},{7,5},{8,10},{9,11},{10,... | collective-permute-start | bytes 2359304 | tf_op jit(solution)/shard_map/ppermute | solution.py:38
  23.7 32.6 %collective-permute-start.3 = (bf16[512,768]{1,0:T(8,128)(2,1)S(1)}, bf16[512,768]{1,0:T(8,128)(2,1)}, u32[]{:S(2)}, u32[]{:S(2)}) collective-permute-start(bf16[512,768]{1,0:T(8,128)(2,1)S(1)} %broadcast_select_fusion.ga_ref.g0.cot_ref), channel_id=1, source_target_pairs={{0,2},{1,3},{2,0},{3,1},{4,6},{5,7},{6,4},{7,5},{8,10},{9,11},{10,... | collective-permute-start | bytes 2359304 | tf_op jit(solution)/shard_map/ppermute | solution.py:38
  54.2 16.0 %collective-permute-start.5 = (bf16[1024,192]{1,0:T(8,128)(2,1)}, bf16[1024,192]{1,0:T(8,128)(2,1)S(1)}, u32[]{:S(2)}, u32[]{:S(2)}) collective-permute-start(bf16[1024,192]{1,0:T(8,128)(2,1)} %get-tuple-element.116.rest_5_), channel_id=1, source_target_pairs={{0,2},{1,3},{2,0},{3,1},{4,6},{5,7},{6,4},{7,5},{8,10},{9,11},{10,... | collective-permute-start | bytes 1179656 | tf_op jit(solution)/shard_map/ppermute | solution.py:38
  54.2 20.5 %collective-permute-start.8 = (bf16[192,768]{1,0:T(8,128)(2,1)S(1)}, bf16[192,768]{1,0:T(8,128)(2,1)S(1)}, u32[]{:S(2)}, u32[]{:S(2)}) collective-permute-start(bf16[192,768]{1,0:T(8,128)(2,1)S(1)} %bitcast.21), channel_id=1, source_target_pairs={{0,2},{1,3},{2,0},{3,1},{4,6},{5,7},{6,4},{7,5},{8,10},{9,11},{10,... | collective-permute-start | bytes 884744 | tf_op jit(solution)/shard_map/ppermute | solution.py:38
  81.4 23.4 %collective-permute-start.12 = (bf16[512,768]{1,0:T(8,128)(2,1)}, bf16[512,768]{1,0:T(8,128)(2,1)S(1)}, u32[]{:S(2)}, u32[]{:S(2)}) collective-permute-start(bf16[512,768]{1,0:T(8,128)(2,1)} %get-tuple-element.122.ha_ref.h0), channel_id=1, source_target_pairs={{0,2},{1,3},{2,0},{3,1},{4,6},{5,7},{6,4},{7,5},{8,10},{9,11},{10,... | collective-permute-start | bytes 2359304 | tf_op jit(solution)/shard_map/ppermute | solution.py:38
  86.6 18.3 %collective-permute-start.14 = (bf16[512,768]{1,0:T(8,128)(2,1)}, bf16[512,768]{1,0:T(8,128)(2,1)S(1)}, u32[]{:S(2)}, u32[]{:S(2)}) collective-permute-start(bf16[512,768]{1,0:T(8,128)(2,1)} %collective-permute-done.3.ga_ref.g2), channel_id=1, source_target_pairs={{0,1},{1,0},{2,3},{3,2},{4,5},{5,4},{6,7},{7,6},{8,9},{9,8},{10,11... | collective-permute-start | bytes 2359304 | tf_op jit(solution)/shard_map/ppermute | solution.py:38
  121.9 14.9 %collective-permute-start.16 = (bf16[512,768]{1,0:T(8,128)(2,1)}, bf16[512,768]{1,0:T(8,128)(2,1)}, u32[]{:S(2)}, u32[]{:S(2)}) collective-permute-start(bf16[512,768]{1,0:T(8,128)(2,1)} %get-tuple-element.130), channel_id=1, source_target_pairs={{0,1},{1,0},{2,3},{3,2},{4,5},{5,4},{6,7},{7,6},{8,9},{9,8},{10,11... | collective-permute-start | bytes 2359304 | tf_op jit(solution)/shard_map/ppermute | solution.py:38
  122.1 14.7 %collective-permute-start.19 = (bf16[512,768]{1,0:T(8,128)(2,1)}, bf16[512,768]{1,0:T(8,128)(2,1)S(1)}, u32[]{:S(2)}, u32[]{:S(2)}) collective-permute-start(bf16[512,768]{1,0:T(8,128)(2,1)} %get-tuple-element.139), channel_id=1, source_target_pairs={{0,1},{1,0},{2,3},{3,2},{4,5},{5,4},{6,7},{7,6},{8,9},{9,8},{10,11... | collective-permute-start | bytes 2359304 | tf_op jit(solution)/shard_map/ppermute | solution.py:38
  122.5 19.7 %collective-permute-start.18 = (bf16[512,768]{1,0:T(8,128)(2,1)S(1)}, bf16[512,768]{1,0:T(8,128)(2,1)}, u32[]{:S(2)}, u32[]{:S(2)}) collective-permute-start(bf16[512,768]{1,0:T(8,128)(2,1)S(1)} %add_convert_fusion.4), channel_id=1, source_target_pairs={{0,2},{1,3},{2,0},{3,1},{4,6},{5,7},{6,4},{7,5},{8,10},{9,11},{10,... | collective-permute-start | bytes 2359304 | tf_op jit(solution)/shard_map/ppermute | solution.py:38
  124.2 18.0 %collective-permute-start.17 = (bf16[512,768]{1,0:T(8,128)(2,1)}, bf16[512,768]{1,0:T(8,128)(2,1)}, u32[]{:S(2)}, u32[]{:S(2)}) collective-permute-start(bf16[512,768]{1,0:T(8,128)(2,1)} %get-tuple-element.133), channel_id=1, source_target_pairs={{0,1},{1,0},{2,3},{3,2},{4,5},{5,4},{6,7},{7,6},{8,9},{9,8},{10,11... | collective-permute-start | bytes 2359304 | tf_op jit(solution)/shard_map/ppermute | solution.py:38
  136.8 28.6 %collective-permute-start.21 = (bf16[768,768]{1,0:T(8,128)(2,1)}, bf16[768,768]{1,0:T(8,128)(2,1)S(1)}, u32[]{:S(2)}, u32[]{:S(2)}) collective-permute-start(bf16[768,768]{1,0:T(8,128)(2,1)} %get-tuple-element.146), channel_id=1, source_target_pairs={{0,4},{4,0},{8,12},{12,8},{16,20},{20,16},{24,28},{28,24},{1,5},{5... | collective-permute-start | bytes 3538952 | tf_op jit(solution)/shard_map/ppermute | solution.py:38
  148.3 14.5 %collective-permute-start.22 = (bf16[512,192]{1,0:T(8,128)(2,1)}, bf16[512,192]{1,0:T(8,128)(2,1)S(1)}, u32[]{:S(2)}, u32[]{:S(2)}) collective-permute-start(bf16[512,192]{1,0:T(8,128)(2,1)} %get-tuple-element.147), channel_id=1, source_target_pairs={{0,2},{1,3},{2,0},{3,1},{4,6},{5,7},{6,4},{7,5},{8,10},{9,11},{10,... | collective-permute-start | bytes 589832 | tf_op jit(solution)/shard_map/ppermute | solution.py:38
  150.1 12.7 %collective-permute-start.25 = (bf16[512,192]{1,0:T(8,128)(2,1)}, bf16[512,192]{1,0:T(8,128)(2,1)S(1)}, u32[]{:S(2)}, u32[]{:S(2)}) collective-permute-start(bf16[512,192]{1,0:T(8,128)(2,1)} %get-tuple-element.153), channel_id=1, source_target_pairs={{0,2},{1,3},{2,0},{3,1},{4,6},{5,7},{6,4},{7,5},{8,10},{9,11},{10,... | collective-permute-start | bytes 589832 | tf_op jit(solution)/shard_map/ppermute | solution.py:38
  152.0 15.7 %collective-permute-start.24 = (bf16[192,768]{1,0:T(8,128)(2,1)S(1)}, bf16[192,768]{1,0:T(8,128)(2,1)S(1)}, u32[]{:S(2)}, u32[]{:S(2)}) collective-permute-start(bf16[192,768]{1,0:T(8,128)(2,1)S(1)} %convolution_convert_fusion.1), channel_id=1, source_target_pairs={{0,1},{1,0},{2,3},{3,2},{4,5},{5,4},{6,7},{7,6},{8,9},{9,8},{10,11... | collective-permute-start | bytes 884744 | tf_op jit(solution)/shard_map/ppermute | solution.py:38
  153.8 16.8 %collective-permute-start.30 = (bf16[192,768]{1,0:T(8,128)(2,1)S(1)}, bf16[192,768]{1,0:T(8,128)(2,1)S(1)}, u32[]{:S(2)}, u32[]{:S(2)}) collective-permute-start(bf16[192,768]{1,0:T(8,128)(2,1)S(1)} %convolution_convert_fusion), channel_id=1, source_target_pairs={{0,1},{1,0},{2,3},{3,2},{4,5},{5,4},{6,7},{7,6},{8,9},{9,8},{10,11... | collective-permute-start | bytes 884744 | tf_op jit(solution)/shard_map/ppermute | solution.py:38
  165.8 48.0 %collective-permute-start.23 = (bf16[512,768]{1,0:T(8,128)(2,1)}, bf16[512,768]{1,0:T(8,128)(2,1)}, u32[]{:S(2)}, u32[]{:S(2)}) collective-permute-start(bf16[512,768]{1,0:T(8,128)(2,1)} %add_convert_fusion.3), channel_id=1, source_target_pairs={{0,2},{1,3},{2,0},{3,1},{4,6},{5,7},{6,4},{7,5},{8,10},{9,11},{10,... | collective-permute-start | bytes 2359304 | tf_op jit(solution)/shard_map/ppermute | solution.py:38
  166.2 40.2 %collective-permute-start.27 = (bf16[192,768]{1,0:T(8,128)(2,1)S(1)}, bf16[192,768]{1,0:T(8,128)(2,1)S(1)}, u32[]{:S(2)}, u32[]{:S(2)}) collective-permute-start(bf16[192,768]{1,0:T(8,128)(2,1)S(1)} %get-tuple-element.208), channel_id=1, source_target_pairs={{0,8},{4,12},{8,0},{12,4},{16,24},{20,28},{24,16},{28,20},{1,9},{5... | collective-permute-start | bytes 884744 | tf_op jit(solution)/shard_map/ppermute | solution.py:38
  167.7 38.6 %collective-permute-start.29 = (bf16[192,768]{1,0:T(8,128)(2,1)S(1)}, bf16[192,768]{1,0:T(8,128)(2,1)}, u32[]{:S(2)}, u32[]{:S(2)}) collective-permute-start(bf16[192,768]{1,0:T(8,128)(2,1)S(1)} %get-tuple-element.209), channel_id=1, source_target_pairs={{0,24},{4,28},{8,16},{12,20},{16,8},{20,12},{24,0},{28,4},{1,25},{... | collective-permute-start | bytes 884744 | tf_op jit(solution)/shard_map/ppermute | solution.py:38
  170.6 35.8 %collective-permute-start.28 = (bf16[192,768]{1,0:T(8,128)(2,1)S(1)}, bf16[192,768]{1,0:T(8,128)(2,1)}, u32[]{:S(2)}, u32[]{:S(2)}) collective-permute-start(bf16[192,768]{1,0:T(8,128)(2,1)S(1)} %get-tuple-element.210), channel_id=1, source_target_pairs={{0,16},{4,20},{8,24},{12,28},{16,0},{20,4},{24,8},{28,12},{1,17},{... | collective-permute-start | bytes 884744 | tf_op jit(solution)/shard_map/ppermute | solution.py:38
  171.2 40.8 %collective-permute-start.31 = (bf16[192,768]{1,0:T(8,128)(2,1)S(1)}, bf16[192,768]{1,0:T(8,128)(2,1)}, u32[]{:S(2)}, u32[]{:S(2)}) collective-permute-start(bf16[192,768]{1,0:T(8,128)(2,1)S(1)} %fusion.10), channel_id=1, source_target_pairs={{0,2},{1,3},{2,0},{3,1},{4,6},{5,7},{6,4},{7,5},{8,10},{9,11},{10,... | collective-permute-start | bytes 884744 | tf_op jit(solution)/shard_map/ppermute | solution.py:38
  207.6 21.1 %collective-permute-start.35 = (bf16[192,768]{1,0:T(8,128)(2,1)S(1)}, bf16[192,768]{1,0:T(8,128)(2,1)S(1)}, u32[]{:S(2)}, u32[]{:S(2)}) collective-permute-start(bf16[192,768]{1,0:T(8,128)(2,1)S(1)} %add_convert_fusion.6), channel_id=1, source_target_pairs={{0,24},{4,28},{8,16},{12,20},{16,8},{20,12},{24,0},{28,4},{1,25},{... | collective-permute-start | bytes 884744 | tf_op jit(solution)/shard_map/ppermute | solution.py:38
  209.5 24.4 %collective-permute-start.34 = (bf16[192,768]{1,0:T(8,128)(2,1)S(1)}, bf16[192,768]{1,0:T(8,128)(2,1)S(1)}, u32[]{:S(2)}, u32[]{:S(2)}) collective-permute-start(bf16[192,768]{1,0:T(8,128)(2,1)S(1)} %add_convert_fusion.6), channel_id=1, source_target_pairs={{0,16},{4,20},{8,24},{12,28},{16,0},{20,4},{24,8},{28,12},{1,17},{... | collective-permute-start | bytes 884744 | tf_op jit(solution)/shard_map/ppermute | solution.py:38
  209.8 24.1 %collective-permute-start.33 = (bf16[192,768]{1,0:T(8,128)(2,1)S(1)}, bf16[192,768]{1,0:T(8,128)(2,1)S(1)}, u32[]{:S(2)}, u32[]{:S(2)}) collective-permute-start(bf16[192,768]{1,0:T(8,128)(2,1)S(1)} %add_convert_fusion.6), channel_id=1, source_target_pairs={{0,8},{4,12},{8,0},{12,4},{16,24},{20,28},{24,16},{28,20},{1,9},{5... | collective-permute-start | bytes 884744 | tf_op jit(solution)/shard_map/ppermute | solution.py:38
  221.6 13.4 %collective-permute-start.32 = (bf16[392,768]{1,0:T(8,128)(2,1)}, bf16[392,768]{1,0:T(8,128)(2,1)S(1)}, u32[]{:S(2)}, u32[]{:S(2)}) collective-permute-start(bf16[392,768]{1,0:T(8,128)(2,1)} %get-tuple-element.165), channel_id=1, source_target_pairs={{0,4},{4,0},{8,12},{12,8},{16,20},{20,16},{24,28},{28,24},{1,5},{5... | collective-permute-start | bytes 1806344 | tf_op jit(solution)/shard_map/ppermute | solution.py:38
  235.5 15.7 %collective-permute-start.37 = (bf16[384,768]{1,0:T(8,128)(2,1)S(1)}, bf16[384,768]{1,0:T(8,128)(2,1)S(1)}, u32[]{:S(2)}, u32[]{:S(2)}) collective-permute-start(bf16[384,768]{1,0:T(8,128)(2,1)S(1)} %pad_maximum_fusion.rest_0_), channel_id=1, source_target_pairs={{0,4},{4,0},{8,12},{12,8},{16,20},{20,16},{24,28},{28,24},{1,5},{5... | collective-permute-start | bytes 1769480 | tf_op jit(solution)/shard_map/ppermute | solution.py:38
  235.7 15.6 %collective-permute-start.40 = (bf16[104,768]{1,0:T(8,128)(2,1)S(1)}, bf16[104,768]{1,0:T(8,128)(2,1)S(1)}, u32[]{:S(2)}, u32[]{:S(2)}) collective-permute-start(bf16[104,768]{1,0:T(8,128)(2,1)S(1)} %concatenate.24), channel_id=1, source_target_pairs={{0,24},{4,28},{8,16},{12,20},{16,8},{20,12},{24,0},{28,4},{1,25},{... | collective-permute-start | bytes 479240 | tf_op jit(solution)/shard_map/ppermute | solution.py:38
  238.6 14.7 %collective-permute-start.39 = (bf16[104,768]{1,0:T(8,128)(2,1)S(1)}, bf16[104,768]{1,0:T(8,128)(2,1)S(1)}, u32[]{:S(2)}, u32[]{:S(2)}) collective-permute-start(bf16[104,768]{1,0:T(8,128)(2,1)S(1)} %get-tuple-element.213), channel_id=1, source_target_pairs={{0,16},{4,20},{8,24},{12,28},{16,0},{20,4},{24,8},{28,12},{1,17},{... | collective-permute-start | bytes 479240 | tf_op jit(solution)/shard_map/ppermute | solution.py:38
  238.9 14.4 %collective-permute-start.36 = (bf16[104,768]{1,0:T(8,128)(2,1)S(1)}, bf16[104,768]{1,0:T(8,128)(2,1)S(1)}, u32[]{:S(2)}, u32[]{:S(2)}) collective-permute-start(bf16[104,768]{1,0:T(8,128)(2,1)S(1)} %get-tuple-element.214), channel_id=1, source_target_pairs={{0,8},{4,12},{8,0},{12,4},{16,24},{20,28},{24,16},{28,20},{1,9},{5... | collective-permute-start | bytes 479240 | tf_op jit(solution)/shard_map/ppermute | solution.py:38
  253.4 14.7 %collective-permute-start.42 = (bf16[384,768]{1,0:T(8,128)(2,1)S(1)}, bf16[384,768]{1,0:T(8,128)(2,1)}, u32[]{:S(2)}, u32[]{:S(2)}) collective-permute-start(bf16[384,768]{1,0:T(8,128)(2,1)S(1)} %constant_dynamic-update-slice_fusion.rest_1_), channel_id=1, source_target_pairs={{0,4},{4,0},{8,12},{12,8},{16,20},{20,16},{24,28},{28,24},{1,5},{5... | collective-permute-start | bytes 1769480 | tf_op jit(solution)/shard_map/ppermute | solution.py:38
  255.4 12.7 %collective-permute-start.43 = (bf16[96,768]{1,0:T(8,128)(2,1)S(1)}, bf16[96,768]{1,0:T(8,128)(2,1)S(1)}, u32[]{:S(2)}, u32[]{:S(2)}) collective-permute-start(bf16[96,768]{1,0:T(8,128)(2,1)S(1)} %add_convert_fusion.7), channel_id=1, source_target_pairs={{0,16},{4,20},{8,24},{12,28},{16,0},{20,4},{24,8},{28,12},{1,17},{... | collective-permute-start | bytes 442376 | tf_op jit(solution)/shard_map/ppermute | solution.py:38
  258.9 21.2 %collective-permute-start.46 = (bf16[512,768]{1,0:T(8,128)(2,1)}, bf16[512,768]{1,0:T(8,128)(2,1)S(1)}, u32[]{:S(2)}, u32[]{:S(2)}) collective-permute-start(bf16[512,768]{1,0:T(8,128)(2,1)} %add_convert_fusion.2), channel_id=1, source_target_pairs={{0,2},{1,3},{2,0},{3,1},{4,6},{5,7},{6,4},{7,5},{8,10},{9,11},{10,... | collective-permute-start | bytes 2359304 | tf_op jit(solution)/shard_map/ppermute | solution.py:38
  269.9 15.1 %collective-permute-start.49 = (bf16[384,768]{1,0:T(8,128)(2,1)}, bf16[384,768]{1,0:T(8,128)(2,1)}, u32[]{:S(2)}, u32[]{:S(2)}) collective-permute-start(bf16[384,768]{1,0:T(8,128)(2,1)} %pad_maximum_fusion.1.rest_0_), channel_id=1, source_target_pairs={{0,4},{4,0},{8,12},{12,8},{16,20},{20,16},{24,28},{28,24},{1,5},{5... | collective-permute-start | bytes 1769480 | tf_op jit(solution)/shard_map/ppermute | solution.py:38
  (55 other events, 396.9 us)

commit v4 on v3

--- a/solution.py
+++ b/solution.py
@@ -123,9 +123,18 @@
     return jnp.where(i >= stop, i, start), i
 
 
-def attend_kernel(heads, first, per, scale, len_ref, h_ref, q_ref, k_ref, vt_ref, o_ref, l_ref, m_s, z_s, acc_s):
+def slot_at(slots, t, per):
+    at = jnp.int32(slots[0])
+    for k, slot in enumerate(slots[1:], 1):
+        at = jnp.where(t >= k * per, slot, at)
+    return at
+
+
+def attend_kernel(heads, slots, per, scale, len_ref, h_ref, q_ref, k_ref, vt_ref, *rest):
+    o_refs, l_refs = rest[: len(slots)], rest[len(slots) : -3]
+    m_s, z_s, acc_s = rest[-3:]
     t = pl.program_id(0)
-    row = ((h_ref[0] ^ (first + t // per)) * per + t % per) * BLK
+    row = ((h_ref[0] ^ slot_at(slots, t, per)) * per + t % per) * BLK
     start, i = lane_starts(len_ref, row, BLK)
     low, _ = row_segment(len_ref, row)
     m_s[...] = jnp.full_like(m_s, NEG)
@@ -152,37 +161,43 @@
         return carry
 
     lax.fori_loop(low // BLK, row // BLK + 1, body, 0)
-    outs = []
-    for h in range(heads):
-        z = z_s[h : h + 1, :]
-        outs.append((acc_s[h] / z).T)
-        l_ref[h : h + 1, :] = m_s[h : h + 1, :] + jnp.log(z)
-    o_ref[...] = jnp.concatenate(outs, axis=1).astype(BF)
-
-
-def attend_call(lengths, hid, q, k, vt, first, chunk):
+    for k, (o_ref, l_ref) in enumerate(zip(o_refs, l_refs, strict=True)):
+
+        @pl.when(t // per == k)
+        def _(o_ref=o_ref, l_ref=l_ref):
+            outs = []
+            for h in range(heads):
+                z = z_s[h : h + 1, :]
+                outs.append((acc_s[h] / z).T)
+                l_ref[h : h + 1, :] = m_s[h : h + 1, :] + jnp.log(z)
+            o_ref[...] = jnp.concatenate(outs, axis=1).astype(BF)
+
+
+def attend_call(lengths, hid, q, k, vt, slots, chunk):
     heads, rows, hd = q.shape
     per = chunk // BLK
-    steps = 2 * per
-    place = lambda t, n, h: (0, (h[0] ^ (first + t // per)) * per + t % per, 0)
+    count = len(slots)
+    place = lambda t, n, h: (0, (h[0] ^ slot_at(slots, t, per)) * per + t % per, 0)
     whole = lambda t, n, h: (0, 0, 0)
-    return pl.pallas_call(
-        functools.partial(attend_kernel, heads, first, per, 1.0 / math.sqrt(hd)),
-        out_shape=(
-            jax.ShapeDtypeStruct((steps * BLK, heads * hd), BF),
-            jax.ShapeDtypeStruct((8, steps * BLK), F32),
-        ),
+    out = pl.pallas_call(
+        functools.partial(attend_kernel, heads, slots, per, 1.0 / math.sqrt(hd)),
+        out_shape=(jax.ShapeDtypeStruct((chunk, heads * hd), BF),) * count
+        + (jax.ShapeDtypeStruct((8, chunk), F32),) * count,
         grid_spec=pltpu.PrefetchScalarGridSpec(
             num_scalar_prefetch=2,
-            grid=(steps,),
+            grid=(count * per,),
             in_specs=[
                 pl.BlockSpec((heads, BLK, hd), place),
                 pl.BlockSpec((heads, rows, hd), whole),
                 pl.BlockSpec((heads, hd, rows), whole),
             ],
             out_specs=[
-                pl.BlockSpec((BLK, heads * hd), lambda t, n, h: (t, 0)),
-                pl.BlockSpec((8, BLK), lambda t, n, h: (0, t)),
+                pl.BlockSpec((BLK, heads * hd), lambda t, n, h, k=k: (jnp.clip(t - k * per, 0, per - 1), 0))
+                for k in range(count)
+            ]
+            + [
+                pl.BlockSpec((8, BLK), lambda t, n, h, k=k: (0, jnp.clip(t - k * per, 0, per - 1)))
+                for k in range(count)
             ],
             scratch_shapes=[
                 pltpu.VMEM((8, BLK), F32),
@@ -190,29 +205,29 @@
                 pltpu.VMEM((heads, hd, BLK), F32),
             ],
         ),
-        cost_estimate=cost(heads * rows * rows * hd * 4, 12 * rows * heads * hd, heads * rows * rows // 4),
+        cost_estimate=cost(heads * rows * chunk * count * hd * 2, 6 * rows * heads * hd, heads * rows * chunk * count // 8),
         name="attend",
     )(lengths, hid, q, k, vt)
+    return out[:count], out[count:]
 
 
 def attend_back_kernel(chunk, scale, len_ref, h_ref, q_ref, k_ref, v_ref, *rest):
-    g_refs, o_refs, l_refs = rest[0:4], rest[4:6], rest[6:8]
-    gp_ref, q_s, g_s, kt_s, l_s, c_s, d_s, dq_s, dk_s, dv_s = rest[8:]
+    g_refs, o_refs, l_refs = rest[0:4], rest[4:8], rest[8:12]
+    gp_ref, q_s, g_s, kt_s, l_s, c_s, d_s, dq_s, dk_s, dv_s = rest[12:]
     heads, rows, hd = q_ref.shape
     blocks = rows // BLK
     per = chunk // BLK
     own = h_ref[0]
     for c in range(4):
         r0 = pl.multiple_of((own ^ c) * chunk, chunk)
-        part = slice((c % 2) * chunk, (c % 2 + 1) * chunk)
         g = g_refs[c][...]
-        o = o_refs[c // 2][part, :]
+        o = o_refs[c][...]
         for h in range(heads):
             gh = g[:, h * hd : (h + 1) * hd]
             g_s[h, pl.ds(r0, chunk), :] = gh
             both = gh.astype(F32) * o[:, h * hd : (h + 1) * hd].astype(F32)
             d_s[h : h + 1, pl.ds(r0, chunk)] = jnp.sum(both.T, axis=0, keepdims=True)
-        level = l_refs[c // 2][:, part]
+        level = l_refs[c][...]
         l_s[:, pl.ds(r0, chunk)] = level
         c_s[:, pl.ds(r0, chunk)] = jnp.exp(-level)
     for h in range(heads):
@@ -280,7 +295,7 @@
     return pl.pallas_call(
         functools.partial(attend_back_kernel, chunk, 1.0 / math.sqrt(hd)),
         out_shape=jax.ShapeDtypeStruct((rows, heads * 3 * hd), BF),
-        in_specs=[sm, sm] + [vm] * 11,
+        in_specs=[sm, sm] + [vm] * 15,
         out_specs=vm,
         scratch_shapes=[
             pltpu.VMEM((heads, rows, hd), BF),
@@ -453,13 +468,12 @@
     per = rows // BLK
     inner = parts[0].shape[1]
     low = pl.BlockSpec((BLK, inner), lambda t: (t, 0))
-    high = pl.BlockSpec((BLK, inner), lambda t: (t + per, 0))
     whole = lambda t: (0, 0)
     return pl.pallas_call(
         mix_kernel,
         out_shape=(jax.ShapeDtypeStruct((rows, width), F32), jax.ShapeDtypeStruct((rows, width), BF)),
         grid=(per,),
-        in_specs=[low, high, low, high]
+        in_specs=[low] * 4
         + [pl.BlockSpec(projs[0].shape, whole)] * 4
         + [pl.BlockSpec((BLK, width), lambda t: (t, 0)), pl.BlockSpec(vectors.shape, whole)],
         out_specs=[pl.BlockSpec((BLK, width), lambda t: (t, 0))] * 2,
@@ -708,13 +722,20 @@
     proj_far = swap(tie(proj, x_far), "head", 2)
     projs = (proj, swap(proj, "head", 1), proj_far, swap(proj_far, "head", 1))
 
-    merged_far, level_far = attend_call(lens, hid, queries, keys, values_t, 2, chunk)
-    from_far = swap(merged_far, "head", 2)
-    merged_near, level_near = attend_call(
-        lens, hid, tie(queries, merged_far, grad_far), keys, values_t, 0, chunk
+    (out_far, out_own), (level_far, level_own) = attend_call(
+        lens, hid, queries, keys, values_t, (2, 0), chunk
+    )
+    from_far = swap(out_far, "head", 2)
+    (out_last,), (level_last,) = attend_call(
+        lens, hid, tie(queries, out_own, grad_far), keys, values_t, (3,), chunk
+    )
+    from_last = swap(out_last, "head", 2)
+    (out_mate,), (level_mate,) = attend_call(
+        lens, hid, tie(queries, out_last, from_far), keys, values_t, (1,), chunk
     )
     grads = (grad_own, swap(grad_own, "head", 1), grad_far, swap(grad_far, "head", 1))
-    parts = (merged_near, swap(merged_near, "head", 1), from_far, swap(from_far, "head", 1))
+    from_last = swap(tie(from_last, out_mate), "head", 1)
+    parts = (out_own, swap(out_mate, "head", 1), from_far, from_last)
     resid, h_own = mix_call(parts, projs, inputs, vectors)
     h_far = swap(h_own, "head", 2)
     h_near = swap(h_own, "head", 1)
@@ -748,11 +769,7 @@
     got = swap(grad_cross, "head", 2)
     grad_mate = swap(grad_mate, "head", 1)
     grad_att = tie(grad_att, grad_mate)
-    low = slice(0, chunk)
-    high = slice(chunk, 2 * chunk)
-    grad_proj = [
-        dot_tn(p[at], grad_att) for p, at in zip(parts, (low, high, low, high), strict=True)
-    ]
+    grad_proj = [dot_tn(p, grad_att) for p in parts]
     near_sent, far_sent = grad_proj[1].astype(BF), grad_proj[3].astype(BF)
     down_far = tie(down_far, grad_att)
     down_sum = (down_far.astype(F32) + down_swapped.astype(F32)).astype(BF)
@@ -773,8 +790,8 @@
         keys,
         values,
         merged_grads,
-        (merged_near, merged_far),
-        (level_near, level_far),
+        (out_own, out_mate, out_far, out_last),
+        (level_own, level_mate, level_far, level_last),
         chunk,
     )
     got_feed = [tie(g, grad_packed) for g in got_feed]

time: 289 us -> 297 us (1.028)
  starting transfers between devices: 41.9 us -> 56.8 us
  waiting for transfers between devices: 63.8 us -> 53.9 us
  Pallas kernels: 146 us -> 140 us
  local copies, waits for them, and re-layouts: 12.4 us -> 17.4 us
  other arithmetic: 18.7 us -> 22 us
    ppermute x50 -> x51, starting transfers between devices: 41.9 us -> 56.8 us  [swap(): return lax.ppermute(x, axis, [(i, i ^ bits) for i in range(size)])]
    ppermute x50 -> x51, waiting for transfers between devices: 63.8 us -> 53.9 us  [swap(): return lax.ppermute(x, axis, [(i, i ^ bits) for i in range(size)])]
    pallas_call x1, Pallas kernels: 33.4 us -> 29.2 us  [attend_back_call(): pl.pallas_call(functools.partial(attend_back_kernel, chunk, 1.0 / math.sq...]
    unnamed x75 -> x81, local copies, waits for them, and re-layouts: 4.87 us -> 8.17 us
    pallas_call x2 -> x3, Pallas kernels: 35.5 us -> 33.6 us  [attend_call(): pl.pallas_call(functools.partial(attend_kernel, heads, slots, per, 1.0 /...]
  transfers between devices with their start and end apart: 50 -> 51, of which waited for: 15 -> 14; matrix products, arithmetic and copies ran while one was open for 10% -> 12% of each run, Pallas kernels for 46% -> 43%
where the time goes in v4:
time: 297 us; the launch traced here: 296 us
  Pallas kernels  140 us (47%)
  starting transfers between devices  56.8 us (19%)
  waiting for transfers between devices  53.9 us (18%)
  other arithmetic  22 us (7%)
  local copies, waits for them, and re-layouts  17.4 us (6%)
  matrix products  4.54 us (2%)
    ppermute x51, starting transfers between devices, swap(): return lax.ppermute(x, axis, [(i, i ^ bits) for i in range(size)])  56.8 us
    ppermute x51, waiting for transfers between devices, swap(): return lax.ppermute(x, axis, [(i, i ^ bits) for i in range(size)])  53.9 us
    pallas_call x3, Pallas kernels, attend_call(): pl.pallas_call(functools.partial(attend_kernel, heads, slots, per, 1.0 /...  33.6 us
    pallas_call x1, Pallas kernels, attend_back_call(): pl.pallas_call(functools.partial(attend_back_kernel, chunk, 1.0 / math.sq...  29.2 us
    pallas_call x2, Pallas kernels, feed_call(): pl.pallas_call(functools.partial(feed_kernel, steps), out_shape=(jax.Shap...  20 us
    pallas_call x2, Pallas kernels, qkv_call(): pl.pallas_call(functools.partial(qkv_kernel, heads, hd, steps), out_shape...  12.7 us
    pallas_call x1, Pallas kernels, weigh_call(): pl.pallas_call(functools.partial(weigh_kernel, tiles), out_shape=(half, h...  12.7 us
    unnamed x81, local copies, waits for them, and re-layouts  8.17 us
  transfers between devices with their start and end apart: 51, of which 14 were waited for; matrix products, arithmetic and copies ran while one was open for 12% of the time, Pallas kernels for 43%

profile of v4, /device:TPU:0, one launch (start us, length us, event | category | flops | bytes accessed | tf_op | source)
XLA Modules:
  0.0 296.3 jit_solution(15216374110702757448)
XLA Ops:
  1.2 2.6 collective-permute-start
  12.1 6.3 %qkv.2 = (bf16[3,2048,64]{2,1,0:T(8,128)(2,1)}, bf16[3,2048,64]{2,1,0:T(8,128)(2,1)}, bf16[3,2048,64]{2,1,0:T(8,128)(2,1)}, bf16[3,64,2048]{2,1,0:T(8,128)(2,1)}, bf16[2048,768]{1,0:T(8,128)(2,1)}) custom-call(s32[1]{0:T(128)} %bitcast.1.h_ref, bf16[512,768]{1,0:T(8,128)(2,1)} %x_ref.1, bf16[512,768]{1,0:T(8,128)(2,1)} %copy-done.36, f32[8,768]{1,0:T(8,128)} %stack.31.v_ref, ...), custom_call_target="tpu_custom_call" | custom-call | flops 905969664 | bytes 4718592 | tf_op jit(solution)/shard_map/qkv/pallas_call | solution.py:84
  18.4 3.7 %collective-permute-done.a_ref = bf16[512,768]{1,0:T(8,128)(2,1)S(1)} collective-permute-done((bf16[512,768]{1,0:T(8,128)(2,1)}, bf16[512,768]{1,0:T(8,128)(2,1)S(1)}, u32[]{:S(2)}, u32[]{:S(2)}) %collective-permute-start) | collective-permute-done | bytes 786464 | tf_op jit(solution)/shard_map/ppermute | solution.py:38
  26.7 6.3 %qkv.3 = (bf16[3,2048,64]{2,1,0:T(8,128)(2,1)}, bf16[3,2048,64]{2,1,0:T(8,128)(2,1)}, bf16[3,2048,64]{2,1,0:T(8,128)(2,1)}, bf16[3,64,2048]{2,1,0:T(8,128)(2,1)}, bf16[2048,768]{1,0:T(8,128)(2,1)}) custom-call(s32[1]{0:T(128)} %bitcast.1.h_ref, ...), custom_call_target="tpu_custom_call", output_to_operand_aliasing={{0}: (6, {}), {1}: (7, {}), {2}: (8, {}), {3}: (9, {}), {4}... | custom-call | flops 905969664 | bytes 4718592 | tf_op jit(solution)/shard_map/qkv/pallas_call | solution.py:84
  33.0 11.7 %attend.3 = (bf16[512,192]{1,0:T(8,128)(2,1)}, bf16[512,192]{1,0:T(8,128)(2,1)}, f32[8,512]{1,0:T(8,128)}, f32[8,512]{1,0:T(8,128)}) custom-call(s32[8]{0:T(128)} %bitcast.27, s32[1]{0:T(128)} %bitcast.1.h_ref, bf16[3,2048,64]{2,1,0:T(8,128)(2,1)} %get-tuple-element.160.q_ref, bf16[3,2048,64]{2,1,0:T(8,128)(2,1)} %get-tuple-element.120.k_ref, ...), custom_call_target="tpu_custom_call" | custom-call | flops 805306368 | bytes 2359296 | tf_op jit(solution)/shard_map/attend/pallas_call | solution.py:182
  46.5 9.7 %attend.4 = (bf16[512,192]{1,0:T(8,128)(2,1)}, f32[8,512]{1,0:T(8,128)}) custom-call(s32[8]{0:T(128)} %bitcast.28, s32[1]{0:T(128)} %bitcast.1.h_ref, bf16[3,2048,64]{2,1,0:T(8,128)(2,1)} %get-tuple-element.160.q_ref, bf16[3,2048,64]{2,1,0:T(8,128)(2,1)} %get-tuple-element.120.k_ref, bf16[3,64,2048]{2,1,0:T(8,128)(2,1)} %get-tuple-element.121.vt_ref), custom_call_target="tpu_custom_call" | custom-call | flops 402653184 | bytes 2359296 | tf_op jit(solution)/shard_map/attend/pallas_call | solution.py:182
  56.2 2.7 collective-permute-start.6
  60.7 12.2 %attend.5 = (bf16[512,192]{1,0:T(8,128)(2,1)}, f32[8,512]{1,0:T(8,128)}) custom-call(s32[8]{0:T(128)} %bitcast.29, s32[1]{0:T(128)} %bitcast.1.h_ref, bf16[3,2048,64]{2,1,0:T(8,128)(2,1)} %get-tuple-element.160.q_ref, bf16[3,2048,64]{2,1,0:T(8,128)(2,1)} %get-tuple-element.120.k_ref, bf16[3,64,2048]{2,1,0:T(8,128)(2,1)} %get-tuple-element.121.vt_ref), custom_call_target="tpu_custom_call" | custom-call | flops 402653184 | bytes 2359296 | tf_op jit(solution)/shard_map/attend/pallas_call | solution.py:182
  76.1 4.1 %mix.1 = (f32[512,768]{1,0:T(8,128)}, bf16[512,768]{1,0:T(8,128)(2,1)}) custom-call(bf16[512,192]{1,0:T(8,128)(2,1)} %get-tuple-element.122.m0.rest_4_, bf16[512,192]{1,0:T(8,128)(2,1)} %copy-done.15, bf16[512,192]{1,0:T(8,128)(2,1)} %copy-done.13, bf16[512,192]{1,0:T(8,128)(2,1)} %copy-done.17, bf16[192,768]{1,0:T(8,128)(2,1)} %bitcast.23, ...), custom_call_target="tpu_custom_call" | custom-call | flops 603979776 | bytes 4718592 | tf_op jit(solution)/shard_map/mix/pallas_call | solution.py:472
  83.7 10.0 %feed.2 = (bf16[2048,768]{1,0:T(8,128)(2,1)}, bf16[2048,768]{1,0:T(8,128)(2,1)}, bf16[512,768]{1,0:T(8,128)(2,1)}, bf16[512,768]{1,0:T(8,128)(2,1)}, bf16[512,768]{1,0:T(8,128)(2,1)}, /*index=5*/bf16[512,768]{1,0:T(8,128)(2,1)}) custom-call(bf16[512,768]{1,0:T(8,128)(2,1)} %get-tuple-element.132.ha_ref.h0, bf16[512,768]{1,0:T(8,128)(2,1)} %copy-done.31, ...), custom_call_target="tpu_custom_call" | custom-call | flops 4831838208 | bytes 6291456 | tf_op jit(solution)/shard_map/feed/pallas_call | solution.py:352
  93.7 6.7 %collective-permute-done.13.ha_ref.h2 = bf16[512,768]{1,0:T(8,128)(2,1)S(1)} collective-permute-done((bf16[512,768]{1,0:T(8,128)(2,1)}, bf16[512,768]{1,0:T(8,128)(2,1)S(1)}, u32[]{:S(2)}, u32[]{:S(2)}) %collective-permute-start.13) | collective-permute-done | bytes 786464 | tf_op jit(solution)/shard_map/ppermute | solution.py:38
  103.6 10.0 %feed.3 = (bf16[2048,768]{1,0:T(8,128)(2,1)}, bf16[2048,768]{1,0:T(8,128)(2,1)}, bf16[512,768]{1,0:T(8,128)(2,1)}, bf16[512,768]{1,0:T(8,128)(2,1)}, bf16[512,768]{1,0:T(8,128)(2,1)}, /*index=5*/bf16[512,768]{1,0:T(8,128)(2,1)}) custom-call(bf16[512,768]{1,0:T(8,128)(2,1)} %copy-done.32, ...), custom_call_target="tpu_custom_call", output_to_operand_aliasing={{0}: (7, {}), {1}: (8, {})} | custom-call | flops 4831838208 | bytes 6291456 | tf_op jit(solution)/shard_map/feed/pallas_call | solution.py:352
  118.3 12.7 %weigh.1 = (bf16[768,768]{1,0:T(8,128)(2,1)}, bf16[768,768]{1,0:T(8,128)(2,1)}, f32[1,768]{1,0:T(1,128)}) custom-call(s32[1]{0:T(128)} %bitcast.5.b_ref, bf16[512,768]{1,0:T(8,128)(2,1)} %get-tuple-element.132.ha_ref.h0, bf16[512,768]{1,0:T(8,128)(2,1)} %copy-done.31, bf16[512,768]{1,0:T(8,128)(2,1)} %copy-done.32, bf16[512,768]{1,0:T(8,128)(2,1)} %copy-done.34, ...), custom_call_target="tpu_custom_call" | custom-call | flops 4831838208 | bytes 18874368 | tf_op jit(solution)/shard_map/weigh/pallas_call | solution.py:433
  131.0 9.2 %collective-permute-start.22 = (bf16[768,768]{1,0:T(8,128)(2,1)}, bf16[768,768]{1,0:T(8,128)(2,1)S(1)}, u32[]{:S(2)}, u32[]{:S(2)}) collective-permute-start(bf16[768,768]{1,0:T(8,128)(2,1)} %get-tuple-element.156), channel_id=1, source_target_pairs={{0,4},{4,0},{8,12},{12,8},{16,20},{20,16},{24,28},{28,24},{1,5},{5... | collective-permute-start | bytes 3538952 | tf_op jit(solution)/shard_map/ppermute | solution.py:38
  140.2 6.1 %turn.1 = (f32[512,768]{1,0:T(8,128)}, bf16[512,768]{1,0:T(8,128)(2,1)}, bf16[512,192]{1,0:T(8,128)(2,1)}, bf16[512,192]{1,0:T(8,128)(2,1)}, bf16[512,192]{1,0:T...) custom-call(bf16[512,768]{1,0:T(8,128)(2,1)} %get-tuple-element.142.n_ref, ...), custom_call_target="tpu_custom_call" | custom-call | flops 512 | bytes 768 | tf_op jit(solution)/shard_map/turn/pallas_call | solution.py:512
  153.4 7.6 %collective-permute-done.26 = bf16[512,192]{1,0:T(8,128)(2,1)S(1)} collective-permute-done((bf16[512,192]{1,0:T(8,128)(2,1)}, bf16[512,192]{1,0:T(8,128)(2,1)S(1)}, u32[]{:S(2)}, u32[]{:S(2)}) %collective-permute-start.26) | collective-permute-done | bytes 196640 | tf_op jit(solution)/shard_map/ppermute | solution.py:38
  161.0 5.8 %collective-permute-done.22 = bf16[768,768]{1,0:T(8,128)(2,1)S(1)} collective-permute-done((bf16[768,768]{1,0:T(8,128)(2,1)}, bf16[768,768]{1,0:T(8,128)(2,1)S(1)}, u32[]{:S(2)}, u32[]{:S(2)}) %collective-permute-start.22) | collective-permute-done | bytes 1179680 | tf_op jit(solution)/shard_map/ppermute | solution.py:38
  170.1 3.6 %collective-permute-start.30 = (bf16[192,768]{1,0:T(8,128)(2,1)S(1)}, bf16[192,768]{1,0:T(8,128)(2,1)}, u32[]{:S(2)}, u32[]{:S(2)}) collective-permute-start(bf16[192,768]{1,0:T(8,128)(2,1)S(1)} %get-tuple-element.221), channel_id=1, source_target_pairs={{0,24},{4,28},{8,16},{12,20},{16,8},{20,12},{24,0},{28,4},{1,25},{... | collective-permute-start | bytes 884744 | tf_op jit(solution)/shard_map/ppermute | solution.py:38
  177.7 29.2 %attend_back.1.gp_ref = bf16[2048,576]{1,0:T(8,128)(2,1)} custom-call(s32[8]{0:T(128)} %bitcast.30, s32[1]{0:T(128)} %bitcast.1.h_ref, bf16[3,2048,64]{2,1,0:T(8,128)(2,1)} %get-tuple-element.160.q_ref, bf16[3,2048,64]{2,1,0:T(8,128)(2,1)} %get-tuple-element.120.k_ref, bf16[3,2048,64]{2,1,0:T(8,128)(2,1)} %get-tuple-element.161.v_ref, ...), custom_call_target="tpu_custom_call" | custom-call | flops 16106127360 | bytes 11796480 | tf_op jit(solution)/shard_map/attend_back/pallas_call | solution.py:295
  208.2 3.6 %collective-permute-start.36 = (bf16[192,768]{1,0:T(8,128)(2,1)S(1)}, bf16[192,768]{1,0:T(8,128)(2,1)S(1)}, u32[]{:S(2)}, u32[]{:S(2)}) collective-permute-start(bf16[192,768]{1,0:T(8,128)(2,1)S(1)} %add_convert_fusion.6), channel_id=1, source_target_pairs={{0,24},{4,28},{8,16},{12,20},{16,8},{20,12},{24,0},{28,4},{1,25},{... | collective-permute-start | bytes 884744 | tf_op jit(solution)/shard_map/ppermute | solution.py:38
  211.8 3.6 %collective-permute-start.35 = (bf16[192,768]{1,0:T(8,128)(2,1)S(1)}, bf16[192,768]{1,0:T(8,128)(2,1)S(1)}, u32[]{:S(2)}, u32[]{:S(2)}) collective-permute-start(bf16[192,768]{1,0:T(8,128)(2,1)S(1)} %add_convert_fusion.6), channel_id=1, source_target_pairs={{0,16},{4,20},{8,24},{12,28},{16,0},{20,4},{24,8},{28,12},{1,17},{... | collective-permute-start | bytes 884744 | tf_op jit(solution)/shard_map/ppermute | solution.py:38
  217.7 8.0 %tally.1 = (bf16[392,768]{1,0:T(8,128)(2,1)}, bf16[392,768]{1,0:T(8,128)(2,1)}) custom-call(s32[1]{0:T(128)} %bitcast.5.b_ref, bf16[2048,576]{1,0:T(8,128)(2,1)} %attend_back.1.gp_ref, bf16[2048,768]{1,0:T(8,128)(2,1)} %get-tuple-element.173.hat_ref, bf16[576,768]{1,0:T(8,128)(2,1)} %bitcast.21, f32[8,768]{1,0:T(8,128)} %stack.31.v_ref, ...), custom_call_target="tpu_custom_call" | custom-call | flops 576 | bytes 768 | tf_op jit(solution)/shard_map/tally/pallas_call | solution.py:573
  226.0 6.8 %spread.1 = (bf16[512,768]{1,0:T(8,128)(2,1)}, bf16[512,768]{1,0:T(8,128)(2,1)}, bf16[512,768]{1,0:T(8,128)(2,1)}, bf16[512,768]{1,0:T(8,128)(2,1)}) custom-call(bf16[2048,576]{1,0:T(8,128)(2,1)} %attend_back.1.gp_ref, bf16[576,768]{1,0:T(8,128)(2,1)} %bitcast.22), custom_call_target="tpu_custom_call" | custom-call | flops 576 | bytes 768 | tf_op jit(solution)/shard_map/spread/pallas_call | solution.py:604
  232.8 3.4 %collective-permute-done.35 = bf16[192,768]{1,0:T(8,128)(2,1)S(1)} collective-permute-done((bf16[192,768]{1,0:T(8,128)(2,1)S(1)}, bf16[192,768]{1,0:T(8,128)(2,1)S(1)}, u32[]{:S(2)}, u32[]{:S(2)}) %collective-permute-start.35) | collective-permute-done | bytes 294944 | tf_op jit(solution)/shard_map/ppermute | solution.py:38
  241.5 3.7 %collective-permute-start.38 = (bf16[384,768]{1,0:T(8,128)(2,1)S(1)}, bf16[384,768]{1,0:T(8,128)(2,1)S(1)}, u32[]{:S(2)}, u32[]{:S(2)}) collective-permute-start(bf16[384,768]{1,0:T(8,128)(2,1)S(1)} %pad_maximum_fusion.rest_0_), channel_id=1, source_target_pairs={{0,4},{4,0},{8,12},{12,8},{16,20},{20,16},{24,28},{28,24},{1,5},{5... | collective-permute-start | bytes 1769480 | tf_op jit(solution)/shard_map/ppermute | solution.py:38
  245.3 2.5 collective-permute-start.41
  250.8 8.5 %collective-permute-done.38.rest_2_ = bf16[384,768]{1,0:T(8,128)(2,1)S(1)} collective-permute-done((bf16[384,768]{1,0:T(8,128)(2,1)S(1)}, bf16[384,768]{1,0:T(8,128)(2,1)S(1)}, u32[]{:S(2)}, u32[]{:S(2)}) %collective-permute-start.38) | collective-permute-done | bytes 589856 | tf_op jit(solution)/shard_map/ppermute | solution.py:38
  269.9 6.0 %collective-permute-done.43.rest_3_ = bf16[384,768]{1,0:T(8,128)(2,1)} collective-permute-done((bf16[384,768]{1,0:T(8,128)(2,1)S(1)}, bf16[384,768]{1,0:T(8,128)(2,1)}, u32[]{:S(2)}, u32[]{:S(2)}) %collective-permute-start.43) | collective-permute-done | bytes 589856 | tf_op jit(solution)/shard_map/ppermute | solution.py:38
  279.5 3.0 add_convert_fusion.1
  283.6 4.2 %unpack.2 = (f32[768,768]{1,0:T(8,128)}, f32[768,768]{1,0:T(8,128)}) custom-call(s32[1]{0:T(128)} %bitcast.5.b_ref, bf16[384,768]{1,0:T(8,128)(2,1)} %copy-done.5, bf16[384,768]{1,0:T(8,128)(2,1)} %copy-done.7, bf16[384,768]{1,0:T(8,128)(2,1)} %copy-done.26, bf16[384,768]{1,0:T(8,128)(2,1)} %collective-permute-done.43.rest_3_), custom_call_target="tpu_custom_call" | custom-call | flops 1536 | bytes 768 | tf_op jit(solution)/shard_map/unpack/pallas_call | solution.py:633
  290.6 2.8 fusion.8
  293.4 2.9 unpack.3
  (213 shorter events, 75.7 us)
Async XLA Ops:
  1.2 20.9 %collective-permute-start = (bf16[512,768]{1,0:T(8,128)(2,1)}, bf16[512,768]{1,0:T(8,128)(2,1)S(1)}, u32[]{:S(2)}, u32[]{:S(2)}) collective-permute-start(bf16[512,768]{1,0:T(8,128)(2,1)} %x_ref.1), channel_id=1, source_target_pairs={{0,2},{1,3},{2,0},{3,1},{4,6},{5,7},{6,4},{7,5},{8,10},{9,11},{10,... | collective-permute-start | bytes 2359304 | tf_op jit(solution)/shard_map/ppermute | solution.py:38
  23.7 22.8 %collective-permute-start.3 = (bf16[512,768]{1,0:T(8,128)(2,1)S(1)}, bf16[512,768]{1,0:T(8,128)(2,1)}, u32[]{:S(2)}, u32[]{:S(2)}) collective-permute-start(bf16[512,768]{1,0:T(8,128)(2,1)S(1)} %broadcast_select_fusion.ga_ref.g0.cot_ref), channel_id=1, source_target_pairs={{0,2},{1,3},{2,0},{3,1},{4,6},{5,7},{6,4},{7,5},{8,10},{9,11},{10,... | collective-permute-start | bytes 2359304 | tf_op jit(solution)/shard_map/ppermute | solution.py:38
  25.5 35.1 %collective-permute-start.9 = (bf16[192,768]{1,0:T(8,128)(2,1)S(1)}, bf16[192,768]{1,0:T(8,128)(2,1)S(1)}, u32[]{:S(2)}, u32[]{:S(2)}) collective-permute-start(bf16[192,768]{1,0:T(8,128)(2,1)S(1)} %bitcast.25), channel_id=1, source_target_pairs={{0,2},{1,3},{2,0},{3,1},{4,6},{5,7},{6,4},{7,5},{8,10},{9,11},{10,... | collective-permute-start | bytes 884744 | tf_op jit(solution)/shard_map/ppermute | solution.py:38
  44.7 16.0 %collective-permute-start.4 = (bf16[512,192]{1,0:T(8,128)(2,1)}, bf16[512,192]{1,0:T(8,128)(2,1)S(1)}, u32[]{:S(2)}, u32[]{:S(2)}) collective-permute-start(bf16[512,192]{1,0:T(8,128)(2,1)} %get-tuple-element.126.rest_6_), channel_id=1, source_target_pairs={{0,2},{1,3},{2,0},{3,1},{4,6},{5,7},{6,4},{7,5},{8,10},{9,11},{10,... | collective-permute-start | bytes 589832 | tf_op jit(solution)/shard_map/ppermute | solution.py:38
  56.2 16.8 %collective-permute-start.6 = (bf16[512,192]{1,0:T(8,128)(2,1)}, bf16[512,192]{1,0:T(8,128)(2,1)S(1)}, u32[]{:S(2)}, u32[]{:S(2)}) collective-permute-start(bf16[512,192]{1,0:T(8,128)(2,1)} %get-tuple-element.125.rest_7_), channel_id=1, source_target_pairs={{0,2},{1,3},{2,0},{3,1},{4,6},{5,7},{6,4},{7,5},{8,10},{9,11},{10,... | collective-permute-start | bytes 589832 | tf_op jit(solution)/shard_map/ppermute | solution.py:38
  59.0 14.6 %collective-permute-start.8 = (bf16[192,768]{1,0:T(8,128)(2,1)S(1)}, bf16[192,768]{1,0:T(8,128)(2,1)S(1)}, u32[]{:S(2)}, u32[]{:S(2)}) collective-permute-start(bf16[192,768]{1,0:T(8,128)(2,1)S(1)} %bitcast.26), channel_id=1, source_target_pairs={{0,1},{1,0},{2,3},{3,2},{4,5},{5,4},{6,7},{7,6},{8,9},{9,8},{10,11... | collective-permute-start | bytes 884744 | tf_op jit(solution)/shard_map/ppermute | solution.py:38
  80.4 20.0 %collective-permute-start.13 = (bf16[512,768]{1,0:T(8,128)(2,1)}, bf16[512,768]{1,0:T(8,128)(2,1)S(1)}, u32[]{:S(2)}, u32[]{:S(2)}) collective-permute-start(bf16[512,768]{1,0:T(8,128)(2,1)} %get-tuple-element.132.ha_ref.h0), channel_id=1, source_target_pairs={{0,2},{1,3},{2,0},{3,1},{4,6},{5,7},{6,4},{7,5},{8,10},{9,11},{10,... | collective-permute-start | bytes 2359304 | tf_op jit(solution)/shard_map/ppermute | solution.py:38
  80.4 20.0 %collective-permute-start.15 = (bf16[512,768]{1,0:T(8,128)(2,1)}, bf16[512,768]{1,0:T(8,128)(2,1)S(1)}, u32[]{:S(2)}, u32[]{:S(2)}) collective-permute-start(bf16[512,768]{1,0:T(8,128)(2,1)} %collective-permute-done.3.ga_ref.g2), channel_id=1, source_target_pairs={{0,1},{1,0},{2,3},{3,2},{4,5},{5,4},{6,7},{7,6},{8,9},{9,8},{10,11... | collective-permute-start | bytes 2359304 | tf_op jit(solution)/shard_map/ppermute | solution.py:38
  117.5 22.7 %collective-permute-start.17 = (bf16[512,768]{1,0:T(8,128)(2,1)}, bf16[512,768]{1,0:T(8,128)(2,1)}, u32[]{:S(2)}, u32[]{:S(2)}) collective-permute-start(bf16[512,768]{1,0:T(8,128)(2,1)} %get-tuple-element.140), channel_id=1, source_target_pairs={{0,1},{1,0},{2,3},{3,2},{4,5},{5,4},{6,7},{7,6},{8,9},{9,8},{10,11... | collective-permute-start | bytes 2359304 | tf_op jit(solution)/shard_map/ppermute | solution.py:38
  117.7 22.5 %collective-permute-start.20 = (bf16[512,768]{1,0:T(8,128)(2,1)}, bf16[512,768]{1,0:T(8,128)(2,1)S(1)}, u32[]{:S(2)}, u32[]{:S(2)}) collective-permute-start(bf16[512,768]{1,0:T(8,128)(2,1)} %get-tuple-element.149), channel_id=1, source_target_pairs={{0,1},{1,0},{2,3},{3,2},{4,5},{5,4},{6,7},{7,6},{8,9},{9,8},{10,11... | collective-permute-start | bytes 2359304 | tf_op jit(solution)/shard_map/ppermute | solution.py:38
  118.0 22.2 %collective-permute-start.19 = (bf16[512,768]{1,0:T(8,128)(2,1)S(1)}, bf16[512,768]{1,0:T(8,128)(2,1)}, u32[]{:S(2)}, u32[]{:S(2)}) collective-permute-start(bf16[512,768]{1,0:T(8,128)(2,1)S(1)} %add_convert_fusion.4), channel_id=1, source_target_pairs={{0,2},{1,3},{2,0},{3,1},{4,6},{5,7},{6,4},{7,5},{8,10},{9,11},{10,... | collective-permute-start | bytes 2359304 | tf_op jit(solution)/shard_map/ppermute | solution.py:38
  118.3 21.9 %collective-permute-start.18 = (bf16[512,768]{1,0:T(8,128)(2,1)}, bf16[512,768]{1,0:T(8,128)(2,1)}, u32[]{:S(2)}, u32[]{:S(2)}) collective-permute-start(bf16[512,768]{1,0:T(8,128)(2,1)} %get-tuple-element.143), channel_id=1, source_target_pairs={{0,1},{1,0},{2,3},{3,2},{4,5},{5,4},{6,7},{7,6},{8,9},{9,8},{10,11... | collective-permute-start | bytes 2359304 | tf_op jit(solution)/shard_map/ppermute | solution.py:38
  131.0 35.8 %collective-permute-start.22 = (bf16[768,768]{1,0:T(8,128)(2,1)}, bf16[768,768]{1,0:T(8,128)(2,1)S(1)}, u32[]{:S(2)}, u32[]{:S(2)}) collective-permute-start(bf16[768,768]{1,0:T(8,128)(2,1)} %get-tuple-element.156), channel_id=1, source_target_pairs={{0,4},{4,0},{8,12},{12,8},{16,20},{20,16},{24,28},{28,24},{1,5},{5... | collective-permute-start | bytes 3538952 | tf_op jit(solution)/shard_map/ppermute | solution.py:38
  146.5 14.5 %collective-permute-start.23 = (bf16[512,192]{1,0:T(8,128)(2,1)}, bf16[512,192]{1,0:T(8,128)(2,1)S(1)}, u32[]{:S(2)}, u32[]{:S(2)}) collective-permute-start(bf16[512,192]{1,0:T(8,128)(2,1)} %get-tuple-element.157), channel_id=1, source_target_pairs={{0,2},{1,3},{2,0},{3,1},{4,6},{5,7},{6,4},{7,5},{8,10},{9,11},{10,... | collective-permute-start | bytes 589832 | tf_op jit(solution)/shard_map/ppermute | solution.py:38
  146.8 14.2 %collective-permute-start.26 = (bf16[512,192]{1,0:T(8,128)(2,1)}, bf16[512,192]{1,0:T(8,128)(2,1)S(1)}, u32[]{:S(2)}, u32[]{:S(2)}) collective-permute-start(bf16[512,192]{1,0:T(8,128)(2,1)} %get-tuple-element.163), channel_id=1, source_target_pairs={{0,2},{1,3},{2,0},{3,1},{4,6},{5,7},{6,4},{7,5},{8,10},{9,11},{10,... | collective-permute-start | bytes 589832 | tf_op jit(solution)/shard_map/ppermute | solution.py:38
  150.2 19.9 %collective-permute-start.25 = (bf16[192,768]{1,0:T(8,128)(2,1)S(1)}, bf16[192,768]{1,0:T(8,128)(2,1)S(1)}, u32[]{:S(2)}, u32[]{:S(2)}) collective-permute-start(bf16[192,768]{1,0:T(8,128)(2,1)S(1)} %convolution_convert_fusion.1), channel_id=1, source_target_pairs={{0,1},{1,0},{2,3},{3,2},{4,5},{5,4},{6,7},{7,6},{8,9},{9,8},{10,11... | collective-permute-start | bytes 884744 | tf_op jit(solution)/shard_map/ppermute | solution.py:38
  151.8 22.3 %collective-permute-start.31 = (bf16[192,768]{1,0:T(8,128)(2,1)S(1)}, bf16[192,768]{1,0:T(8,128)(2,1)S(1)}, u32[]{:S(2)}, u32[]{:S(2)}) collective-permute-start(bf16[192,768]{1,0:T(8,128)(2,1)S(1)} %convolution_convert_fusion), channel_id=1, source_target_pairs={{0,1},{1,0},{2,3},{3,2},{4,5},{5,4},{6,7},{7,6},{8,9},{9,8},{10,11... | collective-permute-start | bytes 884744 | tf_op jit(solution)/shard_map/ppermute | solution.py:38
  161.0 14.2 %collective-permute-start.27 = (bf16[512,192]{1,0:T(8,128)(2,1)S(1)}, bf16[512,192]{1,0:T(8,128)(2,1)S(1)}, u32[]{:S(2)}, u32[]{:S(2)}) collective-permute-start(bf16[512,192]{1,0:T(8,128)(2,1)S(1)} %collective-permute-done.26), channel_id=1, source_target_pairs={{0,1},{1,0},{2,3},{3,2},{4,5},{5,4},{6,7},{7,6},{8,9},{9,8},{10,11... | collective-permute-start | bytes 589832 | tf_op jit(solution)/shard_map/ppermute | solution.py:38
  168.0 49.7 %collective-permute-start.24 = (bf16[512,768]{1,0:T(8,128)(2,1)}, bf16[512,768]{1,0:T(8,128)(2,1)S(1)}, u32[]{:S(2)}, u32[]{:S(2)}) collective-permute-start(bf16[512,768]{1,0:T(8,128)(2,1)} %add_convert_fusion.3), channel_id=1, source_target_pairs={{0,2},{1,3},{2,0},{3,1},{4,6},{5,7},{6,4},{7,5},{8,10},{9,11},{10,... | collective-permute-start | bytes 2359304 | tf_op jit(solution)/shard_map/ppermute | solution.py:38
  168.3 38.6 %collective-permute-start.28 = (bf16[192,768]{1,0:T(8,128)(2,1)}, bf16[192,768]{1,0:T(8,128)(2,1)}, u32[]{:S(2)}, u32[]{:S(2)}) collective-permute-start(bf16[192,768]{1,0:T(8,128)(2,1)} %get-tuple-element.220), channel_id=1, source_target_pairs={{0,8},{4,12},{8,0},{12,4},{16,24},{20,28},{24,16},{28,20},{1,9},{5... | collective-permute-start | bytes 884744 | tf_op jit(solution)/shard_map/ppermute | solution.py:38
  170.1 36.8 %collective-permute-start.30 = (bf16[192,768]{1,0:T(8,128)(2,1)S(1)}, bf16[192,768]{1,0:T(8,128)(2,1)}, u32[]{:S(2)}, u32[]{:S(2)}) collective-permute-start(bf16[192,768]{1,0:T(8,128)(2,1)S(1)} %get-tuple-element.221), channel_id=1, source_target_pairs={{0,24},{4,28},{8,16},{12,20},{16,8},{20,12},{24,0},{28,4},{1,25},{... | collective-permute-start | bytes 884744 | tf_op jit(solution)/shard_map/ppermute | solution.py:38
  174.1 32.8 %collective-permute-start.29 = (bf16[192,768]{1,0:T(8,128)(2,1)S(1)}, bf16[192,768]{1,0:T(8,128)(2,1)}, u32[]{:S(2)}, u32[]{:S(2)}) collective-permute-start(bf16[192,768]{1,0:T(8,128)(2,1)S(1)} %get-tuple-element.222), channel_id=1, source_target_pairs={{0,16},{4,20},{8,24},{12,28},{16,0},{20,4},{24,8},{28,12},{1,17},{... | collective-permute-start | bytes 884744 | tf_op jit(solution)/shard_map/ppermute | solution.py:38
  176.0 40.0 %collective-permute-start.32 = (bf16[192,768]{1,0:T(8,128)(2,1)}, bf16[192,768]{1,0:T(8,128)(2,1)}, u32[]{:S(2)}, u32[]{:S(2)}) collective-permute-start(bf16[192,768]{1,0:T(8,128)(2,1)} %fusion.10), channel_id=1, source_target_pairs={{0,2},{1,3},{2,0},{3,1},{4,6},{5,7},{6,4},{7,5},{8,10},{9,11},{10,... | collective-permute-start | bytes 884744 | tf_op jit(solution)/shard_map/ppermute | solution.py:38
  208.2 24.6 %collective-permute-start.36 = (bf16[192,768]{1,0:T(8,128)(2,1)S(1)}, bf16[192,768]{1,0:T(8,128)(2,1)S(1)}, u32[]{:S(2)}, u32[]{:S(2)}) collective-permute-start(bf16[192,768]{1,0:T(8,128)(2,1)S(1)} %add_convert_fusion.6), channel_id=1, source_target_pairs={{0,24},{4,28},{8,16},{12,20},{16,8},{20,12},{24,0},{28,4},{1,25},{... | collective-permute-start | bytes 884744 | tf_op jit(solution)/shard_map/ppermute | solution.py:38
  211.8 24.5 %collective-permute-start.35 = (bf16[192,768]{1,0:T(8,128)(2,1)S(1)}, bf16[192,768]{1,0:T(8,128)(2,1)S(1)}, u32[]{:S(2)}, u32[]{:S(2)}) collective-permute-start(bf16[192,768]{1,0:T(8,128)(2,1)S(1)} %add_convert_fusion.6), channel_id=1, source_target_pairs={{0,16},{4,20},{8,24},{12,28},{16,0},{20,4},{24,8},{28,12},{1,17},{... | collective-permute-start | bytes 884744 | tf_op jit(solution)/shard_map/ppermute | solution.py:38
  215.4 20.8 %collective-permute-start.34 = (bf16[192,768]{1,0:T(8,128)(2,1)S(1)}, bf16[192,768]{1,0:T(8,128)(2,1)}, u32[]{:S(2)}, u32[]{:S(2)}) collective-permute-start(bf16[192,768]{1,0:T(8,128)(2,1)S(1)} %add_convert_fusion.6), channel_id=1, source_target_pairs={{0,8},{4,12},{8,0},{12,4},{16,24},{20,28},{24,16},{28,20},{1,9},{5... | collective-permute-start | bytes 884744 | tf_op jit(solution)/shard_map/ppermute | solution.py:38
  225.8 14.4 %collective-permute-start.33 = (bf16[392,768]{1,0:T(8,128)(2,1)}, bf16[392,768]{1,0:T(8,128)(2,1)S(1)}, u32[]{:S(2)}, u32[]{:S(2)}) collective-permute-start(bf16[392,768]{1,0:T(8,128)(2,1)} %get-tuple-element.177), channel_id=1, source_target_pairs={{0,4},{4,0},{8,12},{12,8},{16,20},{20,16},{24,28},{28,24},{1,5},{5... | collective-permute-start | bytes 1806344 | tf_op jit(solution)/shard_map/ppermute | solution.py:38
  241.5 17.7 %collective-permute-start.38 = (bf16[384,768]{1,0:T(8,128)(2,1)S(1)}, bf16[384,768]{1,0:T(8,128)(2,1)S(1)}, u32[]{:S(2)}, u32[]{:S(2)}) collective-permute-start(bf16[384,768]{1,0:T(8,128)(2,1)S(1)} %pad_maximum_fusion.rest_0_), channel_id=1, source_target_pairs={{0,4},{4,0},{8,12},{12,8},{16,20},{20,16},{24,28},{28,24},{1,5},{5... | collective-permute-start | bytes 1769480 | tf_op jit(solution)/shard_map/ppermute | solution.py:38
  245.3 14.0 %collective-permute-start.41 = (bf16[104,768]{1,0:T(8,128)(2,1)S(1)}, bf16[104,768]{1,0:T(8,128)(2,1)S(1)}, u32[]{:S(2)}, u32[]{:S(2)}) collective-permute-start(bf16[104,768]{1,0:T(8,128)(2,1)S(1)} %concatenate.24), channel_id=1, source_target_pairs={{0,24},{4,28},{8,16},{12,20},{16,8},{20,12},{24,0},{28,4},{1,25},{... | collective-permute-start | bytes 479240 | tf_op jit(solution)/shard_map/ppermute | solution.py:38
  261.0 14.9 %collective-permute-start.43 = (bf16[384,768]{1,0:T(8,128)(2,1)S(1)}, bf16[384,768]{1,0:T(8,128)(2,1)}, u32[]{:S(2)}, u32[]{:S(2)}) collective-permute-start(bf16[384,768]{1,0:T(8,128)(2,1)S(1)} %constant_dynamic-update-slice_fusion.rest_1_), channel_id=1, source_target_pairs={{0,4},{4,0},{8,12},{12,8},{16,20},{20,16},{24,28},{28,24},{1,5},{5... | collective-permute-start | bytes 1769480 | tf_op jit(solution)/shard_map/ppermute | solution.py:38
  266.4 22.1 %collective-permute-start.47 = (bf16[512,768]{1,0:T(8,128)(2,1)}, bf16[512,768]{1,0:T(8,128)(2,1)S(1)}, u32[]{:S(2)}, u32[]{:S(2)}) collective-permute-start(bf16[512,768]{1,0:T(8,128)(2,1)} %add_convert_fusion.2), channel_id=1, source_target_pairs={{0,2},{1,3},{2,0},{3,1},{4,6},{5,7},{6,4},{7,5},{8,10},{9,11},{10,... | collective-permute-start | bytes 2359304 | tf_op jit(solution)/shard_map/ppermute | solution.py:38
  277.7 15.7 %collective-permute-start.50 = (bf16[384,768]{1,0:T(8,128)(2,1)}, bf16[384,768]{1,0:T(8,128)(2,1)}, u32[]{:S(2)}, u32[]{:S(2)}) collective-permute-start(bf16[384,768]{1,0:T(8,128)(2,1)} %pad_maximum_fusion.1.rest_0_), channel_id=1, source_target_pairs={{0,4},{4,0},{8,12},{12,8},{16,20},{20,16},{24,28},{28,24},{1,5},{5... | collective-permute-start | bytes 1769480 | tf_op jit(solution)/shard_map/ppermute | solution.py:38
  (59 other events, 445.5 us)

commit v5 on v3

--- a/solution.py
+++ b/solution.py
@@ -123,40 +123,56 @@
     return jnp.where(i >= stop, i, start), i
 
 
-def attend_kernel(heads, first, per, scale, len_ref, h_ref, q_ref, k_ref, vt_ref, o_ref, l_ref, m_s, z_s, acc_s):
+def attend_kernel(heads, first, per, scale, len_ref, h_ref, q_ref, k_ref, vt_ref, o_ref, l_ref, s_s, m_s, z_s, acc_s):
     t = pl.program_id(0)
     row = ((h_ref[0] ^ (first + t // per)) * per + t % per) * BLK
     start, i = lane_starts(len_ref, row, BLK)
     low, _ = row_segment(len_ref, row)
-    m_s[...] = jnp.full_like(m_s, NEG)
+    m_s[...] = jnp.zeros_like(m_s)
     z_s[...] = jnp.zeros_like(z_s)
     acc_s[...] = jnp.zeros_like(acc_s)
     qs = [q_ref[h] * jnp.asarray(scale, BF) for h in range(heads)]
-
-    def body(jb, carry):
+    blocks = (low // BLK, row // BLK + 1)
+
+    def measure(jb, carry):
         j0 = pl.multiple_of(jb * BLK, BLK)
         j = j0 + lax.broadcasted_iota(jnp.int32, (BLK, BLK), 0)
         mask = (j >= start) & (j <= i)
+        scores = [dot_nt(k_ref[h, pl.ds(j0, BLK), :], qs[h]) for h in range(heads)]
+        tops = [m_s[h : h + 1, :] for h in range(heads)]
         for h in range(heads):
-            s = dot_nt(k_ref[h, pl.ds(j0, BLK), :], qs[h])
-            magnitude = jnp.where(mask, jnp.abs(s), NEG)
-            old = m_s[h : h + 1, :]
-            top = jnp.maximum(old, jnp.max(magnitude, axis=0, keepdims=True))
-            decay = jnp.exp(old - top)
-            e = jnp.exp(magnitude - top)
-            z_s[h : h + 1, :] = z_s[h : h + 1, :] * decay + jnp.sum(e, axis=0, keepdims=True)
-            m_s[h : h + 1, :] = top
-            u = e - jnp.where(mask, jnp.exp(-top), 0.0)
-            w = jnp.where(s < 0, -u, u).astype(BF)
-            acc_s[h] = acc_s[h] * decay + dot_nn(vt_ref[h, :, pl.ds(j0, BLK)], w)
+            s = jnp.where(mask, scores[h], 0.0)
+            s_s[h, pl.ds(j0, BLK), :] = s
+            tops[h] = jnp.maximum(tops[h], jnp.max(jnp.abs(s), axis=0, keepdims=True))
+        for h in range(heads):
+            m_s[h : h + 1, :] = tops[h]
         return carry
 
-    lax.fori_loop(low // BLK, row // BLK + 1, body, 0)
+    lax.fori_loop(*blocks, measure, 0)
+    tops = [m_s[h : h + 1, :] for h in range(heads)]
+    offsets = [jnp.exp(-top) for top in tops]
+
+    def gather(jb, carry):
+        j0 = pl.multiple_of(jb * BLK, BLK)
+        sums, weights = [], []
+        for h in range(heads):
+            s = s_s[h, pl.ds(j0, BLK), :]
+            u = jnp.exp(jnp.abs(s) - tops[h]) - offsets[h]
+            sums.append(jnp.sum(u, axis=0, keepdims=True))
+            weights.append(jnp.where(s < 0, -u, u).astype(BF))
+        adds = [dot_nn(vt_ref[h, :, pl.ds(j0, BLK)], weights[h]) for h in range(heads)]
+        for h in range(heads):
+            z_s[h : h + 1, :] += sums[h]
+            acc_s[h] += adds[h]
+        return carry
+
+    lax.fori_loop(*blocks, gather, 0)
+    count = (i - start + 1).astype(F32)
     outs = []
     for h in range(heads):
-        z = z_s[h : h + 1, :]
+        z = z_s[h : h + 1, :] + count * offsets[h]
         outs.append((acc_s[h] / z).T)
-        l_ref[h : h + 1, :] = m_s[h : h + 1, :] + jnp.log(z)
+        l_ref[h : h + 1, :] = tops[h] + jnp.log(z)
     o_ref[...] = jnp.concatenate(outs, axis=1).astype(BF)
 
 
@@ -185,6 +201,7 @@
                 pl.BlockSpec((8, BLK), lambda t, n, h: (0, t)),
             ],
             scratch_shapes=[
+                pltpu.VMEM((heads, rows, BLK), F32),
                 pltpu.VMEM((8, BLK), F32),
                 pltpu.VMEM((8, BLK), F32),
                 pltpu.VMEM((heads, hd, BLK), F32),
@@ -235,23 +252,31 @@
             i0 = pl.multiple_of(ib * BLK, BLK)
             start, i = lane_starts(len_ref, i0, BLK)
             mask = (j >= start) & (j <= i)
+            at = pl.ds(i0, BLK)
+            qh = [q_s[h, at, :] for h in range(heads)]
+            gh = [g_s[h, at, :] for h in range(heads)]
+            scores = [dot_nt(k_ref[h, pl.ds(j0, BLK), :], qh[h]) for h in range(heads)]
+            gws = [dot_nt(v_ref[h, pl.ds(j0, BLK), :], gh[h]) for h in range(heads)]
+            ws, gss = [], []
             for h in range(heads):
-                qh = q_s[h, pl.ds(i0, BLK), :]
-                gh = g_s[h, pl.ds(i0, BLK), :]
-                s = dot_nt(k_ref[h, pl.ds(j0, BLK), :], qh)
-                gw = dot_nt(v_ref[h, pl.ds(j0, BLK), :], gh)
-                level = l_s[h : h + 1, pl.ds(i0, BLK)]
-                offset = c_s[h : h + 1, pl.ds(i0, BLK)]
-                d = d_s[h : h + 1, pl.ds(i0, BLK)]
+                s, gw = scores[h], gws[h]
+                level = l_s[h : h + 1, at]
+                offset = c_s[h : h + 1, at]
+                d = d_s[h : h + 1, at]
                 p = jnp.exp(jnp.where(mask, jnp.abs(s), NEG) - level)
                 u = p - jnp.where(mask, offset, 0.0)
-                minus = s < 0
-                w = jnp.where(minus, -u, u).astype(BF)
-                signed = jnp.where(minus, -d, jnp.where(s == 0, 0.0, d))
-                gs = (p * (gw - signed)).astype(BF)
-                dv_s[h] += dot_nn(w, gh)
-                dk_s[h] += dot_nn(gs, qh)
-                dq_s[h, :, pl.ds(i0, BLK)] += dot_nn(kt_s[h], gs)
+                sign = jnp.clip(s * 1e38, -1.0, 1.0)
+                w = (sign * u).astype(BF)
+                gs = (p * (gw - sign * d)).astype(BF)
+                ws.append(w)
+                gss.append(gs)
+            dvs = [dot_nn(ws[h], gh[h]) for h in range(heads)]
+            dks = [dot_nn(gss[h], qh[h]) for h in range(heads)]
+            dqs = [dot_nn(kt_s[h], gss[h]) for h in range(heads)]
+            for h in range(heads):
+                dv_s[h] += dvs[h]
+                dk_s[h] += dks[h]
+                dq_s[h, :, at] += dqs[h]
             return carry
 
         lax.fori_loop(jb, (stop - 1) // BLK + 1, inner, 0)

time: 289 us -> 274 us (0.948)
  Pallas kernels: 146 us -> 124 us
  starting transfers between devices: 41.9 us -> 51.2 us
    pallas_call x2, Pallas kernels: 35.5 us -> 20.4 us  [attend_call(): pl.pallas_call(functools.partial(attend_kernel, heads, first, per, 1.0 /...]
    ppermute x50, starting transfers between devices: 41.9 us -> 51.2 us  [swap(): return lax.ppermute(x, axis, [(i, i ^ bits) for i in range(size)])]
    pallas_call x1, Pallas kernels: 33.4 us -> 26.3 us  [attend_back_call(): pl.pallas_call(functools.partial(attend_back_kernel, chunk, 1.0 / math.sq...]
  transfers between devices with their start and end apart: 50 -> 50, of which waited for: 15 -> 17; matrix products, arithmetic and copies ran while one was open for 10% -> 10% of each run, Pallas kernels for 46% -> 41%
where the time goes in v5:
time: 274 us; the launch traced here: 273 us
  Pallas kernels  124 us (45%)
  waiting for transfers between devices  61.8 us (23%)
  starting transfers between devices  51.2 us (19%)
  other arithmetic  18.7 us (7%)
  local copies, waits for them, and re-layouts  12.4 us (5%)
  matrix products  3.91 us (1%)
    ppermute x50, waiting for transfers between devices, swap(): return lax.ppermute(x, axis, [(i, i ^ bits) for i in range(size)])  61.8 us
    ppermute x50, starting transfers between devices, swap(): return lax.ppermute(x, axis, [(i, i ^ bits) for i in range(size)])  51.2 us
    pallas_call x1, Pallas kernels, attend_back_call(): pl.pallas_call(functools.partial(attend_back_kernel, chunk, 1.0 / math.sq...  26.3 us
    pallas_call x2, Pallas kernels, attend_call(): pl.pallas_call(functools.partial(attend_kernel, heads, first, per, 1.0 /...  20.4 us
    pallas_call x2, Pallas kernels, feed_call(): pl.pallas_call(functools.partial(feed_kernel, steps), out_shape=(jax.Shap...  20 us
    pallas_call x2, Pallas kernels, qkv_call(): pl.pallas_call(functools.partial(qkv_kernel, heads, hd, steps), out_shape...  12.8 us
    pallas_call x1, Pallas kernels, weigh_call(): pl.pallas_call(functools.partial(weigh_kernel, tiles), out_shape=(half, h...  12.5 us
    pallas_call x1, Pallas kernels, tally_call(): pl.pallas_call(functools.partial(tally_kernel, steps), out_shape=(half, h...  7.71 us
  transfers between devices with their start and end apart: 50, of which 17 were waited for; matrix products, arithmetic and copies ran while one was open for 10% of the time, Pallas kernels for 41%

profile of v5, /device:TPU:0, one launch (start us, length us, event | category | flops | bytes accessed | tf_op | source)
XLA Modules:
  0.0 273.2 jit_solution(14289043468645244767)
XLA Ops:
  1.2 2.6 collective-permute-start
  10.1 6.5 %qkv.2 = (bf16[3,2048,64]{2,1,0:T(8,128)(2,1)}, bf16[3,2048,64]{2,1,0:T(8,128)(2,1)}, bf16[3,2048,64]{2,1,0:T(8,128)(2,1)}, bf16[3,64,2048]{2,1,0:T(8,128)(2,1)}, bf16[2048,768]{1,0:T(8,128)(2,1)}) custom-call(s32[1]{0:T(128)} %bitcast.1.h_ref, bf16[512,768]{1,0:T(8,128)(2,1)} %x_ref.1, bf16[512,768]{1,0:T(8,128)(2,1)} %copy-done.32, f32[8,768]{1,0:T(8,128)} %stack.31.v_ref, ...), custom_call_target="tpu_custom_call" | custom-call | flops 905969664 | bytes 4718592 | tf_op jit(solution)/shard_map/qkv/pallas_call | solution.py:84
  16.6 5.5 %collective-permute-done.a_ref = bf16[512,768]{1,0:T(8,128)(2,1)S(1)} collective-permute-done((bf16[512,768]{1,0:T(8,128)(2,1)}, bf16[512,768]{1,0:T(8,128)(2,1)S(1)}, u32[]{:S(2)}, u32[]{:S(2)}) %collective-permute-start) | collective-permute-done | bytes 786464 | tf_op jit(solution)/shard_map/ppermute | solution.py:38
  26.4 6.3 %qkv.3 = (bf16[3,2048,64]{2,1,0:T(8,128)(2,1)}, bf16[3,2048,64]{2,1,0:T(8,128)(2,1)}, bf16[3,2048,64]{2,1,0:T(8,128)(2,1)}, bf16[3,64,2048]{2,1,0:T(8,128)(2,1)}, bf16[2048,768]{1,0:T(8,128)(2,1)}) custom-call(s32[1]{0:T(128)} %bitcast.1.h_ref, ...), custom_call_target="tpu_custom_call", output_to_operand_aliasing={{0}: (6, {}), {1}: (7, {}), {2}: (8, {}), {3}: (9, {}), {4}... | custom-call | flops 905969664 | bytes 4718592 | tf_op jit(solution)/shard_map/qkv/pallas_call | solution.py:84
  32.7 9.6 %attend.2 = (bf16[1024,192]{1,0:T(8,128)(2,1)}, f32[8,1024]{1,0:T(8,128)}) custom-call(s32[8]{0:T(128)} %bitcast.25, s32[1]{0:T(128)} %bitcast.1.h_ref, bf16[3,2048,64]{2,1,0:T(8,128)(2,1)} %get-tuple-element.150.q_ref, bf16[3,2048,64]{2,1,0:T(8,128)(2,1)} %get-tuple-element.114.k_ref, bf16[3,64,2048]{2,1,0:T(8,128)(2,1)} %get-tuple-element.115.vt_ref), custom_call_target="tpu_custom_call" | custom-call | flops 3221225472 | bytes 4718592 | tf_op jit(solution)/shard_map/attend/pallas_call | solution.py:185
  44.4 10.8 %attend.3 = (bf16[1024,192]{1,0:T(8,128)(2,1)}, f32[8,1024]{1,0:T(8,128)}) custom-call(s32[8]{0:T(128)} %bitcast.26, s32[1]{0:T(128)} %bitcast.1.h_ref, bf16[3,2048,64]{2,1,0:T(8,128)(2,1)} %get-tuple-element.150.q_ref, bf16[3,2048,64]{2,1,0:T(8,128)(2,1)} %get-tuple-element.114.k_ref, bf16[3,64,2048]{2,1,0:T(8,128)(2,1)} %get-tuple-element.115.vt_ref), custom_call_target="tpu_custom_call" | custom-call | flops 3221225472 | bytes 4718592 | tf_op jit(solution)/shard_map/attend/pallas_call | solution.py:185
  57.9 5.2 %collective-permute-done.8.p2 = bf16[192,768]{1,0:T(8,128)(2,1)S(1)} collective-permute-done((bf16[192,768]{1,0:T(8,128)(2,1)S(1)}, bf16[192,768]{1,0:T(8,128)(2,1)S(1)}, u32[]{:S(2)}, u32[]{:S(2)}) %collective-permute-start.8) | collective-permute-done | bytes 294944 | tf_op jit(solution)/shard_map/ppermute | solution.py:38
  65.5 4.1 %mix.1 = (f32[512,768]{1,0:T(8,128)}, bf16[512,768]{1,0:T(8,128)(2,1)}) custom-call(bf16[1024,192]{1,0:T(8,128)(2,1)} %get-tuple-element.119.m0.rest_4_, bf16[1024,192]{1,0:T(8,128)(2,1)} %copy-done.15, bf16[1024,192]{1,0:T(8,128)(2,1)} %copy-done.13, bf16[1024,192]{1,0:T(8,128)(2,1)} %collective-permute-done.6.m3, bf16[192,768]{1,0:T(8,128)(2,1)} %bitcast.19, ...), custom_call_target="tpu_custom_call" | custom-call | flops 603979776 | bytes 4718592 | tf_op jit(solution)/shard_map/mix/pallas_call | solution.py:483
  73.0 10.0 %feed.2 = (bf16[2048,768]{1,0:T(8,128)(2,1)}, bf16[2048,768]{1,0:T(8,128)(2,1)}, bf16[512,768]{1,0:T(8,128)(2,1)}, bf16[512,768]{1,0:T(8,128)(2,1)}, bf16[512,768]{1,0:T(8,128)(2,1)}, /*index=5*/bf16[512,768]{1,0:T(8,128)(2,1)}) custom-call(bf16[512,768]{1,0:T(8,128)(2,1)} %get-tuple-element.122.ha_ref.h0, bf16[512,768]{1,0:T(8,128)(2,1)} %copy-done.27, ...), custom_call_target="tpu_custom_call" | custom-call | flops 4831838208 | bytes 6291456 | tf_op jit(solution)/shard_map/feed/pallas_call | solution.py:362
  83.0 6.8 %collective-permute-done.12.ha_ref.h2 = bf16[512,768]{1,0:T(8,128)(2,1)S(1)} collective-permute-done((bf16[512,768]{1,0:T(8,128)(2,1)}, bf16[512,768]{1,0:T(8,128)(2,1)S(1)}, u32[]{:S(2)}, u32[]{:S(2)}) %collective-permute-start.12) | collective-permute-done | bytes 786464 | tf_op jit(solution)/shard_map/ppermute | solution.py:38
  93.0 10.0 %feed.3 = (bf16[2048,768]{1,0:T(8,128)(2,1)}, bf16[2048,768]{1,0:T(8,128)(2,1)}, bf16[512,768]{1,0:T(8,128)(2,1)}, bf16[512,768]{1,0:T(8,128)(2,1)}, bf16[512,768]{1,0:T(8,128)(2,1)}, /*index=5*/bf16[512,768]{1,0:T(8,128)(2,1)}) custom-call(bf16[512,768]{1,0:T(8,128)(2,1)} %copy-done.28, ...), custom_call_target="tpu_custom_call", output_to_operand_aliasing={{0}: (7, {}), {1}: (8, {})} | custom-call | flops 4831838208 | bytes 6291456 | tf_op jit(solution)/shard_map/feed/pallas_call | solution.py:362
  109.1 12.5 %weigh.1 = (bf16[768,768]{1,0:T(8,128)(2,1)}, bf16[768,768]{1,0:T(8,128)(2,1)}, f32[1,768]{1,0:T(1,128)}) custom-call(s32[1]{0:T(128)} %bitcast.5.b_ref, bf16[512,768]{1,0:T(8,128)(2,1)} %get-tuple-element.122.ha_ref.h0, bf16[512,768]{1,0:T(8,128)(2,1)} %copy-done.27, bf16[512,768]{1,0:T(8,128)(2,1)} %copy-done.28, bf16[512,768]{1,0:T(8,128)(2,1)} %copy-done.30, ...), custom_call_target="tpu_custom_call" | custom-call | flops 4831838208 | bytes 18874368 | tf_op jit(solution)/shard_map/weigh/pallas_call | solution.py:443
  121.7 3.8 %collective-permute-start.21 = (bf16[768,768]{1,0:T(8,128)(2,1)}, bf16[768,768]{1,0:T(8,128)(2,1)S(1)}, u32[]{:S(2)}, u32[]{:S(2)}) collective-permute-start(bf16[768,768]{1,0:T(8,128)(2,1)} %get-tuple-element.146), channel_id=1, source_target_pairs={{0,4},{4,0},{8,12},{12,8},{16,20},{20,16},{24,28},{28,24},{1,5},{5... | collective-permute-start | bytes 3538952 | tf_op jit(solution)/shard_map/ppermute | solution.py:38
  127.1 6.2 %turn.1 = (f32[512,768]{1,0:T(8,128)}, bf16[512,768]{1,0:T(8,128)(2,1)}, bf16[512,192]{1,0:T(8,128)(2,1)}, bf16[512,192]{1,0:T(8,128)(2,1)}, bf16[512,192]{1,0:T...) custom-call(bf16[512,768]{1,0:T(8,128)(2,1)} %get-tuple-element.132.n_ref, ...), custom_call_target="tpu_custom_call" | custom-call | flops 512 | bytes 768 | tf_op jit(solution)/shard_map/turn/pallas_call | solution.py:523
  140.4 7.6 %collective-permute-done.25 = bf16[512,192]{1,0:T(8,128)(2,1)S(1)} collective-permute-done((bf16[512,192]{1,0:T(8,128)(2,1)}, bf16[512,192]{1,0:T(8,128)(2,1)S(1)}, u32[]{:S(2)}, u32[]{:S(2)}) %collective-permute-start.25) | collective-permute-done | bytes 196640 | tf_op jit(solution)/shard_map/ppermute | solution.py:38
  147.9 4.4 %collective-permute-done.21 = bf16[768,768]{1,0:T(8,128)(2,1)S(1)} collective-permute-done((bf16[768,768]{1,0:T(8,128)(2,1)}, bf16[768,768]{1,0:T(8,128)(2,1)S(1)}, u32[]{:S(2)}, u32[]{:S(2)}) %collective-permute-start.21) | collective-permute-done | bytes 1179680 | tf_op jit(solution)/shard_map/ppermute | solution.py:38
  154.5 4.0 %collective-permute-start.29 = (bf16[192,768]{1,0:T(8,128)(2,1)S(1)}, bf16[192,768]{1,0:T(8,128)(2,1)}, u32[]{:S(2)}, u32[]{:S(2)}) collective-permute-start(bf16[192,768]{1,0:T(8,128)(2,1)S(1)} %get-tuple-element.209), channel_id=1, source_target_pairs={{0,24},{4,28},{8,16},{12,20},{16,8},{20,12},{24,0},{28,4},{1,25},{... | collective-permute-start | bytes 884744 | tf_op jit(solution)/shard_map/ppermute | solution.py:38
  160.1 26.3 %attend_back.1.gp_ref = bf16[2048,576]{1,0:T(8,128)(2,1)} custom-call(s32[8]{0:T(128)} %bitcast.27, s32[1]{0:T(128)} %bitcast.1.h_ref, bf16[3,2048,64]{2,1,0:T(8,128)(2,1)} %get-tuple-element.150.q_ref, bf16[3,2048,64]{2,1,0:T(8,128)(2,1)} %get-tuple-element.114.k_ref, bf16[3,2048,64]{2,1,0:T(8,128)(2,1)} %get-tuple-element.151.v_ref, ...), custom_call_target="tpu_custom_call" | custom-call | flops 16106127360 | bytes 11796480 | tf_op jit(solution)/shard_map/attend_back/pallas_call | solution.py:305
  187.7 2.9 %collective-permute-start.35 = (bf16[192,768]{1,0:T(8,128)(2,1)S(1)}, bf16[192,768]{1,0:T(8,128)(2,1)S(1)}, u32[]{:S(2)}, u32[]{:S(2)}) collective-permute-start(bf16[192,768]{1,0:T(8,128)(2,1)S(1)} %add_convert_fusion.6), channel_id=1, source_target_pairs={{0,24},{4,28},{8,16},{12,20},{16,8},{20,12},{24,0},{28,4},{1,25},{... | collective-permute-start | bytes 884744 | tf_op jit(solution)/shard_map/ppermute | solution.py:38
  194.8 7.7 %tally.1 = (bf16[392,768]{1,0:T(8,128)(2,1)}, bf16[392,768]{1,0:T(8,128)(2,1)}) custom-call(s32[1]{0:T(128)} %bitcast.5.b_ref, bf16[2048,576]{1,0:T(8,128)(2,1)} %attend_back.1.gp_ref, bf16[2048,768]{1,0:T(8,128)(2,1)} %get-tuple-element.161.hat_ref, bf16[576,768]{1,0:T(8,128)(2,1)} %bitcast.17, f32[8,768]{1,0:T(8,128)} %stack.31.v_ref, ...), custom_call_target="tpu_custom_call" | custom-call | flops 576 | bytes 768 | tf_op jit(solution)/shard_map/tally/pallas_call | solution.py:584
  202.5 3.6 %collective-permute-start.32 = (bf16[392,768]{1,0:T(8,128)(2,1)}, bf16[392,768]{1,0:T(8,128)(2,1)S(1)}, u32[]{:S(2)}, u32[]{:S(2)}) collective-permute-start(bf16[392,768]{1,0:T(8,128)(2,1)} %get-tuple-element.165), channel_id=1, source_target_pairs={{0,4},{4,0},{8,12},{12,8},{16,20},{20,16},{24,28},{28,24},{1,5},{5... | collective-permute-start | bytes 1806344 | tf_op jit(solution)/shard_map/ppermute | solution.py:38
  206.1 6.8 %spread.1 = (bf16[512,768]{1,0:T(8,128)(2,1)}, bf16[512,768]{1,0:T(8,128)(2,1)}, bf16[512,768]{1,0:T(8,128)(2,1)}, bf16[512,768]{1,0:T(8,128)(2,1)}) custom-call(bf16[2048,576]{1,0:T(8,128)(2,1)} %attend_back.1.gp_ref, bf16[576,768]{1,0:T(8,128)(2,1)} %bitcast.18), custom_call_target="tpu_custom_call" | custom-call | flops 576 | bytes 768 | tf_op jit(solution)/shard_map/spread/pallas_call | solution.py:615
  212.9 3.6 %collective-permute-done.34 = bf16[192,768]{1,0:T(8,128)(2,1)S(1)} collective-permute-done((bf16[192,768]{1,0:T(8,128)(2,1)S(1)}, bf16[192,768]{1,0:T(8,128)(2,1)S(1)}, u32[]{:S(2)}, u32[]{:S(2)}) %collective-permute-start.34) | collective-permute-done | bytes 294944 | tf_op jit(solution)/shard_map/ppermute | solution.py:38
  218.4 3.9 %collective-permute-start.37 = (bf16[384,768]{1,0:T(8,128)(2,1)S(1)}, bf16[384,768]{1,0:T(8,128)(2,1)S(1)}, u32[]{:S(2)}, u32[]{:S(2)}) collective-permute-start(bf16[384,768]{1,0:T(8,128)(2,1)S(1)} %pad_maximum_fusion.rest_0_), channel_id=1, source_target_pairs={{0,4},{4,0},{8,12},{12,8},{16,20},{20,16},{24,28},{28,24},{1,5},{5... | collective-permute-start | bytes 1769480 | tf_op jit(solution)/shard_map/ppermute | solution.py:38
  223.2 3.5 %collective-permute-start.36 = (bf16[104,768]{1,0:T(8,128)(2,1)S(1)}, bf16[104,768]{1,0:T(8,128)(2,1)S(1)}, u32[]{:S(2)}, u32[]{:S(2)}) collective-permute-start(bf16[104,768]{1,0:T(8,128)(2,1)S(1)} %get-tuple-element.214), channel_id=1, source_target_pairs={{0,8},{4,12},{8,0},{12,4},{16,24},{20,28},{24,16},{28,20},{1,9},{5... | collective-permute-start | bytes 479240 | tf_op jit(solution)/shard_map/ppermute | solution.py:38
  227.8 8.5 %collective-permute-done.37.rest_2_ = bf16[384,768]{1,0:T(8,128)(2,1)S(1)} collective-permute-done((bf16[384,768]{1,0:T(8,128)(2,1)S(1)}, bf16[384,768]{1,0:T(8,128)(2,1)S(1)}, u32[]{:S(2)}, u32[]{:S(2)}) %collective-permute-start.37) | collective-permute-done | bytes 589856 | tf_op jit(solution)/shard_map/ppermute | solution.py:38
  238.2 2.4 collective-permute-start.44
  246.8 5.6 %collective-permute-done.42.rest_3_ = bf16[384,768]{1,0:T(8,128)(2,1)} collective-permute-done((bf16[384,768]{1,0:T(8,128)(2,1)S(1)}, bf16[384,768]{1,0:T(8,128)(2,1)}, u32[]{:S(2)}, u32[]{:S(2)}) %collective-permute-start.42) | collective-permute-done | bytes 589856 | tf_op jit(solution)/shard_map/ppermute | solution.py:38
  255.9 3.0 %add_convert_fusion.1 = bf16[512,768]{1,0:T(8,128)(2,1)} fusion(bf16[512,768]{1,0:T(8,128)(2,1)} %collective-permute-done.23, f32[512,768]{1,0:T(8,128)S(1)} %copy-done.2, bf16[512,768]{1,0:T(8,128)(2,1)} %collective-permute-done.16, bf16[512,768]{1,0:T(8,128)(2,1)} %get-tuple-element.123, f32[768]{0:T(1024)S(1)} %copy-done.26), kind=kLoop, calls=%fused_computation.14 | loop fusion | flops 3145728 | bytes 4721664 | tf_op jit(solution)/shard_map/convert_element_type | solution.py:841
  260.6 4.2 %unpack.2 = (f32[768,768]{1,0:T(8,128)}, f32[768,768]{1,0:T(8,128)}) custom-call(s32[1]{0:T(128)} %bitcast.5.b_ref, bf16[384,768]{1,0:T(8,128)(2,1)} %copy-done.5, bf16[384,768]{1,0:T(8,128)(2,1)} %copy-done.7, bf16[384,768]{1,0:T(8,128)(2,1)} %copy-done.24, bf16[384,768]{1,0:T(8,128)(2,1)} %collective-permute-done.42.rest_3_), custom_call_target="tpu_custom_call" | custom-call | flops 1536 | bytes 768 | tf_op jit(solution)/shard_map/unpack/pallas_call | solution.py:644
  267.5 2.8 %fusion.8 = bf16[512,768]{1,0:T(8,128)(2,1)} fusion(f32[512,768]{1,0:T(8,128)S(1)} %copy-done.6, bf16[512,768]{1,0:T(8,128)(2,1)S(1)} %copy-done, f32[512]{0:T(512)S(1)} %get-tuple-element.215, f32[512]{0:T(512)S(1)} %get-tuple-element.216, f32[512]{0:T(512)S(1)} %add_rsqrt_fusion, f32[512]{0:T(512)S(1)} %broadcast_multiply_fusion.2, f32[768]{0:T(1024)S(1)} %copy-done.25, ...), kind=kLoop, calls=%fused_computation.11 | loop fusion | flops 5898240 | bytes 5516288 | tf_op jit(solution)/shard_map/convert_element_type | solution.py:852
  270.3 2.9 %unpack.3 = (f32[576,768]{1,0:T(8,128)}, f32[192,768]{1,0:T(8,128)}) custom-call(s32[1]{0:T(128)} %bitcast.5.b_ref, bf16[384,768]{1,0:T(8,128)(2,1)} %pad_maximum_fusion.1.rest_0_, bf16[384,768]{1,0:T(8,128)(2,1)} %collective-permute-done.49.rest_1_), custom_call_target="tpu_custom_call" | custom-call | flops 768 | bytes 768 | tf_op jit(solution)/shard_map/unpack/pallas_call | solution.py:644
  (204 shorter events, 68.5 us)
Async XLA Ops:
  1.2 20.9 %collective-permute-start = (bf16[512,768]{1,0:T(8,128)(2,1)}, bf16[512,768]{1,0:T(8,128)(2,1)S(1)}, u32[]{:S(2)}, u32[]{:S(2)}) collective-permute-start(bf16[512,768]{1,0:T(8,128)(2,1)} %x_ref.1), channel_id=1, source_target_pairs={{0,2},{1,3},{2,0},{3,1},{4,6},{5,7},{6,4},{7,5},{8,10},{9,11},{10,... | collective-permute-start | bytes 2359304 | tf_op jit(solution)/shard_map/ppermute | solution.py:38
  23.7 20.7 %collective-permute-start.3 = (bf16[512,768]{1,0:T(8,128)(2,1)S(1)}, bf16[512,768]{1,0:T(8,128)(2,1)}, u32[]{:S(2)}, u32[]{:S(2)}) collective-permute-start(bf16[512,768]{1,0:T(8,128)(2,1)S(1)} %broadcast_select_fusion.ga_ref.g0.cot_ref), channel_id=1, source_target_pairs={{0,2},{1,3},{2,0},{3,1},{4,6},{5,7},{6,4},{7,5},{8,10},{9,11},{10,... | collective-permute-start | bytes 2359304 | tf_op jit(solution)/shard_map/ppermute | solution.py:38
  42.3 15.0 %collective-permute-start.5 = (bf16[1024,192]{1,0:T(8,128)(2,1)}, bf16[1024,192]{1,0:T(8,128)(2,1)S(1)}, u32[]{:S(2)}, u32[]{:S(2)}) collective-permute-start(bf16[1024,192]{1,0:T(8,128)(2,1)} %get-tuple-element.116.rest_5_), channel_id=1, source_target_pairs={{0,2},{1,3},{2,0},{3,1},{4,6},{5,7},{6,4},{7,5},{8,10},{9,11},{10,... | collective-permute-start | bytes 1179656 | tf_op jit(solution)/shard_map/ppermute | solution.py:38
  44.3 18.7 %collective-permute-start.8 = (bf16[192,768]{1,0:T(8,128)(2,1)S(1)}, bf16[192,768]{1,0:T(8,128)(2,1)S(1)}, u32[]{:S(2)}, u32[]{:S(2)}) collective-permute-start(bf16[192,768]{1,0:T(8,128)(2,1)S(1)} %bitcast.21), channel_id=1, source_target_pairs={{0,2},{1,3},{2,0},{3,1},{4,6},{5,7},{6,4},{7,5},{8,10},{9,11},{10,... | collective-permute-start | bytes 884744 | tf_op jit(solution)/shard_map/ppermute | solution.py:38
  69.8 20.0 %collective-permute-start.12 = (bf16[512,768]{1,0:T(8,128)(2,1)}, bf16[512,768]{1,0:T(8,128)(2,1)S(1)}, u32[]{:S(2)}, u32[]{:S(2)}) collective-permute-start(bf16[512,768]{1,0:T(8,128)(2,1)} %get-tuple-element.122.ha_ref.h0), channel_id=1, source_target_pairs={{0,2},{1,3},{2,0},{3,1},{4,6},{5,7},{6,4},{7,5},{8,10},{9,11},{10,... | collective-permute-start | bytes 2359304 | tf_op jit(solution)/shard_map/ppermute | solution.py:38
  71.5 18.3 %collective-permute-start.14 = (bf16[512,768]{1,0:T(8,128)(2,1)}, bf16[512,768]{1,0:T(8,128)(2,1)S(1)}, u32[]{:S(2)}, u32[]{:S(2)}) collective-permute-start(bf16[512,768]{1,0:T(8,128)(2,1)} %collective-permute-done.3.ga_ref.g2), channel_id=1, source_target_pairs={{0,1},{1,0},{2,3},{3,2},{4,5},{5,4},{6,7},{7,6},{8,9},{9,8},{10,11... | collective-permute-start | bytes 2359304 | tf_op jit(solution)/shard_map/ppermute | solution.py:38
  106.8 18.6 %collective-permute-start.16 = (bf16[512,768]{1,0:T(8,128)(2,1)}, bf16[512,768]{1,0:T(8,128)(2,1)}, u32[]{:S(2)}, u32[]{:S(2)}) collective-permute-start(bf16[512,768]{1,0:T(8,128)(2,1)} %get-tuple-element.130), channel_id=1, source_target_pairs={{0,1},{1,0},{2,3},{3,2},{4,5},{5,4},{6,7},{7,6},{8,9},{9,8},{10,11... | collective-permute-start | bytes 2359304 | tf_op jit(solution)/shard_map/ppermute | solution.py:38
  107.0 18.4 %collective-permute-start.19 = (bf16[512,768]{1,0:T(8,128)(2,1)}, bf16[512,768]{1,0:T(8,128)(2,1)S(1)}, u32[]{:S(2)}, u32[]{:S(2)}) collective-permute-start(bf16[512,768]{1,0:T(8,128)(2,1)} %get-tuple-element.139), channel_id=1, source_target_pairs={{0,1},{1,0},{2,3},{3,2},{4,5},{5,4},{6,7},{7,6},{8,9},{9,8},{10,11... | collective-permute-start | bytes 2359304 | tf_op jit(solution)/shard_map/ppermute | solution.py:38
  107.4 19.7 %collective-permute-start.18 = (bf16[512,768]{1,0:T(8,128)(2,1)S(1)}, bf16[512,768]{1,0:T(8,128)(2,1)}, u32[]{:S(2)}, u32[]{:S(2)}) collective-permute-start(bf16[512,768]{1,0:T(8,128)(2,1)S(1)} %add_convert_fusion.4), channel_id=1, source_target_pairs={{0,2},{1,3},{2,0},{3,1},{4,6},{5,7},{6,4},{7,5},{8,10},{9,11},{10,... | collective-permute-start | bytes 2359304 | tf_op jit(solution)/shard_map/ppermute | solution.py:38
  109.1 17.9 %collective-permute-start.17 = (bf16[512,768]{1,0:T(8,128)(2,1)}, bf16[512,768]{1,0:T(8,128)(2,1)}, u32[]{:S(2)}, u32[]{:S(2)}) collective-permute-start(bf16[512,768]{1,0:T(8,128)(2,1)} %get-tuple-element.133), channel_id=1, source_target_pairs={{0,1},{1,0},{2,3},{3,2},{4,5},{5,4},{6,7},{7,6},{8,9},{9,8},{10,11... | collective-permute-start | bytes 2359304 | tf_op jit(solution)/shard_map/ppermute | solution.py:38
  121.7 30.6 %collective-permute-start.21 = (bf16[768,768]{1,0:T(8,128)(2,1)}, bf16[768,768]{1,0:T(8,128)(2,1)S(1)}, u32[]{:S(2)}, u32[]{:S(2)}) collective-permute-start(bf16[768,768]{1,0:T(8,128)(2,1)} %get-tuple-element.146), channel_id=1, source_target_pairs={{0,4},{4,0},{8,12},{12,8},{16,20},{20,16},{24,28},{28,24},{1,5},{5... | collective-permute-start | bytes 3538952 | tf_op jit(solution)/shard_map/ppermute | solution.py:38
  133.4 14.5 %collective-permute-start.22 = (bf16[512,192]{1,0:T(8,128)(2,1)}, bf16[512,192]{1,0:T(8,128)(2,1)S(1)}, u32[]{:S(2)}, u32[]{:S(2)}) collective-permute-start(bf16[512,192]{1,0:T(8,128)(2,1)} %get-tuple-element.147), channel_id=1, source_target_pairs={{0,2},{1,3},{2,0},{3,1},{4,6},{5,7},{6,4},{7,5},{8,10},{9,11},{10,... | collective-permute-start | bytes 589832 | tf_op jit(solution)/shard_map/ppermute | solution.py:38
  135.2 12.7 %collective-permute-start.25 = (bf16[512,192]{1,0:T(8,128)(2,1)}, bf16[512,192]{1,0:T(8,128)(2,1)S(1)}, u32[]{:S(2)}, u32[]{:S(2)}) collective-permute-start(bf16[512,192]{1,0:T(8,128)(2,1)} %get-tuple-element.153), channel_id=1, source_target_pairs={{0,2},{1,3},{2,0},{3,1},{4,6},{5,7},{6,4},{7,5},{8,10},{9,11},{10,... | collective-permute-start | bytes 589832 | tf_op jit(solution)/shard_map/ppermute | solution.py:38
  137.1 17.5 %collective-permute-start.24 = (bf16[192,768]{1,0:T(8,128)(2,1)S(1)}, bf16[192,768]{1,0:T(8,128)(2,1)S(1)}, u32[]{:S(2)}, u32[]{:S(2)}) collective-permute-start(bf16[192,768]{1,0:T(8,128)(2,1)S(1)} %convolution_convert_fusion.1), channel_id=1, source_target_pairs={{0,1},{1,0},{2,3},{3,2},{4,5},{5,4},{6,7},{7,6},{8,9},{9,8},{10,11... | collective-permute-start | bytes 884744 | tf_op jit(solution)/shard_map/ppermute | solution.py:38
  138.8 20.1 %collective-permute-start.30 = (bf16[192,768]{1,0:T(8,128)(2,1)S(1)}, bf16[192,768]{1,0:T(8,128)(2,1)S(1)}, u32[]{:S(2)}, u32[]{:S(2)}) collective-permute-start(bf16[192,768]{1,0:T(8,128)(2,1)S(1)} %convolution_convert_fusion), channel_id=1, source_target_pairs={{0,1},{1,0},{2,3},{3,2},{4,5},{5,4},{6,7},{7,6},{8,9},{9,8},{10,11... | collective-permute-start | bytes 884744 | tf_op jit(solution)/shard_map/ppermute | solution.py:38
  152.7 42.1 %collective-permute-start.23 = (bf16[512,768]{1,0:T(8,128)(2,1)}, bf16[512,768]{1,0:T(8,128)(2,1)}, u32[]{:S(2)}, u32[]{:S(2)}) collective-permute-start(bf16[512,768]{1,0:T(8,128)(2,1)} %add_convert_fusion.3), channel_id=1, source_target_pairs={{0,2},{1,3},{2,0},{3,1},{4,6},{5,7},{6,4},{7,5},{8,10},{9,11},{10,... | collective-permute-start | bytes 2359304 | tf_op jit(solution)/shard_map/ppermute | solution.py:38
  154.5 31.9 %collective-permute-start.27 = (bf16[192,768]{1,0:T(8,128)(2,1)S(1)}, bf16[192,768]{1,0:T(8,128)(2,1)S(1)}, u32[]{:S(2)}, u32[]{:S(2)}) collective-permute-start(bf16[192,768]{1,0:T(8,128)(2,1)S(1)} %get-tuple-element.208), channel_id=1, source_target_pairs={{0,8},{4,12},{8,0},{12,4},{16,24},{20,28},{24,16},{28,20},{1,9},{5... | collective-permute-start | bytes 884744 | tf_op jit(solution)/shard_map/ppermute | solution.py:38
  154.5 31.9 %collective-permute-start.29 = (bf16[192,768]{1,0:T(8,128)(2,1)S(1)}, bf16[192,768]{1,0:T(8,128)(2,1)}, u32[]{:S(2)}, u32[]{:S(2)}) collective-permute-start(bf16[192,768]{1,0:T(8,128)(2,1)S(1)} %get-tuple-element.209), channel_id=1, source_target_pairs={{0,24},{4,28},{8,16},{12,20},{16,8},{20,12},{24,0},{28,4},{1,25},{... | collective-permute-start | bytes 884744 | tf_op jit(solution)/shard_map/ppermute | solution.py:38
  159.0 27.5 %collective-permute-start.28 = (bf16[192,768]{1,0:T(8,128)(2,1)S(1)}, bf16[192,768]{1,0:T(8,128)(2,1)}, u32[]{:S(2)}, u32[]{:S(2)}) collective-permute-start(bf16[192,768]{1,0:T(8,128)(2,1)S(1)} %get-tuple-element.210), channel_id=1, source_target_pairs={{0,16},{4,20},{8,24},{12,28},{16,0},{20,4},{24,8},{28,12},{1,17},{... | collective-permute-start | bytes 884744 | tf_op jit(solution)/shard_map/ppermute | solution.py:38
  159.4 33.5 %collective-permute-start.31 = (bf16[192,768]{1,0:T(8,128)(2,1)S(1)}, bf16[192,768]{1,0:T(8,128)(2,1)}, u32[]{:S(2)}, u32[]{:S(2)}) collective-permute-start(bf16[192,768]{1,0:T(8,128)(2,1)S(1)} %fusion.10), channel_id=1, source_target_pairs={{0,2},{1,3},{2,0},{3,1},{4,6},{5,7},{6,4},{7,5},{8,10},{9,11},{10,... | collective-permute-start | bytes 884744 | tf_op jit(solution)/shard_map/ppermute | solution.py:38
  187.7 25.2 %collective-permute-start.35 = (bf16[192,768]{1,0:T(8,128)(2,1)S(1)}, bf16[192,768]{1,0:T(8,128)(2,1)S(1)}, u32[]{:S(2)}, u32[]{:S(2)}) collective-permute-start(bf16[192,768]{1,0:T(8,128)(2,1)S(1)} %add_convert_fusion.6), channel_id=1, source_target_pairs={{0,24},{4,28},{8,16},{12,20},{16,8},{20,12},{24,0},{28,4},{1,25},{... | collective-permute-start | bytes 884744 | tf_op jit(solution)/shard_map/ppermute | solution.py:38
  190.6 26.0 %collective-permute-start.34 = (bf16[192,768]{1,0:T(8,128)(2,1)S(1)}, bf16[192,768]{1,0:T(8,128)(2,1)S(1)}, u32[]{:S(2)}, u32[]{:S(2)}) collective-permute-start(bf16[192,768]{1,0:T(8,128)(2,1)S(1)} %add_convert_fusion.6), channel_id=1, source_target_pairs={{0,16},{4,20},{8,24},{12,28},{16,0},{20,4},{24,8},{28,12},{1,17},{... | collective-permute-start | bytes 884744 | tf_op jit(solution)/shard_map/ppermute | solution.py:38
  192.5 24.0 %collective-permute-start.33 = (bf16[192,768]{1,0:T(8,128)(2,1)S(1)}, bf16[192,768]{1,0:T(8,128)(2,1)S(1)}, u32[]{:S(2)}, u32[]{:S(2)}) collective-permute-start(bf16[192,768]{1,0:T(8,128)(2,1)S(1)} %add_convert_fusion.6), channel_id=1, source_target_pairs={{0,8},{4,12},{8,0},{12,4},{16,24},{20,28},{24,16},{28,20},{1,9},{5... | collective-permute-start | bytes 884744 | tf_op jit(solution)/shard_map/ppermute | solution.py:38
  202.5 15.6 %collective-permute-start.32 = (bf16[392,768]{1,0:T(8,128)(2,1)}, bf16[392,768]{1,0:T(8,128)(2,1)S(1)}, u32[]{:S(2)}, u32[]{:S(2)}) collective-permute-start(bf16[392,768]{1,0:T(8,128)(2,1)} %get-tuple-element.165), channel_id=1, source_target_pairs={{0,4},{4,0},{8,12},{12,8},{16,20},{20,16},{24,28},{28,24},{1,5},{5... | collective-permute-start | bytes 1806344 | tf_op jit(solution)/shard_map/ppermute | solution.py:38
  218.4 17.9 %collective-permute-start.37 = (bf16[384,768]{1,0:T(8,128)(2,1)S(1)}, bf16[384,768]{1,0:T(8,128)(2,1)S(1)}, u32[]{:S(2)}, u32[]{:S(2)}) collective-permute-start(bf16[384,768]{1,0:T(8,128)(2,1)S(1)} %pad_maximum_fusion.rest_0_), channel_id=1, source_target_pairs={{0,4},{4,0},{8,12},{12,8},{16,20},{20,16},{24,28},{28,24},{1,5},{5... | collective-permute-start | bytes 1769480 | tf_op jit(solution)/shard_map/ppermute | solution.py:38
  222.3 14.0 %collective-permute-start.40 = (bf16[104,768]{1,0:T(8,128)(2,1)S(1)}, bf16[104,768]{1,0:T(8,128)(2,1)S(1)}, u32[]{:S(2)}, u32[]{:S(2)}) collective-permute-start(bf16[104,768]{1,0:T(8,128)(2,1)S(1)} %concatenate.24), channel_id=1, source_target_pairs={{0,24},{4,28},{8,16},{12,20},{16,8},{20,12},{24,0},{28,4},{1,25},{... | collective-permute-start | bytes 479240 | tf_op jit(solution)/shard_map/ppermute | solution.py:38
  222.9 14.8 %collective-permute-start.39 = (bf16[104,768]{1,0:T(8,128)(2,1)S(1)}, bf16[104,768]{1,0:T(8,128)(2,1)S(1)}, u32[]{:S(2)}, u32[]{:S(2)}) collective-permute-start(bf16[104,768]{1,0:T(8,128)(2,1)S(1)} %get-tuple-element.213), channel_id=1, source_target_pairs={{0,16},{4,20},{8,24},{12,28},{16,0},{20,4},{24,8},{28,12},{1,17},{... | collective-permute-start | bytes 479240 | tf_op jit(solution)/shard_map/ppermute | solution.py:38
  223.2 14.4 %collective-permute-start.36 = (bf16[104,768]{1,0:T(8,128)(2,1)S(1)}, bf16[104,768]{1,0:T(8,128)(2,1)S(1)}, u32[]{:S(2)}, u32[]{:S(2)}) collective-permute-start(bf16[104,768]{1,0:T(8,128)(2,1)S(1)} %get-tuple-element.214), channel_id=1, source_target_pairs={{0,8},{4,12},{8,0},{12,4},{16,24},{20,28},{24,16},{28,20},{1,9},{5... | collective-permute-start | bytes 479240 | tf_op jit(solution)/shard_map/ppermute | solution.py:38
  237.7 14.7 %collective-permute-start.42 = (bf16[384,768]{1,0:T(8,128)(2,1)S(1)}, bf16[384,768]{1,0:T(8,128)(2,1)}, u32[]{:S(2)}, u32[]{:S(2)}) collective-permute-start(bf16[384,768]{1,0:T(8,128)(2,1)S(1)} %constant_dynamic-update-slice_fusion.rest_1_), channel_id=1, source_target_pairs={{0,4},{4,0},{8,12},{12,8},{16,20},{20,16},{24,28},{28,24},{1,5},{5... | collective-permute-start | bytes 1769480 | tf_op jit(solution)/shard_map/ppermute | solution.py:38
  240.6 11.8 %collective-permute-start.43 = (bf16[96,768]{1,0:T(8,128)(2,1)S(1)}, bf16[96,768]{1,0:T(8,128)(2,1)S(1)}, u32[]{:S(2)}, u32[]{:S(2)}) collective-permute-start(bf16[96,768]{1,0:T(8,128)(2,1)S(1)} %add_convert_fusion.7), channel_id=1, source_target_pairs={{0,16},{4,20},{8,24},{12,28},{16,0},{20,4},{24,8},{28,12},{1,17},{... | collective-permute-start | bytes 442376 | tf_op jit(solution)/shard_map/ppermute | solution.py:38
  243.3 22.1 %collective-permute-start.46 = (bf16[512,768]{1,0:T(8,128)(2,1)}, bf16[512,768]{1,0:T(8,128)(2,1)S(1)}, u32[]{:S(2)}, u32[]{:S(2)}) collective-permute-start(bf16[512,768]{1,0:T(8,128)(2,1)} %add_convert_fusion.2), channel_id=1, source_target_pairs={{0,2},{1,3},{2,0},{3,1},{4,6},{5,7},{6,4},{7,5},{8,10},{9,11},{10,... | collective-permute-start | bytes 2359304 | tf_op jit(solution)/shard_map/ppermute | solution.py:38
  254.2 16.1 %collective-permute-start.49 = (bf16[384,768]{1,0:T(8,128)(2,1)}, bf16[384,768]{1,0:T(8,128)(2,1)}, u32[]{:S(2)}, u32[]{:S(2)}) collective-permute-start(bf16[384,768]{1,0:T(8,128)(2,1)} %pad_maximum_fusion.1.rest_0_), channel_id=1, source_target_pairs={{0,4},{4,0},{8,12},{12,8},{16,20},{20,16},{24,28},{28,24},{1,5},{5... | collective-permute-start | bytes 1769480 | tf_op jit(solution)/shard_map/ppermute | solution.py:38
  (55 other events, 392.2 us)

commit v6 on v5

--- a/solution.py
+++ b/solution.py
@@ -123,7 +123,7 @@
     return jnp.where(i >= stop, i, start), i
 
 
-def attend_kernel(heads, first, per, scale, len_ref, h_ref, q_ref, k_ref, vt_ref, o_ref, l_ref, s_s, m_s, z_s, acc_s):
+def attend_kernel(heads, first, per, scale, len_ref, h_ref, q_ref, k_ref, vt_ref, oa_ref, ob_ref, la_ref, lb_ref, s_s, m_s, z_s, acc_s):
     t = pl.program_id(0)
     row = ((h_ref[0] ^ (first + t // per)) * per + t % per) * BLK
     start, i = lane_starts(len_ref, row, BLK)
@@ -168,12 +168,25 @@
 
     lax.fori_loop(*blocks, gather, 0)
     count = (i - start + 1).astype(F32)
-    outs = []
+    outs, levels = [], []
     for h in range(heads):
         z = z_s[h : h + 1, :] + count * offsets[h]
         outs.append((acc_s[h] / z).T)
-        l_ref[h : h + 1, :] = tops[h] + jnp.log(z)
-    o_ref[...] = jnp.concatenate(outs, axis=1).astype(BF)
+        levels.append(tops[h] + jnp.log(z))
+    out = jnp.concatenate(outs, axis=1).astype(BF)
+
+    def store(o_ref, l_ref):
+        o_ref[...] = out
+        for h in range(heads):
+            l_ref[h : h + 1, :] = levels[h]
+
+    @pl.when(t < per)
+    def _():
+        store(oa_ref, la_ref)
+
+    @pl.when(t >= per)
+    def _():
+        store(ob_ref, lb_ref)
 
 
 def attend_call(lengths, hid, q, k, vt, first, chunk):
@@ -184,10 +197,8 @@
     whole = lambda t, n, h: (0, 0, 0)
     return pl.pallas_call(
         functools.partial(attend_kernel, heads, first, per, 1.0 / math.sqrt(hd)),
-        out_shape=(
-            jax.ShapeDtypeStruct((steps * BLK, heads * hd), BF),
-            jax.ShapeDtypeStruct((8, steps * BLK), F32),
-        ),
+        out_shape=(jax.ShapeDtypeStruct((chunk, heads * hd), BF),) * 2
+        + (jax.ShapeDtypeStruct((8, chunk), F32),) * 2,
         grid_spec=pltpu.PrefetchScalarGridSpec(
             num_scalar_prefetch=2,
             grid=(steps,),
@@ -197,8 +208,10 @@
                 pl.BlockSpec((heads, hd, rows), whole),
             ],
             out_specs=[
-                pl.BlockSpec((BLK, heads * hd), lambda t, n, h: (t, 0)),
-                pl.BlockSpec((8, BLK), lambda t, n, h: (0, t)),
+                pl.BlockSpec((BLK, heads * hd), lambda t, n, h: (jnp.minimum(t, per - 1), 0)),
+                pl.BlockSpec((BLK, heads * hd), lambda t, n, h: (jnp.maximum(t - per, 0), 0)),
+                pl.BlockSpec((8, BLK), lambda t, n, h: (0, jnp.minimum(t, per - 1))),
+                pl.BlockSpec((8, BLK), lambda t, n, h: (0, jnp.maximum(t - per, 0))),
             ],
             scratch_shapes=[
                 pltpu.VMEM((heads, rows, BLK), F32),
@@ -213,23 +226,22 @@
 
 
 def attend_back_kernel(chunk, scale, len_ref, h_ref, q_ref, k_ref, v_ref, *rest):
-    g_refs, o_refs, l_refs = rest[0:4], rest[4:6], rest[6:8]
-    gp_ref, q_s, g_s, kt_s, l_s, c_s, d_s, dq_s, dk_s, dv_s = rest[8:]
+    g_refs, o_refs, l_refs = rest[0:4], rest[4:8], rest[8:12]
+    gp_ref, q_s, g_s, kt_s, l_s, c_s, d_s, dq_s, dk_s, dv_s = rest[12:]
     heads, rows, hd = q_ref.shape
     blocks = rows // BLK
     per = chunk // BLK
     own = h_ref[0]
     for c in range(4):
         r0 = pl.multiple_of((own ^ c) * chunk, chunk)
-        part = slice((c % 2) * chunk, (c % 2 + 1) * chunk)
         g = g_refs[c][...]
-        o = o_refs[c // 2][part, :]
+        o = o_refs[c][...]
         for h in range(heads):
             gh = g[:, h * hd : (h + 1) * hd]
             g_s[h, pl.ds(r0, chunk), :] = gh
             both = gh.astype(F32) * o[:, h * hd : (h + 1) * hd].astype(F32)
             d_s[h : h + 1, pl.ds(r0, chunk)] = jnp.sum(both.T, axis=0, keepdims=True)
-        level = l_refs[c // 2][:, part]
+        level = l_refs[c][...]
         l_s[:, pl.ds(r0, chunk)] = level
         c_s[:, pl.ds(r0, chunk)] = jnp.exp(-level)
     for h in range(heads):
@@ -305,7 +317,7 @@
     return pl.pallas_call(
         functools.partial(attend_back_kernel, chunk, 1.0 / math.sqrt(hd)),
         out_shape=jax.ShapeDtypeStruct((rows, heads * 3 * hd), BF),
-        in_specs=[sm, sm] + [vm] * 11,
+        in_specs=[sm, sm] + [vm] * 15,
         out_specs=vm,
         scratch_shapes=[
             pltpu.VMEM((heads, rows, hd), BF),
@@ -478,13 +490,12 @@
     per = rows // BLK
     inner = parts[0].shape[1]
     low = pl.BlockSpec((BLK, inner), lambda t: (t, 0))
-    high = pl.BlockSpec((BLK, inner), lambda t: (t + per, 0))
     whole = lambda t: (0, 0)
     return pl.pallas_call(
         mix_kernel,
         out_shape=(jax.ShapeDtypeStruct((rows, width), F32), jax.ShapeDtypeStruct((rows, width), BF)),
         grid=(per,),
-        in_specs=[low, high, low, high]
+        in_specs=[low] * 4
         + [pl.BlockSpec(projs[0].shape, whole)] * 4
         + [pl.BlockSpec((BLK, width), lambda t: (t, 0)), pl.BlockSpec(vectors.shape, whole)],
         out_specs=[pl.BlockSpec((BLK, width), lambda t: (t, 0))] * 2,
@@ -623,26 +634,24 @@
     )(gp, w)
 
 
-def unpack_kernel(counts, parts, b_ref, *rest):
+def unpack_kernel(counts, places, b_ref, *rest):
     acc = rest[-1]
     piece = acc.shape[0] // 8
-    per = 8 // parts
-    for spot, block in enumerate(spots(b_ref, 8)):
-        at = spot % per * piece
-        value = rest[spot // per][at : at + piece, :].astype(F32)
+    for (part, at), block in zip(places, spots(b_ref, 8), strict=True):
+        value = rest[part][at : at + piece, :].astype(F32)
         acc[pl.ds(pl.multiple_of(block * piece, 8), piece), :] = value
     start = 0
-    for out, count in zip(rest[parts:-1], counts, strict=True):
+    for out, count in zip(rest[-1 - len(counts) : -1], counts, strict=True):
         out[...] = acc[start : start + count, :]
         start += count
 
 
-def unpack_call(bid, parts, counts):
-    total = sum(part.shape[0] for part in parts)
+def unpack_call(bid, parts, places, counts):
+    total = sum(counts)
     width = parts[0].shape[1]
     vm = pl.BlockSpec(memory_space=pltpu.VMEM)
     return pl.pallas_call(
-        functools.partial(unpack_kernel, counts, len(parts)),
+        functools.partial(unpack_kernel, counts, places),
         out_shape=tuple(jax.ShapeDtypeStruct((n, width), F32) for n in counts),
         in_specs=[pl.BlockSpec(memory_space=pltpu.SMEM)] + [vm] * len(parts),
         out_specs=[vm] * len(counts),
@@ -731,15 +740,19 @@
     grad_own = jnp.where(live, cotangent, jnp.zeros_like(cotangent))
     grad_far = swap(tie(grad_own, x_far), "head", 2)
     proj_far = swap(tie(proj, x_far), "head", 2)
-    projs = (proj, swap(proj, "head", 1), proj_far, swap(proj_far, "head", 1))
-
-    merged_far, level_far = attend_call(lens, hid, queries, keys, values_t, 2, chunk)
-    from_far = swap(merged_far, "head", 2)
-    merged_near, level_near = attend_call(
-        lens, hid, tie(queries, merged_far, grad_far), keys, values_t, 0, chunk
+    out_far, out_last, level_far, level_last = attend_call(
+        lens, hid, queries, keys, values_t, 2, chunk
+    )
+    from_last = swap(out_last, "head", 2)
+    from_far = swap(out_far, "head", 2)
+    out_own, out_mate, level_own, level_mate = attend_call(
+        lens, hid, tie(queries, out_far, grad_far, proj_far), keys, values_t, 0, chunk
     )
     grads = (grad_own, swap(grad_own, "head", 1), grad_far, swap(grad_far, "head", 1))
-    parts = (merged_near, swap(merged_near, "head", 1), from_far, swap(from_far, "head", 1))
+    from_last = swap(tie(from_last, out_own, from_far), "head", 1)
+    parts = (out_own, swap(out_mate, "head", 1), from_far, from_last)
+    proj_last = swap(tie(proj_far, out_own), "head", 1)
+    projs = (proj, swap(tie(proj, out_far), "head", 1), proj_far, proj_last)
     resid, h_own = mix_call(parts, projs, inputs, vectors)
     h_far = swap(h_own, "head", 2)
     h_near = swap(h_own, "head", 1)
@@ -773,11 +786,7 @@
     got = swap(grad_cross, "head", 2)
     grad_mate = swap(grad_mate, "head", 1)
     grad_att = tie(grad_att, grad_mate)
-    low = slice(0, chunk)
-    high = slice(chunk, 2 * chunk)
-    grad_proj = [
-        dot_tn(p[at], grad_att) for p, at in zip(parts, (low, high, low, high), strict=True)
-    ]
+    grad_proj = [dot_tn(p, grad_att) for p in parts]
     near_sent, far_sent = grad_proj[1].astype(BF), grad_proj[3].astype(BF)
     down_far = tie(down_far, grad_att)
     down_sum = (down_far.astype(F32) + down_swapped.astype(F32)).astype(BF)
@@ -798,8 +807,8 @@
         keys,
         values,
         merged_grads,
-        (merged_near, merged_far),
-        (level_near, level_far),
+        (out_own, out_mate, out_far, out_last),
+        (level_own, level_mate, level_far, level_last),
         chunk,
     )
     got_feed = [tie(g, grad_packed) for g in got_feed]
@@ -814,31 +823,31 @@
     gathered_feed, spread = lax.optimization_barrier((gathered_feed, spread))
     e_own, e_near, e_far, e_last = spread
 
-    feed_a = jnp.concatenate((total_feed, gathered_feed[0]), axis=0)
-    feed_b = jnp.concatenate(gathered_feed[1:], axis=0)
-    last_a = swap(feed_a, "batch", 1)
-    summed = (keep.astype(F32) + tie(other, feed_a, feed_b).astype(F32)).astype(BF)
+    feed_first = jnp.concatenate((total_feed, gathered_feed[0]), axis=0)
+    feed_second = jnp.concatenate(gathered_feed[1:], axis=0)
+    feed_got = swap(feed_first, "batch", 1)
+    summed = (keep.astype(F32) + tie(other, feed_first, feed_second).astype(F32)).astype(BF)
     kept, small = summed[:-8], summed[-8:]
     pieces = [jnp.concatenate((q, small), axis=0) for q in quarters(kept)]
     e_swapped = swap(tie(e_last, *pieces), "head", 1)
     e_sum = (e_far.astype(F32) + e_swapped.astype(F32)).astype(BF)
-    got_attn = [tie(g, last_a, e_sum) for g in across(pieces)]
+    output = resid + near[4].astype(F32) + near_down.astype(F32) + tie(down_other, e_sum).astype(F32)
+    output = (output + bias_down).astype(BF)
+    got_attn = [tie(g, feed_got, output) for g in across(pieces)]
 
     tiny = [small.astype(F32)] + [g[-8:].astype(F32) for g in got_attn]
     small = sum_rest((tiny[0] + tiny[1]) + (tiny[2] + tiny[3]))
     total_attn = fold(kept, got_attn)
     gathered_attn = across([total_attn] * 3)
-    last_b = swap(tie(feed_b, total_attn), "batch", 1)
+    second_got = swap(tie(feed_second, total_attn), "batch", 1)
     e_other = swap(tie(e_sum, total_attn), "head", 2)
-    half = jnp.concatenate([total_attn] + [tie(g, last_b) for g in gathered_attn], axis=0)
+    half = jnp.concatenate([total_attn] + [tie(g, second_got) for g in gathered_attn], axis=0)
     e_mate = swap(tie(e_near, half), "head", 1)
     last = swap(half, "batch", 1)
     biases = small[2:4]
     small = sum_group(tie(small, half))
     e_own = e_own.astype(F32) + e_mate.astype(F32) + tie(e_other, half).astype(F32)
 
-    near_down = near[4].astype(F32) + near_down.astype(F32)
-    output = (resid + near_down + tie(down_other, half).astype(F32) + bias_down).astype(BF)
     x_hat, x_rstd = normalize(tie(inputs, half).astype(F32))
     e_own = e_own * gain_attn
     grad_inputs = (
@@ -850,8 +859,13 @@
             - x_hat * jnp.mean(e_own * x_hat, axis=-1, keepdims=True)
         )
     ).astype(BF)
-    sum_wup, sum_wdown = unpack_call(bid, (feed_a, feed_b, last_a, tie(last_b, half)), (width, width))
-    sum_wqkv, sum_wproj = unpack_call(bid, (half, tie(last, sum_wup, grad_inputs)), (cols, inner))
+    pair = tuple(k * total_feed.shape[0] for k in range(2))
+    places = tuple((k, at) for k in range(4) for at in pair)
+    parts = (feed_first, feed_second, feed_got, tie(second_got, half))
+    sum_wup, sum_wdown = unpack_call(bid, parts, places, (width, width))
+    places = tuple((k, at * total_attn.shape[0]) for k in range(2) for at in range(4))
+    parts = (half, tie(last, sum_wup, grad_inputs))
+    sum_wqkv, sum_wproj = unpack_call(bid, parts, places, (cols, inner))
     return (
         output,
         grad_inputs,

time: 274 us -> 277 us (1.011)
  local copies, waits for them, and re-layouts: 12.4 us -> 17 us
  waiting for transfers between devices: 61.8 us -> 58.9 us
    ppermute x50 -> x51, waiting for transfers between devices: 61.8 us -> 58.9 us  [swap(): return lax.ppermute(x, axis, [(i, i ^ bits) for i in range(size)])]
    unnamed x75 -> x81, local copies, waits for them, and re-layouts: 4.87 us -> 7.34 us
    ppermute x50 -> x51, starting transfers between devices: 51.2 us -> 50.2 us  [swap(): return lax.ppermute(x, axis, [(i, i ^ bits) for i in range(size)])]
  transfers between devices with their start and end apart: 50 -> 51, of which waited for: 17 -> 18; matrix products, arithmetic and copies ran while one was open for 10% -> 11% of each run, Pallas kernels for 41% -> 41%
where the time goes in v6:
time: 277 us; the launch traced here: 275 us
  Pallas kernels  124 us (45%)
  waiting for transfers between devices  58.9 us (21%)
  starting transfers between devices  50.2 us (18%)
  other arithmetic  18.8 us (7%)
  local copies, waits for them, and re-layouts  17 us (6%)
  matrix products  4.54 us (2%)
    ppermute x51, waiting for transfers between devices, swap(): return lax.ppermute(x, axis, [(i, i ^ bits) for i in range(size)])  58.9 us
    ppermute x51, starting transfers between devices, swap(): return lax.ppermute(x, axis, [(i, i ^ bits) for i in range(size)])  50.2 us
    pallas_call x1, Pallas kernels, attend_back_call(): pl.pallas_call(functools.partial(attend_back_kernel, chunk, 1.0 / math.sq...  26.3 us
    pallas_call x2, Pallas kernels, attend_call(): pl.pallas_call(functools.partial(attend_kernel, heads, first, per, 1.0 /...  20.7 us
    pallas_call x2, Pallas kernels, feed_call(): pl.pallas_call(functools.partial(feed_kernel, steps), out_shape=(jax.Shap...  20 us
    pallas_call x2, Pallas kernels, qkv_call(): pl.pallas_call(functools.partial(qkv_kernel, heads, hd, steps), out_shape...  12.7 us
    pallas_call x1, Pallas kernels, weigh_call(): pl.pallas_call(functools.partial(weigh_kernel, tiles), out_shape=(half, h...  12.5 us
    pallas_call x1, Pallas kernels, tally_call(): pl.pallas_call(functools.partial(tally_kernel, steps), out_shape=(half, h...  7.74 us
  transfers between devices with their start and end apart: 51, of which 18 were waited for; matrix products, arithmetic and copies ran while one was open for 11% of the time, Pallas kernels for 41%

profile of v6, /device:TPU:0, one launch (start us, length us, event | category | flops | bytes accessed | tf_op | source)
XLA Modules:
  0.0 275.0 jit_solution(14487685365178969875)
XLA Ops:
  1.2 2.6 collective-permute-start
  10.1 6.4 %qkv.2 = (bf16[3,2048,64]{2,1,0:T(8,128)(2,1)}, bf16[3,2048,64]{2,1,0:T(8,128)(2,1)}, bf16[3,2048,64]{2,1,0:T(8,128)(2,1)}, bf16[3,64,2048]{2,1,0:T(8,128)(2,1)}, bf16[2048,768]{1,0:T(8,128)(2,1)}) custom-call(s32[1]{0:T(128)} %bitcast.1.h_ref, bf16[512,768]{1,0:T(8,128)(2,1)} %x_ref.1, bf16[512,768]{1,0:T(8,128)(2,1)} %copy-done.35, f32[8,768]{1,0:T(8,128)} %stack.31.v_ref, ...), custom_call_target="tpu_custom_call" | custom-call | flops 905969664 | bytes 4718592 | tf_op jit(solution)/shard_map/qkv/pallas_call | solution.py:84
  16.5 5.6 %collective-permute-done.a_ref = bf16[512,768]{1,0:T(8,128)(2,1)S(1)} collective-permute-done((bf16[512,768]{1,0:T(8,128)(2,1)}, bf16[512,768]{1,0:T(8,128)(2,1)S(1)}, u32[]{:S(2)}, u32[]{:S(2)}) %collective-permute-start) | collective-permute-done | bytes 786464 | tf_op jit(solution)/shard_map/ppermute | solution.py:38
  27.8 6.3 %qkv.3 = (bf16[3,2048,64]{2,1,0:T(8,128)(2,1)}, bf16[3,2048,64]{2,1,0:T(8,128)(2,1)}, bf16[3,2048,64]{2,1,0:T(8,128)(2,1)}, bf16[3,64,2048]{2,1,0:T(8,128)(2,1)}, bf16[2048,768]{1,0:T(8,128)(2,1)}) custom-call(s32[1]{0:T(128)} %bitcast.1.h_ref, ...), custom_call_target="tpu_custom_call", output_to_operand_aliasing={{0}: (6, {}), {1}: (7, {}), {2}: (8, {}), {3}: (9, {}), {4}... | custom-call | flops 905969664 | bytes 4718592 | tf_op jit(solution)/shard_map/qkv/pallas_call | solution.py:84
  34.1 9.7 %attend.2 = (bf16[512,192]{1,0:T(8,128)(2,1)}, bf16[512,192]{1,0:T(8,128)(2,1)}, f32[8,512]{1,0:T(8,128)}, f32[8,512]{1,0:T(8,128)}) custom-call(s32[8]{0:T(128)} %bitcast.29, s32[1]{0:T(128)} %bitcast.1.h_ref, bf16[3,2048,64]{2,1,0:T(8,128)(2,1)} %get-tuple-element.162.q_ref, bf16[3,2048,64]{2,1,0:T(8,128)(2,1)} %get-tuple-element.121.k_ref, ...), custom_call_target="tpu_custom_call" | custom-call | flops 3221225472 | bytes 4718592 | tf_op jit(solution)/shard_map/attend/pallas_call | solution.py:198
  43.8 3.1 %collective-permute-start.6 = (bf16[512,192]{1,0:T(8,128)(2,1)}, bf16[512,192]{1,0:T(8,128)(2,1)S(1)}, u32[]{:S(2)}, u32[]{:S(2)}) collective-permute-start(bf16[512,192]{1,0:T(8,128)(2,1)} %get-tuple-element.123.rest_6_), channel_id=1, source_target_pairs={{0,2},{1,3},{2,0},{3,1},{4,6},{5,7},{6,4},{7,5},{8,10},{9,11},{10,... | collective-permute-start | bytes 589832 | tf_op jit(solution)/shard_map/ppermute | solution.py:38
  46.9 4.7 %collective-permute-done.4.p2 = bf16[192,768]{1,0:T(8,128)(2,1)S(1)} collective-permute-done((bf16[192,768]{1,0:T(8,128)(2,1)S(1)}, bf16[192,768]{1,0:T(8,128)(2,1)S(1)}, u32[]{:S(2)}, u32[]{:S(2)}) %collective-permute-start.4) | collective-permute-done | bytes 294944 | tf_op jit(solution)/shard_map/ppermute | solution.py:38
  53.4 11.0 %attend.3 = (bf16[512,192]{1,0:T(8,128)(2,1)}, bf16[512,192]{1,0:T(8,128)(2,1)}, f32[8,512]{1,0:T(8,128)}, f32[8,512]{1,0:T(8,128)}) custom-call(s32[8]{0:T(128)} %bitcast.30, s32[1]{0:T(128)} %bitcast.1.h_ref, bf16[3,2048,64]{2,1,0:T(8,128)(2,1)} %get-tuple-element.162.q_ref, bf16[3,2048,64]{2,1,0:T(8,128)(2,1)} %get-tuple-element.121.k_ref, ...), custom_call_target="tpu_custom_call" | custom-call | flops 3221225472 | bytes 4718592 | tf_op jit(solution)/shard_map/attend/pallas_call | solution.py:198
  68.4 4.1 %mix.1 = (f32[512,768]{1,0:T(8,128)}, bf16[512,768]{1,0:T(8,128)(2,1)}) custom-call(bf16[512,192]{1,0:T(8,128)(2,1)} %get-tuple-element.127.m0.rest_4_, bf16[512,192]{1,0:T(8,128)(2,1)} %copy-done.15, bf16[512,192]{1,0:T(8,128)(2,1)} %copy-done.13, bf16[512,192]{1,0:T(8,128)(2,1)} %copy-done.17, bf16[192,768]{1,0:T(8,128)(2,1)} %bitcast.23, ...), custom_call_target="tpu_custom_call" | custom-call | flops 603979776 | bytes 4718592 | tf_op jit(solution)/shard_map/mix/pallas_call | solution.py:494
  76.0 10.0 %feed.2 = (bf16[2048,768]{1,0:T(8,128)(2,1)}, bf16[2048,768]{1,0:T(8,128)(2,1)}, bf16[512,768]{1,0:T(8,128)(2,1)}, bf16[512,768]{1,0:T(8,128)(2,1)}, bf16[512,768]{1,0:T(8,128)(2,1)}, /*index=5*/bf16[512,768]{1,0:T(8,128)(2,1)}) custom-call(bf16[512,768]{1,0:T(8,128)(2,1)} %get-tuple-element.134.ha_ref.h0, bf16[512,768]{1,0:T(8,128)(2,1)} %copy-done.30, ...), custom_call_target="tpu_custom_call" | custom-call | flops 4831838208 | bytes 6291456 | tf_op jit(solution)/shard_map/feed/pallas_call | solution.py:374
  86.0 6.7 %collective-permute-done.13.ha_ref.h2 = bf16[512,768]{1,0:T(8,128)(2,1)S(1)} collective-permute-done((bf16[512,768]{1,0:T(8,128)(2,1)}, bf16[512,768]{1,0:T(8,128)(2,1)S(1)}, u32[]{:S(2)}, u32[]{:S(2)}) %collective-permute-start.13) | collective-permute-done | bytes 786464 | tf_op jit(solution)/shard_map/ppermute | solution.py:38
  95.9 10.0 %feed.3 = (bf16[2048,768]{1,0:T(8,128)(2,1)}, bf16[2048,768]{1,0:T(8,128)(2,1)}, bf16[512,768]{1,0:T(8,128)(2,1)}, bf16[512,768]{1,0:T(8,128)(2,1)}, bf16[512,768]{1,0:T(8,128)(2,1)}, /*index=5*/bf16[512,768]{1,0:T(8,128)(2,1)}) custom-call(bf16[512,768]{1,0:T(8,128)(2,1)} %copy-done.31, ...), custom_call_target="tpu_custom_call", output_to_operand_aliasing={{0}: (7, {}), {1}: (8, {})} | custom-call | flops 4831838208 | bytes 6291456 | tf_op jit(solution)/shard_map/feed/pallas_call | solution.py:374
  106.1 2.4 collective-permute-done.16
  110.6 12.5 %weigh.1 = (bf16[768,768]{1,0:T(8,128)(2,1)}, bf16[768,768]{1,0:T(8,128)(2,1)}, f32[1,768]{1,0:T(1,128)}) custom-call(s32[1]{0:T(128)} %bitcast.5.b_ref, bf16[512,768]{1,0:T(8,128)(2,1)} %get-tuple-element.134.ha_ref.h0, bf16[512,768]{1,0:T(8,128)(2,1)} %copy-done.30, bf16[512,768]{1,0:T(8,128)(2,1)} %copy-done.31, bf16[512,768]{1,0:T(8,128)(2,1)} %copy-done.33, ...), custom_call_target="tpu_custom_call" | custom-call | flops 4831838208 | bytes 18874368 | tf_op jit(solution)/shard_map/weigh/pallas_call | solution.py:455
  123.2 3.1 %collective-permute-start.22 = (bf16[768,768]{1,0:T(8,128)(2,1)}, bf16[768,768]{1,0:T(8,128)(2,1)S(1)}, u32[]{:S(2)}, u32[]{:S(2)}) collective-permute-start(bf16[768,768]{1,0:T(8,128)(2,1)} %get-tuple-element.158), channel_id=1, source_target_pairs={{0,4},{4,0},{8,12},{12,8},{16,20},{20,16},{24,28},{28,24},{1,5},{5... | collective-permute-start | bytes 3538952 | tf_op jit(solution)/shard_map/ppermute | solution.py:38
  126.3 3.8 %collective-permute-done.19.f_ref = bf16[512,768]{1,0:T(8,128)(2,1)} collective-permute-done((bf16[512,768]{1,0:T(8,128)(2,1)S(1)}, bf16[512,768]{1,0:T(8,128)(2,1)}, u32[]{:S(2)}, u32[]{:S(2)}) %collective-permute-start.19) | collective-permute-done | bytes 786464 | tf_op jit(solution)/shard_map/ppermute | solution.py:38
  130.1 6.2 %turn.1 = (f32[512,768]{1,0:T(8,128)}, bf16[512,768]{1,0:T(8,128)(2,1)}, bf16[512,192]{1,0:T(8,128)(2,1)}, bf16[512,192]{1,0:T(8,128)(2,1)}, bf16[512,192]{1,0:T...) custom-call(bf16[512,768]{1,0:T(8,128)(2,1)} %get-tuple-element.144.n_ref, ...), custom_call_target="tpu_custom_call" | custom-call | flops 512 | bytes 768 | tf_op jit(solution)/shard_map/turn/pallas_call | solution.py:534
  143.3 7.6 %collective-permute-done.27 = bf16[512,192]{1,0:T(8,128)(2,1)S(1)} collective-permute-done((bf16[512,192]{1,0:T(8,128)(2,1)}, bf16[512,192]{1,0:T(8,128)(2,1)S(1)}, u32[]{:S(2)}, u32[]{:S(2)}) %collective-permute-start.27) | collective-permute-done | bytes 196640 | tf_op jit(solution)/shard_map/ppermute | solution.py:38
  154.6 2.8 %collective-permute-start.25 = (bf16[192,768]{1,0:T(8,128)(2,1)}, bf16[192,768]{1,0:T(8,128)(2,1)}, u32[]{:S(2)}, u32[]{:S(2)}) collective-permute-start(bf16[192,768]{1,0:T(8,128)(2,1)} %get-tuple-element.222), channel_id=1, source_target_pairs={{0,8},{4,12},{8,0},{12,4},{16,24},{20,28},{24,16},{28,20},{1,9},{5... | collective-permute-start | bytes 884744 | tf_op jit(solution)/shard_map/ppermute | solution.py:38
  164.0 26.3 %attend_back.1.gp_ref = bf16[2048,576]{1,0:T(8,128)(2,1)} custom-call(s32[8]{0:T(128)} %bitcast.31, s32[1]{0:T(128)} %bitcast.1.h_ref, bf16[3,2048,64]{2,1,0:T(8,128)(2,1)} %get-tuple-element.162.q_ref, bf16[3,2048,64]{2,1,0:T(8,128)(2,1)} %get-tuple-element.121.k_ref, bf16[3,2048,64]{2,1,0:T(8,128)(2,1)} %get-tuple-element.163.v_ref, ...), custom_call_target="tpu_custom_call" | custom-call | flops 16106127360 | bytes 11796480 | tf_op jit(solution)/shard_map/attend_back/pallas_call | solution.py:317
  191.7 5.9 %collective-permute-start.32 = (bf16[192,768]{1,0:T(8,128)(2,1)S(1)}, bf16[192,768]{1,0:T(8,128)(2,1)S(1)}, u32[]{:S(2)}, u32[]{:S(2)}) collective-permute-start(bf16[192,768]{1,0:T(8,128)(2,1)S(1)} %add_convert_fusion.6), channel_id=1, source_target_pairs={{0,16},{4,20},{8,24},{12,28},{16,0},{20,4},{24,8},{28,12},{1,17},{... | collective-permute-start | bytes 884744 | tf_op jit(solution)/shard_map/ppermute | solution.py:38
  199.4 7.7 %tally.1 = (bf16[392,768]{1,0:T(8,128)(2,1)}, bf16[392,768]{1,0:T(8,128)(2,1)}) custom-call(s32[1]{0:T(128)} %bitcast.5.b_ref, bf16[2048,576]{1,0:T(8,128)(2,1)} %attend_back.1.gp_ref, bf16[2048,768]{1,0:T(8,128)(2,1)} %get-tuple-element.175.hat_ref, bf16[576,768]{1,0:T(8,128)(2,1)} %bitcast.21, f32[8,768]{1,0:T(8,128)} %stack.31.v_ref, ...), custom_call_target="tpu_custom_call" | custom-call | flops 576 | bytes 768 | tf_op jit(solution)/shard_map/tally/pallas_call | solution.py:595
  209.2 6.8 %spread.1 = (bf16[512,768]{1,0:T(8,128)(2,1)}, bf16[512,768]{1,0:T(8,128)(2,1)}, bf16[512,768]{1,0:T(8,128)(2,1)}, bf16[512,768]{1,0:T(8,128)(2,1)}) custom-call(bf16[2048,576]{1,0:T(8,128)(2,1)} %attend_back.1.gp_ref, bf16[576,768]{1,0:T(8,128)(2,1)} %bitcast.22), custom_call_target="tpu_custom_call" | custom-call | flops 576 | bytes 768 | tf_op jit(solution)/shard_map/spread/pallas_call | solution.py:626
  216.0 4.1 %collective-permute-done.32 = bf16[192,768]{1,0:T(8,128)(2,1)S(1)} collective-permute-done((bf16[192,768]{1,0:T(8,128)(2,1)S(1)}, bf16[192,768]{1,0:T(8,128)(2,1)S(1)}, u32[]{:S(2)}, u32[]{:S(2)}) %collective-permute-start.32) | collective-permute-done | bytes 294944 | tf_op jit(solution)/shard_map/ppermute | solution.py:38
  222.8 3.2 %collective-permute-start.39 = (bf16[384,768]{1,0:T(8,128)(2,1)S(1)}, bf16[384,768]{1,0:T(8,128)(2,1)S(1)}, u32[]{:S(2)}, u32[]{:S(2)}) collective-permute-start(bf16[384,768]{1,0:T(8,128)(2,1)S(1)} %pad_maximum_fusion.rest_0_), channel_id=1, source_target_pairs={{0,4},{4,0},{8,12},{12,8},{16,20},{20,16},{24,28},{28,24},{1,5},{5... | collective-permute-start | bytes 1769480 | tf_op jit(solution)/shard_map/ppermute | solution.py:38
  227.3 3.2 %collective-permute-start.38 = (bf16[104,768]{1,0:T(8,128)(2,1)S(1)}, bf16[104,768]{1,0:T(8,128)(2,1)S(1)}, u32[]{:S(2)}, u32[]{:S(2)}) collective-permute-start(bf16[104,768]{1,0:T(8,128)(2,1)S(1)} %get-tuple-element.228), channel_id=1, source_target_pairs={{0,8},{4,12},{8,0},{12,4},{16,24},{20,28},{24,16},{28,20},{1,9},{5... | collective-permute-start | bytes 479240 | tf_op jit(solution)/shard_map/ppermute | solution.py:38
  231.5 2.5 add_convert_fusion.1
  234.0 6.0 %collective-permute-done.39.rest_2_ = bf16[384,768]{1,0:T(8,128)(2,1)S(1)} collective-permute-done((bf16[384,768]{1,0:T(8,128)(2,1)S(1)}, bf16[384,768]{1,0:T(8,128)(2,1)S(1)}, u32[]{:S(2)}, u32[]{:S(2)}) %collective-permute-start.39) | collective-permute-done | bytes 589856 | tf_op jit(solution)/shard_map/ppermute | solution.py:38
  243.4 2.9 %collective-permute-start.42 = (bf16[96,768]{1,0:T(8,128)(2,1)S(1)}, bf16[96,768]{1,0:T(8,128)(2,1)S(1)}, u32[]{:S(2)}, u32[]{:S(2)}) collective-permute-start(bf16[96,768]{1,0:T(8,128)(2,1)S(1)} %add_convert_fusion.7), channel_id=1, source_target_pairs={{0,8},{4,12},{8,0},{12,4},{16,24},{20,28},{24,16},{28,20},{1,9},{5... | collective-permute-start | bytes 442376 | tf_op jit(solution)/shard_map/ppermute | solution.py:38
  250.8 5.6 %collective-permute-done.43.rest_3_ = bf16[384,768]{1,0:T(8,128)(2,1)S(1)} collective-permute-done((bf16[384,768]{1,0:T(8,128)(2,1)S(1)}, bf16[384,768]{1,0:T(8,128)(2,1)S(1)}, u32[]{:S(2)}, u32[]{:S(2)}) %collective-permute-start.43) | collective-permute-done | bytes 589856 | tf_op jit(solution)/shard_map/ppermute | solution.py:38
  262.2 4.2 %unpack.2 = (f32[768,768]{1,0:T(8,128)}, f32[768,768]{1,0:T(8,128)}) custom-call(s32[1]{0:T(128)} %bitcast.5.b_ref, bf16[384,768]{1,0:T(8,128)(2,1)} %copy-done.5, bf16[384,768]{1,0:T(8,128)(2,1)} %copy-done.7, bf16[384,768]{1,0:T(8,128)(2,1)} %copy-done.26, bf16[384,768]{1,0:T(8,128)(2,1)} %copy-done.27), custom_call_target="tpu_custom_call" | custom-call | flops 1536 | bytes 768 | tf_op jit(solution)/shard_map/unpack/pallas_call | solution.py:653
  272.1 2.9 %unpack.3 = (f32[576,768]{1,0:T(8,128)}, f32[192,768]{1,0:T(8,128)}) custom-call(s32[1]{0:T(128)} %bitcast.5.b_ref, bf16[384,768]{1,0:T(8,128)(2,1)} %pad_maximum_fusion.1.rest_0_, bf16[384,768]{1,0:T(8,128)(2,1)} %collective-permute-done.50.rest_1_), custom_call_target="tpu_custom_call" | custom-call | flops 768 | bytes 768 | tf_op jit(solution)/shard_map/unpack/pallas_call | solution.py:653
  (212 shorter events, 73.8 us)
Async XLA Ops:
  1.2 20.9 %collective-permute-start = (bf16[512,768]{1,0:T(8,128)(2,1)}, bf16[512,768]{1,0:T(8,128)(2,1)S(1)}, u32[]{:S(2)}, u32[]{:S(2)}) collective-permute-start(bf16[512,768]{1,0:T(8,128)(2,1)} %x_ref.1), channel_id=1, source_target_pairs={{0,2},{1,3},{2,0},{3,1},{4,6},{5,7},{6,4},{7,5},{8,10},{9,11},{10,... | collective-permute-start | bytes 2359304 | tf_op jit(solution)/shard_map/ppermute | solution.py:38
  24.8 26.8 %collective-permute-start.3 = (bf16[512,768]{1,0:T(8,128)(2,1)S(1)}, bf16[512,768]{1,0:T(8,128)(2,1)}, u32[]{:S(2)}, u32[]{:S(2)}) collective-permute-start(bf16[512,768]{1,0:T(8,128)(2,1)S(1)} %broadcast_select_fusion.ga_ref.g0.cot_ref), channel_id=1, source_target_pairs={{0,2},{1,3},{2,0},{3,1},{4,6},{5,7},{6,4},{7,5},{8,10},{9,11},{10,... | collective-permute-start | bytes 2359304 | tf_op jit(solution)/shard_map/ppermute | solution.py:38
  26.6 25.0 %collective-permute-start.4 = (bf16[192,768]{1,0:T(8,128)(2,1)S(1)}, bf16[192,768]{1,0:T(8,128)(2,1)S(1)}, u32[]{:S(2)}, u32[]{:S(2)}) collective-permute-start(bf16[192,768]{1,0:T(8,128)(2,1)S(1)} %bitcast.25), channel_id=1, source_target_pairs={{0,2},{1,3},{2,0},{3,1},{4,6},{5,7},{6,4},{7,5},{8,10},{9,11},{10,... | collective-permute-start | bytes 884744 | tf_op jit(solution)/shard_map/ppermute | solution.py:38
  43.8 21.2 %collective-permute-start.6 = (bf16[512,192]{1,0:T(8,128)(2,1)}, bf16[512,192]{1,0:T(8,128)(2,1)S(1)}, u32[]{:S(2)}, u32[]{:S(2)}) collective-permute-start(bf16[512,192]{1,0:T(8,128)(2,1)} %get-tuple-element.123.rest_6_), channel_id=1, source_target_pairs={{0,2},{1,3},{2,0},{3,1},{4,6},{5,7},{6,4},{7,5},{8,10},{9,11},{10,... | collective-permute-start | bytes 589832 | tf_op jit(solution)/shard_map/ppermute | solution.py:38
  51.6 13.4 %collective-permute-start.7 = (bf16[512,192]{1,0:T(8,128)(2,1)}, bf16[512,192]{1,0:T(8,128)(2,1)S(1)}, u32[]{:S(2)}, u32[]{:S(2)}) collective-permute-start(bf16[512,192]{1,0:T(8,128)(2,1)} %get-tuple-element.129.rest_7_), channel_id=1, source_target_pairs={{0,2},{1,3},{2,0},{3,1},{4,6},{5,7},{6,4},{7,5},{8,10},{9,11},{10,... | collective-permute-start | bytes 589832 | tf_op jit(solution)/shard_map/ppermute | solution.py:38
  72.7 20.0 %collective-permute-start.13 = (bf16[512,768]{1,0:T(8,128)(2,1)}, bf16[512,768]{1,0:T(8,128)(2,1)S(1)}, u32[]{:S(2)}, u32[]{:S(2)}) collective-permute-start(bf16[512,768]{1,0:T(8,128)(2,1)} %get-tuple-element.134.ha_ref.h0), channel_id=1, source_target_pairs={{0,2},{1,3},{2,0},{3,1},{4,6},{5,7},{6,4},{7,5},{8,10},{9,11},{10,... | collective-permute-start | bytes 2359304 | tf_op jit(solution)/shard_map/ppermute | solution.py:38
  72.7 20.0 %collective-permute-start.15 = (bf16[512,768]{1,0:T(8,128)(2,1)}, bf16[512,768]{1,0:T(8,128)(2,1)S(1)}, u32[]{:S(2)}, u32[]{:S(2)}) collective-permute-start(bf16[512,768]{1,0:T(8,128)(2,1)} %collective-permute-done.3.ga_ref.g2), channel_id=1, source_target_pairs={{0,1},{1,0},{2,3},{3,2},{4,5},{5,4},{6,7},{7,6},{8,9},{9,8},{10,11... | collective-permute-start | bytes 2359304 | tf_op jit(solution)/shard_map/ppermute | solution.py:38
  109.8 16.5 %collective-permute-start.17 = (bf16[512,768]{1,0:T(8,128)(2,1)}, bf16[512,768]{1,0:T(8,128)(2,1)}, u32[]{:S(2)}, u32[]{:S(2)}) collective-permute-start(bf16[512,768]{1,0:T(8,128)(2,1)} %get-tuple-element.142), channel_id=1, source_target_pairs={{0,1},{1,0},{2,3},{3,2},{4,5},{5,4},{6,7},{7,6},{8,9},{9,8},{10,11... | collective-permute-start | bytes 2359304 | tf_op jit(solution)/shard_map/ppermute | solution.py:38
  110.0 16.3 %collective-permute-start.20 = (bf16[512,768]{1,0:T(8,128)(2,1)}, bf16[512,768]{1,0:T(8,128)(2,1)S(1)}, u32[]{:S(2)}, u32[]{:S(2)}) collective-permute-start(bf16[512,768]{1,0:T(8,128)(2,1)} %get-tuple-element.151), channel_id=1, source_target_pairs={{0,1},{1,0},{2,3},{3,2},{4,5},{5,4},{6,7},{7,6},{8,9},{9,8},{10,11... | collective-permute-start | bytes 2359304 | tf_op jit(solution)/shard_map/ppermute | solution.py:38
  110.4 19.7 %collective-permute-start.19 = (bf16[512,768]{1,0:T(8,128)(2,1)S(1)}, bf16[512,768]{1,0:T(8,128)(2,1)}, u32[]{:S(2)}, u32[]{:S(2)}) collective-permute-start(bf16[512,768]{1,0:T(8,128)(2,1)S(1)} %add_convert_fusion.4), channel_id=1, source_target_pairs={{0,2},{1,3},{2,0},{3,1},{4,6},{5,7},{6,4},{7,5},{8,10},{9,11},{10,... | collective-permute-start | bytes 2359304 | tf_op jit(solution)/shard_map/ppermute | solution.py:38
  110.6 19.4 %collective-permute-start.18 = (bf16[512,768]{1,0:T(8,128)(2,1)}, bf16[512,768]{1,0:T(8,128)(2,1)}, u32[]{:S(2)}, u32[]{:S(2)}) collective-permute-start(bf16[512,768]{1,0:T(8,128)(2,1)} %get-tuple-element.145), channel_id=1, source_target_pairs={{0,1},{1,0},{2,3},{3,2},{4,5},{5,4},{6,7},{7,6},{8,9},{9,8},{10,11... | collective-permute-start | bytes 2359304 | tf_op jit(solution)/shard_map/ppermute | solution.py:38
  123.2 29.9 %collective-permute-start.22 = (bf16[768,768]{1,0:T(8,128)(2,1)}, bf16[768,768]{1,0:T(8,128)(2,1)S(1)}, u32[]{:S(2)}, u32[]{:S(2)}) collective-permute-start(bf16[768,768]{1,0:T(8,128)(2,1)} %get-tuple-element.158), channel_id=1, source_target_pairs={{0,4},{4,0},{8,12},{12,8},{16,20},{20,16},{24,28},{28,24},{1,5},{5... | collective-permute-start | bytes 3538952 | tf_op jit(solution)/shard_map/ppermute | solution.py:38
  136.4 14.5 %collective-permute-start.23 = (bf16[512,192]{1,0:T(8,128)(2,1)}, bf16[512,192]{1,0:T(8,128)(2,1)S(1)}, u32[]{:S(2)}, u32[]{:S(2)}) collective-permute-start(bf16[512,192]{1,0:T(8,128)(2,1)} %get-tuple-element.159), channel_id=1, source_target_pairs={{0,2},{1,3},{2,0},{3,1},{4,6},{5,7},{6,4},{7,5},{8,10},{9,11},{10,... | collective-permute-start | bytes 589832 | tf_op jit(solution)/shard_map/ppermute | solution.py:38
  136.7 14.2 %collective-permute-start.27 = (bf16[512,192]{1,0:T(8,128)(2,1)}, bf16[512,192]{1,0:T(8,128)(2,1)S(1)}, u32[]{:S(2)}, u32[]{:S(2)}) collective-permute-start(bf16[512,192]{1,0:T(8,128)(2,1)} %get-tuple-element.165), channel_id=1, source_target_pairs={{0,2},{1,3},{2,0},{3,1},{4,6},{5,7},{6,4},{7,5},{8,10},{9,11},{10,... | collective-permute-start | bytes 589832 | tf_op jit(solution)/shard_map/ppermute | solution.py:38
  140.1 17.3 %collective-permute-start.26 = (bf16[192,768]{1,0:T(8,128)(2,1)S(1)}, bf16[192,768]{1,0:T(8,128)(2,1)S(1)}, u32[]{:S(2)}, u32[]{:S(2)}) collective-permute-start(bf16[192,768]{1,0:T(8,128)(2,1)S(1)} %convolution_convert_fusion.1), channel_id=1, source_target_pairs={{0,1},{1,0},{2,3},{3,2},{4,5},{5,4},{6,7},{7,6},{8,9},{9,8},{10,11... | collective-permute-start | bytes 884744 | tf_op jit(solution)/shard_map/ppermute | solution.py:38
  141.7 18.1 %collective-permute-start.34 = (bf16[192,768]{1,0:T(8,128)(2,1)S(1)}, bf16[192,768]{1,0:T(8,128)(2,1)S(1)}, u32[]{:S(2)}, u32[]{:S(2)}) collective-permute-start(bf16[192,768]{1,0:T(8,128)(2,1)S(1)} %convolution_convert_fusion), channel_id=1, source_target_pairs={{0,1},{1,0},{2,3},{3,2},{4,5},{5,4},{6,7},{7,6},{8,9},{9,8},{10,11... | collective-permute-start | bytes 884744 | tf_op jit(solution)/shard_map/ppermute | solution.py:38
  154.2 45.2 %collective-permute-start.24 = (bf16[512,768]{1,0:T(8,128)(2,1)}, bf16[512,768]{1,0:T(8,128)(2,1)S(1)}, u32[]{:S(2)}, u32[]{:S(2)}) collective-permute-start(bf16[512,768]{1,0:T(8,128)(2,1)} %add_convert_fusion.3), channel_id=1, source_target_pairs={{0,2},{1,3},{2,0},{3,1},{4,6},{5,7},{6,4},{7,5},{8,10},{9,11},{10,... | collective-permute-start | bytes 2359304 | tf_op jit(solution)/shard_map/ppermute | solution.py:38
  154.6 35.7 %collective-permute-start.25 = (bf16[192,768]{1,0:T(8,128)(2,1)}, bf16[192,768]{1,0:T(8,128)(2,1)}, u32[]{:S(2)}, u32[]{:S(2)}) collective-permute-start(bf16[192,768]{1,0:T(8,128)(2,1)} %get-tuple-element.222), channel_id=1, source_target_pairs={{0,8},{4,12},{8,0},{12,4},{16,24},{20,28},{24,16},{28,20},{1,9},{5... | collective-permute-start | bytes 884744 | tf_op jit(solution)/shard_map/ppermute | solution.py:38
  157.4 32.9 %collective-permute-start.30 = (bf16[192,768]{1,0:T(8,128)(2,1)S(1)}, bf16[192,768]{1,0:T(8,128)(2,1)}, u32[]{:S(2)}, u32[]{:S(2)}) collective-permute-start(bf16[192,768]{1,0:T(8,128)(2,1)S(1)} %get-tuple-element.223), channel_id=1, source_target_pairs={{0,24},{4,28},{8,16},{12,20},{16,8},{20,12},{24,0},{28,4},{1,25},{... | collective-permute-start | bytes 884744 | tf_op jit(solution)/shard_map/ppermute | solution.py:38
  159.8 30.5 %collective-permute-start.29 = (bf16[192,768]{1,0:T(8,128)(2,1)S(1)}, bf16[192,768]{1,0:T(8,128)(2,1)}, u32[]{:S(2)}, u32[]{:S(2)}) collective-permute-start(bf16[192,768]{1,0:T(8,128)(2,1)S(1)} %get-tuple-element.224), channel_id=1, source_target_pairs={{0,16},{4,20},{8,24},{12,28},{16,0},{20,4},{24,8},{28,12},{1,17},{... | collective-permute-start | bytes 884744 | tf_op jit(solution)/shard_map/ppermute | solution.py:38
  162.2 35.4 %collective-permute-start.35 = (bf16[192,768]{1,0:T(8,128)(2,1)}, bf16[192,768]{1,0:T(8,128)(2,1)}, u32[]{:S(2)}, u32[]{:S(2)}) collective-permute-start(bf16[192,768]{1,0:T(8,128)(2,1)} %fusion.10), channel_id=1, source_target_pairs={{0,2},{1,3},{2,0},{3,1},{4,6},{5,7},{6,4},{7,5},{8,10},{9,11},{10,... | collective-permute-start | bytes 884744 | tf_op jit(solution)/shard_map/ppermute | solution.py:38
  191.6 24.4 %collective-permute-start.33 = (bf16[192,768]{1,0:T(8,128)(2,1)S(1)}, bf16[192,768]{1,0:T(8,128)(2,1)S(1)}, u32[]{:S(2)}, u32[]{:S(2)}) collective-permute-start(bf16[192,768]{1,0:T(8,128)(2,1)S(1)} %add_convert_fusion.6), channel_id=1, source_target_pairs={{0,24},{4,28},{8,16},{12,20},{16,8},{20,12},{24,0},{28,4},{1,25},{... | collective-permute-start | bytes 884744 | tf_op jit(solution)/shard_map/ppermute | solution.py:38
  191.7 28.4 %collective-permute-start.32 = (bf16[192,768]{1,0:T(8,128)(2,1)S(1)}, bf16[192,768]{1,0:T(8,128)(2,1)S(1)}, u32[]{:S(2)}, u32[]{:S(2)}) collective-permute-start(bf16[192,768]{1,0:T(8,128)(2,1)S(1)} %add_convert_fusion.6), channel_id=1, source_target_pairs={{0,16},{4,20},{8,24},{12,28},{16,0},{20,4},{24,8},{28,12},{1,17},{... | collective-permute-start | bytes 884744 | tf_op jit(solution)/shard_map/ppermute | solution.py:38
  197.6 22.6 %collective-permute-start.31 = (bf16[192,768]{1,0:T(8,128)(2,1)S(1)}, bf16[192,768]{1,0:T(8,128)(2,1)}, u32[]{:S(2)}, u32[]{:S(2)}) collective-permute-start(bf16[192,768]{1,0:T(8,128)(2,1)S(1)} %add_convert_fusion.6), channel_id=1, source_target_pairs={{0,8},{4,12},{8,0},{12,4},{16,24},{20,28},{24,16},{28,20},{1,9},{5... | collective-permute-start | bytes 884744 | tf_op jit(solution)/shard_map/ppermute | solution.py:38
  207.1 14.3 %collective-permute-start.36 = (bf16[392,768]{1,0:T(8,128)(2,1)}, bf16[392,768]{1,0:T(8,128)(2,1)S(1)}, u32[]{:S(2)}, u32[]{:S(2)}) collective-permute-start(bf16[392,768]{1,0:T(8,128)(2,1)} %get-tuple-element.186), channel_id=1, source_target_pairs={{0,4},{4,0},{8,12},{12,8},{16,20},{20,16},{24,28},{28,24},{1,5},{5... | collective-permute-start | bytes 1806344 | tf_op jit(solution)/shard_map/ppermute | solution.py:38
  222.8 17.2 %collective-permute-start.39 = (bf16[384,768]{1,0:T(8,128)(2,1)S(1)}, bf16[384,768]{1,0:T(8,128)(2,1)S(1)}, u32[]{:S(2)}, u32[]{:S(2)}) collective-permute-start(bf16[384,768]{1,0:T(8,128)(2,1)S(1)} %pad_maximum_fusion.rest_0_), channel_id=1, source_target_pairs={{0,4},{4,0},{8,12},{12,8},{16,20},{20,16},{24,28},{28,24},{1,5},{5... | collective-permute-start | bytes 1769480 | tf_op jit(solution)/shard_map/ppermute | solution.py:38
  226.0 14.0 %collective-permute-start.41 = (bf16[104,768]{1,0:T(8,128)(2,1)S(1)}, bf16[104,768]{1,0:T(8,128)(2,1)S(1)}, u32[]{:S(2)}, u32[]{:S(2)}) collective-permute-start(bf16[104,768]{1,0:T(8,128)(2,1)S(1)} %concatenate.24), channel_id=1, source_target_pairs={{0,24},{4,28},{8,16},{12,20},{16,8},{20,12},{24,0},{28,4},{1,25},{... | collective-permute-start | bytes 479240 | tf_op jit(solution)/shard_map/ppermute | solution.py:38
  227.3 13.7 %collective-permute-start.40 = (bf16[104,768]{1,0:T(8,128)(2,1)S(1)}, bf16[104,768]{1,0:T(8,128)(2,1)S(1)}, u32[]{:S(2)}, u32[]{:S(2)}) collective-permute-start(bf16[104,768]{1,0:T(8,128)(2,1)S(1)} %get-tuple-element.227), channel_id=1, source_target_pairs={{0,16},{4,20},{8,24},{12,28},{16,0},{20,4},{24,8},{28,12},{1,17},{... | collective-permute-start | bytes 479240 | tf_op jit(solution)/shard_map/ppermute | solution.py:38
  227.3 13.7 %collective-permute-start.38 = (bf16[104,768]{1,0:T(8,128)(2,1)S(1)}, bf16[104,768]{1,0:T(8,128)(2,1)S(1)}, u32[]{:S(2)}, u32[]{:S(2)}) collective-permute-start(bf16[104,768]{1,0:T(8,128)(2,1)S(1)} %get-tuple-element.228), channel_id=1, source_target_pairs={{0,8},{4,12},{8,0},{12,4},{16,24},{20,28},{24,16},{28,20},{1,9},{5... | collective-permute-start | bytes 479240 | tf_op jit(solution)/shard_map/ppermute | solution.py:38
  241.0 15.3 %collective-permute-start.43 = (bf16[384,768]{1,0:T(8,128)(2,1)S(1)}, bf16[384,768]{1,0:T(8,128)(2,1)S(1)}, u32[]{:S(2)}, u32[]{:S(2)}) collective-permute-start(bf16[384,768]{1,0:T(8,128)(2,1)S(1)} %constant_dynamic-update-slice_fusion.rest_1_), channel_id=1, source_target_pairs={{0,4},{4,0},{8,12},{12,8},{16,20},{20,16},{24,28},{28,24},{1,5},{5... | collective-permute-start | bytes 1769480 | tf_op jit(solution)/shard_map/ppermute | solution.py:38
  248.4 19.4 %collective-permute-start.47 = (bf16[512,768]{1,0:T(8,128)(2,1)}, bf16[512,768]{1,0:T(8,128)(2,1)S(1)}, u32[]{:S(2)}, u32[]{:S(2)}) collective-permute-start(bf16[512,768]{1,0:T(8,128)(2,1)} %add_convert_fusion.2), channel_id=1, source_target_pairs={{0,2},{1,3},{2,0},{3,1},{4,6},{5,7},{6,4},{7,5},{8,10},{9,11},{10,... | collective-permute-start | bytes 2359304 | tf_op jit(solution)/shard_map/ppermute | solution.py:38
  257.4 14.7 %collective-permute-start.50 = (bf16[384,768]{1,0:T(8,128)(2,1)}, bf16[384,768]{1,0:T(8,128)(2,1)}, u32[]{:S(2)}, u32[]{:S(2)}) collective-permute-start(bf16[384,768]{1,0:T(8,128)(2,1)} %pad_maximum_fusion.1.rest_0_), channel_id=1, source_target_pairs={{0,4},{4,0},{8,12},{12,8},{16,20},{20,16},{24,28},{28,24},{1,5},{5... | collective-permute-start | bytes 1769480 | tf_op jit(solution)/shard_map/ppermute | solution.py:38
  (59 other events, 388.0 us)

commit v7 on v6

--- a/solution.py
+++ b/solution.py
@@ -220,7 +220,7 @@
                 pltpu.VMEM((heads, hd, BLK), F32),
             ],
         ),
-        cost_estimate=cost(heads * rows * rows * hd * 4, 12 * rows * heads * hd, heads * rows * rows // 4),
+        cost_estimate=cost(rows, hd),
         name="attend",
     )(lengths, hid, q, k, vt)
 
@@ -738,22 +738,23 @@
         hid, x_far, x_last, vectors, qkv_t, bias_qkv, 2, group_rows, begun
     )
     grad_own = jnp.where(live, cotangent, jnp.zeros_like(cotangent))
-    grad_far = swap(tie(grad_own, x_far), "head", 2)
     proj_far = swap(tie(proj, x_far), "head", 2)
+    grad_far = swap(tie(grad_own, x_last), "head", 2)
+
     out_far, out_last, level_far, level_last = attend_call(
         lens, hid, queries, keys, values_t, 2, chunk
     )
     from_last = swap(out_last, "head", 2)
     from_far = swap(out_far, "head", 2)
     out_own, out_mate, level_own, level_mate = attend_call(
-        lens, hid, tie(queries, out_far, grad_far, proj_far), keys, values_t, 0, chunk
-    )
-    grads = (grad_own, swap(grad_own, "head", 1), grad_far, swap(grad_far, "head", 1))
+        lens, hid, tie(queries, out_far), keys, values_t, 0, chunk
+    )
+    grads = (grad_own, swap(tie(grad_own, out_far), "head", 1), grad_far, swap(grad_far, "head", 1))
     from_last = swap(tie(from_last, out_own, from_far), "head", 1)
     parts = (out_own, swap(out_mate, "head", 1), from_far, from_last)
     proj_last = swap(tie(proj_far, out_own), "head", 1)
     projs = (proj, swap(tie(proj, out_far), "head", 1), proj_far, proj_last)
-    resid, h_own = mix_call(parts, projs, inputs, vectors)
+    resid, h_own = mix_call(parts, projs, tie(inputs, grad_far), vectors)
     h_far = swap(h_own, "head", 2)
     h_near = swap(h_own, "head", 1)
 

time: 277 us -> 272 us (0.982)
  starting transfers between devices: 50.2 us -> 41.5 us
  Pallas kernels: 124 us -> 129 us
    ppermute x51, starting transfers between devices: 50.2 us -> 41.5 us  [swap(): return lax.ppermute(x, axis, [(i, i ^ bits) for i in range(size)])]
  transfers between devices with their start and end apart: 51 -> 51, of which waited for: 18 -> 15; matrix products, arithmetic and copies ran while one was open for 11% -> 12% of each run, Pallas kernels for 41% -> 43%
where the time goes in v7:
time: 272 us; the launch traced here: 270 us
  Pallas kernels  129 us (47%)
  waiting for transfers between devices  59.2 us (22%)
  starting transfers between devices  41.5 us (15%)
  other arithmetic  18.8 us (7%)
  local copies, waits for them, and re-layouts  15.7 us (6%)
  matrix products  4.54 us (2%)
    ppermute x51, waiting for transfers between devices, swap(): return lax.ppermute(x, axis, [(i, i ^ bits) for i in range(size)])  59.2 us
    ppermute x51, starting transfers between devices, swap(): return lax.ppermute(x, axis, [(i, i ^ bits) for i in range(size)])  41.5 us
    pallas_call x1, Pallas kernels, attend_back_call(): pl.pallas_call(functools.partial(attend_back_kernel, chunk, 1.0 / math.sq...  29 us
    pallas_call x2, Pallas kernels, attend_call(): pl.pallas_call(functools.partial(attend_kernel, heads, first, per, 1.0 /...  22.7 us
    pallas_call x2, Pallas kernels, feed_call(): pl.pallas_call(functools.partial(feed_kernel, steps), out_shape=(jax.Shap...  20 us
    pallas_call x2, Pallas kernels, qkv_call(): pl.pallas_call(functools.partial(qkv_kernel, heads, hd, steps), out_shape...  12.8 us
    pallas_call x1, Pallas kernels, weigh_call(): pl.pallas_call(functools.partial(weigh_kernel, tiles), out_shape=(half, h...  12.5 us
    pallas_call x1, Pallas kernels, tally_call(): pl.pallas_call(functools.partial(tally_kernel, steps), out_shape=(half, h...  7.74 us
  transfers between devices with their start and end apart: 51, of which 15 were waited for; matrix products, arithmetic and copies ran while one was open for 12% of the time, Pallas kernels for 43%

profile of v7, /device:TPU:0, one launch (start us, length us, event | category | flops | bytes accessed | tf_op | source)
XLA Modules:
  0.0 270.1 jit_solution(9650672277494030394)
XLA Ops:
  1.2 2.6 collective-permute-start
  10.1 6.4 %qkv.2 = (bf16[3,2048,64]{2,1,0:T(8,128)(2,1)}, bf16[3,2048,64]{2,1,0:T(8,128)(2,1)}, bf16[3,2048,64]{2,1,0:T(8,128)(2,1)}, bf16[3,64,2048]{2,1,0:T(8,128)(2,1)}, bf16[2048,768]{1,0:T(8,128)(2,1)}) custom-call(s32[1]{0:T(128)} %bitcast.1.h_ref, bf16[512,768]{1,0:T(8,128)(2,1)} %x_ref, bf16[512,768]{1,0:T(8,128)(2,1)} %copy-done.36, f32[8,768]{1,0:T(8,128)} %stack.31.v_ref, ...), custom_call_target="tpu_custom_call" | custom-call | flops 905969664 | bytes 4718592 | tf_op jit(solution)/shard_map/qkv/pallas_call | solution.py:84
  16.5 5.6 %collective-permute-done.a_ref = bf16[512,768]{1,0:T(8,128)(2,1)S(1)} collective-permute-done((bf16[512,768]{1,0:T(8,128)(2,1)}, bf16[512,768]{1,0:T(8,128)(2,1)S(1)}, u32[]{:S(2)}, u32[]{:S(2)}) %collective-permute-start) | collective-permute-done | bytes 786464 | tf_op jit(solution)/shard_map/ppermute | solution.py:38
  26.9 6.4 %qkv.3 = (bf16[3,2048,64]{2,1,0:T(8,128)(2,1)}, bf16[3,2048,64]{2,1,0:T(8,128)(2,1)}, bf16[3,2048,64]{2,1,0:T(8,128)(2,1)}, bf16[3,64,2048]{2,1,0:T(8,128)(2,1)}, bf16[2048,768]{1,0:T(8,128)(2,1)}) custom-call(s32[1]{0:T(128)} %bitcast.1.h_ref, ...), custom_call_target="tpu_custom_call", output_to_operand_aliasing={{0}: (6, {}), {1}: (7, {}), {2}: (8, {}), {3}: (9, {}), {4}... | custom-call | flops 905969664 | bytes 4718592 | tf_op jit(solution)/shard_map/qkv/pallas_call | solution.py:84
  33.3 13.7 %attend.2 = (bf16[512,192]{1,0:T(8,128)(2,1)}, bf16[512,192]{1,0:T(8,128)(2,1)}, f32[8,512]{1,0:T(8,128)}, f32[8,512]{1,0:T(8,128)}) custom-call(s32[8]{0:T(128)} %bitcast.27, s32[1]{0:T(128)} %bitcast.1.h_ref, bf16[3,2048,64]{2,1,0:T(8,128)(2,1)} %get-tuple-element.166.q_ref, bf16[3,2048,64]{2,1,0:T(8,128)(2,1)} %get-tuple-element.123.k_ref, ...), custom_call_target="tpu_custom_call" | custom-call | flops 2048 | bytes 64 | tf_op jit(solution)/shard_map/attend/pallas_call | solution.py:198
  49.1 9.0 %attend.3 = (bf16[512,192]{1,0:T(8,128)(2,1)}, bf16[512,192]{1,0:T(8,128)(2,1)}, f32[8,512]{1,0:T(8,128)}, f32[8,512]{1,0:T(8,128)}) custom-call(s32[8]{0:T(128)} %bitcast.28, s32[1]{0:T(128)} %bitcast.1.h_ref, bf16[3,2048,64]{2,1,0:T(8,128)(2,1)} %get-tuple-element.166.q_ref, bf16[3,2048,64]{2,1,0:T(8,128)(2,1)} %get-tuple-element.123.k_ref, ...), custom_call_target="tpu_custom_call" | custom-call | flops 2048 | bytes 64 | tf_op jit(solution)/shard_map/attend/pallas_call | solution.py:198
  58.8 3.5 %collective-permute-done.4.m2 = bf16[512,192]{1,0:T(8,128)(2,1)S(1)} collective-permute-done((bf16[512,192]{1,0:T(8,128)(2,1)}, bf16[512,192]{1,0:T(8,128)(2,1)S(1)}, u32[]{:S(2)}, u32[]{:S(2)}) %collective-permute-start.4) | collective-permute-done | bytes 196640 | tf_op jit(solution)/shard_map/ppermute | solution.py:38
  64.6 4.1 %mix.1 = (f32[512,768]{1,0:T(8,128)}, bf16[512,768]{1,0:T(8,128)(2,1)}) custom-call(bf16[512,192]{1,0:T(8,128)(2,1)} %get-tuple-element.127.m0.rest_4_, bf16[512,192]{1,0:T(8,128)(2,1)} %copy-done.15, bf16[512,192]{1,0:T(8,128)(2,1)} %copy-done.13, bf16[512,192]{1,0:T(8,128)(2,1)} %copy-done.17, bf16[192,768]{1,0:T(8,128)(2,1)} %bitcast.23, ...), custom_call_target="tpu_custom_call" | custom-call | flops 603979776 | bytes 4718592 | tf_op jit(solution)/shard_map/mix/pallas_call | solution.py:494
  68.8 2.3 collective-permute-start.13
  72.2 10.0 %feed.2 = (bf16[2048,768]{1,0:T(8,128)(2,1)}, bf16[2048,768]{1,0:T(8,128)(2,1)}, bf16[512,768]{1,0:T(8,128)(2,1)}, bf16[512,768]{1,0:T(8,128)(2,1)}, bf16[512,768]{1,0:T(8,128)(2,1)}, /*index=5*/bf16[512,768]{1,0:T(8,128)(2,1)}) custom-call(bf16[512,768]{1,0:T(8,128)(2,1)} %get-tuple-element.137.ha_ref.h0, bf16[512,768]{1,0:T(8,128)(2,1)} %copy-done.31, ...), custom_call_target="tpu_custom_call" | custom-call | flops 4831838208 | bytes 6291456 | tf_op jit(solution)/shard_map/feed/pallas_call | solution.py:374
  82.2 7.3 %collective-permute-done.13.ha_ref.h2 = bf16[512,768]{1,0:T(8,128)(2,1)S(1)} collective-permute-done((bf16[512,768]{1,0:T(8,128)(2,1)}, bf16[512,768]{1,0:T(8,128)(2,1)S(1)}, u32[]{:S(2)}, u32[]{:S(2)}) %collective-permute-start.13) | collective-permute-done | bytes 786464 | tf_op jit(solution)/shard_map/ppermute | solution.py:38
  89.5 2.3 collective-permute-done.14.hb_ref.h3
  92.6 10.0 %feed.3 = (bf16[2048,768]{1,0:T(8,128)(2,1)}, bf16[2048,768]{1,0:T(8,128)(2,1)}, bf16[512,768]{1,0:T(8,128)(2,1)}, bf16[512,768]{1,0:T(8,128)(2,1)}, bf16[512,768]{1,0:T(8,128)(2,1)}, /*index=5*/bf16[512,768]{1,0:T(8,128)(2,1)}) custom-call(bf16[512,768]{1,0:T(8,128)(2,1)} %copy-done.32, ...), custom_call_target="tpu_custom_call", output_to_operand_aliasing={{0}: (7, {}), {1}: (8, {})} | custom-call | flops 4831838208 | bytes 6291456 | tf_op jit(solution)/shard_map/feed/pallas_call | solution.py:374
  102.8 2.4 collective-permute-done.16
  108.8 12.5 %weigh.1 = (bf16[768,768]{1,0:T(8,128)(2,1)}, bf16[768,768]{1,0:T(8,128)(2,1)}, f32[1,768]{1,0:T(1,128)}) custom-call(s32[1]{0:T(128)} %bitcast.5.b_ref, bf16[512,768]{1,0:T(8,128)(2,1)} %get-tuple-element.137.ha_ref.h0, bf16[512,768]{1,0:T(8,128)(2,1)} %copy-done.31, bf16[512,768]{1,0:T(8,128)(2,1)} %copy-done.32, bf16[512,768]{1,0:T(8,128)(2,1)} %copy-done.34, ...), custom_call_target="tpu_custom_call" | custom-call | flops 4831838208 | bytes 18874368 | tf_op jit(solution)/shard_map/weigh/pallas_call | solution.py:455
  122.3 4.5 %collective-permute-done.19.f_ref = bf16[512,768]{1,0:T(8,128)(2,1)} collective-permute-done((bf16[512,768]{1,0:T(8,128)(2,1)S(1)}, bf16[512,768]{1,0:T(8,128)(2,1)}, u32[]{:S(2)}, u32[]{:S(2)}) %collective-permute-start.19) | collective-permute-done | bytes 786464 | tf_op jit(solution)/shard_map/ppermute | solution.py:38
  126.8 6.2 %turn.1 = (f32[512,768]{1,0:T(8,128)}, bf16[512,768]{1,0:T(8,128)(2,1)}, bf16[512,192]{1,0:T(8,128)(2,1)}, bf16[512,192]{1,0:T(8,128)(2,1)}, bf16[512,192]{1,0:T...) custom-call(bf16[512,768]{1,0:T(8,128)(2,1)} %get-tuple-element.148.n_ref, ...), custom_call_target="tpu_custom_call" | custom-call | flops 512 | bytes 768 | tf_op jit(solution)/shard_map/turn/pallas_call | solution.py:534
  140.0 7.6 %collective-permute-done.27 = bf16[512,192]{1,0:T(8,128)(2,1)S(1)} collective-permute-done((bf16[512,192]{1,0:T(8,128)(2,1)}, bf16[512,192]{1,0:T(8,128)(2,1)S(1)}, u32[]{:S(2)}, u32[]{:S(2)}) %collective-permute-start.27) | collective-permute-done | bytes 196640 | tf_op jit(solution)/shard_map/ppermute | solution.py:38
  147.6 2.3 collective-permute-done.22
  153.2 2.5 collective-permute-start.30
  159.6 29.0 %attend_back.1.gp_ref = bf16[2048,576]{1,0:T(8,128)(2,1)} custom-call(s32[8]{0:T(128)} %bitcast.29, s32[1]{0:T(128)} %bitcast.1.h_ref, bf16[3,2048,64]{2,1,0:T(8,128)(2,1)} %get-tuple-element.166.q_ref, bf16[3,2048,64]{2,1,0:T(8,128)(2,1)} %get-tuple-element.123.k_ref, bf16[3,2048,64]{2,1,0:T(8,128)(2,1)} %get-tuple-element.167.v_ref, ...), custom_call_target="tpu_custom_call" | custom-call | flops 16106127360 | bytes 11796480 | tf_op jit(solution)/shard_map/attend_back/pallas_call | solution.py:317
  190.0 4.2 %collective-permute-start.32 = (bf16[192,768]{1,0:T(8,128)(2,1)S(1)}, bf16[192,768]{1,0:T(8,128)(2,1)S(1)}, u32[]{:S(2)}, u32[]{:S(2)}) collective-permute-start(bf16[192,768]{1,0:T(8,128)(2,1)S(1)} %add_convert_fusion.6), channel_id=1, source_target_pairs={{0,16},{4,20},{8,24},{12,28},{16,0},{20,4},{24,8},{28,12},{1,17},{... | collective-permute-start | bytes 884744 | tf_op jit(solution)/shard_map/ppermute | solution.py:38
  196.2 7.7 %tally.1 = (bf16[392,768]{1,0:T(8,128)(2,1)}, bf16[392,768]{1,0:T(8,128)(2,1)}) custom-call(s32[1]{0:T(128)} %bitcast.5.b_ref, bf16[2048,576]{1,0:T(8,128)(2,1)} %attend_back.1.gp_ref, bf16[2048,768]{1,0:T(8,128)(2,1)} %get-tuple-element.179.hat_ref, bf16[576,768]{1,0:T(8,128)(2,1)} %bitcast.21, f32[8,768]{1,0:T(8,128)} %stack.31.v_ref, ...), custom_call_target="tpu_custom_call" | custom-call | flops 576 | bytes 768 | tf_op jit(solution)/shard_map/tally/pallas_call | solution.py:595
  204.7 6.8 %spread.1 = (bf16[512,768]{1,0:T(8,128)(2,1)}, bf16[512,768]{1,0:T(8,128)(2,1)}, bf16[512,768]{1,0:T(8,128)(2,1)}, bf16[512,768]{1,0:T(8,128)(2,1)}) custom-call(bf16[2048,576]{1,0:T(8,128)(2,1)} %attend_back.1.gp_ref, bf16[576,768]{1,0:T(8,128)(2,1)} %bitcast.22), custom_call_target="tpu_custom_call" | custom-call | flops 576 | bytes 768 | tf_op jit(solution)/shard_map/spread/pallas_call | solution.py:626
  211.5 6.7 %collective-permute-done.32 = bf16[192,768]{1,0:T(8,128)(2,1)S(1)} collective-permute-done((bf16[192,768]{1,0:T(8,128)(2,1)S(1)}, bf16[192,768]{1,0:T(8,128)(2,1)S(1)}, u32[]{:S(2)}, u32[]{:S(2)}) %collective-permute-start.32) | collective-permute-done | bytes 294944 | tf_op jit(solution)/shard_map/ppermute | solution.py:38
  221.2 4.1 %collective-permute-start.38 = (bf16[104,768]{1,0:T(8,128)(2,1)S(1)}, bf16[104,768]{1,0:T(8,128)(2,1)S(1)}, u32[]{:S(2)}, u32[]{:S(2)}) collective-permute-start(bf16[104,768]{1,0:T(8,128)(2,1)S(1)} %get-tuple-element.232), channel_id=1, source_target_pairs={{0,8},{4,12},{8,0},{12,4},{16,24},{20,28},{24,16},{28,20},{1,9},{5... | collective-permute-start | bytes 479240 | tf_op jit(solution)/shard_map/ppermute | solution.py:38
  226.4 2.5 add_convert_fusion.1
  228.9 7.7 %collective-permute-done.39.rest_2_ = bf16[384,768]{1,0:T(8,128)(2,1)S(1)} collective-permute-done((bf16[384,768]{1,0:T(8,128)(2,1)S(1)}, bf16[384,768]{1,0:T(8,128)(2,1)S(1)}, u32[]{:S(2)}, u32[]{:S(2)}) %collective-permute-start.39) | collective-permute-done | bytes 589856 | tf_op jit(solution)/shard_map/ppermute | solution.py:38
  237.4 2.5 collective-permute-start.45
  246.2 5.4 %collective-permute-done.43.rest_3_ = bf16[384,768]{1,0:T(8,128)(2,1)S(1)} collective-permute-done((bf16[384,768]{1,0:T(8,128)(2,1)S(1)}, bf16[384,768]{1,0:T(8,128)(2,1)S(1)}, u32[]{:S(2)}, u32[]{:S(2)}) %collective-permute-start.43) | collective-permute-done | bytes 589856 | tf_op jit(solution)/shard_map/ppermute | solution.py:38
  257.6 4.2 %unpack.2 = (f32[768,768]{1,0:T(8,128)}, f32[768,768]{1,0:T(8,128)}) custom-call(s32[1]{0:T(128)} %bitcast.5.b_ref, bf16[384,768]{1,0:T(8,128)(2,1)} %copy-done.5, bf16[384,768]{1,0:T(8,128)(2,1)} %copy-done.7, bf16[384,768]{1,0:T(8,128)(2,1)} %copy-done.26, bf16[384,768]{1,0:T(8,128)(2,1)} %copy-done.27), custom_call_target="tpu_custom_call" | custom-call | flops 1536 | bytes 768 | tf_op jit(solution)/shard_map/unpack/pallas_call | solution.py:653
  267.2 2.9 %unpack.3 = (f32[576,768]{1,0:T(8,128)}, f32[192,768]{1,0:T(8,128)}) custom-call(s32[1]{0:T(128)} %bitcast.5.b_ref, bf16[384,768]{1,0:T(8,128)(2,1)} %pad_maximum_fusion.1.rest_0_, bf16[384,768]{1,0:T(8,128)(2,1)} %collective-permute-done.50.rest_1_), custom_call_target="tpu_custom_call" | custom-call | flops 768 | bytes 768 | tf_op jit(solution)/shard_map/unpack/pallas_call | solution.py:653
  (212 shorter events, 64.0 us)
Async XLA Ops:
  1.2 20.9 %collective-permute-start = (bf16[512,768]{1,0:T(8,128)(2,1)}, bf16[512,768]{1,0:T(8,128)(2,1)S(1)}, u32[]{:S(2)}, u32[]{:S(2)}) collective-permute-start(bf16[512,768]{1,0:T(8,128)(2,1)} %x_ref), channel_id=1, source_target_pairs={{0,2},{1,3},{2,0},{3,1},{4,6},{5,7},{6,4},{7,5},{8,10},{9,11},{10,... | collective-permute-start | bytes 2359304 | tf_op jit(solution)/shard_map/ppermute | solution.py:38
  24.8 37.5 %collective-permute-start.10 = (bf16[512,768]{1,0:T(8,128)(2,1)S(1)}, bf16[512,768]{1,0:T(8,128)(2,1)}, u32[]{:S(2)}, u32[]{:S(2)}) collective-permute-start(bf16[512,768]{1,0:T(8,128)(2,1)S(1)} %broadcast_select_fusion.ga_ref.g0.cot_ref), channel_id=1, source_target_pairs={{0,2},{1,3},{2,0},{3,1},{4,6},{5,7},{6,4},{7,5},{8,10},{9,11},{10,... | collective-permute-start | bytes 2359304 | tf_op jit(solution)/shard_map/ppermute | solution.py:38
  26.6 31.5 %collective-permute-start.8 = (bf16[192,768]{1,0:T(8,128)(2,1)S(1)}, bf16[192,768]{1,0:T(8,128)(2,1)S(1)}, u32[]{:S(2)}, u32[]{:S(2)}) collective-permute-start(bf16[192,768]{1,0:T(8,128)(2,1)S(1)} %bitcast.25), channel_id=1, source_target_pairs={{0,2},{1,3},{2,0},{3,1},{4,6},{5,7},{6,4},{7,5},{8,10},{9,11},{10,... | collective-permute-start | bytes 884744 | tf_op jit(solution)/shard_map/ppermute | solution.py:38
  47.0 11.7 %collective-permute-start.5 = (bf16[512,192]{1,0:T(8,128)(2,1)}, bf16[512,192]{1,0:T(8,128)(2,1)S(1)}, u32[]{:S(2)}, u32[]{:S(2)}) collective-permute-start(bf16[512,192]{1,0:T(8,128)(2,1)} %get-tuple-element.129.rest_7_), channel_id=1, source_target_pairs={{0,2},{1,3},{2,0},{3,1},{4,6},{5,7},{6,4},{7,5},{8,10},{9,11},{10,... | collective-permute-start | bytes 589832 | tf_op jit(solution)/shard_map/ppermute | solution.py:38
  47.1 15.2 %collective-permute-start.4 = (bf16[512,192]{1,0:T(8,128)(2,1)}, bf16[512,192]{1,0:T(8,128)(2,1)S(1)}, u32[]{:S(2)}, u32[]{:S(2)}) collective-permute-start(bf16[512,192]{1,0:T(8,128)(2,1)} %get-tuple-element.125.rest_6_), channel_id=1, source_target_pairs={{0,2},{1,3},{2,0},{3,1},{4,6},{5,7},{6,4},{7,5},{8,10},{9,11},{10,... | collective-permute-start | bytes 589832 | tf_op jit(solution)/shard_map/ppermute | solution.py:38
  68.8 20.6 %collective-permute-start.13 = (bf16[512,768]{1,0:T(8,128)(2,1)}, bf16[512,768]{1,0:T(8,128)(2,1)S(1)}, u32[]{:S(2)}, u32[]{:S(2)}) collective-permute-start(bf16[512,768]{1,0:T(8,128)(2,1)} %get-tuple-element.137.ha_ref.h0), channel_id=1, source_target_pairs={{0,2},{1,3},{2,0},{3,1},{4,6},{5,7},{6,4},{7,5},{8,10},{9,11},{10,... | collective-permute-start | bytes 2359304 | tf_op jit(solution)/shard_map/ppermute | solution.py:38
  71.2 18.3 %collective-permute-start.15 = (bf16[512,768]{1,0:T(8,128)(2,1)}, bf16[512,768]{1,0:T(8,128)(2,1)S(1)}, u32[]{:S(2)}, u32[]{:S(2)}) collective-permute-start(bf16[512,768]{1,0:T(8,128)(2,1)} %collective-permute-done.10.ga_ref.g2), channel_id=1, source_target_pairs={{0,1},{1,0},{2,3},{3,2},{4,5},{5,4},{6,7},{7,6},{8,9},{9,8},{10,11... | collective-permute-start | bytes 2359304 | tf_op jit(solution)/shard_map/ppermute | solution.py:38
  106.5 15.8 %collective-permute-start.17 = (bf16[512,768]{1,0:T(8,128)(2,1)}, bf16[512,768]{1,0:T(8,128)(2,1)}, u32[]{:S(2)}, u32[]{:S(2)}) collective-permute-start(bf16[512,768]{1,0:T(8,128)(2,1)} %get-tuple-element.146), channel_id=1, source_target_pairs={{0,1},{1,0},{2,3},{3,2},{4,5},{5,4},{6,7},{7,6},{8,9},{9,8},{10,11... | collective-permute-start | bytes 2359304 | tf_op jit(solution)/shard_map/ppermute | solution.py:38
  106.7 15.6 %collective-permute-start.20 = (bf16[512,768]{1,0:T(8,128)(2,1)}, bf16[512,768]{1,0:T(8,128)(2,1)S(1)}, u32[]{:S(2)}, u32[]{:S(2)}) collective-permute-start(bf16[512,768]{1,0:T(8,128)(2,1)} %get-tuple-element.155), channel_id=1, source_target_pairs={{0,1},{1,0},{2,3},{3,2},{4,5},{5,4},{6,7},{7,6},{8,9},{9,8},{10,11... | collective-permute-start | bytes 2359304 | tf_op jit(solution)/shard_map/ppermute | solution.py:38
  107.1 19.7 %collective-permute-start.19 = (bf16[512,768]{1,0:T(8,128)(2,1)S(1)}, bf16[512,768]{1,0:T(8,128)(2,1)}, u32[]{:S(2)}, u32[]{:S(2)}) collective-permute-start(bf16[512,768]{1,0:T(8,128)(2,1)S(1)} %add_convert_fusion.4), channel_id=1, source_target_pairs={{0,2},{1,3},{2,0},{3,1},{4,6},{5,7},{6,4},{7,5},{8,10},{9,11},{10,... | collective-permute-start | bytes 2359304 | tf_op jit(solution)/shard_map/ppermute | solution.py:38
  108.8 17.9 %collective-permute-start.18 = (bf16[512,768]{1,0:T(8,128)(2,1)}, bf16[512,768]{1,0:T(8,128)(2,1)}, u32[]{:S(2)}, u32[]{:S(2)}) collective-permute-start(bf16[512,768]{1,0:T(8,128)(2,1)} %get-tuple-element.149), channel_id=1, source_target_pairs={{0,1},{1,0},{2,3},{3,2},{4,5},{5,4},{6,7},{7,6},{8,9},{9,8},{10,11... | collective-permute-start | bytes 2359304 | tf_op jit(solution)/shard_map/ppermute | solution.py:38
  121.3 28.6 %collective-permute-start.22 = (bf16[768,768]{1,0:T(8,128)(2,1)}, bf16[768,768]{1,0:T(8,128)(2,1)S(1)}, u32[]{:S(2)}, u32[]{:S(2)}) collective-permute-start(bf16[768,768]{1,0:T(8,128)(2,1)} %get-tuple-element.162), channel_id=1, source_target_pairs={{0,4},{4,0},{8,12},{12,8},{16,20},{20,16},{24,28},{28,24},{1,5},{5... | collective-permute-start | bytes 3538952 | tf_op jit(solution)/shard_map/ppermute | solution.py:38
  133.1 14.5 %collective-permute-start.23 = (bf16[512,192]{1,0:T(8,128)(2,1)}, bf16[512,192]{1,0:T(8,128)(2,1)S(1)}, u32[]{:S(2)}, u32[]{:S(2)}) collective-permute-start(bf16[512,192]{1,0:T(8,128)(2,1)} %get-tuple-element.163), channel_id=1, source_target_pairs={{0,2},{1,3},{2,0},{3,1},{4,6},{5,7},{6,4},{7,5},{8,10},{9,11},{10,... | collective-permute-start | bytes 589832 | tf_op jit(solution)/shard_map/ppermute | solution.py:38
  134.9 12.7 %collective-permute-start.27 = (bf16[512,192]{1,0:T(8,128)(2,1)}, bf16[512,192]{1,0:T(8,128)(2,1)S(1)}, u32[]{:S(2)}, u32[]{:S(2)}) collective-permute-start(bf16[512,192]{1,0:T(8,128)(2,1)} %get-tuple-element.169), channel_id=1, source_target_pairs={{0,2},{1,3},{2,0},{3,1},{4,6},{5,7},{6,4},{7,5},{8,10},{9,11},{10,... | collective-permute-start | bytes 589832 | tf_op jit(solution)/shard_map/ppermute | solution.py:38
  136.8 16.4 %collective-permute-start.26 = (bf16[192,768]{1,0:T(8,128)(2,1)S(1)}, bf16[192,768]{1,0:T(8,128)(2,1)S(1)}, u32[]{:S(2)}, u32[]{:S(2)}) collective-permute-start(bf16[192,768]{1,0:T(8,128)(2,1)S(1)} %convolution_convert_fusion.1), channel_id=1, source_target_pairs={{0,1},{1,0},{2,3},{3,2},{4,5},{5,4},{6,7},{7,6},{8,9},{9,8},{10,11... | collective-permute-start | bytes 884744 | tf_op jit(solution)/shard_map/ppermute | solution.py:38
  138.4 17.6 %collective-permute-start.34 = (bf16[192,768]{1,0:T(8,128)(2,1)S(1)}, bf16[192,768]{1,0:T(8,128)(2,1)S(1)}, u32[]{:S(2)}, u32[]{:S(2)}) collective-permute-start(bf16[192,768]{1,0:T(8,128)(2,1)S(1)} %convolution_convert_fusion), channel_id=1, source_target_pairs={{0,1},{1,0},{2,3},{3,2},{4,5},{5,4},{6,7},{7,6},{8,9},{9,8},{10,11... | collective-permute-start | bytes 884744 | tf_op jit(solution)/shard_map/ppermute | solution.py:38
  151.1 45.2 %collective-permute-start.24 = (bf16[512,768]{1,0:T(8,128)(2,1)}, bf16[512,768]{1,0:T(8,128)(2,1)S(1)}, u32[]{:S(2)}, u32[]{:S(2)}) collective-permute-start(bf16[512,768]{1,0:T(8,128)(2,1)} %add_convert_fusion.3), channel_id=1, source_target_pairs={{0,2},{1,3},{2,0},{3,1},{4,6},{5,7},{6,4},{7,5},{8,10},{9,11},{10,... | collective-permute-start | bytes 2359304 | tf_op jit(solution)/shard_map/ppermute | solution.py:38
  151.3 37.3 %collective-permute-start.25 = (bf16[192,768]{1,0:T(8,128)(2,1)}, bf16[192,768]{1,0:T(8,128)(2,1)}, u32[]{:S(2)}, u32[]{:S(2)}) collective-permute-start(bf16[192,768]{1,0:T(8,128)(2,1)} %get-tuple-element.226), channel_id=1, source_target_pairs={{0,8},{4,12},{8,0},{12,4},{16,24},{20,28},{24,16},{28,20},{1,9},{5... | collective-permute-start | bytes 884744 | tf_op jit(solution)/shard_map/ppermute | solution.py:38
  153.2 35.5 %collective-permute-start.30 = (bf16[192,768]{1,0:T(8,128)(2,1)S(1)}, bf16[192,768]{1,0:T(8,128)(2,1)}, u32[]{:S(2)}, u32[]{:S(2)}) collective-permute-start(bf16[192,768]{1,0:T(8,128)(2,1)S(1)} %get-tuple-element.227), channel_id=1, source_target_pairs={{0,24},{4,28},{8,16},{12,20},{16,8},{20,12},{24,0},{28,4},{1,25},{... | collective-permute-start | bytes 884744 | tf_op jit(solution)/shard_map/ppermute | solution.py:38
  156.0 32.6 %collective-permute-start.29 = (bf16[192,768]{1,0:T(8,128)(2,1)S(1)}, bf16[192,768]{1,0:T(8,128)(2,1)}, u32[]{:S(2)}, u32[]{:S(2)}) collective-permute-start(bf16[192,768]{1,0:T(8,128)(2,1)S(1)} %get-tuple-element.228), channel_id=1, source_target_pairs={{0,16},{4,20},{8,24},{12,28},{16,0},{20,4},{24,8},{28,12},{1,17},{... | collective-permute-start | bytes 884744 | tf_op jit(solution)/shard_map/ppermute | solution.py:38
  157.9 36.5 %collective-permute-start.35 = (bf16[192,768]{1,0:T(8,128)(2,1)}, bf16[192,768]{1,0:T(8,128)(2,1)}, u32[]{:S(2)}, u32[]{:S(2)}) collective-permute-start(bf16[192,768]{1,0:T(8,128)(2,1)} %fusion.10), channel_id=1, source_target_pairs={{0,2},{1,3},{2,0},{3,1},{4,6},{5,7},{6,4},{7,5},{8,10},{9,11},{10,... | collective-permute-start | bytes 884744 | tf_op jit(solution)/shard_map/ppermute | solution.py:38
  189.9 21.6 %collective-permute-start.33 = (bf16[192,768]{1,0:T(8,128)(2,1)S(1)}, bf16[192,768]{1,0:T(8,128)(2,1)S(1)}, u32[]{:S(2)}, u32[]{:S(2)}) collective-permute-start(bf16[192,768]{1,0:T(8,128)(2,1)S(1)} %add_convert_fusion.6), channel_id=1, source_target_pairs={{0,24},{4,28},{8,16},{12,20},{16,8},{20,12},{24,0},{28,4},{1,25},{... | collective-permute-start | bytes 884744 | tf_op jit(solution)/shard_map/ppermute | solution.py:38
  190.0 28.2 %collective-permute-start.32 = (bf16[192,768]{1,0:T(8,128)(2,1)S(1)}, bf16[192,768]{1,0:T(8,128)(2,1)S(1)}, u32[]{:S(2)}, u32[]{:S(2)}) collective-permute-start(bf16[192,768]{1,0:T(8,128)(2,1)S(1)} %add_convert_fusion.6), channel_id=1, source_target_pairs={{0,16},{4,20},{8,24},{12,28},{16,0},{20,4},{24,8},{28,12},{1,17},{... | collective-permute-start | bytes 884744 | tf_op jit(solution)/shard_map/ppermute | solution.py:38
  194.2 24.0 %collective-permute-start.31 = (bf16[192,768]{1,0:T(8,128)(2,1)S(1)}, bf16[192,768]{1,0:T(8,128)(2,1)}, u32[]{:S(2)}, u32[]{:S(2)}) collective-permute-start(bf16[192,768]{1,0:T(8,128)(2,1)S(1)} %add_convert_fusion.6), channel_id=1, source_target_pairs={{0,8},{4,12},{8,0},{12,4},{16,24},{20,28},{24,16},{28,20},{1,9},{5... | collective-permute-start | bytes 884744 | tf_op jit(solution)/shard_map/ppermute | solution.py:38
  204.0 15.5 %collective-permute-start.36 = (bf16[392,768]{1,0:T(8,128)(2,1)}, bf16[392,768]{1,0:T(8,128)(2,1)S(1)}, u32[]{:S(2)}, u32[]{:S(2)}) collective-permute-start(bf16[392,768]{1,0:T(8,128)(2,1)} %get-tuple-element.190), channel_id=1, source_target_pairs={{0,4},{4,0},{8,12},{12,8},{16,20},{20,16},{24,28},{28,24},{1,5},{5... | collective-permute-start | bytes 1806344 | tf_op jit(solution)/shard_map/ppermute | solution.py:38
  220.9 15.7 %collective-permute-start.39 = (bf16[384,768]{1,0:T(8,128)(2,1)S(1)}, bf16[384,768]{1,0:T(8,128)(2,1)S(1)}, u32[]{:S(2)}, u32[]{:S(2)}) collective-permute-start(bf16[384,768]{1,0:T(8,128)(2,1)S(1)} %pad_maximum_fusion.rest_0_), channel_id=1, source_target_pairs={{0,4},{4,0},{8,12},{12,8},{16,20},{20,16},{24,28},{28,24},{1,5},{5... | collective-permute-start | bytes 1769480 | tf_op jit(solution)/shard_map/ppermute | solution.py:38
  220.9 15.7 %collective-permute-start.41 = (bf16[104,768]{1,0:T(8,128)(2,1)S(1)}, bf16[104,768]{1,0:T(8,128)(2,1)S(1)}, u32[]{:S(2)}, u32[]{:S(2)}) collective-permute-start(bf16[104,768]{1,0:T(8,128)(2,1)S(1)} %concatenate.24), channel_id=1, source_target_pairs={{0,24},{4,28},{8,16},{12,20},{16,8},{20,12},{24,0},{28,4},{1,25},{... | collective-permute-start | bytes 479240 | tf_op jit(solution)/shard_map/ppermute | solution.py:38
  221.2 15.4 %collective-permute-start.40 = (bf16[104,768]{1,0:T(8,128)(2,1)S(1)}, bf16[104,768]{1,0:T(8,128)(2,1)S(1)}, u32[]{:S(2)}, u32[]{:S(2)}) collective-permute-start(bf16[104,768]{1,0:T(8,128)(2,1)S(1)} %get-tuple-element.231), channel_id=1, source_target_pairs={{0,16},{4,20},{8,24},{12,28},{16,0},{20,4},{24,8},{28,12},{1,17},{... | collective-permute-start | bytes 479240 | tf_op jit(solution)/shard_map/ppermute | solution.py:38
  221.2 15.4 %collective-permute-start.38 = (bf16[104,768]{1,0:T(8,128)(2,1)S(1)}, bf16[104,768]{1,0:T(8,128)(2,1)S(1)}, u32[]{:S(2)}, u32[]{:S(2)}) collective-permute-start(bf16[104,768]{1,0:T(8,128)(2,1)S(1)} %get-tuple-element.232), channel_id=1, source_target_pairs={{0,8},{4,12},{8,0},{12,4},{16,24},{20,28},{24,16},{28,20},{1,9},{5... | collective-permute-start | bytes 479240 | tf_op jit(solution)/shard_map/ppermute | solution.py:38
  236.7 14.9 %collective-permute-start.43 = (bf16[384,768]{1,0:T(8,128)(2,1)S(1)}, bf16[384,768]{1,0:T(8,128)(2,1)S(1)}, u32[]{:S(2)}, u32[]{:S(2)}) collective-permute-start(bf16[384,768]{1,0:T(8,128)(2,1)S(1)} %constant_dynamic-update-slice_fusion.rest_1_), channel_id=1, source_target_pairs={{0,4},{4,0},{8,12},{12,8},{16,20},{20,16},{24,28},{28,24},{1,5},{5... | collective-permute-start | bytes 1769480 | tf_op jit(solution)/shard_map/ppermute | solution.py:38
  243.9 19.2 %collective-permute-start.47 = (bf16[512,768]{1,0:T(8,128)(2,1)}, bf16[512,768]{1,0:T(8,128)(2,1)S(1)}, u32[]{:S(2)}, u32[]{:S(2)}) collective-permute-start(bf16[512,768]{1,0:T(8,128)(2,1)} %add_convert_fusion.2), channel_id=1, source_target_pairs={{0,2},{1,3},{2,0},{3,1},{4,6},{5,7},{6,4},{7,5},{8,10},{9,11},{10,... | collective-permute-start | bytes 2359304 | tf_op jit(solution)/shard_map/ppermute | solution.py:38
  252.7 14.5 %collective-permute-start.50 = (bf16[384,768]{1,0:T(8,128)(2,1)}, bf16[384,768]{1,0:T(8,128)(2,1)}, u32[]{:S(2)}, u32[]{:S(2)}) collective-permute-start(bf16[384,768]{1,0:T(8,128)(2,1)} %pad_maximum_fusion.1.rest_0_), channel_id=1, source_target_pairs={{0,4},{4,0},{8,12},{12,8},{16,20},{20,16},{24,28},{28,24},{1,5},{5... | collective-permute-start | bytes 1769480 | tf_op jit(solution)/shard_map/ppermute | solution.py:38
  (59 other events, 362.4 us)

commit v8 on v7

--- a/solution.py
+++ b/solution.py
@@ -549,6 +549,26 @@
         cost_estimate=cost(rows, width),
         name="turn",
     )(near, swapped, far, resid, cot, vectors, *projs)
+
+
+def outer_kernel(m0, m1, m2, m3, g_ref, k0, s1, k2, s3):
+    g = g_ref[...]
+    for m, out in ((m1, s1), (m3, s3), (m0, k0), (m2, k2)):
+        out[...] = dot_tn(m[...], g).astype(out.dtype)
+
+
+def outer_call(parts, grad):
+    rows, width = grad.shape
+    shape = (parts[0].shape[1], width)
+    vm = pl.BlockSpec(memory_space=pltpu.VMEM)
+    return pl.pallas_call(
+        outer_kernel,
+        out_shape=tuple(jax.ShapeDtypeStruct(shape, t) for t in (F32, BF, F32, BF)),
+        in_specs=[vm] * 5,
+        out_specs=[vm] * 4,
+        cost_estimate=cost(8 * rows * width * shape[0] * 8, 8 * rows * width),
+        name="outer",
+    )(*parts, grad)
 
 
 def tally_kernel(steps, b_ref, gp_ref, hat_ref, w_ref, v_ref, pw_ref, up_ref, s_ref, keep_ref, send_ref, acc, col):
@@ -764,11 +784,12 @@
     act, grad_up, norm_far, norm_last, down_far, down_last = feed_call(
         h_far, h_last, grads[2], grads[3], weight_up, vectors, weight_down, 2, group_rows, near[:2]
     )
+    near_swapped = swap(near[3], "head", 1)
+    near_down = swap(near[5], "head", 1)
+    norm_far = tie(norm_far, near_swapped, near_down)
     far_sum = (norm_far.astype(F32) + swap(norm_last, "head", 1).astype(F32)).astype(BF)
     grad_far_sum = swap(far_sum, "head", 2)
-    near_swapped = swap(near[3], "head", 1)
     down_swapped = swap(tie(down_last, far_sum), "head", 1)
-    near_down = swap(tie(near[5], far_sum), "head", 1)
 
     keep_feed, send_feed, grad_bup = weigh_call(
         bid, (h_own, h_near, h_far, h_last), tie(act, far_sum), grad_up, grads
@@ -777,7 +798,7 @@
     grad_resid, grad_att, grad_near, grad_mate, grad_cross, grad_last, sums = turn_call(
         near[2],
         near_swapped,
-        tie(grad_far_sum, grad_bup, down_swapped, near_down),
+        tie(grad_far_sum, grad_bup, down_swapped),
         resid,
         grad_own,
         vectors,
@@ -786,18 +807,18 @@
     got_last = swap(grad_last, "head", 2)
     got = swap(grad_cross, "head", 2)
     grad_mate = swap(grad_mate, "head", 1)
-    grad_att = tie(grad_att, grad_mate)
-    grad_proj = [dot_tn(p, grad_att) for p in parts]
-    near_sent, far_sent = grad_proj[1].astype(BF), grad_proj[3].astype(BF)
+    own_proj, near_sent, cross_proj, far_sent = outer_call(parts, grad_att)
     down_far = tie(down_far, grad_att)
     down_sum = (down_far.astype(F32) + down_swapped.astype(F32)).astype(BF)
-    got_last = tie(got_last, near_sent, far_sent, down_sum)
+    got_last, near_sent, far_sent, down_sum = lax.optimization_barrier(
+        (got_last, near_sent, far_sent, down_sum)
+    )
     merged_grads = (grad_near, grad_mate, got, swap(got_last, "head", 1))
-    grad_near_proj = grad_proj[0] + swap(near_sent, "head", 1).astype(F32)
-    far_proj = (grad_proj[2] + swap(far_sent, "head", 1).astype(F32)).astype(BF)
-    far_proj = swap(far_proj, "head", 2)
-
-    kept_feed = (keep_feed.astype(F32) + tie(other_feed, got).astype(F32)).astype(BF)
+    grad_near_proj = own_proj + swap(near_sent, "head", 1).astype(F32)
+    pair_proj = (cross_proj + swap(far_sent, "head", 1).astype(F32)).astype(BF)
+    far_proj = swap(pair_proj, "head", 2)
+
+    kept_feed = (keep_feed.astype(F32) + tie(other_feed, got, got_last).astype(F32)).astype(BF)
     got_feed = across(quarters(kept_feed))
     down_other = swap(tie(down_sum, kept_feed), "head", 2)
 

time: 272 us -> 270 us (level)
  Pallas kernels: 129 us -> 134 us
  matrix products: 4.54 us -> 0 us
    dot_general x4 -> x0, matrix products: 4.54 us -> none  [dot_tn(): lax.dot_general(a, b, (((0,), (0,)), ((), ())), preferred_element_type=F32)]
    pallas_call x0 -> x1, Pallas kernels: none -> 3.26 us  [outer_call(): pl.pallas_call(outer_kernel, out_shape=tuple((jax.ShapeDtypeStruct(shape,...]
  transfers between devices with their start and end apart: 51 -> 51, of which waited for: 15 -> 17; matrix products, arithmetic and copies ran while one was open for 12% -> 9% of each run, Pallas kernels for 43% -> 49%
where the time goes in v8:
time: 270 us
  Pallas kernels  134 us (50%)
  waiting for transfers between devices  60.5 us (22%)
  starting transfers between devices  41.9 us (16%)
  other arithmetic  18.6 us (7%)
  local copies, waits for them, and re-layouts  13.6 us (5%)
    ppermute x51, waiting for transfers between devices, swap(): return lax.ppermute(x, axis, [(i, i ^ bits) for i in range(size)])  60.5 us
    ppermute x51, starting transfers between devices, swap(): return lax.ppermute(x, axis, [(i, i ^ bits) for i in range(size)])  41.9 us
    pallas_call x1, Pallas kernels, attend_back_call(): pl.pallas_call(functools.partial(attend_back_kernel, chunk, 1.0 / math.sq...  29.9 us
    pallas_call x2, Pallas kernels, attend_call(): pl.pallas_call(functools.partial(attend_kernel, heads, first, per, 1.0 /...  23.4 us
    pallas_call x2, Pallas kernels, feed_call(): pl.pallas_call(functools.partial(feed_kernel, steps), out_shape=(jax.Shap...  20 us
    pallas_call x2, Pallas kernels, qkv_call(): pl.pallas_call(functools.partial(qkv_kernel, heads, hd, steps), out_shape...  12.8 us
    pallas_call x1, Pallas kernels, weigh_call(): pl.pallas_call(functools.partial(weigh_kernel, tiles), out_shape=(half, h...  12.5 us
    pallas_call x1, Pallas kernels, tally_call(): pl.pallas_call(functools.partial(tally_kernel, steps), out_shape=(half, h...  7.71 us
  transfers between devices with their start and end apart: 51, of which 17 were waited for; matrix products, arithmetic and copies ran while one was open for 9% of the time, Pallas kernels for 49%

profile of v8, /device:TPU:0, one launch (start us, length us, event | category | flops | bytes accessed | tf_op | source)
XLA Modules:
  0.0 269.7 jit_solution(12820283176018726221)
XLA Ops:
  1.2 2.6 collective-permute-start
  10.1 6.4 %qkv.2 = (bf16[3,2048,64]{2,1,0:T(8,128)(2,1)}, bf16[3,2048,64]{2,1,0:T(8,128)(2,1)}, bf16[3,2048,64]{2,1,0:T(8,128)(2,1)}, bf16[3,64,2048]{2,1,0:T(8,128)(2,1)}, bf16[2048,768]{1,0:T(8,128)(2,1)}) custom-call(s32[1]{0:T(128)} %bitcast.1.h_ref, bf16[512,768]{1,0:T(8,128)(2,1)} %x_ref, bf16[512,768]{1,0:T(8,128)(2,1)} %copy-done.36, f32[8,768]{1,0:T(8,128)} %stack.31.v_ref, ...), custom_call_target="tpu_custom_call" | custom-call | flops 905969664 | bytes 4718592 | tf_op jit(solution)/shard_map/qkv/pallas_call | solution.py:84
  16.5 5.6 %collective-permute-done.a_ref = bf16[512,768]{1,0:T(8,128)(2,1)S(1)} collective-permute-done((bf16[512,768]{1,0:T(8,128)(2,1)}, bf16[512,768]{1,0:T(8,128)(2,1)S(1)}, u32[]{:S(2)}, u32[]{:S(2)}) %collective-permute-start) | collective-permute-done | bytes 786464 | tf_op jit(solution)/shard_map/ppermute | solution.py:38
  26.9 6.4 %qkv.3 = (bf16[3,2048,64]{2,1,0:T(8,128)(2,1)}, bf16[3,2048,64]{2,1,0:T(8,128)(2,1)}, bf16[3,2048,64]{2,1,0:T(8,128)(2,1)}, bf16[3,64,2048]{2,1,0:T(8,128)(2,1)}, bf16[2048,768]{1,0:T(8,128)(2,1)}) custom-call(s32[1]{0:T(128)} %bitcast.1.h_ref, ...), custom_call_target="tpu_custom_call", output_to_operand_aliasing={{0}: (6, {}), {1}: (7, {}), {2}: (8, {}), {3}: (9, {}), {4}... | custom-call | flops 905969664 | bytes 4718592 | tf_op jit(solution)/shard_map/qkv/pallas_call | solution.py:84
  33.3 13.7 %attend.2 = (bf16[512,192]{1,0:T(8,128)(2,1)}, bf16[512,192]{1,0:T(8,128)(2,1)}, f32[8,512]{1,0:T(8,128)}, f32[8,512]{1,0:T(8,128)}) custom-call(s32[8]{0:T(128)} %bitcast.19, s32[1]{0:T(128)} %bitcast.1.h_ref, bf16[3,2048,64]{2,1,0:T(8,128)(2,1)} %get-tuple-element.177.q_ref, bf16[3,2048,64]{2,1,0:T(8,128)(2,1)} %get-tuple-element.129.k_ref, ...), custom_call_target="tpu_custom_call" | custom-call | flops 2048 | bytes 64 | tf_op jit(solution)/shard_map/attend/pallas_call | solution.py:198
  49.1 9.7 %attend.3 = (bf16[512,192]{1,0:T(8,128)(2,1)}, bf16[512,192]{1,0:T(8,128)(2,1)}, f32[8,512]{1,0:T(8,128)}, f32[8,512]{1,0:T(8,128)}) custom-call(s32[8]{0:T(128)} %bitcast.20, s32[1]{0:T(128)} %bitcast.1.h_ref, bf16[3,2048,64]{2,1,0:T(8,128)(2,1)} %get-tuple-element.177.q_ref, bf16[3,2048,64]{2,1,0:T(8,128)(2,1)} %get-tuple-element.129.k_ref, ...), custom_call_target="tpu_custom_call" | custom-call | flops 2048 | bytes 64 | tf_op jit(solution)/shard_map/attend/pallas_call | solution.py:198
  59.5 2.8 %collective-permute-done.4.m2 = bf16[512,192]{1,0:T(8,128)(2,1)S(1)} collective-permute-done((bf16[512,192]{1,0:T(8,128)(2,1)}, bf16[512,192]{1,0:T(8,128)(2,1)S(1)}, u32[]{:S(2)}, u32[]{:S(2)}) %collective-permute-start.4) | collective-permute-done | bytes 196640 | tf_op jit(solution)/shard_map/ppermute | solution.py:38
  64.6 4.1 %mix.1 = (f32[512,768]{1,0:T(8,128)}, bf16[512,768]{1,0:T(8,128)(2,1)}) custom-call(bf16[512,192]{1,0:T(8,128)(2,1)} %get-tuple-element.133.m0.rest_4_, bf16[512,192]{1,0:T(8,128)(2,1)} %copy-done.27, bf16[512,192]{1,0:T(8,128)(2,1)} %copy-done.26, bf16[512,192]{1,0:T(8,128)(2,1)} %copy-done.28, bf16[192,768]{1,0:T(8,128)(2,1)} %bitcast.15, ...), custom_call_target="tpu_custom_call" | custom-call | flops 603979776 | bytes 4718592 | tf_op jit(solution)/shard_map/mix/pallas_call | solution.py:494
  68.8 2.4 collective-permute-start.15
  72.2 10.0 %feed.2 = (bf16[2048,768]{1,0:T(8,128)(2,1)}, bf16[2048,768]{1,0:T(8,128)(2,1)}, bf16[512,768]{1,0:T(8,128)(2,1)}, bf16[512,768]{1,0:T(8,128)(2,1)}, bf16[512,768]{1,0:T(8,128)(2,1)}, /*index=5*/bf16[512,768]{1,0:T(8,128)(2,1)}) custom-call(bf16[512,768]{1,0:T(8,128)(2,1)} %get-tuple-element.143.ha_ref.h0, bf16[512,768]{1,0:T(8,128)(2,1)} %copy-done.32, ...), custom_call_target="tpu_custom_call" | custom-call | flops 4831838208 | bytes 6291456 | tf_op jit(solution)/shard_map/feed/pallas_call | solution.py:374
  82.2 7.3 %collective-permute-done.15.ha_ref.h2 = bf16[512,768]{1,0:T(8,128)(2,1)S(1)} collective-permute-done((bf16[512,768]{1,0:T(8,128)(2,1)}, bf16[512,768]{1,0:T(8,128)(2,1)S(1)}, u32[]{:S(2)}, u32[]{:S(2)}) %collective-permute-start.15) | collective-permute-done | bytes 786464 | tf_op jit(solution)/shard_map/ppermute | solution.py:38
  92.7 10.0 %feed.3 = (bf16[2048,768]{1,0:T(8,128)(2,1)}, bf16[2048,768]{1,0:T(8,128)(2,1)}, bf16[512,768]{1,0:T(8,128)(2,1)}, bf16[512,768]{1,0:T(8,128)(2,1)}, bf16[512,768]{1,0:T(8,128)(2,1)}, /*index=5*/bf16[512,768]{1,0:T(8,128)(2,1)}) custom-call(bf16[512,768]{1,0:T(8,128)(2,1)} %copy-done.33, ...), custom_call_target="tpu_custom_call", output_to_operand_aliasing={{0}: (7, {}), {1}: (8, {})} | custom-call | flops 4831838208 | bytes 6291456 | tf_op jit(solution)/shard_map/feed/pallas_call | solution.py:374
  108.4 12.5 %weigh.1 = (bf16[768,768]{1,0:T(8,128)(2,1)}, bf16[768,768]{1,0:T(8,128)(2,1)}, f32[1,768]{1,0:T(1,128)}) custom-call(s32[1]{0:T(128)} %bitcast.5.b_ref, bf16[512,768]{1,0:T(8,128)(2,1)} %get-tuple-element.143.ha_ref.h0, bf16[512,768]{1,0:T(8,128)(2,1)} %copy-done.32, bf16[512,768]{1,0:T(8,128)(2,1)} %copy-done.33, bf16[512,768]{1,0:T(8,128)(2,1)} %copy-done.34, ...), custom_call_target="tpu_custom_call" | custom-call | flops 4831838208 | bytes 18874368 | tf_op jit(solution)/shard_map/weigh/pallas_call | solution.py:455
  121.8 4.5 %collective-permute-done.19.f_ref = bf16[512,768]{1,0:T(8,128)(2,1)} collective-permute-done((bf16[512,768]{1,0:T(8,128)(2,1)S(1)}, bf16[512,768]{1,0:T(8,128)(2,1)}, u32[]{:S(2)}, u32[]{:S(2)}) %collective-permute-start.19) | collective-permute-done | bytes 786464 | tf_op jit(solution)/shard_map/ppermute | solution.py:38
  126.3 6.2 %turn.1 = (f32[512,768]{1,0:T(8,128)}, bf16[512,768]{1,0:T(8,128)(2,1)}, bf16[512,192]{1,0:T(8,128)(2,1)}, bf16[512,192]{1,0:T(8,128)(2,1)}, bf16[512,192]{1,0:T...) custom-call(bf16[512,768]{1,0:T(8,128)(2,1)} %get-tuple-element.147.n_ref, bf16[512,768]{1,0:T(8,128)(2,1)} %copy-done.20, ...), custom_call_target="tpu_custom_call" | custom-call | flops 512 | bytes 768 | tf_op jit(solution)/shard_map/turn/pallas_call | solution.py:534
  134.6 3.3 %outer.1 = (f32[192,768]{1,0:T(8,128)}, bf16[192,768]{1,0:T(8,128)(2,1)}, f32[192,768]{1,0:T(8,128)}, bf16[192,768]{1,0:T(8,128)(2,1)}) custom-call(bf16[512,192]{1,0:T(8,128)(2,1)} %get-tuple-element.133.m0.rest_4_, bf16[512,192]{1,0:T(8,128)(2,1)} %copy-done.27, bf16[512,192]{1,0:T(8,128)(2,1)} %copy-done.26, bf16[512,192]{1,0:T(8,128)(2,1)} %copy-done.28, ...), custom_call_target="tpu_custom_call" | custom-call | flops 4831838208 | bytes 3145728 | tf_op jit(solution)/shard_map/outer/pallas_call | solution.py:564
  139.4 2.7 %collective-permute-done.21 = bf16[512,192]{1,0:T(8,128)(2,1)} collective-permute-done((bf16[512,192]{1,0:T(8,128)(2,1)}, bf16[512,192]{1,0:T(8,128)(2,1)}, u32[]{:S(2)}, u32[]{:S(2)}) %collective-permute-start.21) | collective-permute-done | bytes 196640 | tf_op jit(solution)/shard_map/ppermute | solution.py:38
  142.6 3.3 %collective-permute-done.23.rest_2_ = bf16[512,192]{1,0:T(8,128)(2,1)S(1)} collective-permute-done((bf16[512,192]{1,0:T(8,128)(2,1)}, bf16[512,192]{1,0:T(8,128)(2,1)S(1)}, u32[]{:S(2)}, u32[]{:S(2)}) %collective-permute-start.23) | collective-permute-done | bytes 196640 | tf_op jit(solution)/shard_map/ppermute | solution.py:38
  145.9 3.6 %collective-permute-done.22 = bf16[768,768]{1,0:T(8,128)(2,1)S(1)} collective-permute-done((bf16[768,768]{1,0:T(8,128)(2,1)}, bf16[768,768]{1,0:T(8,128)(2,1)S(1)}, u32[]{:S(2)}, u32[]{:S(2)}) %collective-permute-start.22) | collective-permute-done | bytes 1179680 | tf_op jit(solution)/shard_map/ppermute | solution.py:38
  152.7 2.5 collective-permute-start.30
  158.2 29.9 %attend_back.1.gp_ref = bf16[2048,576]{1,0:T(8,128)(2,1)} custom-call(s32[8]{0:T(128)} %bitcast.21, s32[1]{0:T(128)} %bitcast.1.h_ref, bf16[3,2048,64]{2,1,0:T(8,128)(2,1)} %get-tuple-element.177.q_ref, bf16[3,2048,64]{2,1,0:T(8,128)(2,1)} %get-tuple-element.129.k_ref, bf16[3,2048,64]{2,1,0:T(8,128)(2,1)} %get-tuple-element.178.v_ref, ...), custom_call_target="tpu_custom_call" | custom-call | flops 16106127360 | bytes 11796480 | tf_op jit(solution)/shard_map/attend_back/pallas_call | solution.py:317
  195.6 7.7 %tally.1 = (bf16[392,768]{1,0:T(8,128)(2,1)}, bf16[392,768]{1,0:T(8,128)(2,1)}) custom-call(s32[1]{0:T(128)} %bitcast.5.b_ref, bf16[2048,576]{1,0:T(8,128)(2,1)} %attend_back.1.gp_ref, bf16[2048,768]{1,0:T(8,128)(2,1)} %get-tuple-element.189.hat_ref, bf16[576,768]{1,0:T(8,128)(2,1)} %bitcast.13, f32[8,768]{1,0:T(8,128)} %stack.31.v_ref, ...), custom_call_target="tpu_custom_call" | custom-call | flops 576 | bytes 768 | tf_op jit(solution)/shard_map/tally/pallas_call | solution.py:615
  203.8 6.8 %spread.1 = (bf16[512,768]{1,0:T(8,128)(2,1)}, bf16[512,768]{1,0:T(8,128)(2,1)}, bf16[512,768]{1,0:T(8,128)(2,1)}, bf16[512,768]{1,0:T(8,128)(2,1)}) custom-call(bf16[2048,576]{1,0:T(8,128)(2,1)} %attend_back.1.gp_ref, bf16[576,768]{1,0:T(8,128)(2,1)} %bitcast.14), custom_call_target="tpu_custom_call" | custom-call | flops 576 | bytes 768 | tf_op jit(solution)/shard_map/spread/pallas_call | solution.py:646
  210.6 5.3 %collective-permute-done.32 = bf16[192,768]{1,0:T(8,128)(2,1)S(1)} collective-permute-done((bf16[192,768]{1,0:T(8,128)(2,1)S(1)}, bf16[192,768]{1,0:T(8,128)(2,1)S(1)}, u32[]{:S(2)}, u32[]{:S(2)}) %collective-permute-start.32) | collective-permute-done | bytes 294944 | tf_op jit(solution)/shard_map/ppermute | solution.py:38
  219.9 3.4 %collective-permute-start.41 = (bf16[104,768]{1,0:T(8,128)(2,1)S(1)}, bf16[104,768]{1,0:T(8,128)(2,1)S(1)}, u32[]{:S(2)}, u32[]{:S(2)}) collective-permute-start(bf16[104,768]{1,0:T(8,128)(2,1)S(1)} %concatenate.24), channel_id=1, source_target_pairs={{0,24},{4,28},{8,16},{12,20},{16,8},{20,12},{24,0},{28,4},{1,25},{... | collective-permute-start | bytes 479240 | tf_op jit(solution)/shard_map/ppermute | solution.py:38
  225.4 2.5 add_convert_fusion.1
  227.9 6.3 %collective-permute-done.39.rest_2_ = bf16[384,768]{1,0:T(8,128)(2,1)S(1)} collective-permute-done((bf16[384,768]{1,0:T(8,128)(2,1)S(1)}, bf16[384,768]{1,0:T(8,128)(2,1)S(1)}, u32[]{:S(2)}, u32[]{:S(2)}) %collective-permute-start.39) | collective-permute-done | bytes 589856 | tf_op jit(solution)/shard_map/ppermute | solution.py:38
  236.9 2.3 collective-permute-start.45
  243.0 2.4 collective-permute-done.45
  245.5 5.8 %collective-permute-done.43.rest_3_ = bf16[384,768]{1,0:T(8,128)(2,1)S(1)} collective-permute-done((bf16[384,768]{1,0:T(8,128)(2,1)S(1)}, bf16[384,768]{1,0:T(8,128)(2,1)S(1)}, u32[]{:S(2)}, u32[]{:S(2)}) %collective-permute-start.43) | collective-permute-done | bytes 589856 | tf_op jit(solution)/shard_map/ppermute | solution.py:38
  256.6 4.2 %unpack.2 = (f32[768,768]{1,0:T(8,128)}, f32[768,768]{1,0:T(8,128)}) custom-call(s32[1]{0:T(128)} %bitcast.5.b_ref, bf16[384,768]{1,0:T(8,128)(2,1)} %copy-done.4, bf16[384,768]{1,0:T(8,128)(2,1)} %copy-done.6, bf16[384,768]{1,0:T(8,128)(2,1)} %copy-done.22, bf16[384,768]{1,0:T(8,128)(2,1)} %copy-done.23), custom_call_target="tpu_custom_call" | custom-call | flops 1536 | bytes 768 | tf_op jit(solution)/shard_map/unpack/pallas_call | solution.py:673
  266.7 2.9 %unpack.3 = (f32[576,768]{1,0:T(8,128)}, f32[192,768]{1,0:T(8,128)}) custom-call(s32[1]{0:T(128)} %bitcast.5.b_ref, bf16[384,768]{1,0:T(8,128)(2,1)} %pad_maximum_fusion.1.rest_0_, bf16[384,768]{1,0:T(8,128)(2,1)} %collective-permute-done.50.rest_1_), custom_call_target="tpu_custom_call" | custom-call | flops 768 | bytes 768 | tf_op jit(solution)/shard_map/unpack/pallas_call | solution.py:673
  (211 shorter events, 69.4 us)
Async XLA Ops:
  1.2 20.9 %collective-permute-start = (bf16[512,768]{1,0:T(8,128)(2,1)}, bf16[512,768]{1,0:T(8,128)(2,1)S(1)}, u32[]{:S(2)}, u32[]{:S(2)}) collective-permute-start(bf16[512,768]{1,0:T(8,128)(2,1)} %x_ref), channel_id=1, source_target_pairs={{0,2},{1,3},{2,0},{3,1},{4,6},{5,7},{6,4},{7,5},{8,10},{9,11},{10,... | collective-permute-start | bytes 2359304 | tf_op jit(solution)/shard_map/ppermute | solution.py:38
  24.8 37.5 %collective-permute-start.10 = (bf16[512,768]{1,0:T(8,128)(2,1)S(1)}, bf16[512,768]{1,0:T(8,128)(2,1)}, u32[]{:S(2)}, u32[]{:S(2)}) collective-permute-start(bf16[512,768]{1,0:T(8,128)(2,1)S(1)} %broadcast_select_fusion.ga_ref.g0.cot_ref), channel_id=1, source_target_pairs={{0,2},{1,3},{2,0},{3,1},{4,6},{5,7},{6,4},{7,5},{8,10},{9,11},{10,... | collective-permute-start | bytes 2359304 | tf_op jit(solution)/shard_map/ppermute | solution.py:38
  26.6 32.2 %collective-permute-start.8 = (bf16[192,768]{1,0:T(8,128)(2,1)S(1)}, bf16[192,768]{1,0:T(8,128)(2,1)S(1)}, u32[]{:S(2)}, u32[]{:S(2)}) collective-permute-start(bf16[192,768]{1,0:T(8,128)(2,1)S(1)} %bitcast.17), channel_id=1, source_target_pairs={{0,2},{1,3},{2,0},{3,1},{4,6},{5,7},{6,4},{7,5},{8,10},{9,11},{10,... | collective-permute-start | bytes 884744 | tf_op jit(solution)/shard_map/ppermute | solution.py:38
  47.0 12.4 %collective-permute-start.5 = (bf16[512,192]{1,0:T(8,128)(2,1)}, bf16[512,192]{1,0:T(8,128)(2,1)S(1)}, u32[]{:S(2)}, u32[]{:S(2)}) collective-permute-start(bf16[512,192]{1,0:T(8,128)(2,1)} %get-tuple-element.135.rest_7_), channel_id=1, source_target_pairs={{0,2},{1,3},{2,0},{3,1},{4,6},{5,7},{6,4},{7,5},{8,10},{9,11},{10,... | collective-permute-start | bytes 589832 | tf_op jit(solution)/shard_map/ppermute | solution.py:38
  47.1 15.2 %collective-permute-start.4 = (bf16[512,192]{1,0:T(8,128)(2,1)}, bf16[512,192]{1,0:T(8,128)(2,1)S(1)}, u32[]{:S(2)}, u32[]{:S(2)}) collective-permute-start(bf16[512,192]{1,0:T(8,128)(2,1)} %get-tuple-element.131.rest_6_), channel_id=1, source_target_pairs={{0,2},{1,3},{2,0},{3,1},{4,6},{5,7},{6,4},{7,5},{8,10},{9,11},{10,... | collective-permute-start | bytes 589832 | tf_op jit(solution)/shard_map/ppermute | solution.py:38
  68.8 20.7 %collective-permute-start.15 = (bf16[512,768]{1,0:T(8,128)(2,1)}, bf16[512,768]{1,0:T(8,128)(2,1)S(1)}, u32[]{:S(2)}, u32[]{:S(2)}) collective-permute-start(bf16[512,768]{1,0:T(8,128)(2,1)} %get-tuple-element.143.ha_ref.h0), channel_id=1, source_target_pairs={{0,2},{1,3},{2,0},{3,1},{4,6},{5,7},{6,4},{7,5},{8,10},{9,11},{10,... | collective-permute-start | bytes 2359304 | tf_op jit(solution)/shard_map/ppermute | solution.py:38
  71.2 18.8 %collective-permute-start.17 = (bf16[512,768]{1,0:T(8,128)(2,1)}, bf16[512,768]{1,0:T(8,128)(2,1)}, u32[]{:S(2)}, u32[]{:S(2)}) collective-permute-start(bf16[512,768]{1,0:T(8,128)(2,1)} %collective-permute-done.10.ga_ref.g2), channel_id=1, source_target_pairs={{0,1},{1,0},{2,3},{3,2},{4,5},{5,4},{6,7},{7,6},{8,9},{9,8},{10,11... | collective-permute-start | bytes 2359304 | tf_op jit(solution)/shard_map/ppermute | solution.py:38
  89.5 13.4 %collective-permute-start.13 = (bf16[512,768]{1,0:T(8,128)(2,1)}, bf16[512,768]{1,0:T(8,128)(2,1)S(1)}, u32[]{:S(2)}, u32[]{:S(2)}) collective-permute-start(bf16[512,768]{1,0:T(8,128)(2,1)} %get-tuple-element.146), channel_id=1, source_target_pairs={{0,1},{1,0},{2,3},{3,2},{4,5},{5,4},{6,7},{7,6},{8,9},{9,8},{10,11... | collective-permute-start | bytes 2359304 | tf_op jit(solution)/shard_map/ppermute | solution.py:38
  90.0 12.9 %collective-permute-start.14 = (bf16[512,768]{1,0:T(8,128)(2,1)}, bf16[512,768]{1,0:T(8,128)(2,1)S(1)}, u32[]{:S(2)}, u32[]{:S(2)}) collective-permute-start(bf16[512,768]{1,0:T(8,128)(2,1)} %get-tuple-element.148), channel_id=1, source_target_pairs={{0,1},{1,0},{2,3},{3,2},{4,5},{5,4},{6,7},{7,6},{8,9},{9,8},{10,11... | collective-permute-start | bytes 2359304 | tf_op jit(solution)/shard_map/ppermute | solution.py:38
  106.5 19.8 %collective-permute-start.19 = (bf16[512,768]{1,0:T(8,128)(2,1)S(1)}, bf16[512,768]{1,0:T(8,128)(2,1)}, u32[]{:S(2)}, u32[]{:S(2)}) collective-permute-start(bf16[512,768]{1,0:T(8,128)(2,1)S(1)} %add_convert_fusion.4), channel_id=1, source_target_pairs={{0,2},{1,3},{2,0},{3,1},{4,6},{5,7},{6,4},{7,5},{8,10},{9,11},{10,... | collective-permute-start | bytes 2359304 | tf_op jit(solution)/shard_map/ppermute | solution.py:38
  108.4 13.5 %collective-permute-start.20 = (bf16[512,768]{1,0:T(8,128)(2,1)}, bf16[512,768]{1,0:T(8,128)(2,1)S(1)}, u32[]{:S(2)}, u32[]{:S(2)}) collective-permute-start(bf16[512,768]{1,0:T(8,128)(2,1)} %get-tuple-element.160), channel_id=1, source_target_pairs={{0,1},{1,0},{2,3},{3,2},{4,5},{5,4},{6,7},{7,6},{8,9},{9,8},{10,11... | collective-permute-start | bytes 2359304 | tf_op jit(solution)/shard_map/ppermute | solution.py:38
  120.9 28.6 %collective-permute-start.22 = (bf16[768,768]{1,0:T(8,128)(2,1)}, bf16[768,768]{1,0:T(8,128)(2,1)S(1)}, u32[]{:S(2)}, u32[]{:S(2)}) collective-permute-start(bf16[768,768]{1,0:T(8,128)(2,1)} %get-tuple-element.170), channel_id=1, source_target_pairs={{0,4},{4,0},{8,12},{12,8},{16,20},{20,16},{24,28},{28,24},{1,5},{5... | collective-permute-start | bytes 3538952 | tf_op jit(solution)/shard_map/ppermute | solution.py:38
  134.6 21.4 %collective-permute-start.27 = (bf16[512,192]{1,0:T(8,128)(2,1)}, bf16[512,192]{1,0:T(8,128)(2,1)}, u32[]{:S(2)}, u32[]{:S(2)}) collective-permute-start(bf16[512,192]{1,0:T(8,128)(2,1)} %get-tuple-element.180), channel_id=1, source_target_pairs={{0,1},{1,0},{2,3},{3,2},{4,5},{5,4},{6,7},{7,6},{8,9},{9,8},{10,11... | collective-permute-start | bytes 589832 | tf_op jit(solution)/shard_map/ppermute | solution.py:38
  142.1 14.3 %collective-permute-start.28 = (bf16[512,192]{1,0:T(8,128)(2,1)}, bf16[512,192]{1,0:T(8,128)(2,1)}, u32[]{:S(2)}, u32[]{:S(2)}) collective-permute-start(bf16[512,192]{1,0:T(8,128)(2,1)} %collective-permute-done.21), channel_id=1, source_target_pairs={{0,1},{1,0},{2,3},{3,2},{4,5},{5,4},{6,7},{7,6},{8,9},{9,8},{10,11... | collective-permute-start | bytes 589832 | tf_op jit(solution)/shard_map/ppermute | solution.py:38
  150.8 44.8 %collective-permute-start.24 = (bf16[512,768]{1,0:T(8,128)(2,1)S(1)}, bf16[512,768]{1,0:T(8,128)(2,1)}, u32[]{:S(2)}, u32[]{:S(2)}) collective-permute-start(bf16[512,768]{1,0:T(8,128)(2,1)S(1)} %add_convert_fusion.3), channel_id=1, source_target_pairs={{0,2},{1,3},{2,0},{3,1},{4,6},{5,7},{6,4},{7,5},{8,10},{9,11},{10,... | collective-permute-start | bytes 2359304 | tf_op jit(solution)/shard_map/ppermute | solution.py:38
  151.0 37.0 %collective-permute-start.25 = (bf16[192,768]{1,0:T(8,128)(2,1)}, bf16[192,768]{1,0:T(8,128)(2,1)}, u32[]{:S(2)}, u32[]{:S(2)}) collective-permute-start(bf16[192,768]{1,0:T(8,128)(2,1)} %get-tuple-element.238), channel_id=1, source_target_pairs={{0,8},{4,12},{8,0},{12,4},{16,24},{20,28},{24,16},{28,20},{1,9},{5... | collective-permute-start | bytes 884744 | tf_op jit(solution)/shard_map/ppermute | solution.py:38
  152.7 35.3 %collective-permute-start.30 = (bf16[192,768]{1,0:T(8,128)(2,1)}, bf16[192,768]{1,0:T(8,128)(2,1)}, u32[]{:S(2)}, u32[]{:S(2)}) collective-permute-start(bf16[192,768]{1,0:T(8,128)(2,1)} %get-tuple-element.239), channel_id=1, source_target_pairs={{0,24},{4,28},{8,16},{12,20},{16,8},{20,12},{24,0},{28,4},{1,25},{... | collective-permute-start | bytes 884744 | tf_op jit(solution)/shard_map/ppermute | solution.py:38
  156.1 32.0 %collective-permute-start.29 = (bf16[192,768]{1,0:T(8,128)(2,1)S(1)}, bf16[192,768]{1,0:T(8,128)(2,1)S(1)}, u32[]{:S(2)}, u32[]{:S(2)}) collective-permute-start(bf16[192,768]{1,0:T(8,128)(2,1)S(1)} %get-tuple-element.240), channel_id=1, source_target_pairs={{0,16},{4,20},{8,24},{12,28},{16,0},{20,4},{24,8},{28,12},{1,17},{... | collective-permute-start | bytes 884744 | tf_op jit(solution)/shard_map/ppermute | solution.py:38
  156.4 37.3 %collective-permute-start.35 = (bf16[192,768]{1,0:T(8,128)(2,1)}, bf16[192,768]{1,0:T(8,128)(2,1)}, u32[]{:S(2)}, u32[]{:S(2)}) collective-permute-start(bf16[192,768]{1,0:T(8,128)(2,1)} %add_convert_fusion.6), channel_id=1, source_target_pairs={{0,2},{1,3},{2,0},{3,1},{4,6},{5,7},{6,4},{7,5},{8,10},{9,11},{10,... | collective-permute-start | bytes 884744 | tf_op jit(solution)/shard_map/ppermute | solution.py:38
  189.3 21.3 %collective-permute-start.33 = (bf16[192,768]{1,0:T(8,128)(2,1)S(1)}, bf16[192,768]{1,0:T(8,128)(2,1)S(1)}, u32[]{:S(2)}, u32[]{:S(2)}) collective-permute-start(bf16[192,768]{1,0:T(8,128)(2,1)S(1)} %add_convert_fusion.7), channel_id=1, source_target_pairs={{0,24},{4,28},{8,16},{12,20},{16,8},{20,12},{24,0},{28,4},{1,25},{... | collective-permute-start | bytes 884744 | tf_op jit(solution)/shard_map/ppermute | solution.py:38
  191.4 24.5 %collective-permute-start.32 = (bf16[192,768]{1,0:T(8,128)(2,1)S(1)}, bf16[192,768]{1,0:T(8,128)(2,1)S(1)}, u32[]{:S(2)}, u32[]{:S(2)}) collective-permute-start(bf16[192,768]{1,0:T(8,128)(2,1)S(1)} %add_convert_fusion.7), channel_id=1, source_target_pairs={{0,16},{4,20},{8,24},{12,28},{16,0},{20,4},{24,8},{28,12},{1,17},{... | collective-permute-start | bytes 884744 | tf_op jit(solution)/shard_map/ppermute | solution.py:38
  191.5 24.4 %collective-permute-start.31 = (bf16[192,768]{1,0:T(8,128)(2,1)S(1)}, bf16[192,768]{1,0:T(8,128)(2,1)}, u32[]{:S(2)}, u32[]{:S(2)}) collective-permute-start(bf16[192,768]{1,0:T(8,128)(2,1)S(1)} %add_convert_fusion.7), channel_id=1, source_target_pairs={{0,8},{4,12},{8,0},{12,4},{16,24},{20,28},{24,16},{28,20},{1,9},{5... | collective-permute-start | bytes 884744 | tf_op jit(solution)/shard_map/ppermute | solution.py:38
  203.3 13.9 %collective-permute-start.36 = (bf16[392,768]{1,0:T(8,128)(2,1)}, bf16[392,768]{1,0:T(8,128)(2,1)S(1)}, u32[]{:S(2)}, u32[]{:S(2)}) collective-permute-start(bf16[392,768]{1,0:T(8,128)(2,1)} %get-tuple-element.202), channel_id=1, source_target_pairs={{0,4},{4,0},{8,12},{12,8},{16,20},{20,16},{24,28},{28,24},{1,5},{5... | collective-permute-start | bytes 1806344 | tf_op jit(solution)/shard_map/ppermute | solution.py:38
  218.5 15.7 %collective-permute-start.39 = (bf16[384,768]{1,0:T(8,128)(2,1)S(1)}, bf16[384,768]{1,0:T(8,128)(2,1)S(1)}, u32[]{:S(2)}, u32[]{:S(2)}) collective-permute-start(bf16[384,768]{1,0:T(8,128)(2,1)S(1)} %pad_maximum_fusion.rest_0_), channel_id=1, source_target_pairs={{0,4},{4,0},{8,12},{12,8},{16,20},{20,16},{24,28},{28,24},{1,5},{5... | collective-permute-start | bytes 1769480 | tf_op jit(solution)/shard_map/ppermute | solution.py:38
  219.9 14.3 %collective-permute-start.41 = (bf16[104,768]{1,0:T(8,128)(2,1)S(1)}, bf16[104,768]{1,0:T(8,128)(2,1)S(1)}, u32[]{:S(2)}, u32[]{:S(2)}) collective-permute-start(bf16[104,768]{1,0:T(8,128)(2,1)S(1)} %concatenate.24), channel_id=1, source_target_pairs={{0,24},{4,28},{8,16},{12,20},{16,8},{20,12},{24,0},{28,4},{1,25},{... | collective-permute-start | bytes 479240 | tf_op jit(solution)/shard_map/ppermute | solution.py:38
  223.3 13.1 %collective-permute-start.40 = (bf16[104,768]{1,0:T(8,128)(2,1)S(1)}, bf16[104,768]{1,0:T(8,128)(2,1)S(1)}, u32[]{:S(2)}, u32[]{:S(2)}) collective-permute-start(bf16[104,768]{1,0:T(8,128)(2,1)S(1)} %get-tuple-element.243), channel_id=1, source_target_pairs={{0,16},{4,20},{8,24},{12,28},{16,0},{20,4},{24,8},{28,12},{1,17},{... | collective-permute-start | bytes 479240 | tf_op jit(solution)/shard_map/ppermute | solution.py:38
  223.4 13.1 %collective-permute-start.38 = (bf16[104,768]{1,0:T(8,128)(2,1)S(1)}, bf16[104,768]{1,0:T(8,128)(2,1)S(1)}, u32[]{:S(2)}, u32[]{:S(2)}) collective-permute-start(bf16[104,768]{1,0:T(8,128)(2,1)S(1)} %get-tuple-element.244), channel_id=1, source_target_pairs={{0,8},{4,12},{8,0},{12,4},{16,24},{20,28},{24,16},{28,20},{1,9},{5... | collective-permute-start | bytes 479240 | tf_op jit(solution)/shard_map/ppermute | solution.py:38
  236.6 14.7 %collective-permute-start.43 = (bf16[384,768]{1,0:T(8,128)(2,1)S(1)}, bf16[384,768]{1,0:T(8,128)(2,1)S(1)}, u32[]{:S(2)}, u32[]{:S(2)}) collective-permute-start(bf16[384,768]{1,0:T(8,128)(2,1)S(1)} %constant_dynamic-update-slice_fusion.rest_1_), channel_id=1, source_target_pairs={{0,4},{4,0},{8,12},{12,8},{16,20},{20,16},{24,28},{28,24},{1,5},{5... | collective-permute-start | bytes 1769480 | tf_op jit(solution)/shard_map/ppermute | solution.py:38
  239.3 12.0 %collective-permute-start.44 = (bf16[96,768]{1,0:T(8,128)(2,1)S(1)}, bf16[96,768]{1,0:T(8,128)(2,1)S(1)}, u32[]{:S(2)}, u32[]{:S(2)}) collective-permute-start(bf16[96,768]{1,0:T(8,128)(2,1)S(1)} %add_convert_fusion.8), channel_id=1, source_target_pairs={{0,16},{4,20},{8,24},{12,28},{16,0},{20,4},{24,8},{28,12},{1,17},{... | collective-permute-start | bytes 442376 | tf_op jit(solution)/shard_map/ppermute | solution.py:38
  239.3 12.0 %collective-permute-start.42 = (bf16[96,768]{1,0:T(8,128)(2,1)S(1)}, bf16[96,768]{1,0:T(8,128)(2,1)S(1)}, u32[]{:S(2)}, u32[]{:S(2)}) collective-permute-start(bf16[96,768]{1,0:T(8,128)(2,1)S(1)} %add_convert_fusion.8), channel_id=1, source_target_pairs={{0,8},{4,12},{8,0},{12,4},{16,24},{20,28},{24,16},{28,20},{1,9},{5... | collective-permute-start | bytes 442376 | tf_op jit(solution)/shard_map/ppermute | solution.py:38
  242.0 19.5 %collective-permute-start.47 = (bf16[512,768]{1,0:T(8,128)(2,1)}, bf16[512,768]{1,0:T(8,128)(2,1)S(1)}, u32[]{:S(2)}, u32[]{:S(2)}) collective-permute-start(bf16[512,768]{1,0:T(8,128)(2,1)} %add_convert_fusion.2), channel_id=1, source_target_pairs={{0,2},{1,3},{2,0},{3,1},{4,6},{5,7},{6,4},{7,5},{8,10},{9,11},{10,... | collective-permute-start | bytes 2359304 | tf_op jit(solution)/shard_map/ppermute | solution.py:38
  252.3 14.5 %collective-permute-start.50 = (bf16[384,768]{1,0:T(8,128)(2,1)}, bf16[384,768]{1,0:T(8,128)(2,1)}, u32[]{:S(2)}, u32[]{:S(2)}) collective-permute-start(bf16[384,768]{1,0:T(8,128)(2,1)} %pad_maximum_fusion.1.rest_0_), channel_id=1, source_target_pairs={{0,4},{4,0},{8,12},{12,8},{16,20},{20,16},{24,28},{28,24},{1,5},{5... | collective-permute-start | bytes 1769480 | tf_op jit(solution)/shard_map/ppermute | solution.py:38
  (59 other events, 394.8 us)

commit v9 on v8

--- a/solution.py
+++ b/solution.py
@@ -608,7 +608,7 @@
     rows, width = hat.shape
     cols = gp.shape[1]
     total = cols + proj_grad.shape[0]
-    block = 2 * BLK
+    block = 4 * BLK
     steps = rows // block
     whole = lambda t, b: (0, 0)
     half = jax.ShapeDtypeStruct((total // 2 + sums.shape[0], width), BF)

time: 270 us -> 270 us (level)
  transfers between devices with their start and end apart: 51 -> 51, of which waited for: 17 -> 17; matrix products, arithmetic and copies ran while one was open for 9% -> 9% of each run, Pallas kernels for 49% -> 48%
where the time goes in v9:
time: 270 us
  Pallas kernels  132 us (49%)
  waiting for transfers between devices  60.2 us (22%)
  starting transfers between devices  44.3 us (16%)
  other arithmetic  18.6 us (7%)
  local copies, waits for them, and re-layouts  13.6 us (5%)
    ppermute x51, waiting for transfers between devices, swap(): return lax.ppermute(x, axis, [(i, i ^ bits) for i in range(size)])  60.2 us
    ppermute x51, starting transfers between devices, swap(): return lax.ppermute(x, axis, [(i, i ^ bits) for i in range(size)])  44.3 us
    pallas_call x1, Pallas kernels, attend_back_call(): pl.pallas_call(functools.partial(attend_back_kernel, chunk, 1.0 / math.sq...  29 us
    pallas_call x2, Pallas kernels, attend_call(): pl.pallas_call(functools.partial(attend_kernel, heads, first, per, 1.0 /...  22.8 us
    pallas_call x2, Pallas kernels, feed_call(): pl.pallas_call(functools.partial(feed_kernel, steps), out_shape=(jax.Shap...  20 us
    pallas_call x2, Pallas kernels, qkv_call(): pl.pallas_call(functools.partial(qkv_kernel, heads, hd, steps), out_shape...  12.8 us
    pallas_call x1, Pallas kernels, weigh_call(): pl.pallas_call(functools.partial(weigh_kernel, tiles), out_shape=(half, h...  12.5 us
    pallas_call x2, Pallas kernels, unpack_call(): pl.pallas_call(functools.partial(unpack_kernel, counts, places), out_shap...  7.15 us
  transfers between devices with their start and end apart: 51, of which 17 were waited for; matrix products, arithmetic and copies ran while one was open for 9% of the time, Pallas kernels for 48%

profile of v9, /device:TPU:0, one launch (start us, length us, event | category | flops | bytes accessed | tf_op | source)
XLA Modules:
  0.0 269.6 jit_solution(2038107575006606122)
XLA Ops:
  1.2 2.6 collective-permute-start
  10.1 6.4 %qkv.2 = (bf16[3,2048,64]{2,1,0:T(8,128)(2,1)}, bf16[3,2048,64]{2,1,0:T(8,128)(2,1)}, bf16[3,2048,64]{2,1,0:T(8,128)(2,1)}, bf16[3,64,2048]{2,1,0:T(8,128)(2,1)}, bf16[2048,768]{1,0:T(8,128)(2,1)}) custom-call(s32[1]{0:T(128)} %bitcast.1.h_ref, bf16[512,768]{1,0:T(8,128)(2,1)} %x_ref, bf16[512,768]{1,0:T(8,128)(2,1)} %copy-done.36, f32[8,768]{1,0:T(8,128)} %stack.31.v_ref, ...), custom_call_target="tpu_custom_call" | custom-call | flops 905969664 | bytes 4718592 | tf_op jit(solution)/shard_map/qkv/pallas_call | solution.py:84
  16.5 5.6 %collective-permute-done.a_ref = bf16[512,768]{1,0:T(8,128)(2,1)S(1)} collective-permute-done((bf16[512,768]{1,0:T(8,128)(2,1)}, bf16[512,768]{1,0:T(8,128)(2,1)S(1)}, u32[]{:S(2)}, u32[]{:S(2)}) %collective-permute-start) | collective-permute-done | bytes 786464 | tf_op jit(solution)/shard_map/ppermute | solution.py:38
  26.9 6.4 %qkv.3 = (bf16[3,2048,64]{2,1,0:T(8,128)(2,1)}, bf16[3,2048,64]{2,1,0:T(8,128)(2,1)}, bf16[3,2048,64]{2,1,0:T(8,128)(2,1)}, bf16[3,64,2048]{2,1,0:T(8,128)(2,1)}, bf16[2048,768]{1,0:T(8,128)(2,1)}) custom-call(s32[1]{0:T(128)} %bitcast.1.h_ref, ...), custom_call_target="tpu_custom_call", output_to_operand_aliasing={{0}: (6, {}), {1}: (7, {}), {2}: (8, {}), {3}: (9, {}), {4}... | custom-call | flops 905969664 | bytes 4718592 | tf_op jit(solution)/shard_map/qkv/pallas_call | solution.py:84
  33.3 13.7 %attend.2 = (bf16[512,192]{1,0:T(8,128)(2,1)}, bf16[512,192]{1,0:T(8,128)(2,1)}, f32[8,512]{1,0:T(8,128)}, f32[8,512]{1,0:T(8,128)}) custom-call(s32[8]{0:T(128)} %bitcast.19, s32[1]{0:T(128)} %bitcast.1.h_ref, bf16[3,2048,64]{2,1,0:T(8,128)(2,1)} %get-tuple-element.177.q_ref, bf16[3,2048,64]{2,1,0:T(8,128)(2,1)} %get-tuple-element.129.k_ref, ...), custom_call_target="tpu_custom_call" | custom-call | flops 2048 | bytes 64 | tf_op jit(solution)/shard_map/attend/pallas_call | solution.py:198
  49.1 9.1 %attend.3 = (bf16[512,192]{1,0:T(8,128)(2,1)}, bf16[512,192]{1,0:T(8,128)(2,1)}, f32[8,512]{1,0:T(8,128)}, f32[8,512]{1,0:T(8,128)}) custom-call(s32[8]{0:T(128)} %bitcast.20, s32[1]{0:T(128)} %bitcast.1.h_ref, bf16[3,2048,64]{2,1,0:T(8,128)(2,1)} %get-tuple-element.177.q_ref, bf16[3,2048,64]{2,1,0:T(8,128)(2,1)} %get-tuple-element.129.k_ref, ...), custom_call_target="tpu_custom_call" | custom-call | flops 2048 | bytes 64 | tf_op jit(solution)/shard_map/attend/pallas_call | solution.py:198
  58.9 3.4 %collective-permute-done.4.m2 = bf16[512,192]{1,0:T(8,128)(2,1)S(1)} collective-permute-done((bf16[512,192]{1,0:T(8,128)(2,1)}, bf16[512,192]{1,0:T(8,128)(2,1)S(1)}, u32[]{:S(2)}, u32[]{:S(2)}) %collective-permute-start.4) | collective-permute-done | bytes 196640 | tf_op jit(solution)/shard_map/ppermute | solution.py:38
  64.6 4.1 %mix.1 = (f32[512,768]{1,0:T(8,128)}, bf16[512,768]{1,0:T(8,128)(2,1)}) custom-call(bf16[512,192]{1,0:T(8,128)(2,1)} %get-tuple-element.133.m0.rest_4_, bf16[512,192]{1,0:T(8,128)(2,1)} %copy-done.27, bf16[512,192]{1,0:T(8,128)(2,1)} %copy-done.26, bf16[512,192]{1,0:T(8,128)(2,1)} %copy-done.28, bf16[192,768]{1,0:T(8,128)(2,1)} %bitcast.15, ...), custom_call_target="tpu_custom_call" | custom-call | flops 603979776 | bytes 4718592 | tf_op jit(solution)/shard_map/mix/pallas_call | solution.py:494
  68.8 2.4 collective-permute-start.15
  72.2 10.0 %feed.2 = (bf16[2048,768]{1,0:T(8,128)(2,1)}, bf16[2048,768]{1,0:T(8,128)(2,1)}, bf16[512,768]{1,0:T(8,128)(2,1)}, bf16[512,768]{1,0:T(8,128)(2,1)}, bf16[512,768]{1,0:T(8,128)(2,1)}, /*index=5*/bf16[512,768]{1,0:T(8,128)(2,1)}) custom-call(bf16[512,768]{1,0:T(8,128)(2,1)} %get-tuple-element.143.ha_ref.h0, bf16[512,768]{1,0:T(8,128)(2,1)} %copy-done.32, ...), custom_call_target="tpu_custom_call" | custom-call | flops 4831838208 | bytes 6291456 | tf_op jit(solution)/shard_map/feed/pallas_call | solution.py:374
  82.2 7.3 %collective-permute-done.15.ha_ref.h2 = bf16[512,768]{1,0:T(8,128)(2,1)S(1)} collective-permute-done((bf16[512,768]{1,0:T(8,128)(2,1)}, bf16[512,768]{1,0:T(8,128)(2,1)S(1)}, u32[]{:S(2)}, u32[]{:S(2)}) %collective-permute-start.15) | collective-permute-done | bytes 786464 | tf_op jit(solution)/shard_map/ppermute | solution.py:38
  92.7 10.0 %feed.3 = (bf16[2048,768]{1,0:T(8,128)(2,1)}, bf16[2048,768]{1,0:T(8,128)(2,1)}, bf16[512,768]{1,0:T(8,128)(2,1)}, bf16[512,768]{1,0:T(8,128)(2,1)}, bf16[512,768]{1,0:T(8,128)(2,1)}, /*index=5*/bf16[512,768]{1,0:T(8,128)(2,1)}) custom-call(bf16[512,768]{1,0:T(8,128)(2,1)} %copy-done.33, ...), custom_call_target="tpu_custom_call", output_to_operand_aliasing={{0}: (7, {}), {1}: (8, {})} | custom-call | flops 4831838208 | bytes 6291456 | tf_op jit(solution)/shard_map/feed/pallas_call | solution.py:374
  102.9 2.3 collective-permute-done.18
  108.4 12.5 %weigh.1 = (bf16[768,768]{1,0:T(8,128)(2,1)}, bf16[768,768]{1,0:T(8,128)(2,1)}, f32[1,768]{1,0:T(1,128)}) custom-call(s32[1]{0:T(128)} %bitcast.5.b_ref, bf16[512,768]{1,0:T(8,128)(2,1)} %get-tuple-element.143.ha_ref.h0, bf16[512,768]{1,0:T(8,128)(2,1)} %copy-done.32, bf16[512,768]{1,0:T(8,128)(2,1)} %copy-done.33, bf16[512,768]{1,0:T(8,128)(2,1)} %copy-done.34, ...), custom_call_target="tpu_custom_call" | custom-call | flops 4831838208 | bytes 18874368 | tf_op jit(solution)/shard_map/weigh/pallas_call | solution.py:455
  122.7 3.6 %collective-permute-done.19.f_ref = bf16[512,768]{1,0:T(8,128)(2,1)} collective-permute-done((bf16[512,768]{1,0:T(8,128)(2,1)S(1)}, bf16[512,768]{1,0:T(8,128)(2,1)}, u32[]{:S(2)}, u32[]{:S(2)}) %collective-permute-start.19) | collective-permute-done | bytes 786464 | tf_op jit(solution)/shard_map/ppermute | solution.py:38
  126.3 6.2 %turn.1 = (f32[512,768]{1,0:T(8,128)}, bf16[512,768]{1,0:T(8,128)(2,1)}, bf16[512,192]{1,0:T(8,128)(2,1)}, bf16[512,192]{1,0:T(8,128)(2,1)}, bf16[512,192]{1,0:T...) custom-call(bf16[512,768]{1,0:T(8,128)(2,1)} %get-tuple-element.147.n_ref, bf16[512,768]{1,0:T(8,128)(2,1)} %copy-done.20, ...), custom_call_target="tpu_custom_call" | custom-call | flops 512 | bytes 768 | tf_op jit(solution)/shard_map/turn/pallas_call | solution.py:534
  134.6 3.3 %outer.1 = (f32[192,768]{1,0:T(8,128)}, bf16[192,768]{1,0:T(8,128)(2,1)}, f32[192,768]{1,0:T(8,128)}, bf16[192,768]{1,0:T(8,128)(2,1)}) custom-call(bf16[512,192]{1,0:T(8,128)(2,1)} %get-tuple-element.133.m0.rest_4_, bf16[512,192]{1,0:T(8,128)(2,1)} %copy-done.27, bf16[512,192]{1,0:T(8,128)(2,1)} %copy-done.26, bf16[512,192]{1,0:T(8,128)(2,1)} %copy-done.28, ...), custom_call_target="tpu_custom_call" | custom-call | flops 4831838208 | bytes 3145728 | tf_op jit(solution)/shard_map/outer/pallas_call | solution.py:564
  139.4 2.7 %collective-permute-done.21 = bf16[512,192]{1,0:T(8,128)(2,1)} collective-permute-done((bf16[512,192]{1,0:T(8,128)(2,1)}, bf16[512,192]{1,0:T(8,128)(2,1)}, u32[]{:S(2)}, u32[]{:S(2)}) %collective-permute-start.21) | collective-permute-done | bytes 196640 | tf_op jit(solution)/shard_map/ppermute | solution.py:38
  142.6 3.3 %collective-permute-done.23.rest_2_ = bf16[512,192]{1,0:T(8,128)(2,1)S(1)} collective-permute-done((bf16[512,192]{1,0:T(8,128)(2,1)}, bf16[512,192]{1,0:T(8,128)(2,1)S(1)}, u32[]{:S(2)}, u32[]{:S(2)}) %collective-permute-start.23) | collective-permute-done | bytes 196640 | tf_op jit(solution)/shard_map/ppermute | solution.py:38
  145.9 3.6 %collective-permute-done.22 = bf16[768,768]{1,0:T(8,128)(2,1)S(1)} collective-permute-done((bf16[768,768]{1,0:T(8,128)(2,1)}, bf16[768,768]{1,0:T(8,128)(2,1)S(1)}, u32[]{:S(2)}, u32[]{:S(2)}) %collective-permute-start.22) | collective-permute-done | bytes 1179680 | tf_op jit(solution)/shard_map/ppermute | solution.py:38
  157.9 29.0 %attend_back.1.gp_ref = bf16[2048,576]{1,0:T(8,128)(2,1)} custom-call(s32[8]{0:T(128)} %bitcast.21, s32[1]{0:T(128)} %bitcast.1.h_ref, bf16[3,2048,64]{2,1,0:T(8,128)(2,1)} %get-tuple-element.177.q_ref, bf16[3,2048,64]{2,1,0:T(8,128)(2,1)} %get-tuple-element.129.k_ref, bf16[3,2048,64]{2,1,0:T(8,128)(2,1)} %get-tuple-element.178.v_ref, ...), custom_call_target="tpu_custom_call" | custom-call | flops 16106127360 | bytes 11796480 | tf_op jit(solution)/shard_map/attend_back/pallas_call | solution.py:317
  194.4 7.1 %tally.1 = (bf16[392,768]{1,0:T(8,128)(2,1)}, bf16[392,768]{1,0:T(8,128)(2,1)}) custom-call(s32[1]{0:T(128)} %bitcast.5.b_ref, bf16[2048,576]{1,0:T(8,128)(2,1)} %attend_back.1.gp_ref, bf16[2048,768]{1,0:T(8,128)(2,1)} %get-tuple-element.189.hat_ref, bf16[576,768]{1,0:T(8,128)(2,1)} %bitcast.13, f32[8,768]{1,0:T(8,128)} %stack.31.v_ref, ...), custom_call_target="tpu_custom_call" | custom-call | flops 576 | bytes 768 | tf_op jit(solution)/shard_map/tally/pallas_call | solution.py:615
  203.3 6.8 %spread.1 = (bf16[512,768]{1,0:T(8,128)(2,1)}, bf16[512,768]{1,0:T(8,128)(2,1)}, bf16[512,768]{1,0:T(8,128)(2,1)}, bf16[512,768]{1,0:T(8,128)(2,1)}) custom-call(bf16[2048,576]{1,0:T(8,128)(2,1)} %attend_back.1.gp_ref, bf16[576,768]{1,0:T(8,128)(2,1)} %bitcast.14), custom_call_target="tpu_custom_call" | custom-call | flops 576 | bytes 768 | tf_op jit(solution)/shard_map/spread/pallas_call | solution.py:646
  210.1 5.7 %collective-permute-done.32 = bf16[192,768]{1,0:T(8,128)(2,1)S(1)} collective-permute-done((bf16[192,768]{1,0:T(8,128)(2,1)S(1)}, bf16[192,768]{1,0:T(8,128)(2,1)S(1)}, u32[]{:S(2)}, u32[]{:S(2)}) %collective-permute-start.32) | collective-permute-done | bytes 294944 | tf_op jit(solution)/shard_map/ppermute | solution.py:38
  220.7 2.6 collective-permute-start.41
  226.2 2.5 add_convert_fusion.1
  228.7 6.0 %collective-permute-done.39.rest_2_ = bf16[384,768]{1,0:T(8,128)(2,1)S(1)} collective-permute-done((bf16[384,768]{1,0:T(8,128)(2,1)S(1)}, bf16[384,768]{1,0:T(8,128)(2,1)S(1)}, u32[]{:S(2)}, u32[]{:S(2)}) %collective-permute-start.39) | collective-permute-done | bytes 589856 | tf_op jit(solution)/shard_map/ppermute | solution.py:38
  236.9 2.3 collective-permute-start.45
  242.9 2.5 collective-permute-done.45
  245.4 5.8 %collective-permute-done.43.rest_3_ = bf16[384,768]{1,0:T(8,128)(2,1)S(1)} collective-permute-done((bf16[384,768]{1,0:T(8,128)(2,1)S(1)}, bf16[384,768]{1,0:T(8,128)(2,1)S(1)}, u32[]{:S(2)}, u32[]{:S(2)}) %collective-permute-start.43) | collective-permute-done | bytes 589856 | tf_op jit(solution)/shard_map/ppermute | solution.py:38
  256.5 4.2 %unpack.2 = (f32[768,768]{1,0:T(8,128)}, f32[768,768]{1,0:T(8,128)}) custom-call(s32[1]{0:T(128)} %bitcast.5.b_ref, bf16[384,768]{1,0:T(8,128)(2,1)} %copy-done.4, bf16[384,768]{1,0:T(8,128)(2,1)} %copy-done.6, bf16[384,768]{1,0:T(8,128)(2,1)} %copy-done.22, bf16[384,768]{1,0:T(8,128)(2,1)} %copy-done.23), custom_call_target="tpu_custom_call" | custom-call | flops 1536 | bytes 768 | tf_op jit(solution)/shard_map/unpack/pallas_call | solution.py:673
  266.7 2.9 %unpack.3 = (f32[576,768]{1,0:T(8,128)}, f32[192,768]{1,0:T(8,128)}) custom-call(s32[1]{0:T(128)} %bitcast.5.b_ref, bf16[384,768]{1,0:T(8,128)(2,1)} %pad_maximum_fusion.1.rest_0_, bf16[384,768]{1,0:T(8,128)(2,1)} %collective-permute-done.50.rest_1_), custom_call_target="tpu_custom_call" | custom-call | flops 768 | bytes 768 | tf_op jit(solution)/shard_map/unpack/pallas_call | solution.py:673
  (211 shorter events, 72.4 us)
Async XLA Ops:
  1.2 20.9 %collective-permute-start = (bf16[512,768]{1,0:T(8,128)(2,1)}, bf16[512,768]{1,0:T(8,128)(2,1)S(1)}, u32[]{:S(2)}, u32[]{:S(2)}) collective-permute-start(bf16[512,768]{1,0:T(8,128)(2,1)} %x_ref), channel_id=1, source_target_pairs={{0,2},{1,3},{2,0},{3,1},{4,6},{5,7},{6,4},{7,5},{8,10},{9,11},{10,... | collective-permute-start | bytes 2359304 | tf_op jit(solution)/shard_map/ppermute | solution.py:38
  24.8 37.5 %collective-permute-start.10 = (bf16[512,768]{1,0:T(8,128)(2,1)S(1)}, bf16[512,768]{1,0:T(8,128)(2,1)}, u32[]{:S(2)}, u32[]{:S(2)}) collective-permute-start(bf16[512,768]{1,0:T(8,128)(2,1)S(1)} %broadcast_select_fusion.ga_ref.g0.cot_ref), channel_id=1, source_target_pairs={{0,2},{1,3},{2,0},{3,1},{4,6},{5,7},{6,4},{7,5},{8,10},{9,11},{10,... | collective-permute-start | bytes 2359304 | tf_op jit(solution)/shard_map/ppermute | solution.py:38
  26.6 31.5 %collective-permute-start.8 = (bf16[192,768]{1,0:T(8,128)(2,1)S(1)}, bf16[192,768]{1,0:T(8,128)(2,1)S(1)}, u32[]{:S(2)}, u32[]{:S(2)}) collective-permute-start(bf16[192,768]{1,0:T(8,128)(2,1)S(1)} %bitcast.17), channel_id=1, source_target_pairs={{0,2},{1,3},{2,0},{3,1},{4,6},{5,7},{6,4},{7,5},{8,10},{9,11},{10,... | collective-permute-start | bytes 884744 | tf_op jit(solution)/shard_map/ppermute | solution.py:38
  47.1 11.7 %collective-permute-start.5 = (bf16[512,192]{1,0:T(8,128)(2,1)}, bf16[512,192]{1,0:T(8,128)(2,1)S(1)}, u32[]{:S(2)}, u32[]{:S(2)}) collective-permute-start(bf16[512,192]{1,0:T(8,128)(2,1)} %get-tuple-element.135.rest_7_), channel_id=1, source_target_pairs={{0,2},{1,3},{2,0},{3,1},{4,6},{5,7},{6,4},{7,5},{8,10},{9,11},{10,... | collective-permute-start | bytes 589832 | tf_op jit(solution)/shard_map/ppermute | solution.py:38
  47.1 15.2 %collective-permute-start.4 = (bf16[512,192]{1,0:T(8,128)(2,1)}, bf16[512,192]{1,0:T(8,128)(2,1)S(1)}, u32[]{:S(2)}, u32[]{:S(2)}) collective-permute-start(bf16[512,192]{1,0:T(8,128)(2,1)} %get-tuple-element.131.rest_6_), channel_id=1, source_target_pairs={{0,2},{1,3},{2,0},{3,1},{4,6},{5,7},{6,4},{7,5},{8,10},{9,11},{10,... | collective-permute-start | bytes 589832 | tf_op jit(solution)/shard_map/ppermute | solution.py:38
  68.8 20.7 %collective-permute-start.15 = (bf16[512,768]{1,0:T(8,128)(2,1)}, bf16[512,768]{1,0:T(8,128)(2,1)S(1)}, u32[]{:S(2)}, u32[]{:S(2)}) collective-permute-start(bf16[512,768]{1,0:T(8,128)(2,1)} %get-tuple-element.143.ha_ref.h0), channel_id=1, source_target_pairs={{0,2},{1,3},{2,0},{3,1},{4,6},{5,7},{6,4},{7,5},{8,10},{9,11},{10,... | collective-permute-start | bytes 2359304 | tf_op jit(solution)/shard_map/ppermute | solution.py:38
  71.2 18.8 %collective-permute-start.17 = (bf16[512,768]{1,0:T(8,128)(2,1)}, bf16[512,768]{1,0:T(8,128)(2,1)}, u32[]{:S(2)}, u32[]{:S(2)}) collective-permute-start(bf16[512,768]{1,0:T(8,128)(2,1)} %collective-permute-done.10.ga_ref.g2), channel_id=1, source_target_pairs={{0,1},{1,0},{2,3},{3,2},{4,5},{5,4},{6,7},{7,6},{8,9},{9,8},{10,11... | collective-permute-start | bytes 2359304 | tf_op jit(solution)/shard_map/ppermute | solution.py:38
  89.5 13.4 %collective-permute-start.13 = (bf16[512,768]{1,0:T(8,128)(2,1)}, bf16[512,768]{1,0:T(8,128)(2,1)S(1)}, u32[]{:S(2)}, u32[]{:S(2)}) collective-permute-start(bf16[512,768]{1,0:T(8,128)(2,1)} %get-tuple-element.146), channel_id=1, source_target_pairs={{0,1},{1,0},{2,3},{3,2},{4,5},{5,4},{6,7},{7,6},{8,9},{9,8},{10,11... | collective-permute-start | bytes 2359304 | tf_op jit(solution)/shard_map/ppermute | solution.py:38
  90.0 12.9 %collective-permute-start.14 = (bf16[512,768]{1,0:T(8,128)(2,1)}, bf16[512,768]{1,0:T(8,128)(2,1)S(1)}, u32[]{:S(2)}, u32[]{:S(2)}) collective-permute-start(bf16[512,768]{1,0:T(8,128)(2,1)} %get-tuple-element.148), channel_id=1, source_target_pairs={{0,1},{1,0},{2,3},{3,2},{4,5},{5,4},{6,7},{7,6},{8,9},{9,8},{10,11... | collective-permute-start | bytes 2359304 | tf_op jit(solution)/shard_map/ppermute | solution.py:38
  106.6 19.8 %collective-permute-start.19 = (bf16[512,768]{1,0:T(8,128)(2,1)S(1)}, bf16[512,768]{1,0:T(8,128)(2,1)}, u32[]{:S(2)}, u32[]{:S(2)}) collective-permute-start(bf16[512,768]{1,0:T(8,128)(2,1)S(1)} %add_convert_fusion.4), channel_id=1, source_target_pairs={{0,2},{1,3},{2,0},{3,1},{4,6},{5,7},{6,4},{7,5},{8,10},{9,11},{10,... | collective-permute-start | bytes 2359304 | tf_op jit(solution)/shard_map/ppermute | solution.py:38
  108.4 14.4 %collective-permute-start.20 = (bf16[512,768]{1,0:T(8,128)(2,1)}, bf16[512,768]{1,0:T(8,128)(2,1)S(1)}, u32[]{:S(2)}, u32[]{:S(2)}) collective-permute-start(bf16[512,768]{1,0:T(8,128)(2,1)} %get-tuple-element.160), channel_id=1, source_target_pairs={{0,1},{1,0},{2,3},{3,2},{4,5},{5,4},{6,7},{7,6},{8,9},{9,8},{10,11... | collective-permute-start | bytes 2359304 | tf_op jit(solution)/shard_map/ppermute | solution.py:38
  120.9 28.7 %collective-permute-start.22 = (bf16[768,768]{1,0:T(8,128)(2,1)}, bf16[768,768]{1,0:T(8,128)(2,1)S(1)}, u32[]{:S(2)}, u32[]{:S(2)}) collective-permute-start(bf16[768,768]{1,0:T(8,128)(2,1)} %get-tuple-element.170), channel_id=1, source_target_pairs={{0,4},{4,0},{8,12},{12,8},{16,20},{20,16},{24,28},{28,24},{1,5},{5... | collective-permute-start | bytes 3538952 | tf_op jit(solution)/shard_map/ppermute | solution.py:38
  134.6 21.4 %collective-permute-start.27 = (bf16[512,192]{1,0:T(8,128)(2,1)}, bf16[512,192]{1,0:T(8,128)(2,1)}, u32[]{:S(2)}, u32[]{:S(2)}) collective-permute-start(bf16[512,192]{1,0:T(8,128)(2,1)} %get-tuple-element.180), channel_id=1, source_target_pairs={{0,1},{1,0},{2,3},{3,2},{4,5},{5,4},{6,7},{7,6},{8,9},{9,8},{10,11... | collective-permute-start | bytes 589832 | tf_op jit(solution)/shard_map/ppermute | solution.py:38
  142.1 14.0 %collective-permute-start.28 = (bf16[512,192]{1,0:T(8,128)(2,1)}, bf16[512,192]{1,0:T(8,128)(2,1)}, u32[]{:S(2)}, u32[]{:S(2)}) collective-permute-start(bf16[512,192]{1,0:T(8,128)(2,1)} %collective-permute-done.21), channel_id=1, source_target_pairs={{0,1},{1,0},{2,3},{3,2},{4,5},{5,4},{6,7},{7,6},{8,9},{9,8},{10,11... | collective-permute-start | bytes 589832 | tf_op jit(solution)/shard_map/ppermute | solution.py:38
  150.8 43.6 %collective-permute-start.24 = (bf16[512,768]{1,0:T(8,128)(2,1)S(1)}, bf16[512,768]{1,0:T(8,128)(2,1)}, u32[]{:S(2)}, u32[]{:S(2)}) collective-permute-start(bf16[512,768]{1,0:T(8,128)(2,1)S(1)} %add_convert_fusion.3), channel_id=1, source_target_pairs={{0,2},{1,3},{2,0},{3,1},{4,6},{5,7},{6,4},{7,5},{8,10},{9,11},{10,... | collective-permute-start | bytes 2359304 | tf_op jit(solution)/shard_map/ppermute | solution.py:38
  151.1 35.8 %collective-permute-start.25 = (bf16[192,768]{1,0:T(8,128)(2,1)}, bf16[192,768]{1,0:T(8,128)(2,1)}, u32[]{:S(2)}, u32[]{:S(2)}) collective-permute-start(bf16[192,768]{1,0:T(8,128)(2,1)} %get-tuple-element.238), channel_id=1, source_target_pairs={{0,8},{4,12},{8,0},{12,4},{16,24},{20,28},{24,16},{28,20},{1,9},{5... | collective-permute-start | bytes 884744 | tf_op jit(solution)/shard_map/ppermute | solution.py:38
  153.0 34.0 %collective-permute-start.30 = (bf16[192,768]{1,0:T(8,128)(2,1)}, bf16[192,768]{1,0:T(8,128)(2,1)}, u32[]{:S(2)}, u32[]{:S(2)}) collective-permute-start(bf16[192,768]{1,0:T(8,128)(2,1)} %get-tuple-element.239), channel_id=1, source_target_pairs={{0,24},{4,28},{8,16},{12,20},{16,8},{20,12},{24,0},{28,4},{1,25},{... | collective-permute-start | bytes 884744 | tf_op jit(solution)/shard_map/ppermute | solution.py:38
  156.1 30.9 %collective-permute-start.29 = (bf16[192,768]{1,0:T(8,128)(2,1)S(1)}, bf16[192,768]{1,0:T(8,128)(2,1)S(1)}, u32[]{:S(2)}, u32[]{:S(2)}) collective-permute-start(bf16[192,768]{1,0:T(8,128)(2,1)S(1)} %get-tuple-element.240), channel_id=1, source_target_pairs={{0,16},{4,20},{8,24},{12,28},{16,0},{20,4},{24,8},{28,12},{1,17},{... | collective-permute-start | bytes 884744 | tf_op jit(solution)/shard_map/ppermute | solution.py:38
  156.1 36.5 %collective-permute-start.35 = (bf16[192,768]{1,0:T(8,128)(2,1)}, bf16[192,768]{1,0:T(8,128)(2,1)}, u32[]{:S(2)}, u32[]{:S(2)}) collective-permute-start(bf16[192,768]{1,0:T(8,128)(2,1)} %add_convert_fusion.6), channel_id=1, source_target_pairs={{0,2},{1,3},{2,0},{3,1},{4,6},{5,7},{6,4},{7,5},{8,10},{9,11},{10,... | collective-permute-start | bytes 884744 | tf_op jit(solution)/shard_map/ppermute | solution.py:38
  188.1 21.9 %collective-permute-start.33 = (bf16[192,768]{1,0:T(8,128)(2,1)S(1)}, bf16[192,768]{1,0:T(8,128)(2,1)S(1)}, u32[]{:S(2)}, u32[]{:S(2)}) collective-permute-start(bf16[192,768]{1,0:T(8,128)(2,1)S(1)} %add_convert_fusion.7), channel_id=1, source_target_pairs={{0,24},{4,28},{8,16},{12,20},{16,8},{20,12},{24,0},{28,4},{1,25},{... | collective-permute-start | bytes 884744 | tf_op jit(solution)/shard_map/ppermute | solution.py:38
  189.6 26.2 %collective-permute-start.32 = (bf16[192,768]{1,0:T(8,128)(2,1)S(1)}, bf16[192,768]{1,0:T(8,128)(2,1)S(1)}, u32[]{:S(2)}, u32[]{:S(2)}) collective-permute-start(bf16[192,768]{1,0:T(8,128)(2,1)S(1)} %add_convert_fusion.7), channel_id=1, source_target_pairs={{0,16},{4,20},{8,24},{12,28},{16,0},{20,4},{24,8},{28,12},{1,17},{... | collective-permute-start | bytes 884744 | tf_op jit(solution)/shard_map/ppermute | solution.py:38
  191.7 24.1 %collective-permute-start.31 = (bf16[192,768]{1,0:T(8,128)(2,1)S(1)}, bf16[192,768]{1,0:T(8,128)(2,1)}, u32[]{:S(2)}, u32[]{:S(2)}) collective-permute-start(bf16[192,768]{1,0:T(8,128)(2,1)S(1)} %add_convert_fusion.7), channel_id=1, source_target_pairs={{0,8},{4,12},{8,0},{12,4},{16,24},{20,28},{24,16},{28,20},{1,9},{5... | collective-permute-start | bytes 884744 | tf_op jit(solution)/shard_map/ppermute | solution.py:38
  201.6 15.5 %collective-permute-start.36 = (bf16[392,768]{1,0:T(8,128)(2,1)}, bf16[392,768]{1,0:T(8,128)(2,1)S(1)}, u32[]{:S(2)}, u32[]{:S(2)}) collective-permute-start(bf16[392,768]{1,0:T(8,128)(2,1)} %get-tuple-element.202), channel_id=1, source_target_pairs={{0,4},{4,0},{8,12},{12,8},{16,20},{20,16},{24,28},{28,24},{1,5},{5... | collective-permute-start | bytes 1806344 | tf_op jit(solution)/shard_map/ppermute | solution.py:38
  218.4 16.3 %collective-permute-start.39 = (bf16[384,768]{1,0:T(8,128)(2,1)S(1)}, bf16[384,768]{1,0:T(8,128)(2,1)S(1)}, u32[]{:S(2)}, u32[]{:S(2)}) collective-permute-start(bf16[384,768]{1,0:T(8,128)(2,1)S(1)} %pad_maximum_fusion.rest_0_), channel_id=1, source_target_pairs={{0,4},{4,0},{8,12},{12,8},{16,20},{20,16},{24,28},{28,24},{1,5},{5... | collective-permute-start | bytes 1769480 | tf_op jit(solution)/shard_map/ppermute | solution.py:38
  220.7 14.0 %collective-permute-start.41 = (bf16[104,768]{1,0:T(8,128)(2,1)S(1)}, bf16[104,768]{1,0:T(8,128)(2,1)S(1)}, u32[]{:S(2)}, u32[]{:S(2)}) collective-permute-start(bf16[104,768]{1,0:T(8,128)(2,1)S(1)} %concatenate.24), channel_id=1, source_target_pairs={{0,24},{4,28},{8,16},{12,20},{16,8},{20,12},{24,0},{28,4},{1,25},{... | collective-permute-start | bytes 479240 | tf_op jit(solution)/shard_map/ppermute | solution.py:38
  223.3 13.1 %collective-permute-start.40 = (bf16[104,768]{1,0:T(8,128)(2,1)S(1)}, bf16[104,768]{1,0:T(8,128)(2,1)S(1)}, u32[]{:S(2)}, u32[]{:S(2)}) collective-permute-start(bf16[104,768]{1,0:T(8,128)(2,1)S(1)} %get-tuple-element.243), channel_id=1, source_target_pairs={{0,16},{4,20},{8,24},{12,28},{16,0},{20,4},{24,8},{28,12},{1,17},{... | collective-permute-start | bytes 479240 | tf_op jit(solution)/shard_map/ppermute | solution.py:38
  223.3 13.1 %collective-permute-start.38 = (bf16[104,768]{1,0:T(8,128)(2,1)S(1)}, bf16[104,768]{1,0:T(8,128)(2,1)S(1)}, u32[]{:S(2)}, u32[]{:S(2)}) collective-permute-start(bf16[104,768]{1,0:T(8,128)(2,1)S(1)} %get-tuple-element.244), channel_id=1, source_target_pairs={{0,8},{4,12},{8,0},{12,4},{16,24},{20,28},{24,16},{28,20},{1,9},{5... | collective-permute-start | bytes 479240 | tf_op jit(solution)/shard_map/ppermute | solution.py:38
  236.6 14.7 %collective-permute-start.43 = (bf16[384,768]{1,0:T(8,128)(2,1)S(1)}, bf16[384,768]{1,0:T(8,128)(2,1)S(1)}, u32[]{:S(2)}, u32[]{:S(2)}) collective-permute-start(bf16[384,768]{1,0:T(8,128)(2,1)S(1)} %constant_dynamic-update-slice_fusion.rest_1_), channel_id=1, source_target_pairs={{0,4},{4,0},{8,12},{12,8},{16,20},{20,16},{24,28},{28,24},{1,5},{5... | collective-permute-start | bytes 1769480 | tf_op jit(solution)/shard_map/ppermute | solution.py:38
  239.3 12.0 %collective-permute-start.44 = (bf16[96,768]{1,0:T(8,128)(2,1)S(1)}, bf16[96,768]{1,0:T(8,128)(2,1)S(1)}, u32[]{:S(2)}, u32[]{:S(2)}) collective-permute-start(bf16[96,768]{1,0:T(8,128)(2,1)S(1)} %add_convert_fusion.8), channel_id=1, source_target_pairs={{0,16},{4,20},{8,24},{12,28},{16,0},{20,4},{24,8},{28,12},{1,17},{... | collective-permute-start | bytes 442376 | tf_op jit(solution)/shard_map/ppermute | solution.py:38
  239.3 12.0 %collective-permute-start.42 = (bf16[96,768]{1,0:T(8,128)(2,1)S(1)}, bf16[96,768]{1,0:T(8,128)(2,1)S(1)}, u32[]{:S(2)}, u32[]{:S(2)}) collective-permute-start(bf16[96,768]{1,0:T(8,128)(2,1)S(1)} %add_convert_fusion.8), channel_id=1, source_target_pairs={{0,8},{4,12},{8,0},{12,4},{16,24},{20,28},{24,16},{28,20},{1,9},{5... | collective-permute-start | bytes 442376 | tf_op jit(solution)/shard_map/ppermute | solution.py:38
  242.0 19.4 %collective-permute-start.47 = (bf16[512,768]{1,0:T(8,128)(2,1)}, bf16[512,768]{1,0:T(8,128)(2,1)S(1)}, u32[]{:S(2)}, u32[]{:S(2)}) collective-permute-start(bf16[512,768]{1,0:T(8,128)(2,1)} %add_convert_fusion.2), channel_id=1, source_target_pairs={{0,2},{1,3},{2,0},{3,1},{4,6},{5,7},{6,4},{7,5},{8,10},{9,11},{10,... | collective-permute-start | bytes 2359304 | tf_op jit(solution)/shard_map/ppermute | solution.py:38
  252.3 14.5 %collective-permute-start.50 = (bf16[384,768]{1,0:T(8,128)(2,1)}, bf16[384,768]{1,0:T(8,128)(2,1)}, u32[]{:S(2)}, u32[]{:S(2)}) collective-permute-start(bf16[384,768]{1,0:T(8,128)(2,1)} %pad_maximum_fusion.1.rest_0_), channel_id=1, source_target_pairs={{0,4},{4,0},{8,12},{12,8},{16,20},{20,16},{24,28},{28,24},{1,5},{5... | collective-permute-start | bytes 1769480 | tf_op jit(solution)/shard_map/ppermute | solution.py:38
  (59 other events, 400.7 us)
